TPU v7x, 128 devices: a whole 4x4x4 slice. The times are simulated.
128 devices in a mesh: req: 8 (over x, core), exp: 16 (over y, z).
Axes of the slice: x: 4, y: 4, z: 4, core: 2. Of those that a mesh axis runs over, the one named last changes fastest.
Arguments:
- queries: bfloat16 [8192, 2048], P('req', 'exp'), may hold values from -6 to 6
- keys: bfloat16 [8192, 2048], P('req', 'exp'), may hold values from -15 to 15
- values: bfloat16 [8192, 2048], P('req', 'exp'), may hold values from -6 to 6
- prefix_keys: bfloat16 [4, 4096, 2048], P(None, 'req', 'exp'), may hold values from -15 to 15
- prefix_values: bfloat16 [4, 4096, 2048], P(None, 'req', 'exp'), may hold values from -6 to 6
- lengths: int32 [8, 8], P('req'), may hold values from 1 to 512, 1024 in all within a row
- groups: int32 [8, 8], P('req'), may hold values from 0 to 3
- residual: bfloat16 [8192, 2048], P(('req', 'exp')), may hold values from -6 to 6
- out_proj: bfloat16 [2048, 2048], P('exp'), may hold values from -0.125 to 0.125
- norm_gain: bfloat16 [2048], replicated, may hold values from 0.099609375 to 1.8984375
- expert_ids: int32 [8192, 4], P(('req', 'exp')), may hold values from 0 to 31, all different within a row; in each aligned block of 64 rows (0 to 63, 64 to 127, ...) at most 16 rows name the same one
- expert_gates: bfloat16 [8192, 4], P(('req', 'exp')), may hold values from 0.049804688 to 0.5
- w_gate: bfloat16 [32, 2048, 704], P('exp'), may hold values from -0.125 to 0.125
- w_up: bfloat16 [32, 2048, 704], P('exp'), may hold values from -0.125 to 0.125
- w_down: bfloat16 [32, 704, 2048], P('exp'), may hold values from -0.21875 to 0.21875
Outputs:
- layer_out: bfloat16 [8192, 2048], P(('req', 'exp'))
Inputs may be any that keep to these rules, and one draw needn't show every extreme that they name: The 8 lengths of a row sum to 1024; the longest request of each row has half of 1024 tokens. `expert_ids`: each row names 4 different experts. Among the 64 tokens of one device, no expert is named more than 16 times; on some device some expert is named exactly 16 times.
All inputs are finite; a program needn't handle non-finite values.
Results may differ from a plain program's by a relative error of at most 0.02.
Values may be sent and summed in bfloat16 or wider, within the bound.
A program may use at most 256 MiB of HBM per device.

v0:
```python
import math

import jax
import jax.numpy as jnp
from jax import lax
from jax.sharding import PartitionSpec as P

HEAD = 128
TOPK = 4
EXPERTS = 32
G = 4
RQ = 8
ROW_TOK = 1024


NEG = -1e30


def token_layout(lengths, groups):
    req_ends = jnp.cumsum(lengths, axis=-1)
    starts = req_ends - lengths
    position = jnp.arange(ROW_TOK, dtype=jnp.int32)
    request = jnp.sum((position[None, :, None] >= req_ends[:, None, :]).astype(jnp.int32), axis=-1)
    onehot = request[:, :, None] == jnp.arange(RQ, dtype=jnp.int32)[None, None, :]
    first_tok = jnp.sum(jnp.where(onehot, starts[:, None, :], 0), axis=-1)
    tok_group = jnp.sum(jnp.where(onehot, groups[:, None, :], 0), axis=-1)
    return (request, position[None, :] - first_tok, tok_group)


def split_blocks(row_count):
    if row_count % 1024 == 0 and row_count > 1024:
        return row_count // 1024
    return 1


def pack_parts(parts):
    return jnp.concatenate([parts[0], parts[1], parts[2]], axis=1)


def unpack_parts(packed, head_count):
    columns = head_count * HEAD
    return (
        packed[:, :columns],
        packed[:, columns : columns + head_count],
        packed[:, columns + head_count :],
    )


def attend_prefix(query_rows, query_group, prefix_k, prefix_v):
    row_count, columns = query_rows.shape
    head_count = columns // HEAD
    span = prefix_k.shape[1]
    key_grid = prefix_k.reshape(G, span, head_count, HEAD)
    val_grid = prefix_v.reshape(G, span, head_count, HEAD)
    blocks = split_blocks(row_count)
    block_len = row_count // blocks
    scaling = 1.0 / math.sqrt(HEAD)

    def per_block(pieces):
        block_q, block_g = pieces
        query_grid = block_q.reshape(block_len, head_count, HEAD)
        scores = (
            jnp.einsum("qhd,gkhd->hqgk", query_grid, key_grid, preferred_element_type=jnp.float32)
            * scaling
        )
        member = block_g[:, None] == jnp.arange(G, dtype=jnp.int32)[None, :]
        scores = jnp.where(member[None, :, :, None], scores, NEG)
        maxima = jnp.max(scores, axis=(2, 3))
        exp_terms = jnp.exp(scores - maxima[:, :, None, None])
        totals = jnp.sum(exp_terms, axis=(2, 3))
        weighted = jnp.einsum(
            "hqgk,gkhd->qhd",
            exp_terms.astype(jnp.bfloat16),
            val_grid,
            preferred_element_type=jnp.float32,
        )
        return (weighted.reshape(block_len, columns), maxima.T, totals.T)

    weighted, maxima, totals = lax.map(
        per_block,
        (query_rows.reshape(blocks, block_len, columns), query_group.reshape(blocks, block_len)),
    )
    return (
        weighted.reshape(row_count, columns),
        maxima.reshape(row_count, head_count),
        totals.reshape(row_count, head_count),
    )


def attend_suffix(queries, keys, values, request, position):
    row_count, columns = queries.shape
    head_count = columns // HEAD
    blocks = split_blocks(row_count)
    block_len = row_count // blocks
    scaling = 1.0 / math.sqrt(HEAD)
    key_grid = keys.reshape(row_count, head_count, HEAD)
    val_grid = values.reshape(row_count, head_count, HEAD)

    def per_block(pieces):
        block_q, block_req, block_pos = pieces
        query_grid = block_q.reshape(block_len, head_count, HEAD)
        scores = (
            jnp.einsum("qhd,khd->hqk", query_grid, key_grid, preferred_element_type=jnp.float32)
            * scaling
        )
        allowed = (request[None, :] == block_req[:, None]) & (
            position[None, :] <= block_pos[:, None]
        )
        scores = jnp.where(allowed[None, :, :], scores, NEG)
        maxima = jnp.max(scores, axis=2)
        exp_terms = jnp.exp(scores - maxima[:, :, None])
        totals = jnp.sum(exp_terms, axis=2)
        weighted = jnp.einsum(
            "hqk,khd->qhd",
            exp_terms.astype(jnp.bfloat16),
            val_grid,
            preferred_element_type=jnp.float32,
        )
        return (weighted.reshape(block_len, columns), maxima.T, totals.T)

    weighted, maxima, totals = lax.map(
        per_block,
        (
            queries.reshape(blocks, block_len, columns),
            request.reshape(blocks, block_len),
            position.reshape(blocks, block_len),
        ),
    )
    return (
        weighted.reshape(row_count, columns),
        maxima.reshape(row_count, head_count),
        totals.reshape(row_count, head_count),
    )


def combine(former, latter):
    weighted_a, maxima_a, totals_a = former
    weighted_b, maxima_b, totals_b = latter
    row_count, head_count = maxima_a.shape
    maxima = jnp.maximum(maxima_a, maxima_b)
    factor_a = jnp.exp(maxima_a - maxima)
    factor_b = jnp.exp(maxima_b - maxima)
    weighted = (
        weighted_a.reshape(row_count, head_count, HEAD) * factor_a[:, :, None]
        + weighted_b.reshape(row_count, head_count, HEAD) * factor_b[:, :, None]
    )
    return (
        weighted.reshape(row_count, head_count * HEAD),
        maxima,
        totals_a * factor_a + totals_b * factor_b,
    )


def per_device(
    queries,
    keys,
    values,
    prefix_keys,
    prefix_values,
    lengths,
    groups,
    residual,
    out_proj,
    norm_gain,
    expert_ids,
    expert_gates,
    w_gate,
    w_up,
    w_down,
):
    row_tok, columns = queries.shape
    head_count = columns // HEAD
    tok_dev = residual.shape[0]
    request, position, tok_group = token_layout(lengths, groups)
    request, position, tok_group = (request[0], position[0], tok_group[0])
    all_groups = lax.all_gather(tok_group, "req", axis=0, tiled=True)
    partial_value = pack_parts(
        attend_prefix(
            lax.all_gather(queries, "req", axis=0, tiled=True),
            all_groups,
            prefix_keys,
            prefix_values,
        )
    )
    returned = lax.all_to_all(partial_value, "req", split_axis=0, concat_axis=0, tiled=True)
    owners = returned.shape[0] // row_tok
    back_w, back_m, back_t = unpack_parts(returned, head_count)
    all_weighted = back_w.reshape(owners, row_tok, head_count, HEAD)
    all_maxima = back_m.reshape(owners, row_tok, head_count)
    all_totals = back_t.reshape(owners, row_tok, head_count)
    maxima = jnp.max(all_maxima, axis=0)
    factor = jnp.exp(all_maxima - maxima[None])
    weighted = jnp.sum(all_weighted * factor[..., None], axis=0).reshape(row_tok, columns)
    prefix_part = (weighted, maxima, jnp.sum(all_totals * factor, axis=0))
    suffix_part = attend_suffix(queries, keys, values, request, position)
    weighted, maxima, totals = combine(prefix_part, suffix_part)
    attended = (
        (weighted.reshape(row_tok, head_count, HEAD) / totals[:, :, None])
        .reshape(row_tok, columns)
        .astype(jnp.bfloat16)
    )
    projected = lax.psum_scatter(
        jnp.dot(attended, out_proj, preferred_element_type=jnp.float32),
        "exp",
        scatter_dimension=0,
        tiled=True,
    )
    stream = residual.astype(jnp.float32) + projected
    meansq = jnp.mean(stream * stream, axis=-1, keepdims=True)
    normed = (stream * lax.rsqrt(meansq + 1e-06) * norm_gain.astype(jnp.float32)).astype(
        jnp.bfloat16
    )
    capacity = max(2, tok_dev // 4)
    flat_ids = expert_ids.reshape(-1)
    onehot = (flat_ids[:, None] == jnp.arange(EXPERTS, dtype=jnp.int32)[None, :]).astype(jnp.int32)
    slot_of = jnp.sum(onehot * (jnp.cumsum(onehot, axis=0) - 1), axis=1)
    source_rows = jnp.arange(tok_dev * TOPK, dtype=jnp.int32) // TOPK
    buffer = (
        jnp.zeros((EXPERTS, capacity, normed.shape[1]), jnp.bfloat16)
        .at[flat_ids, slot_of]
        .set(normed[source_rows])
    )
    exp_count = lax.axis_size("exp")
    exp_dev = w_gate.shape[0]
    received = lax.all_to_all(buffer, "exp", split_axis=0, concat_axis=0, tiled=True)
    slots = received.shape[1]
    grid_in = received.reshape(exp_count, exp_dev, slots, received.shape[2])
    gate_h = jnp.einsum("secd,edf->secf", grid_in, w_gate, preferred_element_type=jnp.float32)
    up_h = jnp.einsum("secd,edf->secf", grid_in, w_up, preferred_element_type=jnp.float32)
    hidden = (jax.nn.silu(gate_h) * up_h).astype(jnp.bfloat16)
    expert_out = jnp.einsum("secf,efd->secd", hidden, w_down, preferred_element_type=jnp.float32)
    returned = lax.all_to_all(
        expert_out.reshape(EXPERTS, slots, received.shape[2]),
        "exp",
        split_axis=0,
        concat_axis=0,
        tiled=True,
    )
    gathered = returned[flat_ids, slot_of] * expert_gates.reshape(-1).astype(jnp.float32)[:, None]
    mixture = jnp.sum(gathered.reshape(tok_dev, TOPK, gathered.shape[1]), axis=1)
    return (stream + mixture).astype(jnp.bfloat16)


def solution(mesh):
    in_specs = (
        P("req", "exp"),
        P("req", "exp"),
        P("req", "exp"),
        P(None, "req", "exp"),
        P(None, "req", "exp"),
        P("req", None),
        P("req", None),
        P(("req", "exp"), None),
        P("exp", None),
        P(),
        P(("req", "exp"), None),
        P(("req", "exp"), None),
        P("exp", None, None),
        P("exp", None, None),
        P("exp", None, None),
    )
    out_specs = P(("req", "exp"), None)
    return jax.shard_map(
        per_device, mesh=mesh, in_specs=in_specs, out_specs=out_specs, check_vma=False
    )
```

profile of v0, /device:TPU:0, one launch (start us, length us, event | category | flops | bytes accessed | tf_op | source)
XLA Modules:
  0.0 431.8 jit_solution(6236507258747720294)
XLA Ops:
  6.5 0.7 all-gather.2.cloned.1.call-update
  7.3 0.8 reduce_window_sum.24
  8.2 0.7 subtract_bitcast_fusion
  8.9 0.7 select_reduce_fusion.1
  9.6 13.3 %all_gather.6 = s32[8192]{0:T(1024)S(1)} all-gather(s32[1024]{0:T(1024)S(1)} %get-tuple-element.81), channel_id=1, replica_groups=mesh['req'=8,'exp'=16] {'req'}, dimensions={0}, use_global_device_ids=true | all-gather | bytes 36864 | tf_op jit(solution)/shard_map/all_gather | solution.py:176
  22.9 13.8 %all-gather.2.cloned.1.call-done = bf16[8192,128]{1,0:T(8,128)(2,1)} async-done(((bf16[1024,128]{1,0:T(8,128)(2,1)}), bf16[8192,128]{1,0:T(8,128)(2,1)}) %all-gather.2.cloned.1.call-update) | async-done | bytes 2097168 | tf_op jit(solution)/shard_map/all_gather | solution.py:179
  36.7 55.2 %while.2 = (s32[]{:T(128)}, f32[8,1024,128]{1,2,0:T(8,128)}, f32[8,1024,1]{1,2,0:T(1,128)S(1)}, f32[8,1024,1]{1,2,0:T(1,128)S(1)}, s32[8,1024]{1,0:T(8,128)S(1)}...) while((s32[]{:T(128)}, f32[8,1024,128]{1,2,0:T(8,128)}, ...), condition=%wide.region_6.7_spmd, body=%wide.region_3.6_spmd.sunk | while | flops 1096812544 | bytes 29160576 | solution.py:79
  36.7 2.4 fusion.99
  39.1 1.7 fusion.101
  40.9 2.7 fusion.100
  43.6 2.4 fusion.99
  46.0 1.7 fusion.101
  47.7 2.7 fusion.100
  50.5 2.4 fusion.99
  52.9 1.7 fusion.101
  54.7 2.8 fusion.100
  57.4 2.4 fusion.99
  59.8 1.7 fusion.101
  61.6 2.7 fusion.100
  64.3 2.4 fusion.99
  66.7 1.7 fusion.101
  68.5 2.7 fusion.100
  71.2 2.4 fusion.99
  73.6 1.7 fusion.101
  75.4 2.7 fusion.100
  78.1 2.4 fusion.99
  80.5 1.7 fusion.101
  82.3 2.7 fusion.100
  85.0 2.4 fusion.99
  87.4 1.7 fusion.101
  89.2 2.8 fusion.100
  91.9 4.9 %pad_maximum_fusion = f32[8,1024,130]{1,2,0:T(8,128)} fusion(f32[8,1024,1]{1,2,0:T(1,128)S(1)} %get-tuple-element.78, f32[8,1024,1]{1,2,0:T(1,128)S(1)} %get-tuple-element.77, f32[8,1024,128]{1,2,0:T(8,128)} %get-tuple-element.76), kind=kLoop, calls=%fused_computation.30 | loop fusion | flops 2129920 | bytes 8519680 | tf_op jit(solution)/shard_map/concatenate | solution.py:37
  96.9 4.7 %all-to-all-start = ((f32[8,1024,130]{1,2,0:T(8,128)}), f32[8,1024,130]{1,2,0:T(8,128)}, u32[]{:S(2)}, u32[]{:S(2)}) async-start(f32[8,1024,130]{1,2,0:T(8,128)} %pad_maximum_fusion), calls=%async_computation | async-start | bytes 8912896 | tf_op jit(solution)/shard_map/all_to_all | solution.py:185
  101.6 0.5 reduce-scatter.2.cloned.1.call-start
  102.1 1.1 fusion.87
  103.2 2.0 copy-done.1
  105.2 0.6 fusion.27
  105.8 48.2 %all-to-all-done = f32[8,1024,130]{1,2,0:T(8,128)} async-done(((f32[8,1024,130]{1,2,0:T(8,128)}), f32[8,1024,130]{1,2,0:T(8,128)}, u32[]{:S(2)}, u32[]{:S(2)}) %all-to-all-start) | async-done | bytes 4259872 | tf_op jit(solution)/shard_map/all_to_all | solution.py:185
  154.1 4.7 %copy.101 = f32[8,1024,130]{1,0,2:T(8,128)S(1)} copy(f32[8,1024,130]{1,2,0:T(8,128)} %all-to-all-done) | data formatting | bytes 8519680 | tf_op jit(solution)/shard_map/all_to_all | solution.py:185
  158.8 0.3 pad.4
  159.1 3.9 copy.89
  163.2 2.3 slice.26
  165.6 5.6 %copy.90 = f32[16,8,8,1024]{3,2,1,0:T(8,128)S(1)} copy(f32[16,8,8,1024]{3,1,2,0:T(8,128)} %bitcast.182) | data formatting | bytes 8388608
  171.2 1.5 fusion.26
  173.0 8.2 %fusion.71 = f32[1024,2048]{1,0:T(8,128)} fusion(bf16[128,2048]{1,0:T(8,128)(2,1)S(1)} %copy-done, bf16[1024,128]{1,0:T(8,128)(2,1)S(1)} %copy-done.5, f32[1024,1024]{0,1:T(8,128)} %copy-done.1, f32[1024]{0:T(1024)S(1)} %get-tuple-element.109, f32[1024,128]{1,0:T(8,128)S(1)} %copy.68, f32[1024]{0:T(1024)S(1)} %get-tuple-element.99, ...), kind=kOutput, calls=%fused_computation.58 | convolution fusion | flops 808058880 | bytes 13910016 | tf_op jit(solution)/shard_map/dot_general | solution.py:203
  181.2 0.7 copy-done.8
  182.3 0.6 reduce-window.6
  183.3 82.6 %reduce-scatter.2.cloned.1.call-done = f32[64,2048]{1,0:T(8,128)} async-done(((f32[1024,2048]{1,0:T(8,128)}), f32[64,2048]{1,0:T(8,128)}) %reduce-scatter.2.cloned.1.call-update) | async-done | bytes 524304 | tf_op jit(solution)/shard_map/reduce_scatter | solution.py:202
  265.9 1.2 multiply_reduce_fusion.1
  267.1 1.2 multiply_convert_fusion
  268.3 2.3 gather_fusion
  270.6 0.2 broadcast_in_dim.105
  270.9 33.3 %scatter_fusion = bf16[32,16,2048]{2,1,0:T(8,128)(2,1)S(1)} fusion(bf16[32,16,2048]{2,1,0:T(8,128)(2,1)S(1)} %broadcast_in_dim.105, s32[256]{0:T(256)S(1)} %bitcast.180, bf16[256,2048]{1,0:T(8,128)(2,1)} %gather_fusion), kind=kCustom, calls=%fused_computation.2 | custom fusion | bytes 3147776 | tf_op jit(solution)/shard_map/scatter | solution.py:221
  304.1 32.2 %all_to_all.19 = bf16[32,16,2048]{2,1,0:T(8,128)(2,1)S(1)} all-to-all(bf16[32,16,2048]{2,1,0:T(8,128)(2,1)S(1)} %scatter_fusion), channel_id=1, replica_groups=mesh['req'=8,'exp'=16] {'exp'}, dimensions={0} | all-to-all | bytes 4194304 | tf_op jit(solution)/shard_map/all_to_all | solution.py:225
  336.3 1.3 copy-done.4
  337.7 4.5 %fusion.24 = f32[2,16,16,704]{3,2,1,0:T(8,128)S(1)} fusion(bf16[2,2048,704]{1,2,0:T(8,128)(2,1)} %param.29, bf16[16,2,16,2048]{3,2,1,0:T(8,128)(2,1)S(1)} %bitcast.184), kind=kOutput, calls=%fused_computation.28 | convolution fusion | flops 1476395008 | bytes 9306112 | tf_op jit(solution)/shard_map/secd,edf->secf/dot_general | solution.py:228
  342.1 10.6 %fusion.29 = f32[16,2,16,2048]{3,2,0,1:T(8,128)} fusion(bf16[2,704,2048]{2,1,0:T(8,128)(2,1)} %param.31, f32[2,16,16,704]{3,2,1,0:T(8,128)S(1)} %fusion.24, bf16[2,2048,704]{1,2,0:T(8,128)(2,1)} %param.30, bf16[16,2,16,2048]{3,2,1,0:T(8,128)(2,1)} %bitcast.185), kind=kOutput, calls=%fused_computation.38 | convolution fusion | flops 2954952704 | bytes 19267584 | tf_op jit(solution)/shard_map/secf,efd->secd/dot_general | solution.py:231
  352.7 4.7 %copy.75 = f32[16,2,16,2048]{3,2,1,0:T(8,128)} copy(f32[16,2,16,2048]{3,2,0,1:T(8,128)} %fusion.29) | data formatting | bytes 8388608 | tf_op jit(solution)/shard_map/secf,efd->secd/transpose | solution.py:231
  357.4 4.7 %all-to-all-start.2 = ((f32[32,16,2048]{2,1,0:T(8,128)}), f32[32,16,2048]{2,1,0:T(8,128)}, u32[]{:S(2)}, u32[]{:S(2)}) async-start(f32[32,16,2048]{2,1,0:T(8,128)} %bitcast.183), calls=%async_computation.3 | async-start | bytes 8388608 | tf_op jit(solution)/shard_map/all_to_all | solution.py:232
  362.2 52.8 %all-to-all-done.2 = f32[32,16,2048]{2,1,0:T(8,128)} async-done(((f32[32,16,2048]{2,1,0:T(8,128)}), f32[32,16,2048]{2,1,0:T(8,128)}, u32[]{:S(2)}, u32[]{:S(2)}) %all-to-all-start.2) | async-done | bytes 4194336 | tf_op jit(solution)/shard_map/all_to_all | solution.py:232
  415.0 4.0 gather_fusion.1
  419.0 1.7 gather.10
  420.7 3.2 multiply_reduce_fusion
  423.9 0.8 add_convert_fusion
  (91 shorter events, 1.8 us)
Async XLA Ops:
  6.5 166.4 %copy-start = (bf16[128,2048]{1,0:T(8,128)(2,1)S(1)}, bf16[128,2048]{1,0:T(8,128)(2,1)}, u32[]{:S(2)}) copy-start(bf16[128,2048]{1,0:T(8,128)(2,1)} %param.25) | copy-start | bytes 1572868
  6.5 30.2 %all-gather.2.cloned.1.call-start = ((), (), s32[]{:S(2)}) async-start(), calls=%async_computation.4 | async-start | bytes 2359296 | tf_op jit(solution)/shard_map/all_gather | solution.py:179
  39.1 1.7 copy-start.10
  46.0 1.7 copy-start.10
  52.9 1.7 copy-start.10
  59.8 1.7 copy-start.10
  66.7 1.7 copy-start.10
  73.6 1.7 copy-start.10
  80.5 1.7 copy-start.10
  87.4 1.7 copy-start.10
  96.9 5.2 %copy-start.6 = (bf16[1024,128]{1,0:T(8,128)(2,1)S(1)}, bf16[1024,128]{1,0:T(8,128)(2,1)}, u32[]{:S(2)}) copy-start(bf16[1024,128]{1,0:T(8,128)(2,1)} %param.17) | copy-start | bytes 786436
  96.9 5.3 %copy-start.11 = (bf16[1024,128]{1,0:T(8,128)(2,1)S(1)}, bf16[1024,128]{1,0:T(8,128)(2,1)}, u32[]{:S(2)}) copy-start(bf16[1024,128]{1,0:T(8,128)(2,1)} %param.18) | copy-start | bytes 786436
  96.9 57.2 %all-to-all-start = ((f32[8,1024,130]{1,2,0:T(8,128)}), f32[8,1024,130]{1,2,0:T(8,128)}, u32[]{:S(2)}, u32[]{:S(2)}) async-start(f32[8,1024,130]{1,2,0:T(8,128)} %pad_maximum_fusion), calls=%async_computation | async-start | bytes 8912896 | tf_op jit(solution)/shard_map/all_to_all | solution.py:185
  101.6 164.3 %reduce-scatter.2.cloned.1.call-start = ((), (), s32[]{:S(2)}) async-start(), calls=%async_computation.5 | async-start | bytes 8912896 | tf_op jit(solution)/shard_map/reduce_scatter | solution.py:202
  103.2 2.0 copy-start.1
  171.2 1.7 copy-start.5
  181.2 0.7 copy-start.8
  181.2 1.1 copy-start.7
  181.2 84.7 %copy-start.3 = (bf16[64,2048]{1,0:T(8,128)(2,1)S(1)}, bf16[64,2048]{1,0:T(8,128)(2,1)}, u32[]{:S(2)}) copy-start(bf16[64,2048]{1,0:T(8,128)(2,1)} %param.24) | copy-start | bytes 786436
  336.3 1.3 copy-start.4
  357.4 4.7 %copy-start.9 = (bf16[64,4]{0,1:T(4,128)(2,1)S(1)}, bf16[64,4]{0,1:T(4,128)(2,1)}, u32[]{:S(2)}) copy-start(bf16[64,4]{0,1:T(4,128)(2,1)} %param.28) | copy-start | bytes 1540
  357.4 57.6 %all-to-all-start.2 = ((f32[32,16,2048]{2,1,0:T(8,128)}), f32[32,16,2048]{2,1,0:T(8,128)}, u32[]{:S(2)}, u32[]{:S(2)}) async-start(f32[32,16,2048]{2,1,0:T(8,128)} %bitcast.183), calls=%async_computation.3 | async-start | bytes 8388608 | tf_op jit(solution)/shard_map/all_to_all | solution.py:232
  419.0 4.9 %copy-start.2 = (f32[64,2048]{1,0:T(8,128)S(1)}, f32[64,2048]{1,0:T(8,128)}, u32[]{:S(2)}) copy-start(f32[64,2048]{1,0:T(8,128)} %reduce-scatter.2.cloned.1.call-done) | copy-start | bytes 1572868
Sparse Core Ops, SparseCore 0:
  9.1 27.5 all-gather.1
  181.3 84.5 reduce-scatter.1
where the time goes:
time: 438 us; the launch traced here: 432 us
  waiting for transfers between devices  198 us (45%)
  local copies, waits for them, and re-layouts  68.4 us (16%)
  matrix products  65.3 us (15%)
  blocking collectives  45.4 us (10%)
  other arithmetic  30.3 us (7%)
  between operations  14 us (3%)
  starting transfers between devices  9.88 us (2%)
    reduce_scatter x1, waiting for transfers between devices, per_device(): lax.psum_scatter(jnp.dot(attended, out_proj, preferred_element_type=jnp.f...  82.6 us
    all_to_all x1, waiting for transfers between devices, per_device(): lax.all_to_all(expert_out.reshape(EXPERTS, slots, received.shape[2]), 'ex...  52.8 us
    all_to_all x1, waiting for transfers between devices, per_device(): lax.all_to_all(partial_value, 'req', split_axis=0, concat_axis=0, tiled=T...  48.2 us
    scatter x1, local copies, waits for them, and re-layouts, per_device(): buffer = jnp.zeros((EXPERTS, capacity, normed.shape[1]), jnp.bfloat16).at...  33.3 us
    all_to_all x1, blocking collectives, per_device(): lax.all_to_all(buffer, 'exp', split_axis=0, concat_axis=0, tiled=True)  32.2 us
    dot_general x8, matrix products, per_block(): jnp.einsum('hqgk,gkhd->qhd', exp_terms.astype(jnp.bfloat16), val_grid, pr...  21.9 us
    dot_general x8, matrix products, per_block(): jnp.einsum('qhd,gkhd->hqgk', query_grid, key_grid, preferred_element_type...  19.1 us
    unnamed x26, local copies, waits for them, and re-layouts  13.9 us
  transfers between devices with their start and end apart: 4, of which 4 were waited for; matrix products, arithmetic and copies ran while one was open for 1% of the time, Pallas kernels for 0%

commit v1 on v0

--- a/solution.py
+++ b/solution.py
@@ -199,28 +199,26 @@
         .reshape(row_tok, columns)
         .astype(jnp.bfloat16)
     )
-    projected = lax.psum_scatter(
-        jnp.dot(attended, out_proj, preferred_element_type=jnp.float32),
-        "exp",
-        scatter_dimension=0,
-        tiled=True,
-    )
+    exp_count = lax.axis_size("exp")
+    full_proj = lax.all_gather(out_proj, "exp", axis=0, tiled=True)
+    token_rows = lax.all_to_all(attended, "exp", split_axis=0, concat_axis=1, tiled=True)
+    projected = jnp.dot(token_rows, full_proj, preferred_element_type=jnp.float32)
     stream = residual.astype(jnp.float32) + projected
     meansq = jnp.mean(stream * stream, axis=-1, keepdims=True)
     normed = (stream * lax.rsqrt(meansq + 1e-06) * norm_gain.astype(jnp.float32)).astype(
         jnp.bfloat16
     )
     capacity = max(2, tok_dev // 4)
+    slot_count = EXPERTS * capacity
     flat_ids = expert_ids.reshape(-1)
     onehot = (flat_ids[:, None] == jnp.arange(EXPERTS, dtype=jnp.int32)[None, :]).astype(jnp.int32)
     slot_of = jnp.sum(onehot * (jnp.cumsum(onehot, axis=0) - 1), axis=1)
-    source_rows = jnp.arange(tok_dev * TOPK, dtype=jnp.int32) // TOPK
-    buffer = (
-        jnp.zeros((EXPERTS, capacity, normed.shape[1]), jnp.bfloat16)
-        .at[flat_ids, slot_of]
-        .set(normed[source_rows])
-    )
-    exp_count = lax.axis_size("exp")
+    dest = flat_ids * capacity + slot_of
+    dest_hot = dest[:, None] == jnp.arange(slot_count, dtype=jnp.int32)[None, :]
+    select = jnp.sum(dest_hot.reshape(tok_dev, TOPK, slot_count).astype(jnp.float32), axis=1)
+    buffer = jnp.dot(
+        select.T.astype(jnp.bfloat16), normed, preferred_element_type=jnp.float32
+    ).astype(jnp.bfloat16).reshape(EXPERTS, capacity, normed.shape[1])
     exp_dev = w_gate.shape[0]
     received = lax.all_to_all(buffer, "exp", split_axis=0, concat_axis=0, tiled=True)
     slots = received.shape[1]
@@ -230,14 +228,19 @@
     hidden = (jax.nn.silu(gate_h) * up_h).astype(jnp.bfloat16)
     expert_out = jnp.einsum("secf,efd->secd", hidden, w_down, preferred_element_type=jnp.float32)
     returned = lax.all_to_all(
-        expert_out.reshape(EXPERTS, slots, received.shape[2]),
+        expert_out.astype(jnp.bfloat16).reshape(EXPERTS, slots, received.shape[2]),
         "exp",
         split_axis=0,
         concat_axis=0,
         tiled=True,
     )
-    gathered = returned[flat_ids, slot_of] * expert_gates.reshape(-1).astype(jnp.float32)[:, None]
-    mixture = jnp.sum(gathered.reshape(tok_dev, TOPK, gathered.shape[1]), axis=1)
+    gates = expert_gates.astype(jnp.float32).reshape(tok_dev, TOPK, 1)
+    weights = jnp.sum(dest_hot.reshape(tok_dev, TOPK, slot_count).astype(jnp.float32) * gates, axis=1)
+    mixture = jnp.dot(
+        weights.astype(jnp.bfloat16),
+        returned.reshape(slot_count, received.shape[2]),
+        preferred_element_type=jnp.float32,
+    )
     return (stream + mixture).astype(jnp.bfloat16)
 
 

time: 438 us -> 289 us (0.66); the launches traced: 432 us -> 288 us
  waiting for transfers between devices: 198 us -> 69.9 us
  local copies, waits for them, and re-layouts: 68.4 us -> 24.2 us
  blocking collectives: 45.4 us -> 73 us
    reduce_scatter x1 -> x0, waiting for transfers between devices: 82.6 us -> none  [per_device(): lax.psum_scatter(jnp.dot(attended, out_proj, preferred_element_type=jnp.f...]
    all_to_all x1, waiting for transfers between devices: 52.8 us -> 8.34 us  [per_device(): lax.all_to_all(attended, 'exp', split_axis=0, concat_axis=1, tiled=True)]
    scatter x1 -> x0, local copies, waits for them, and re-layouts: 33.3 us -> none  [per_device(): buffer = jnp.zeros((EXPERTS, capacity, normed.shape[1]), jnp.bfloat16).at...]
    all_to_all x0 -> x1, blocking collectives: none -> 29.5 us  [per_device(): lax.all_to_all(expert_out.astype(jnp.bfloat16).reshape(EXPERTS, slots, re...]
    gather x3 -> x0, local copies, waits for them, and re-layouts: 8.06 us -> none  [the longest x2 5.71 us: per_device(): returned[flat_ids, slot_of]]
    transpose x1 -> x0, local copies, waits for them, and re-layouts: 4.65 us -> none  [per_device(): jnp.einsum('secf,efd->secd', hidden, w_down, preferred_element_type=jnp.f...]
    dot_general x1 -> x4, matrix products: 8.18 us -> 11 us  [the longest x1 5.07 us: per_device(): jnp.dot(token_rows, full_proj, preferred_element_type=jnp.float32)]
    unnamed x26 -> x20, local copies, waits for them, and re-layouts: 13.9 us -> 14.2 us
  transfers between devices with their start and end apart: 4 -> 4, of which waited for: 4 -> 3; matrix products, arithmetic and copies ran while one was open for 1% -> 32% of each run, Pallas kernels for 0% -> 0%
where the time goes in v1:
time: 289 us; the launch traced here: 288 us
  blocking collectives  73 us (25%)
  waiting for transfers between devices  69.9 us (24%)
  matrix products  68.5 us (24%)
  other arithmetic  26.5 us (9%)
  local copies, waits for them, and re-layouts  24.2 us (8%)
  between operations  13.7 us (5%)
  starting transfers between devices  11.9 us (4%)
    all_to_all x1, waiting for transfers between devices, per_device(): lax.all_to_all(partial_value, 'req', split_axis=0, concat_axis=0, tiled=T...  47.1 us
    all_to_all x1, blocking collectives, per_device(): lax.all_to_all(buffer, 'exp', split_axis=0, concat_axis=0, tiled=True)  30.3 us
    all_to_all x1, blocking collectives, per_device(): lax.all_to_all(expert_out.astype(jnp.bfloat16).reshape(EXPERTS, slots, re...  29.5 us
    dot_general x8, matrix products, per_block(): jnp.einsum('hqgk,gkhd->qhd', exp_terms.astype(jnp.bfloat16), val_grid, pr...  22 us
    dot_general x8, matrix products, per_block(): jnp.einsum('qhd,gkhd->hqgk', query_grid, key_grid, preferred_element_type...  19.1 us
    unnamed x20, local copies, waits for them, and re-layouts  14.2 us
    reduce_sum x8, other arithmetic, per_block(): totals = jnp.sum(exp_terms, axis=(2, 3))  13.7 us
    all_gather x1, blocking collectives, per_device(): all_groups = lax.all_gather(tok_group, 'req', axis=0, tiled=True)  13.3 us
  transfers between devices with their start and end apart: 4, of which 3 were waited for; matrix products, arithmetic and copies ran while one was open for 32% of the time, Pallas kernels for 0%

profile of v1, /device:TPU:0, one launch (start us, length us, event | category | flops | bytes accessed | tf_op | source)
XLA Modules:
  0.0 288.0 jit_solution(15104359768345971016)
XLA Ops:
  6.5 0.7 all-gather.3.cloned.1.call-update
  7.3 0.7 all-gather.5.cloned.1.call-update
  8.0 0.8 reduce_window_sum.24
  8.9 0.7 subtract_bitcast_fusion
  9.6 0.8 select_reduce_fusion.2
  10.4 13.3 %all_gather.9 = s32[8192]{0:T(1024)S(1)} all-gather(s32[1024]{0:T(1024)S(1)} %get-tuple-element.81), channel_id=1, replica_groups=mesh['req'=8,'exp'=16] {'req'}, dimensions={0}, use_global_device_ids=true | all-gather | bytes 36864 | tf_op jit(solution)/shard_map/all_gather | solution.py:176
  23.6 13.1 %all-gather.3.cloned.1.call-done = bf16[8192,128]{1,0:T(8,128)(2,1)} async-done(((bf16[1024,128]{1,0:T(8,128)(2,1)}), bf16[8192,128]{1,0:T(8,128)(2,1)}) %all-gather.3.cloned.1.call-update) | async-done | bytes 2097168 | tf_op jit(solution)/shard_map/all_gather | solution.py:179
  36.7 55.3 %while.2 = (s32[]{:T(128)}, f32[8,1024,128]{1,2,0:T(8,128)}, f32[8,1024,1]{1,2,0:T(1,128)S(1)}, f32[8,1024,1]{1,2,0:T(1,128)S(1)}, s32[8,1024]{1,0:T(8,128)S(1)}...) while((s32[]{:T(128)}, f32[8,1024,128]{1,2,0:T(8,128)}, ...), condition=%wide.region_6.7_spmd, body=%wide.region_3.6_spmd.sunk | while | flops 1096812544 | bytes 29160576 | solution.py:79
  36.7 2.4 fusion.102
  39.1 1.7 fusion.104
  40.9 2.8 fusion.103
  43.6 2.4 fusion.102
  46.1 1.7 fusion.104
  47.8 2.7 fusion.103
  50.5 2.4 fusion.102
  53.0 1.7 fusion.104
  54.7 2.7 fusion.103
  57.5 2.4 fusion.102
  59.9 1.7 fusion.104
  61.6 2.7 fusion.103
  64.3 2.4 fusion.102
  66.8 1.7 fusion.104
  68.5 2.7 fusion.103
  71.2 2.4 fusion.102
  73.6 1.7 fusion.104
  75.4 2.8 fusion.103
  78.2 2.4 fusion.102
  80.6 1.7 fusion.104
  82.3 2.8 fusion.103
  85.1 2.4 fusion.102
  87.5 1.7 fusion.104
  89.2 2.8 fusion.103
  92.0 4.9 %pad_maximum_fusion = f32[8,1024,130]{1,2,0:T(8,128)} fusion(f32[8,1024,1]{1,2,0:T(1,128)S(1)} %get-tuple-element.78, f32[8,1024,1]{1,2,0:T(1,128)S(1)} %get-tuple-element.77, f32[8,1024,128]{1,2,0:T(8,128)} %get-tuple-element.76), kind=kLoop, calls=%fused_computation.27 | loop fusion | flops 2129920 | bytes 8519680 | tf_op jit(solution)/shard_map/concatenate | solution.py:37
  97.0 4.8 %all-to-all-start = ((f32[8,1024,130]{1,2,0:T(8,128)}), f32[8,1024,130]{1,2,0:T(8,128)}, u32[]{:S(2)}, u32[]{:S(2)}) async-start(f32[8,1024,130]{1,2,0:T(8,128)} %pad_maximum_fusion), calls=%async_computation | async-start | bytes 8912896 | tf_op jit(solution)/shard_map/all_to_all | solution.py:185
  101.9 0.1 eq.113
  102.0 0.1 eq.109
  102.1 0.8 reduce-window.6
  102.8 0.2 slice_reduce_fusion
  103.1 0.1 fusion.79
  103.2 0.1 reduce_sum.112
  103.4 1.1 fusion.86
  104.5 2.0 copy-done.1
  106.5 0.6 fusion.27
  107.1 47.1 %all-to-all-done = f32[8,1024,130]{1,2,0:T(8,128)} async-done(((f32[8,1024,130]{1,2,0:T(8,128)}), f32[8,1024,130]{1,2,0:T(8,128)}, u32[]{:S(2)}, u32[]{:S(2)}) %all-to-all-start) | async-done | bytes 4259872 | tf_op jit(solution)/shard_map/all_to_all | solution.py:185
  154.2 4.7 %copy.132 = f32[8,1024,130]{1,0,2:T(8,128)S(1)} copy(f32[8,1024,130]{1,2,0:T(8,128)} %all-to-all-done) | data formatting | bytes 8519680 | tf_op jit(solution)/shard_map/all_to_all | solution.py:185
  159.0 0.3 pad.3
  159.3 3.9 %copy.114 = f32[17,8,8,1024]{3,1,2,0:T(8,128)S(1)} copy(f32[17,8,8,1024]{3,2,1,0:T(8,128)S(1)} %bitcast.177) | data formatting | bytes 8912896
  163.2 2.4 slice.20
  165.5 0.2 slice_reduce_fusion.1
  165.8 7.9 %copy.115 = f32[16,8,8,1024]{3,2,1,0:T(8,128)} copy(f32[16,8,8,1024]{3,1,2,0:T(8,128)} %bitcast.181) | data formatting | bytes 8388608
  173.7 3.7 %fusion.26 = f32[1024,128]{0,1:T(8,128)S(1)} fusion(f32[16,8,8,1024]{3,2,1,0:T(8,128)} %copy.115, f32[8,1024]{1,0:T(8,128)S(1)} %subtract_exponential_fusion.2), kind=kLoop, calls=%fused_computation.30 | loop fusion | flops 1966080 | bytes 4751360 | tf_op jit(solution)/shard_map/reduce_sum | solution.py:193
  177.5 0.2 copy.91
  177.7 3.9 %fusion.68 = bf16[1024,1,128]{2,0,1:T(8,128)(2,1)} fusion(bf16[1024,128]{1,0:T(8,128)(2,1)S(1)} %copy-done.8, f32[1024,1024]{0,1:T(8,128)} %copy-done.1, f32[1024]{0:T(1024)S(1)} %get-tuple-element.109, f32[1024,128]{1,0:T(8,128)S(1)} %copy.91, f32[1024]{0:T(1024)S(1)} %get-tuple-element.101, f32[1024]{0:T(1024)S(1)} %get-tuple-element.103, ...), kind=kOutput, calls=%fused_computation.57 | convolution fusion | flops 271187968 | bytes 5259264 | tf_op jit(solution)/shard_map/while/body/eval_jaxpr/hqk,khd->qhd/dot_general | solution.py:113
  181.7 7.1 %all-to-all-start.1 = ((bf16[16,64,128]{2,1,0:T(8,128)(2,1)}), bf16[16,64,128]{2,1,0:T(8,128)(2,1)S(1)}, u32[]{:S(2)}, u32[]{:S(2)}) async-start(bf16[16,64,128]{2,1,0:T(8,128)(2,1)} %bitcast.22), calls=%async_computation.1 | async-start | bytes 524288 | tf_op jit(solution)/shard_map/all_to_all | solution.py:204
  188.7 0.2 select_reduce_fusion
  188.9 8.3 %all-to-all-done.1 = bf16[16,64,128]{2,1,0:T(8,128)(2,1)S(1)} async-done(((bf16[16,64,128]{2,1,0:T(8,128)(2,1)}), bf16[16,64,128]{2,1,0:T(8,128)(2,1)S(1)}, u32[]{:S(2)}, u32[]{:S(2)}) %all-to-all-start.1) | async-done | bytes 262176 | tf_op jit(solution)/shard_map/all_to_all | solution.py:204
  197.2 5.1 %multiply_reduce_fusion = (f32[64]{0:T(128)S(1)}, f32[64,2048]{1,0:T(8,128)S(1)}) fusion(bf16[2048,2048]{1,0:T(8,128)(2,1)} %all-gather.5.cloned.1.call-done, bf16[64,2048]{1,0:T(8,128)(2,1)S(1)} %copy-done.2, bf16[16,64,128]{2,1,0:T(8,128)(2,1)S(1)} %all-to-all-done.1), kind=kOutput, calls=%fused_computation.61 | convolution fusion | flops 537395136 | bytes 9437440 | tf_op jit(solution)/shard_map/dot_general | solution.py:205
  202.3 0.8 convolution_convert_fusion
  203.1 30.3 %all_to_all.35 = bf16[32,16,2048]{2,1,0:T(8,128)(2,1)S(1)} all-to-all(bf16[32,16,2048]{2,1,0:T(8,128)(2,1)S(1)} %bitcast.183), channel_id=1, replica_groups=mesh['req'=8,'exp'=16] {'exp'}, dimensions={0} | all-to-all | bytes 4194304 | tf_op jit(solution)/shard_map/all_to_all | solution.py:223
  233.4 5.6 %fusion.24 = f32[2,16,16,704]{3,2,1,0:T(8,128)} fusion(bf16[2,2048,704]{1,2,0:T(8,128)(2,1)} %param.29, bf16[16,2,16,2048]{3,2,1,0:T(8,128)(2,1)S(1)} %bitcast.185), kind=kOutput, calls=%fused_computation.25 | convolution fusion | flops 1476395008 | bytes 9306112 | tf_op jit(solution)/shard_map/secd,edf->secf/dot_general | solution.py:226
  239.0 9.7 %fusion.32 = bf16[16,2,16,2048]{3,2,0,1:T(8,128)(2,1)} fusion(bf16[2,704,2048]{2,1,0:T(8,128)(2,1)} %param.31, f32[2,16,16,704]{3,2,1,0:T(8,128)} %fusion.24, bf16[2,2048,704]{1,2,0:T(8,128)(2,1)} %param.30, bf16[16,2,16,2048]{3,2,1,0:T(8,128)(2,1)S(1)} %bitcast.186), kind=kOutput, calls=%fused_computation.37 | convolution fusion | flops 2956001280 | bytes 17170432 | tf_op jit(solution)/shard_map/secf,efd->secd/dot_general | solution.py:229
  248.8 1.7 copy.99
  250.5 29.5 %all_to_all.36 = bf16[32,16,2048]{2,1,0:T(8,128)(2,1)S(1)} all-to-all(bf16[32,16,2048]{2,1,0:T(8,128)(2,1)S(1)} %bitcast.184), channel_id=1, replica_groups=mesh['req'=8,'exp'=16] {'exp'}, dimensions={0} | all-to-all | bytes 4194304 | tf_op jit(solution)/shard_map/all_to_all | solution.py:230
  280.0 1.2 fusion.35
  (80 shorter events, 0.8 us)
Async XLA Ops:
  6.5 96.9 %copy-start = (bf16[1024,128]{1,0:T(8,128)(2,1)S(1)}, bf16[1024,128]{1,0:T(8,128)(2,1)}, u32[]{:S(2)}) copy-start(bf16[1024,128]{1,0:T(8,128)(2,1)} %param.18) | copy-start | bytes 786436
  6.5 30.2 %all-gather.3.cloned.1.call-start = ((), (), s32[]{:S(2)}) async-start(), calls=%async_computation.4 | async-start | bytes 2359296 | tf_op jit(solution)/shard_map/all_gather | solution.py:179
  7.3 190.0 %all-gather.5.cloned.1.call-start = ((), (), s32[]{:S(2)}) async-start(), calls=%async_computation.5 | async-start | bytes 8912896 | tf_op jit(solution)/shard_map/all_gather | solution.py:203
  39.1 1.7 copy-start.7
  46.0 1.7 copy-start.7
  52.9 1.7 copy-start.7
  59.8 1.7 copy-start.7
  66.7 1.7 copy-start.7
  73.6 1.7 copy-start.7
  80.5 1.7 copy-start.7
  87.5 1.7 copy-start.7
  97.0 4.8 %copy-start.4 = (s32[64,4]{0,1:T(4,128)S(1)}, s32[64,4]{0,1:T(4,128)}, u32[]{:S(2)}) copy-start(s32[64,4]{0,1:T(4,128)} %param.27) | copy-start | bytes 3076
  97.0 6.4 %copy-start.6 = (bf16[64,4]{0,1:T(4,128)(2,1)S(1)}, bf16[64,4]{0,1:T(4,128)(2,1)}, u32[]{:S(2)}) copy-start(bf16[64,4]{0,1:T(4,128)(2,1)} %param.28) | copy-start | bytes 1540
  97.0 6.4 %copy-start.5 = (bf16[2048]{0:T(1024)(128)(2,1)S(1)}, bf16[2048]{0:T(1024)(128)(2,1)}, u32[]{:S(2)}) copy-start(bf16[2048]{0:T(1024)(128)(2,1)} %param.26) | copy-start | bytes 12292
  97.0 6.5 %copy-start.3 = (bf16[1024,128]{1,0:T(8,128)(2,1)S(1)}, bf16[1024,128]{1,0:T(8,128)(2,1)}, u32[]{:S(2)}) copy-start(bf16[1024,128]{1,0:T(8,128)(2,1)} %param.17) | copy-start | bytes 786436
  97.0 57.3 %all-to-all-start = ((f32[8,1024,130]{1,2,0:T(8,128)}), f32[8,1024,130]{1,2,0:T(8,128)}, u32[]{:S(2)}, u32[]{:S(2)}) async-start(f32[8,1024,130]{1,2,0:T(8,128)} %pad_maximum_fusion), calls=%async_computation | async-start | bytes 8912896 | tf_op jit(solution)/shard_map/all_to_all | solution.py:185
  104.5 2.0 copy-start.1
  173.7 4.0 %copy-start.8 = (bf16[1024,128]{1,0:T(8,128)(2,1)S(1)}, bf16[1024,128]{1,0:T(8,128)(2,1)}, u32[]{:S(2)}) copy-start(bf16[1024,128]{1,0:T(8,128)(2,1)} %param.19) | copy-start | bytes 786436
  177.4 19.8 %copy-start.2 = (bf16[64,2048]{1,0:T(8,128)(2,1)S(1)}, bf16[64,2048]{1,0:T(8,128)(2,1)}, u32[]{:S(2)}) copy-start(bf16[64,2048]{1,0:T(8,128)(2,1)} %param.24) | copy-start | bytes 786436
  181.7 15.6 %all-to-all-start.1 = ((bf16[16,64,128]{2,1,0:T(8,128)(2,1)}), bf16[16,64,128]{2,1,0:T(8,128)(2,1)S(1)}, u32[]{:S(2)}, u32[]{:S(2)}) async-start(bf16[16,64,128]{2,1,0:T(8,128)(2,1)} %bitcast.22), calls=%async_computation.1 | async-start | bytes 524288 | tf_op jit(solution)/shard_map/all_to_all | solution.py:204
Sparse Core Ops, SparseCore 0:
  9.1 27.5 all-gather.2
  38.8 71.1 all-gather.4

commit v2 on v1

--- a/solution.py
+++ b/solution.py
@@ -3,6 +3,8 @@
 import jax
 import jax.numpy as jnp
 from jax import lax
+from jax.experimental import pallas as pl
+from jax.experimental.pallas import tpu as pltpu
 from jax.sharding import PartitionSpec as P
 
 HEAD = 128
@@ -85,6 +87,86 @@
         maxima.reshape(row_count, head_count),
         totals.reshape(row_count, head_count),
     )
+
+
+QUERY_BLOCK = 128
+KEY_BLOCK = 1024
+
+
+def prefix_kernel(present_ref, q_ref, grp_ref, k_ref, v_ref, acc_ref, m_ref, l_ref):
+    g = pl.program_id(0)
+    kb = pl.program_id(1)
+    scaling = 1.0 / math.sqrt(HEAD)
+
+    @pl.when((g == 0) & (kb == 0))
+    def _():
+        acc_ref[...] = jnp.zeros_like(acc_ref)
+        m_ref[...] = jnp.full_like(m_ref, NEG)
+        l_ref[...] = jnp.zeros_like(l_ref)
+
+    k = k_ref[0]
+    v = v_ref[0]
+    block_count = q_ref.shape[0] // QUERY_BLOCK
+
+    def body(qb, carry):
+        @pl.when(present_ref[qb * G + g] > 0)
+        def _():
+            rows = pl.ds(pl.multiple_of(qb * QUERY_BLOCK, QUERY_BLOCK), QUERY_BLOCK)
+            s = lax.dot_general(
+                q_ref[rows, :], k, (((1,), (1,)), ((), ())), preferred_element_type=jnp.float32
+            ) * scaling
+            mask = grp_ref[rows, :][:, :1] == g
+            s = jnp.where(mask, s, NEG)
+            m_prev = m_ref[rows, :]
+            m_new = jnp.maximum(m_prev, jnp.max(s, axis=1, keepdims=True))
+            alpha = jnp.exp(m_prev - m_new)
+            p = jnp.where(mask, jnp.exp(s - m_new[:, :1]), 0.0)
+            l_ref[rows, :] = alpha * l_ref[rows, :] + jnp.sum(p, axis=1, keepdims=True)
+            acc_ref[rows, :] = alpha * acc_ref[rows, :] + jnp.dot(
+                p.astype(jnp.bfloat16), v, preferred_element_type=jnp.float32
+            )
+            m_ref[rows, :] = m_new
+
+        return carry
+
+    lax.fori_loop(0, block_count, body, 0)
+
+
+def attend_prefix_local(query_rows, query_group, prefix_k, prefix_v):
+    row_count = query_rows.shape[0]
+    span = prefix_k.shape[1]
+    block_count = row_count // QUERY_BLOCK
+    present = jnp.any(
+        query_group.reshape(block_count, QUERY_BLOCK, 1)
+        == jnp.arange(G, dtype=jnp.int32)[None, None, :],
+        axis=1,
+    ).astype(jnp.int32).reshape(-1)
+    grp = jnp.broadcast_to(query_group[:, None], (row_count, HEAD))
+    full = lambda g, kb, pr: (0, 0)
+    kv_spec = pl.BlockSpec((1, KEY_BLOCK, HEAD), lambda g, kb, pr: (g, kb, 0))
+    out_shape = jax.ShapeDtypeStruct((row_count, HEAD), jnp.float32)
+    acc, maxima, totals = pl.pallas_call(
+        prefix_kernel,
+        grid_spec=pltpu.PrefetchScalarGridSpec(
+            num_scalar_prefetch=1,
+            grid=(G, span // KEY_BLOCK),
+            in_specs=[
+                pl.BlockSpec((row_count, HEAD), full),
+                pl.BlockSpec((row_count, HEAD), full),
+                kv_spec,
+                kv_spec,
+            ],
+            out_specs=[pl.BlockSpec((row_count, HEAD), full)] * 3,
+        ),
+        out_shape=[out_shape] * 3,
+        compiler_params=pltpu.CompilerParams(dimension_semantics=("arbitrary", "arbitrary")),
+        cost_estimate=pl.CostEstimate(
+            flops=4 * row_count * span * HEAD * 2,
+            transcendentals=row_count * span * 2,
+            bytes_accessed=2 * G * span * HEAD * 2 + row_count * HEAD * 14,
+        ),
+    )(present, query_rows, grp, prefix_k, prefix_v)
+    return (acc, maxima[:, :1], totals[:, :1])
 
 
 def attend_suffix(queries, keys, values, request, position):
@@ -173,25 +255,12 @@
     tok_dev = residual.shape[0]
     request, position, tok_group = token_layout(lengths, groups)
     request, position, tok_group = (request[0], position[0], tok_group[0])
-    all_groups = lax.all_gather(tok_group, "req", axis=0, tiled=True)
-    partial_value = pack_parts(
-        attend_prefix(
-            lax.all_gather(queries, "req", axis=0, tiled=True),
-            all_groups,
-            prefix_keys,
-            prefix_values,
-        )
-    )
-    returned = lax.all_to_all(partial_value, "req", split_axis=0, concat_axis=0, tiled=True)
-    owners = returned.shape[0] // row_tok
-    back_w, back_m, back_t = unpack_parts(returned, head_count)
-    all_weighted = back_w.reshape(owners, row_tok, head_count, HEAD)
-    all_maxima = back_m.reshape(owners, row_tok, head_count)
-    all_totals = back_t.reshape(owners, row_tok, head_count)
-    maxima = jnp.max(all_maxima, axis=0)
-    factor = jnp.exp(all_maxima - maxima[None])
-    weighted = jnp.sum(all_weighted * factor[..., None], axis=0).reshape(row_tok, columns)
-    prefix_part = (weighted, maxima, jnp.sum(all_totals * factor, axis=0))
+    prefix_part = attend_prefix_local(
+        queries,
+        tok_group,
+        lax.all_gather(prefix_keys, "req", axis=1, tiled=True),
+        lax.all_gather(prefix_values, "req", axis=1, tiled=True),
+    )
     suffix_part = attend_suffix(queries, keys, values, request, position)
     weighted, maxima, totals = combine(prefix_part, suffix_part)
     attended = (

time: 289 us -> 249 us (0.86)
  matrix products: 68.5 us -> 28.6 us
  Pallas kernels: 0 us -> 39.6 us
  other arithmetic: 26.5 us -> 5.76 us
  local copies, waits for them, and re-layouts: 24.2 us -> 7.22 us
  waiting for transfers between devices: 69.9 us -> 82.5 us
  blocking collectives: 73 us -> 64.2 us
  starting transfers between devices: 11.9 us -> 7.02 us
    all_to_all x1 -> x0, waiting for transfers between devices: 47.1 us -> none  [per_device(): lax.all_to_all(partial_value, 'req', split_axis=0, concat_axis=0, tiled=T...]
    all_gather x1 -> x2, waiting for transfers between devices: 13.1 us -> 58.3 us  [the longest x1 33.8 us: per_device(): lax.all_gather(prefix_values, 'req', axis=1, tiled=True)]
    dot_general x16 -> x0, matrix products: 41.1 us -> none  [the longest x8 22 us: per_block(): jnp.einsum('hqgk,gkhd->qhd', exp_terms.astype(jnp.bfloat16), val_grid, pr...]
    pallas_call x0 -> x1, Pallas kernels: none -> 39.6 us  [attend_prefix_local(): pl.pallas_call(prefix_kernel, grid_spec=pltpu.PrefetchScalarGridSpec(num_...]
    reduce_sum x10 -> x0, other arithmetic: 17.4 us -> none  [the longest x8 13.7 us: per_block(): totals = jnp.sum(exp_terms, axis=(2, 3))]
    all_gather x1 -> x0, blocking collectives: 13.3 us -> none  [per_device(): all_groups = lax.all_gather(tok_group, 'req', axis=0, tiled=True)]
    all_gather x1, waiting for transfers between devices: 0.01 us -> 11.9 us  [per_device(): full_proj = lax.all_gather(out_proj, 'exp', axis=0, tiled=True)]
    unnamed x20 -> x15, local copies, waits for them, and re-layouts: 14.2 us -> 2.75 us
  transfers between devices with their start and end apart: 4 -> 4, of which waited for: 3 -> 4; matrix products, arithmetic and copies ran while one was open for 32% -> 6% of each run, Pallas kernels for 0% -> 16%
where the time goes in v2:
time: 249 us; the launch traced here: 248 us
  waiting for transfers between devices  82.5 us (33%)
  blocking collectives  64.2 us (26%)
  Pallas kernels  39.6 us (16%)
  matrix products  28.6 us (11%)
  between operations  13.3 us (5%)
  local copies, waits for them, and re-layouts  7.22 us (3%)
  starting transfers between devices  7.02 us (3%)
  other arithmetic  5.76 us (2%)
    pallas_call x1, Pallas kernels, attend_prefix_local(): pl.pallas_call(prefix_kernel, grid_spec=pltpu.PrefetchScalarGridSpec(num_...  39.6 us
    all_gather x1, waiting for transfers between devices, per_device(): lax.all_gather(prefix_values, 'req', axis=1, tiled=True)  33.8 us
    all_to_all x1, blocking collectives, per_device(): lax.all_to_all(buffer, 'exp', split_axis=0, concat_axis=0, tiled=True)  33.3 us
    all_to_all x1, blocking collectives, per_device(): lax.all_to_all(expert_out.astype(jnp.bfloat16).reshape(EXPERTS, slots, re...  30.9 us
    all_gather x1, waiting for transfers between devices, per_device(): lax.all_gather(prefix_keys, 'req', axis=1, tiled=True)  24.5 us
    all_gather x1, waiting for transfers between devices, per_device(): full_proj = lax.all_gather(out_proj, 'exp', axis=0, tiled=True)  11.9 us
    all_to_all x1, waiting for transfers between devices, per_device(): lax.all_to_all(attended, 'exp', split_axis=0, concat_axis=1, tiled=True)  10.2 us
    dot_general x1, matrix products, per_device(): jnp.einsum('secf,efd->secd', hidden, w_down, preferred_element_type=jnp.f...  9.73 us
  transfers between devices with their start and end apart: 4, of which 4 were waited for; matrix products, arithmetic and copies ran while one was open for 6% of the time, Pallas kernels for 16%

profile of v2, /device:TPU:0, one launch (start us, length us, event | category | flops | bytes accessed | tf_op | source)
XLA Modules:
  0.0 248.2 jit_solution(6741589104143366900)
XLA Ops:
  6.5 0.0 copy-start
  6.5 0.0 all-gather.4.cloned.1.call-start
  6.5 0.7 all-gather.4.cloned.1.call-update
  7.3 0.0 all-gather.6.cloned.1.call-start
  7.3 0.7 all-gather.6.cloned.1.call-update
  8.0 0.0 all-gather.8.cloned.1.call-start
  8.1 0.7 all-gather.8.cloned.1.call-update
  8.7 0.8 copy.62
  9.5 0.1 eq.113
  9.6 0.1 eq.109
  9.7 0.8 reduce_window_sum.24
  10.6 0.1 convert_reduce_fusion.1
  10.7 0.7 subtract_bitcast_fusion
  11.3 0.7 select_reduce_fusion.2
  12.1 0.0 copy-done
  12.1 2.0 fusion.60
  14.1 0.0 copy-start.1
  14.1 0.0 copy-start.5
  14.1 0.0 copy-start.4
  14.1 1.9 copy-done.1
  16.1 0.6 fusion.6
  16.7 0.2 copy.60
  16.9 0.2 fusion.58
  17.1 0.1 copy.57
  17.2 0.6 reshape.322.present_ref
  17.8 0.2 copy.58
  18.0 0.6 reduce-window.6
  18.6 0.2 slice_reduce_fusion
  18.9 0.1 fusion.56
  19.0 0.1 reduce_sum.80
  19.1 0.1 copy.65
  19.1 0.0 copy-done.5
  19.1 0.0 copy-done.4
  19.2 24.5 %all-gather.4.cloned.1.call-done.k_ref = bf16[4,4096,128]{2,1,0:T(8,128)(2,1)} async-done(((bf16[4,512,128]{2,1,0:T(8,128)(2,1)}), bf16[4,4096,128]{2,1,0:T(8,128)(2,1)}) %all-gather.4.cloned.1.call-update) | async-done | bytes 4194320 | tf_op jit(solution)/shard_map/all_gather | solution.py:261
  43.7 33.8 %all-gather.6.cloned.1.call-done.v_ref = bf16[4,4096,128]{2,1,0:T(8,128)(2,1)} async-done(((bf16[4,512,128]{2,1,0:T(8,128)(2,1)}), bf16[4,4096,128]{2,1,0:T(8,128)(2,1)}) %all-gather.6.cloned.1.call-update) | async-done | bytes 4194320 | tf_op jit(solution)/shard_map/all_gather | solution.py:262
  77.5 1.0 broadcast_in_dim.68.grp_ref
  78.5 0.0 copy-start.6
  78.5 39.6 %shard_map.145 = (f32[1024,128]{1,0:T(8,128)}, f32[1024,128]{1,0:T(8,128)}, f32[1024,128]{1,0:T(8,128)}) custom-call(s32[32]{0:T(128)} %reshape.322.present_ref, bf16[1024,128]{1,0:T(8,128)(2,1)} %q_ref.1, s32[1024,128]{1,0:T(8,128)} %broadcast_in_dim.68.grp_ref, bf16[4,4096,128]{2,1,0:T(8,128)(2,1)} %all-gather.4.cloned.1.call-done.k_ref, ...), custom_call_target="tpu_custom_call" | custom-call | flops 4294967296 | bytes 10223616 | tf_op jit(solution)/shard_map/pallas_call | solution.py:148
  118.1 0.0 copy-start.3
  118.1 0.0 copy-start.2
  118.1 1.7 fusion.52
  119.9 0.0 copy-done.6
  119.9 4.2 %fusion.41 = bf16[1024,128]{1,0:T(8,128)(2,1)} fusion(bf16[1024,128]{1,0:T(8,128)(2,1)S(1)} %copy-done.6, f32[1024,1024]{0,1:T(8,128)} %copy-done.1, f32[1024]{0:T(1024)S(1)} %get-tuple-element.45, f32[1024,128]{1,0:T(8,128)} %get-tuple-element.24, f32[1024]{0:T(1024)S(1)} %get-tuple-element.38, f32[1024]{0:T(1024)S(1)} %get-tuple-element.40, ...), kind=kOutput, calls=%fused_computation.30 | convolution fusion | flops 271187968 | bytes 5259264 | tf_op jit(solution)/shard_map/while/body/eval_jaxpr/hqk,khd->qhd/dot_general | solution.py:195
  124.1 6.9 %all-to-all-start = ((bf16[16,64,128]{2,1,0:T(8,128)(2,1)}), bf16[16,64,128]{2,1,0:T(8,128)(2,1)S(1)}, u32[]{:S(2)}, u32[]{:S(2)}) async-start(bf16[16,64,128]{2,1,0:T(8,128)(2,1)} %bitcast.6), calls=%async_computation | async-start | bytes 524288 | tf_op jit(solution)/shard_map/all_to_all | solution.py:273
  131.0 0.0 copy-done.3
  131.1 0.2 select_reduce_fusion
  131.2 10.2 %all-to-all-done = bf16[16,64,128]{2,1,0:T(8,128)(2,1)S(1)} async-done(((bf16[16,64,128]{2,1,0:T(8,128)(2,1)}), bf16[16,64,128]{2,1,0:T(8,128)(2,1)S(1)}, u32[]{:S(2)}, u32[]{:S(2)}) %all-to-all-start) | async-done | bytes 262176 | tf_op jit(solution)/shard_map/all_to_all | solution.py:273
  141.5 11.9 %all-gather.8.cloned.1.call-done = bf16[2048,2048]{1,0:T(8,128)(2,1)} async-done(((bf16[128,2048]{1,0:T(8,128)(2,1)}), bf16[2048,2048]{1,0:T(8,128)(2,1)}) %all-gather.8.cloned.1.call-update) | async-done | bytes 8388624 | tf_op jit(solution)/shard_map/all_gather | solution.py:272
  153.4 0.0 copy-done.2
  153.4 5.1 %multiply_reduce_fusion = (f32[64]{0:T(128)S(1)}, f32[64,2048]{1,0:T(8,128)S(1)}) fusion(bf16[2048,2048]{1,0:T(8,128)(2,1)} %all-gather.8.cloned.1.call-done, bf16[64,2048]{1,0:T(8,128)(2,1)S(1)} %copy-done.2, bf16[16,64,128]{2,1,0:T(8,128)(2,1)S(1)} %all-to-all-done), kind=kOutput, calls=%fused_computation.37 | convolution fusion | flops 537395136 | bytes 9437440 | tf_op jit(solution)/shard_map/dot_general | solution.py:274
  158.4 0.8 convolution_convert_fusion
  159.2 33.3 %all_to_all.26 = bf16[32,16,2048]{2,1,0:T(8,128)(2,1)S(1)} all-to-all(bf16[32,16,2048]{2,1,0:T(8,128)(2,1)S(1)} %bitcast.91), channel_id=1, replica_groups=mesh['req'=8,'exp'=16] {'exp'}, dimensions={0} | all-to-all | bytes 4194304 | tf_op jit(solution)/shard_map/all_to_all | solution.py:292
  192.6 5.6 %fusion.4 = f32[2,16,16,704]{3,2,1,0:T(8,128)} fusion(bf16[2,2048,704]{1,2,0:T(8,128)(2,1)} %param.27, bf16[16,2,16,2048]{3,2,1,0:T(8,128)(2,1)S(1)} %bitcast.93), kind=kOutput, calls=%fused_computation.4 | convolution fusion | flops 1476395008 | bytes 9306112 | tf_op jit(solution)/shard_map/secd,edf->secf/dot_general | solution.py:295
  198.2 9.7 %fusion.11 = bf16[16,2,16,2048]{3,2,0,1:T(8,128)(2,1)} fusion(bf16[2,704,2048]{2,1,0:T(8,128)(2,1)} %param.29, f32[2,16,16,704]{3,2,1,0:T(8,128)} %fusion.4, bf16[2,2048,704]{1,2,0:T(8,128)(2,1)} %param.28, bf16[16,2,16,2048]{3,2,1,0:T(8,128)(2,1)S(1)} %bitcast.94), kind=kOutput, calls=%fused_computation.12 | convolution fusion | flops 2956001280 | bytes 17170432 | tf_op jit(solution)/shard_map/secf,efd->secd/dot_general | solution.py:298
  207.9 1.7 copy.68
  209.6 30.9 %all_to_all.27 = bf16[32,16,2048]{2,1,0:T(8,128)(2,1)S(1)} all-to-all(bf16[32,16,2048]{2,1,0:T(8,128)(2,1)S(1)} %bitcast.92), channel_id=1, replica_groups=mesh['req'=8,'exp'=16] {'exp'}, dimensions={0} | all-to-all | bytes 4194304 | tf_op jit(solution)/shard_map/all_to_all | solution.py:299
  240.5 1.2 fusion.14
  (9 shorter events, 0.1 us)
Async XLA Ops:
  6.5 5.5 %copy-start = (bf16[1024,128]{1,0:T(8,128)(2,1)S(1)}, bf16[1024,128]{1,0:T(8,128)(2,1)}, u32[]{:S(2)}) copy-start(bf16[1024,128]{1,0:T(8,128)(2,1)} %param.16) | copy-start | bytes 786436
  6.5 37.1 %all-gather.4.cloned.1.call-start = ((), (), s32[]{:S(2)}) async-start(), calls=%async_computation.3 | async-start | bytes 4718592 | tf_op jit(solution)/shard_map/all_gather | solution.py:261
  7.3 70.2 %all-gather.6.cloned.1.call-start = ((), (), s32[]{:S(2)}) async-start(), calls=%async_computation.4 | async-start | bytes 4718592 | tf_op jit(solution)/shard_map/all_gather | solution.py:262
  8.0 145.3 %all-gather.8.cloned.1.call-start = ((), (), s32[]{:S(2)}) async-start(), calls=%async_computation.5 | async-start | bytes 8912896 | tf_op jit(solution)/shard_map/all_gather | solution.py:272
  14.1 2.0 copy-start.1
  14.1 5.0 %copy-start.5 = (bf16[64,4]{0,1:T(4,128)(2,1)S(1)}, bf16[64,4]{0,1:T(4,128)(2,1)}, u32[]{:S(2)}) copy-start(bf16[64,4]{0,1:T(4,128)(2,1)} %param.26) | copy-start | bytes 1540
  14.1 5.0 %copy-start.4 = (bf16[2048]{0:T(1024)(128)(2,1)S(1)}, bf16[2048]{0:T(1024)(128)(2,1)}, u32[]{:S(2)}) copy-start(bf16[2048]{0:T(1024)(128)(2,1)} %param.24) | copy-start | bytes 12292
  78.5 41.4 %copy-start.6 = (bf16[1024,128]{1,0:T(8,128)(2,1)S(1)}, bf16[1024,128]{1,0:T(8,128)(2,1)}, u32[]{:S(2)}) copy-start(bf16[1024,128]{1,0:T(8,128)(2,1)} %param.17) | copy-start | bytes 786436
  118.1 12.9 %copy-start.3 = (s32[64,4]{0,1:T(4,128)S(1)}, s32[64,4]{0,1:T(4,128)}, u32[]{:S(2)}) copy-start(s32[64,4]{0,1:T(4,128)} %param.25) | copy-start | bytes 3076
  118.1 35.2 %copy-start.2 = (bf16[64,2048]{1,0:T(8,128)(2,1)S(1)}, bf16[64,2048]{1,0:T(8,128)(2,1)}, u32[]{:S(2)}) copy-start(bf16[64,2048]{1,0:T(8,128)(2,1)} %param.22) | copy-start | bytes 786436
  124.1 17.4 %all-to-all-start = ((bf16[16,64,128]{2,1,0:T(8,128)(2,1)}), bf16[16,64,128]{2,1,0:T(8,128)(2,1)S(1)}, u32[]{:S(2)}, u32[]{:S(2)}) async-start(bf16[16,64,128]{2,1,0:T(8,128)(2,1)} %bitcast.6), calls=%async_computation | async-start | bytes 524288 | tf_op jit(solution)/shard_map/all_to_all | solution.py:273
Sparse Core Ops, SparseCore 0:
  9.1 34.5 all-gather.3
  45.4 32.0 all-gather.5
  79.6 73.7 all-gather.7

commit v3 on v2

--- a/solution.py
+++ b/solution.py
@@ -90,7 +90,7 @@
 
 
 QUERY_BLOCK = 128
-KEY_BLOCK = 1024
+KEY_BLOCK = 512
 
 
 def prefix_kernel(present_ref, q_ref, grp_ref, k_ref, v_ref, acc_ref, m_ref, l_ref):
@@ -112,9 +112,7 @@
         @pl.when(present_ref[qb * G + g] > 0)
         def _():
             rows = pl.ds(pl.multiple_of(qb * QUERY_BLOCK, QUERY_BLOCK), QUERY_BLOCK)
-            s = lax.dot_general(
-                q_ref[rows, :], k, (((1,), (1,)), ((), ())), preferred_element_type=jnp.float32
-            ) * scaling
+            s = jnp.dot(q_ref[rows, :], k, preferred_element_type=jnp.float32) * scaling
             mask = grp_ref[rows, :][:, :1] == g
             s = jnp.where(mask, s, NEG)
             m_prev = m_ref[rows, :]
@@ -135,6 +133,7 @@
 def attend_prefix_local(query_rows, query_group, prefix_k, prefix_v):
     row_count = query_rows.shape[0]
     span = prefix_k.shape[1]
+    prefix_kt = jnp.swapaxes(prefix_k, 1, 2)
     block_count = row_count // QUERY_BLOCK
     present = jnp.any(
         query_group.reshape(block_count, QUERY_BLOCK, 1)
@@ -143,6 +142,7 @@
     ).astype(jnp.int32).reshape(-1)
     grp = jnp.broadcast_to(query_group[:, None], (row_count, HEAD))
     full = lambda g, kb, pr: (0, 0)
+    kt_spec = pl.BlockSpec((1, HEAD, KEY_BLOCK), lambda g, kb, pr: (g, 0, kb))
     kv_spec = pl.BlockSpec((1, KEY_BLOCK, HEAD), lambda g, kb, pr: (g, kb, 0))
     out_shape = jax.ShapeDtypeStruct((row_count, HEAD), jnp.float32)
     acc, maxima, totals = pl.pallas_call(
@@ -153,7 +153,7 @@
             in_specs=[
                 pl.BlockSpec((row_count, HEAD), full),
                 pl.BlockSpec((row_count, HEAD), full),
-                kv_spec,
+                kt_spec,
                 kv_spec,
             ],
             out_specs=[pl.BlockSpec((row_count, HEAD), full)] * 3,
@@ -165,7 +165,7 @@
             transcendentals=row_count * span * 2,
             bytes_accessed=2 * G * span * HEAD * 2 + row_count * HEAD * 14,
         ),
-    )(present, query_rows, grp, prefix_k, prefix_v)
+    )(present, query_rows, grp, prefix_kt, prefix_v)
     return (acc, maxima[:, :1], totals[:, :1])
 
 
@@ -255,12 +255,22 @@
     tok_dev = residual.shape[0]
     request, position, tok_group = token_layout(lengths, groups)
     request, position, tok_group = (request[0], position[0], tok_group[0])
-    prefix_part = attend_prefix_local(
-        queries,
-        tok_group,
-        lax.all_gather(prefix_keys, "req", axis=1, tiled=True),
-        lax.all_gather(prefix_values, "req", axis=1, tiled=True),
-    )
+    req_count = lax.axis_size("req")
+    local_kv = jnp.stack([prefix_keys, prefix_values])
+    partner = [(i, i ^ 1) for i in range(req_count)]
+    partner_kv = lax.ppermute(local_kv, "req", partner)
+    ring_kv = jnp.concatenate(
+        [
+            lax.ppermute(local_kv, "req", [(i, (i + 2 * s) % req_count) for i in range(req_count)])
+            for s in range(1, req_count // 2)
+        ],
+        axis=2,
+    )
+    forwarded_kv = lax.ppermute(ring_kv, "req", partner)
+    prefix_part = None
+    for chunk in (jnp.concatenate([local_kv, partner_kv], axis=2), ring_kv, forwarded_kv):
+        part = attend_prefix_local(queries, tok_group, chunk[0], chunk[1])
+        prefix_part = part if prefix_part is None else combine(prefix_part, part)
     suffix_part = attend_suffix(queries, keys, values, request, position)
     weighted, maxima, totals = combine(prefix_part, suffix_part)
     attended = (

time: 249 us -> 262 us (1.052)
  waiting for transfers between devices: 82.5 us -> 51 us
  Pallas kernels: 39.6 us -> 64.9 us
  local copies, waits for them, and re-layouts: 7.22 us -> 22.5 us
  starting transfers between devices: 7.02 us -> 13.9 us
  blocking collectives: 64.2 us -> 58.2 us
  other arithmetic: 5.76 us -> 9.31 us
    all_gather x2 -> x0, waiting for transfers between devices: 58.3 us -> none  [the longest x1 33.8 us: per_device(): lax.all_gather(prefix_values, 'req', axis=1, tiled=True)]
    ppermute x0 -> x5, waiting for transfers between devices: none -> 42 us  [the longest x3 42 us: per_device(): lax.ppermute(local_kv, 'req', [(i, (i + 2 * s) % req_count) for i in rang...]
    pallas_call x1 -> x3, Pallas kernels: 39.6 us -> 64.9 us  [attend_prefix_local(): pl.pallas_call(prefix_kernel, grid_spec=pltpu.PrefetchScalarGridSpec(num_...]
    all_gather x1, waiting for transfers between devices: 11.9 us -> 0.01 us  [per_device(): full_proj = lax.all_gather(out_proj, 'exp', axis=0, tiled=True)]
    squeeze x0 -> x3, local copies, waits for them, and re-layouts: none -> 7.75 us  [per_device(): part = attend_prefix_local(queries, tok_group, chunk[0], chunk[1])]
    ppermute x0 -> x5, starting transfers between devices: none -> 5.74 us  [the longest x3 5.74 us: per_device(): lax.ppermute(local_kv, 'req', [(i, (i + 2 * s) % req_count) for i in rang...]
    transpose x0 -> x3, local copies, waits for them, and re-layouts: none -> 4.5 us  [attend_prefix_local(): prefix_kt = jnp.swapaxes(prefix_k, 1, 2)]
    all_to_all x1, blocking collectives: 33.3 us -> 29.8 us  [per_device(): lax.all_to_all(buffer, 'exp', split_axis=0, concat_axis=0, tiled=True)]
  transfers between devices with their start and end apart: 4 -> 7, of which waited for: 4 -> 3; matrix products, arithmetic and copies ran while one was open for 6% -> 13% of each run, Pallas kernels for 16% -> 25%
where the time goes in v3:
time: 262 us; the launch traced here: 261 us
  Pallas kernels  64.9 us (25%)
  blocking collectives  58.2 us (22%)
  waiting for transfers between devices  51 us (19%)
  matrix products  27.4 us (10%)
  local copies, waits for them, and re-layouts  22.5 us (9%)
  starting transfers between devices  13.9 us (5%)
  between operations  13.7 us (5%)
  other arithmetic  9.31 us (4%)
    pallas_call x3, Pallas kernels, attend_prefix_local(): pl.pallas_call(prefix_kernel, grid_spec=pltpu.PrefetchScalarGridSpec(num_...  64.9 us
    ppermute x3, waiting for transfers between devices, per_device(): lax.ppermute(local_kv, 'req', [(i, (i + 2 * s) % req_count) for i in rang...  42 us
    all_to_all x1, blocking collectives, per_device(): lax.all_to_all(buffer, 'exp', split_axis=0, concat_axis=0, tiled=True)  29.8 us
    all_to_all x1, blocking collectives, per_device(): lax.all_to_all(expert_out.astype(jnp.bfloat16).reshape(EXPERTS, slots, re...  28.5 us
    dot_general x1, matrix products, per_device(): jnp.einsum('secf,efd->secd', hidden, w_down, preferred_element_type=jnp.f...  9.73 us
    all_to_all x1, waiting for transfers between devices, per_device(): lax.all_to_all(attended, 'exp', split_axis=0, concat_axis=1, tiled=True)  8.29 us
    all_to_all x1, starting transfers between devices, per_device(): lax.all_to_all(attended, 'exp', split_axis=0, concat_axis=1, tiled=True)  8.12 us
    squeeze x3, local copies, waits for them, and re-layouts, per_device(): part = attend_prefix_local(queries, tok_group, chunk[0], chunk[1])  7.75 us
  transfers between devices with their start and end apart: 7, of which 3 were waited for; matrix products, arithmetic and copies ran while one was open for 13% of the time, Pallas kernels for 25%

profile of v3, /device:TPU:0, one launch (start us, length us, event | category | flops | bytes accessed | tf_op | source)
XLA Modules:
  0.0 260.8 jit_solution(16642047536688600181)
XLA Ops:
  6.5 0.7 all-gather.2.cloned.1.call-update
  7.3 2.3 pad_maximum_fusion.1
  9.6 1.6 collective-permute-start.1
  11.1 2.7 %collective-permute-start.2 = (bf16[2,4,512,128]{3,2,1,0:T(8,128)(2,1)}, bf16[2,4,512,128]{3,2,1,0:T(8,128)(2,1)S(1)}, u32[]{:S(2)}, u32[]{:S(2)}) collective-permute-start(bf16[2,4,512,128]{3,2,1,0:T(8,128)(2,1)} %pad_maximum_fusion.1), channel_id=1, source_target_pairs={{0,64},{16,80},{32,96},{48,112},{64,0},{80,16},{96,32},{112,48},{1... | collective-permute-start | bytes 3145736 | tf_op jit(solution)/shard_map/ppermute | solution.py:264
  13.9 1.4 collective-permute-start.3
  15.3 0.0 collective-permute-start
  15.3 0.8 reduce_window_sum.24
  16.2 19.6 %collective-permute-done.1 = bf16[2,4,512,128]{3,2,1,0:T(8,128)(2,1)S(1)} collective-permute-done((bf16[2,4,512,128]{3,2,1,0:T(8,128)(2,1)}, bf16[2,4,512,128]{3,2,1,0:T(8,128)(2,1)S(1)}, u32[]{:S(2)}, u32[]{:S(2)}) %collective-permute-start.1) | collective-permute-done | bytes 1048608 | tf_op jit(solution)/shard_map/ppermute | solution.py:264
  35.8 1.2 constant_dynamic-update-slice_fusion.2
  37.0 22.4 %collective-permute-done.2 = bf16[2,4,512,128]{3,2,1,0:T(8,128)(2,1)S(1)} collective-permute-done((bf16[2,4,512,128]{3,2,1,0:T(8,128)(2,1)}, bf16[2,4,512,128]{3,2,1,0:T(8,128)(2,1)S(1)}, u32[]{:S(2)}, u32[]{:S(2)}) %collective-permute-start.2) | collective-permute-done | bytes 1048608 | tf_op jit(solution)/shard_map/ppermute | solution.py:264
  59.4 1.2 constant_dynamic-update-slice_fusion.1
  60.6 0.0 collective-permute-done.3
  60.6 1.2 constant_dynamic-update-slice_fusion
  61.8 0.0 collective-permute-start.4
  61.8 0.1 convert_reduce_fusion.1
  61.9 0.1 copy.77
  62.0 0.1 eq.127
  62.1 0.1 eq.123
  62.2 0.0 copy-done.15
  62.2 0.1 select_reduce_fusion.2
  62.3 0.1 fusion.62
  62.5 0.1 copy.69
  62.5 0.6 reshape.344.present_ref
  63.2 1.1 fusion.64
  64.3 0.0 copy-start.12
  64.3 0.0 copy-start.11
  64.3 1.9 copy-done.2
  66.2 0.6 fusion.6
  66.8 0.2 copy.75
  67.1 0.2 copy.73
  67.3 0.6 reduce-window.6
  67.9 0.2 slice_reduce_fusion
  68.1 0.1 fusion.60
  68.2 0.1 reduce_sum.80
  68.4 0.1 copy.80
  68.4 0.0 copy-done.11
  68.5 3.3 %slice_bitcast_fusion.2 = (bf16[4,1536,128]{2,1,0:T(8,128)(2,1)}, bf16[4,128,1536]{1,2,0:T(8,128)(2,1)S(1)}) fusion(bf16[2,4,1536,128]{3,2,1,0:T(8,128)(2,1)} %constant_dynamic-update-slice_fusion), kind=kLoop, calls=%fused_computation.23 | loop fusion | bytes 6291456 | tf_op jit(solution)/shard_map/squeeze | solution.py:272
  71.8 1.6 copy.71.k_ref
  73.4 0.0 collective-permute-done
  73.4 1.5 pad_maximum_fusion
  74.9 1.2 slice_bitcast_fusion.4
  76.1 1.3 copy.70.k_ref
  77.4 1.1 broadcast_in_dim.48.grp_ref
  78.5 17.0 %shard_map.145 = (f32[1024,128]{1,0:T(8,128)}, f32[1024,128]{1,0:T(8,128)}, f32[1024,128]{1,0:T(8,128)}) custom-call(s32[32]{0:T(128)} %reshape.344.present_ref, bf16[1024,128]{1,0:T(8,128)(2,1)} %q_ref.5, s32[1024,128]{1,0:T(8,128)} %broadcast_in_dim.48.grp_ref, bf16[4,128,1024]{2,1,0:T(8,128)(2,1)} %copy.70.k_ref, ...), custom_call_target="tpu_custom_call" | custom-call | flops 1073741824 | bytes 3932160 | tf_op jit(solution)/shard_map/pallas_call | solution.py:148
  95.4 23.9 %shard_map.146 = (f32[1024,128]{1,0:T(8,128)}, f32[1024,128]{1,0:T(8,128)}, f32[1024,128]{1,0:T(8,128)}) custom-call(s32[32]{0:T(128)} %reshape.344.present_ref, bf16[1024,128]{1,0:T(8,128)(2,1)} %q_ref.5, s32[1024,128]{1,0:T(8,128)} %broadcast_in_dim.48.grp_ref, bf16[4,128,1536]{2,1,0:T(8,128)(2,1)} %copy.71.k_ref, ...), custom_call_target="tpu_custom_call" | custom-call | flops 1610612736 | bytes 4980736 | tf_op jit(solution)/shard_map/pallas_call | solution.py:148
  119.3 0.0 collective-permute-done.4
  119.3 3.3 %slice_bitcast_fusion = (bf16[4,1536,128]{2,1,0:T(8,128)(2,1)}, bf16[4,128,1536]{1,2,0:T(8,128)(2,1)S(1)}) fusion(bf16[2,4,1536,128]{3,2,1,0:T(8,128)(2,1)} %collective-permute-done.4), kind=kLoop, calls=%fused_computation.21 | loop fusion | bytes 6291456 | tf_op jit(solution)/shard_map/squeeze | solution.py:272
  122.6 1.6 copy.72.k_ref
  124.2 24.0 %shard_map.147 = (f32[1024,128]{1,0:T(8,128)}, f32[1024,128]{1,0:T(8,128)}, f32[1024,128]{1,0:T(8,128)}) custom-call(s32[32]{0:T(128)} %reshape.344.present_ref, bf16[1024,128]{1,0:T(8,128)(2,1)} %q_ref.5, s32[1024,128]{1,0:T(8,128)} %broadcast_in_dim.48.grp_ref, bf16[4,128,1536]{2,1,0:T(8,128)(2,1)} %copy.72.k_ref, ...), custom_call_target="tpu_custom_call" | custom-call | flops 1610612736 | bytes 4980736 | tf_op jit(solution)/shard_map/pallas_call | solution.py:148
  148.2 2.8 %fusion.56 = (f32[1024]{0:T(1024)S(1)}, f32[1024]{0:T(1024)S(1)}, f32[1024]{0:T(1024)S(1)}, f32[1024]{0:T(1024)S(1)}, f32[1024]{0:T(1024)S(1)}, /*index=5*/f32[1024]{0:T(1024)S(1)}, f32[1024]{0:T(1024)S(1)}) fusion(f32[1024,1]{1,0:T(8,128)S(1)} %copy.73, f32[1024,128]{1,0:T(8,128)} %get-tuple-element.45, f32[1024,1]{1,0:T(8,128)S(1)} %copy.75, ...), kind=kLoop, calls=%fused_computation.65 | loop fusion | flops 18432 | bytes 61440 | tf_op jit(solution)/shard_map/exp | solution.py:223
  151.1 0.0 copy-start.9
  151.1 3.9 %fusion.41 = bf16[1024,128]{1,0:T(8,128)(2,1)} fusion(bf16[1024,128]{1,0:T(8,128)(2,1)} %param.17, f32[1024,1024]{0,1:T(8,128)S(1)} %copy-done.3, f32[1024]{0:T(1024)S(1)} %get-tuple-element.67, f32[1024,128]{1,0:T(8,128)} %get-tuple-element.46, f32[1024,128]{1,0:T(8,128)} %get-tuple-element.44, f32[1024,128]{1,0:T(8,128)} %get-tuple-element.41, ...), kind=kOutput, calls=%fused_computation.35 | convolution fusion | flops 271974400 | bytes 6324224 | tf_op jit(solution)/shard_map/while/body/eval_jaxpr/hqk,khd->qhd/dot_general | solution.py:195
  155.0 8.1 %all-to-all-start = ((bf16[16,64,128]{2,1,0:T(8,128)(2,1)}), bf16[16,64,128]{2,1,0:T(8,128)(2,1)S(1)}, u32[]{:S(2)}, u32[]{:S(2)}) async-start(bf16[16,64,128]{2,1,0:T(8,128)(2,1)} %bitcast.17), calls=%async_computation | async-start | bytes 524288 | tf_op jit(solution)/shard_map/all_to_all | solution.py:283
  163.1 0.2 select_reduce_fusion
  163.3 8.3 %all-to-all-done = bf16[16,64,128]{2,1,0:T(8,128)(2,1)S(1)} async-done(((bf16[16,64,128]{2,1,0:T(8,128)(2,1)}), bf16[16,64,128]{2,1,0:T(8,128)(2,1)S(1)}, u32[]{:S(2)}, u32[]{:S(2)}) %all-to-all-start) | async-done | bytes 262176 | tf_op jit(solution)/shard_map/all_to_all | solution.py:283
  171.6 5.1 %multiply_reduce_fusion = (f32[64]{0:T(128)S(1)}, f32[64,2048]{1,0:T(8,128)S(1)}) fusion(bf16[2048,2048]{1,0:T(8,128)(2,1)} %all-gather.2.cloned.1.call-done, bf16[64,2048]{1,0:T(8,128)(2,1)S(1)} %copy-done.9, bf16[16,64,128]{2,1,0:T(8,128)(2,1)S(1)} %all-to-all-done), kind=kOutput, calls=%fused_computation.45 | convolution fusion | flops 537395136 | bytes 9437440 | tf_op jit(solution)/shard_map/dot_general | solution.py:284
  176.7 0.8 convolution_convert_fusion
  177.5 29.8 %all_to_all.26 = bf16[32,16,2048]{2,1,0:T(8,128)(2,1)S(1)} all-to-all(bf16[32,16,2048]{2,1,0:T(8,128)(2,1)S(1)} %bitcast.111), channel_id=1, replica_groups=mesh['req'=8,'exp'=16] {'exp'}, dimensions={0} | all-to-all | bytes 4194304 | tf_op jit(solution)/shard_map/all_to_all | solution.py:302
  207.2 5.6 %fusion.4 = f32[2,16,16,704]{3,2,1,0:T(8,128)} fusion(bf16[2,2048,704]{1,2,0:T(8,128)(2,1)} %param.27, bf16[16,2,16,2048]{3,2,1,0:T(8,128)(2,1)S(1)} %bitcast.113), kind=kOutput, calls=%fused_computation.4 | convolution fusion | flops 1476395008 | bytes 9306112 | tf_op jit(solution)/shard_map/secd,edf->secf/dot_general | solution.py:305
  212.8 9.7 %fusion.11 = bf16[16,2,16,2048]{3,2,0,1:T(8,128)(2,1)} fusion(bf16[2,704,2048]{2,1,0:T(8,128)(2,1)} %param.29, f32[2,16,16,704]{3,2,1,0:T(8,128)} %fusion.4, bf16[2,2048,704]{1,2,0:T(8,128)(2,1)} %param.28, bf16[16,2,16,2048]{3,2,1,0:T(8,128)(2,1)S(1)} %bitcast.114), kind=kOutput, calls=%fused_computation.12 | convolution fusion | flops 2956001280 | bytes 17170432 | tf_op jit(solution)/shard_map/secf,efd->secd/dot_general | solution.py:308
  222.6 1.7 copy.83
  224.3 0.0 copy-start.1
  224.3 28.5 %all_to_all.27 = bf16[32,16,2048]{2,1,0:T(8,128)(2,1)S(1)} all-to-all(bf16[32,16,2048]{2,1,0:T(8,128)(2,1)S(1)} %bitcast.112), channel_id=1, replica_groups=mesh['req'=8,'exp'=16] {'exp'}, dimensions={0} | all-to-all | bytes 4194304 | tf_op jit(solution)/shard_map/all_to_all | solution.py:309
  252.8 1.2 fusion.14
  (37 shorter events, 0.1 us)
Async XLA Ops:
  6.5 56.6 %copy-start = (bf16[1024,128]{1,0:T(8,128)(2,1)S(1)}, bf16[1024,128]{1,0:T(8,128)(2,1)}, u32[]{:S(2)}) copy-start(bf16[1024,128]{1,0:T(8,128)(2,1)} %param.16) | copy-start | bytes 786436
  6.5 165.1 %all-gather.2.cloned.1.call-start = ((), (), s32[]{:S(2)}) async-start(), calls=%async_computation.3 | async-start | bytes 8912896 | tf_op jit(solution)/shard_map/all_gather | solution.py:282
  9.6 26.2 %collective-permute-start.1 = (bf16[2,4,512,128]{3,2,1,0:T(8,128)(2,1)}, bf16[2,4,512,128]{3,2,1,0:T(8,128)(2,1)S(1)}, u32[]{:S(2)}, u32[]{:S(2)}) collective-permute-start(bf16[2,4,512,128]{3,2,1,0:T(8,128)(2,1)} %pad_maximum_fusion.1), channel_id=1, source_target_pairs={{0,32},{16,48},{32,64},{48,80},{64,96},{80,112},{96,0},{112,16},{1... | collective-permute-start | bytes 3145736 | tf_op jit(solution)/shard_map/ppermute | solution.py:264
  11.1 48.3 %collective-permute-start.2 = (bf16[2,4,512,128]{3,2,1,0:T(8,128)(2,1)}, bf16[2,4,512,128]{3,2,1,0:T(8,128)(2,1)S(1)}, u32[]{:S(2)}, u32[]{:S(2)}) collective-permute-start(bf16[2,4,512,128]{3,2,1,0:T(8,128)(2,1)} %pad_maximum_fusion.1), channel_id=1, source_target_pairs={{0,64},{16,80},{32,96},{48,112},{64,0},{80,16},{96,32},{112,48},{1... | collective-permute-start | bytes 3145736 | tf_op jit(solution)/shard_map/ppermute | solution.py:264
  13.9 46.7 %collective-permute-start.3 = (bf16[2,4,512,128]{3,2,1,0:T(8,128)(2,1)}, bf16[2,4,512,128]{3,2,1,0:T(8,128)(2,1)S(1)}, u32[]{:S(2)}, u32[]{:S(2)}) collective-permute-start(bf16[2,4,512,128]{3,2,1,0:T(8,128)(2,1)} %pad_maximum_fusion.1), channel_id=1, source_target_pairs={{0,96},{16,112},{32,0},{48,16},{64,32},{80,48},{96,64},{112,80},{1... | collective-permute-start | bytes 3145736 | tf_op jit(solution)/shard_map/ppermute | solution.py:264
  15.3 58.1 %collective-permute-start = (bf16[2,4,512,128]{3,2,1,0:T(8,128)(2,1)}, bf16[2,4,512,128]{3,2,1,0:T(8,128)(2,1)}, u32[]{:S(2)}, u32[]{:S(2)}) collective-permute-start(bf16[2,4,512,128]{3,2,1,0:T(8,128)(2,1)} %pad_maximum_fusion.1), channel_id=1, source_target_pairs={{0,16},{16,0},{32,48},{48,32},{64,80},{80,64},{96,112},{112,96},{1... | collective-permute-start | bytes 3145736 | tf_op jit(solution)/shard_map/ppermute | solution.py:261
  16.1 45.7 %copy-start.10 = (s32[64,4]{0,1:T(4,128)S(1)}, s32[64,4]{0,1:T(4,128)}, u32[]{:S(2)}) copy-start(s32[64,4]{0,1:T(4,128)} %param.25) | copy-start | bytes 3076
  16.1 46.0 %copy-start.15 = (s32[1,8]{1,0:T(1,128)S(1)}, s32[1,8]{1,0:T(1,128)}, u32[]{:S(2)}) copy-start(s32[1,8]{1,0:T(1,128)} %param.20) | copy-start | bytes 100
  16.1 46.1 %copy-start.13 = (s32[1,8]{1,0:T(1,128)S(1)}, s32[1,8]{1,0:T(1,128)}, u32[]{:S(2)}) copy-start(s32[1,8]{1,0:T(1,128)} %param.21) | copy-start | bytes 100
  37.0 26.1 %copy-start.14 = (bf16[1024,128]{1,0:T(8,128)(2,1)S(1)}, bf16[1024,128]{1,0:T(8,128)(2,1)}, u32[]{:S(2)}) copy-start(bf16[1024,128]{1,0:T(8,128)(2,1)} %q_ref.5) | copy-start | bytes 786436
  61.8 57.5 %collective-permute-start.4 = (bf16[2,4,1536,128]{3,2,1,0:T(8,128)(2,1)}, bf16[2,4,1536,128]{3,2,1,0:T(8,128)(2,1)}, u32[]{:S(2)}, u32[]{:S(2)}) collective-permute-start(bf16[2,4,1536,128]{3,2,1,0:T(8,128)(2,1)} %constant_dynamic-update-slice_fusion), channel_id=1, source_target_pairs={{0,16},{16,0},{32,48},{48,32},{64,80},{80,64},{96,112},{112,96},{1... | collective-permute-start | bytes 9437192 | tf_op jit(solution)/shard_map/ppermute | solution.py:269
  64.2 2.0 copy-start.2
  64.3 4.2 %copy-start.12 = (bf16[64,4]{0,1:T(4,128)(2,1)S(1)}, bf16[64,4]{0,1:T(4,128)(2,1)}, u32[]{:S(2)}) copy-start(bf16[64,4]{0,1:T(4,128)(2,1)} %param.26) | copy-start | bytes 1540
  64.3 4.2 %copy-start.11 = (bf16[2048]{0:T(1024)(128)(2,1)S(1)}, bf16[2048]{0:T(1024)(128)(2,1)}, u32[]{:S(2)}) copy-start(bf16[2048]{0:T(1024)(128)(2,1)} %param.24) | copy-start | bytes 12292
  71.8 1.6 copy-start.4
  124.2 24.1 %copy-start.5 = (f32[1024,128]{1,0:T(8,128)S(1)}, f32[1024,128]{1,0:T(8,128)}, u32[]{:S(2)}) copy-start(f32[1024,128]{1,0:T(8,128)} %get-tuple-element.42) | copy-start | bytes 1572868
  124.2 24.1 %copy-start.6 = (f32[1024,128]{1,0:T(8,128)S(1)}, f32[1024,128]{1,0:T(8,128)}, u32[]{:S(2)}) copy-start(f32[1024,128]{1,0:T(8,128)} %get-tuple-element.47) | copy-start | bytes 1572868
  124.2 24.1 %copy-start.7 = (f32[1024,128]{1,0:T(8,128)S(1)}, f32[1024,128]{1,0:T(8,128)}, u32[]{:S(2)}) copy-start(f32[1024,128]{1,0:T(8,128)} %get-tuple-element.43) | copy-start | bytes 1572868
  124.2 24.1 %copy-start.8 = (f32[1024,128]{1,0:T(8,128)S(1)}, f32[1024,128]{1,0:T(8,128)}, u32[]{:S(2)}) copy-start(f32[1024,128]{1,0:T(8,128)} %get-tuple-element.48) | copy-start | bytes 1572868
  148.2 2.8 %copy-start.3 = (f32[1024,1024]{0,1:T(8,128)S(1)}, f32[1024,1024]{0,1:T(8,128)}, u32[]{:S(2)}) copy-start(f32[1024,1024]{0,1:T(8,128)} %copy-done.2) | copy-start | bytes 12582916
  151.1 20.5 %copy-start.9 = (bf16[64,2048]{1,0:T(8,128)(2,1)S(1)}, bf16[64,2048]{1,0:T(8,128)(2,1)}, u32[]{:S(2)}) copy-start(bf16[64,2048]{1,0:T(8,128)(2,1)} %param.22) | copy-start | bytes 786436
  155.0 16.6 %all-to-all-start = ((bf16[16,64,128]{2,1,0:T(8,128)(2,1)}), bf16[16,64,128]{2,1,0:T(8,128)(2,1)S(1)}, u32[]{:S(2)}, u32[]{:S(2)}) async-start(bf16[16,64,128]{2,1,0:T(8,128)(2,1)} %bitcast.17), calls=%async_computation | async-start | bytes 524288 | tf_op jit(solution)/shard_map/all_to_all | solution.py:283
  224.3 29.7 %copy-start.1 = (bf16[1024,128]{1,0:T(8,128)(2,1)S(1)}, bf16[1024,128]{1,0:T(8,128)(2,1)}, u32[]{:S(2)}) copy-start(bf16[1024,128]{1,0:T(8,128)(2,1)} %param.16) | copy-start | bytes 786436
Sparse Core Ops, SparseCore 0:
  9.5 73.3 all-gather.1

commit v4 on v2

--- a/solution.py
+++ b/solution.py
@@ -90,7 +90,7 @@
 
 
 QUERY_BLOCK = 128
-KEY_BLOCK = 1024
+KEY_BLOCK = 2048
 
 
 def prefix_kernel(present_ref, q_ref, grp_ref, k_ref, v_ref, acc_ref, m_ref, l_ref):
@@ -115,17 +115,21 @@
             s = lax.dot_general(
                 q_ref[rows, :], k, (((1,), (1,)), ((), ())), preferred_element_type=jnp.float32
             ) * scaling
-            mask = grp_ref[rows, :][:, :1] == g
-            s = jnp.where(mask, s, NEG)
+            mask = grp_ref[rows, :] == g
             m_prev = m_ref[rows, :]
-            m_new = jnp.maximum(m_prev, jnp.max(s, axis=1, keepdims=True))
-            alpha = jnp.exp(m_prev - m_new)
-            p = jnp.where(mask, jnp.exp(s - m_new[:, :1]), 0.0)
-            l_ref[rows, :] = alpha * l_ref[rows, :] + jnp.sum(p, axis=1, keepdims=True)
-            acc_ref[rows, :] = alpha * acc_ref[rows, :] + jnp.dot(
-                p.astype(jnp.bfloat16), v, preferred_element_type=jnp.float32
+            m_cand = jnp.maximum(m_prev, jnp.max(s, axis=1, keepdims=True))
+            p = jnp.exp(s - m_cand[:, :1])
+            alpha = jnp.exp(m_prev - m_cand)
+            l_ref[rows, :] = jnp.where(
+                mask, alpha * l_ref[rows, :] + jnp.sum(p, axis=1, keepdims=True), l_ref[rows, :]
             )
-            m_ref[rows, :] = m_new
+            acc_ref[rows, :] = jnp.where(
+                mask,
+                alpha * acc_ref[rows, :]
+                + jnp.dot(p.astype(jnp.bfloat16), v, preferred_element_type=jnp.float32),
+                acc_ref[rows, :],
+            )
+            m_ref[rows, :] = jnp.where(mask, m_cand, m_prev)
 
         return carry
 

time: 249 us -> 249 us (level)
  waiting for transfers between devices: 82.5 us -> 93.9 us
  Pallas kernels: 39.6 us -> 28.4 us
    pallas_call x1, Pallas kernels: 39.6 us -> 28.4 us  [attend_prefix_local(): pl.pallas_call(prefix_kernel, grid_spec=pltpu.PrefetchScalarGridSpec(num_...]
    all_gather x1, waiting for transfers between devices: 11.9 us -> 22.8 us  [per_device(): full_proj = lax.all_gather(out_proj, 'exp', axis=0, tiled=True)]
  transfers between devices with their start and end apart: 4 -> 4, of which waited for: 4 -> 4; matrix products, arithmetic and copies ran while one was open for 6% -> 6% of each run, Pallas kernels for 16% -> 11%
where the time goes in v4:
time: 249 us; the launch traced here: 248 us
  waiting for transfers between devices  93.9 us (38%)
  blocking collectives  64.2 us (26%)
  matrix products  28.4 us (11%)
  Pallas kernels  28.4 us (11%)
  between operations  13.3 us (5%)
  local copies, waits for them, and re-layouts  7.22 us (3%)
  starting transfers between devices  7.03 us (3%)
  other arithmetic  5.76 us (2%)
    all_gather x1, waiting for transfers between devices, per_device(): lax.all_gather(prefix_values, 'req', axis=1, tiled=True)  33.8 us
    all_to_all x1, blocking collectives, per_device(): lax.all_to_all(buffer, 'exp', split_axis=0, concat_axis=0, tiled=True)  33.3 us
    all_to_all x1, blocking collectives, per_device(): lax.all_to_all(expert_out.astype(jnp.bfloat16).reshape(EXPERTS, slots, re...  30.8 us
    pallas_call x1, Pallas kernels, attend_prefix_local(): pl.pallas_call(prefix_kernel, grid_spec=pltpu.PrefetchScalarGridSpec(num_...  28.4 us
    all_gather x1, waiting for transfers between devices, per_device(): lax.all_gather(prefix_keys, 'req', axis=1, tiled=True)  24.5 us
    all_gather x1, waiting for transfers between devices, per_device(): full_proj = lax.all_gather(out_proj, 'exp', axis=0, tiled=True)  22.8 us
    all_to_all x1, waiting for transfers between devices, per_device(): lax.all_to_all(attended, 'exp', split_axis=0, concat_axis=1, tiled=True)  10.7 us
    dot_general x1, matrix products, per_device(): jnp.einsum('secf,efd->secd', hidden, w_down, preferred_element_type=jnp.f...  9.73 us
  transfers between devices with their start and end apart: 4, of which 4 were waited for; matrix products, arithmetic and copies ran while one was open for 6% of the time, Pallas kernels for 11%

profile of v4, /device:TPU:0, one launch (start us, length us, event | category | flops | bytes accessed | tf_op | source)
XLA Modules:
  0.0 248.2 jit_solution(7861734839390123143)
XLA Ops:
  6.5 0.0 copy-start
  6.5 0.0 all-gather.4.cloned.1.call-start
  6.5 0.7 all-gather.4.cloned.1.call-update
  7.3 0.0 all-gather.6.cloned.1.call-start
  7.3 0.7 all-gather.6.cloned.1.call-update
  8.0 0.0 all-gather.8.cloned.1.call-start
  8.1 0.7 all-gather.8.cloned.1.call-update
  8.7 0.8 copy.62
  9.5 0.1 eq.113
  9.6 0.1 eq.109
  9.7 0.8 reduce_window_sum.24
  10.6 0.1 convert_reduce_fusion.1
  10.7 0.7 subtract_bitcast_fusion
  11.3 0.7 select_reduce_fusion.2
  12.1 0.0 copy-done
  12.1 2.0 fusion.60
  14.1 0.0 copy-start.1
  14.1 0.0 copy-start.5
  14.1 0.0 copy-start.4
  14.1 1.9 copy-done.1
  16.1 0.6 fusion.6
  16.7 0.2 copy.60
  16.9 0.2 fusion.58
  17.1 0.1 copy.57
  17.2 0.6 reshape.322.present_ref
  17.8 0.2 copy.58
  18.0 0.6 reduce-window.6
  18.6 0.2 slice_reduce_fusion
  18.9 0.1 fusion.56
  19.0 0.1 reduce_sum.80
  19.1 0.1 copy.65
  19.1 0.0 copy-done.5
  19.1 0.0 copy-done.4
  19.2 24.5 %all-gather.4.cloned.1.call-done.k_ref = bf16[4,4096,128]{2,1,0:T(8,128)(2,1)} async-done(((bf16[4,512,128]{2,1,0:T(8,128)(2,1)}), bf16[4,4096,128]{2,1,0:T(8,128)(2,1)}) %all-gather.4.cloned.1.call-update) | async-done | bytes 4194320 | tf_op jit(solution)/shard_map/all_gather | solution.py:265
  43.7 33.8 %all-gather.6.cloned.1.call-done.v_ref = bf16[4,4096,128]{2,1,0:T(8,128)(2,1)} async-done(((bf16[4,512,128]{2,1,0:T(8,128)(2,1)}), bf16[4,4096,128]{2,1,0:T(8,128)(2,1)}) %all-gather.6.cloned.1.call-update) | async-done | bytes 4194320 | tf_op jit(solution)/shard_map/all_gather | solution.py:266
  77.5 1.0 broadcast_in_dim.68.grp_ref
  78.5 0.0 copy-start.6
  78.5 28.4 %shard_map.145 = (f32[1024,128]{1,0:T(8,128)}, f32[1024,128]{1,0:T(8,128)}, f32[1024,128]{1,0:T(8,128)}) custom-call(s32[32]{0:T(128)} %reshape.322.present_ref, bf16[1024,128]{1,0:T(8,128)(2,1)} %q_ref.1, s32[1024,128]{1,0:T(8,128)} %broadcast_in_dim.68.grp_ref, bf16[4,4096,128]{2,1,0:T(8,128)(2,1)} %all-gather.4.cloned.1.call-done.k_ref, ...), custom_call_target="tpu_custom_call" | custom-call | flops 4294967296 | bytes 10223616 | tf_op jit(solution)/shard_map/pallas_call | solution.py:152
  106.8 0.0 copy-start.3
  106.8 0.0 copy-start.2
  106.8 1.7 fusion.52
  108.6 0.0 copy-done.6
  108.6 4.1 %fusion.41 = bf16[1024,128]{1,0:T(8,128)(2,1)} fusion(bf16[1024,128]{1,0:T(8,128)(2,1)S(1)} %copy-done.6, f32[1024,1024]{0,1:T(8,128)} %copy-done.1, f32[1024]{0:T(1024)S(1)} %get-tuple-element.45, f32[1024,128]{1,0:T(8,128)} %get-tuple-element.24, f32[1024]{0:T(1024)S(1)} %get-tuple-element.38, f32[1024]{0:T(1024)S(1)} %get-tuple-element.40, ...), kind=kOutput, calls=%fused_computation.30 | convolution fusion | flops 271187968 | bytes 5259264 | tf_op jit(solution)/shard_map/while/body/eval_jaxpr/hqk,khd->qhd/dot_general | solution.py:199
  112.6 6.9 %all-to-all-start = ((bf16[16,64,128]{2,1,0:T(8,128)(2,1)}), bf16[16,64,128]{2,1,0:T(8,128)(2,1)S(1)}, u32[]{:S(2)}, u32[]{:S(2)}) async-start(bf16[16,64,128]{2,1,0:T(8,128)(2,1)} %bitcast.6), calls=%async_computation | async-start | bytes 524288 | tf_op jit(solution)/shard_map/all_to_all | solution.py:277
  119.6 0.0 copy-done.3
  119.6 0.2 select_reduce_fusion
  119.8 10.7 %all-to-all-done = bf16[16,64,128]{2,1,0:T(8,128)(2,1)S(1)} async-done(((bf16[16,64,128]{2,1,0:T(8,128)(2,1)}), bf16[16,64,128]{2,1,0:T(8,128)(2,1)S(1)}, u32[]{:S(2)}, u32[]{:S(2)}) %all-to-all-start) | async-done | bytes 262176 | tf_op jit(solution)/shard_map/all_to_all | solution.py:277
  130.5 22.8 %all-gather.8.cloned.1.call-done = bf16[2048,2048]{1,0:T(8,128)(2,1)} async-done(((bf16[128,2048]{1,0:T(8,128)(2,1)}), bf16[2048,2048]{1,0:T(8,128)(2,1)}) %all-gather.8.cloned.1.call-update) | async-done | bytes 8388624 | tf_op jit(solution)/shard_map/all_gather | solution.py:276
  153.3 0.0 copy-done.2
  153.3 5.1 %multiply_reduce_fusion = (f32[64]{0:T(128)S(1)}, f32[64,2048]{1,0:T(8,128)S(1)}) fusion(bf16[2048,2048]{1,0:T(8,128)(2,1)} %all-gather.8.cloned.1.call-done, bf16[64,2048]{1,0:T(8,128)(2,1)S(1)} %copy-done.2, bf16[16,64,128]{2,1,0:T(8,128)(2,1)S(1)} %all-to-all-done), kind=kOutput, calls=%fused_computation.37 | convolution fusion | flops 537395136 | bytes 9437440 | tf_op jit(solution)/shard_map/dot_general | solution.py:278
  158.4 0.8 convolution_convert_fusion
  159.2 33.3 %all_to_all.26 = bf16[32,16,2048]{2,1,0:T(8,128)(2,1)S(1)} all-to-all(bf16[32,16,2048]{2,1,0:T(8,128)(2,1)S(1)} %bitcast.91), channel_id=1, replica_groups=mesh['req'=8,'exp'=16] {'exp'}, dimensions={0} | all-to-all | bytes 4194304 | tf_op jit(solution)/shard_map/all_to_all | solution.py:296
  192.5 5.6 %fusion.4 = f32[2,16,16,704]{3,2,1,0:T(8,128)} fusion(bf16[2,2048,704]{1,2,0:T(8,128)(2,1)} %param.27, bf16[16,2,16,2048]{3,2,1,0:T(8,128)(2,1)S(1)} %bitcast.93), kind=kOutput, calls=%fused_computation.4 | convolution fusion | flops 1476395008 | bytes 9306112 | tf_op jit(solution)/shard_map/secd,edf->secf/dot_general | solution.py:299
  198.1 9.7 %fusion.11 = bf16[16,2,16,2048]{3,2,0,1:T(8,128)(2,1)} fusion(bf16[2,704,2048]{2,1,0:T(8,128)(2,1)} %param.29, f32[2,16,16,704]{3,2,1,0:T(8,128)} %fusion.4, bf16[2,2048,704]{1,2,0:T(8,128)(2,1)} %param.28, bf16[16,2,16,2048]{3,2,1,0:T(8,128)(2,1)S(1)} %bitcast.94), kind=kOutput, calls=%fused_computation.12 | convolution fusion | flops 2956001280 | bytes 17170432 | tf_op jit(solution)/shard_map/secf,efd->secd/dot_general | solution.py:302
  207.9 1.7 copy.68
  209.6 30.8 %all_to_all.27 = bf16[32,16,2048]{2,1,0:T(8,128)(2,1)S(1)} all-to-all(bf16[32,16,2048]{2,1,0:T(8,128)(2,1)S(1)} %bitcast.92), channel_id=1, replica_groups=mesh['req'=8,'exp'=16] {'exp'}, dimensions={0} | all-to-all | bytes 4194304 | tf_op jit(solution)/shard_map/all_to_all | solution.py:303
  240.5 1.2 fusion.14
  (9 shorter events, 0.1 us)
Async XLA Ops:
  6.5 5.5 %copy-start = (bf16[1024,128]{1,0:T(8,128)(2,1)S(1)}, bf16[1024,128]{1,0:T(8,128)(2,1)}, u32[]{:S(2)}) copy-start(bf16[1024,128]{1,0:T(8,128)(2,1)} %param.16) | copy-start | bytes 786436
  6.5 37.1 %all-gather.4.cloned.1.call-start = ((), (), s32[]{:S(2)}) async-start(), calls=%async_computation.3 | async-start | bytes 4718592 | tf_op jit(solution)/shard_map/all_gather | solution.py:265
  7.3 70.2 %all-gather.6.cloned.1.call-start = ((), (), s32[]{:S(2)}) async-start(), calls=%async_computation.4 | async-start | bytes 4718592 | tf_op jit(solution)/shard_map/all_gather | solution.py:266
  8.0 145.3 %all-gather.8.cloned.1.call-start = ((), (), s32[]{:S(2)}) async-start(), calls=%async_computation.5 | async-start | bytes 8912896 | tf_op jit(solution)/shard_map/all_gather | solution.py:276
  14.1 2.0 copy-start.1
  14.1 5.0 %copy-start.5 = (bf16[64,4]{0,1:T(4,128)(2,1)S(1)}, bf16[64,4]{0,1:T(4,128)(2,1)}, u32[]{:S(2)}) copy-start(bf16[64,4]{0,1:T(4,128)(2,1)} %param.26) | copy-start | bytes 1540
  14.1 5.0 %copy-start.4 = (bf16[2048]{0:T(1024)(128)(2,1)S(1)}, bf16[2048]{0:T(1024)(128)(2,1)}, u32[]{:S(2)}) copy-start(bf16[2048]{0:T(1024)(128)(2,1)} %param.24) | copy-start | bytes 12292
  78.5 30.1 %copy-start.6 = (bf16[1024,128]{1,0:T(8,128)(2,1)S(1)}, bf16[1024,128]{1,0:T(8,128)(2,1)}, u32[]{:S(2)}) copy-start(bf16[1024,128]{1,0:T(8,128)(2,1)} %param.17) | copy-start | bytes 786436
  106.8 12.8 %copy-start.3 = (s32[64,4]{0,1:T(4,128)S(1)}, s32[64,4]{0,1:T(4,128)}, u32[]{:S(2)}) copy-start(s32[64,4]{0,1:T(4,128)} %param.25) | copy-start | bytes 3076
  106.8 46.5 %copy-start.2 = (bf16[64,2048]{1,0:T(8,128)(2,1)S(1)}, bf16[64,2048]{1,0:T(8,128)(2,1)}, u32[]{:S(2)}) copy-start(bf16[64,2048]{1,0:T(8,128)(2,1)} %param.22) | copy-start | bytes 786436
  112.6 17.9 %all-to-all-start = ((bf16[16,64,128]{2,1,0:T(8,128)(2,1)}), bf16[16,64,128]{2,1,0:T(8,128)(2,1)S(1)}, u32[]{:S(2)}, u32[]{:S(2)}) async-start(bf16[16,64,128]{2,1,0:T(8,128)(2,1)} %bitcast.6), calls=%async_computation | async-start | bytes 524288 | tf_op jit(solution)/shard_map/all_to_all | solution.py:277
Sparse Core Ops, SparseCore 0:
  9.1 34.5 all-gather.3
  45.4 32.0 all-gather.5
  79.6 73.6 all-gather.7

commit v5 on v4

--- a/solution.py
+++ b/solution.py
@@ -259,12 +259,25 @@
     tok_dev = residual.shape[0]
     request, position, tok_group = token_layout(lengths, groups)
     request, position, tok_group = (request[0], position[0], tok_group[0])
-    prefix_part = attend_prefix_local(
-        queries,
-        tok_group,
-        lax.all_gather(prefix_keys, "req", axis=1, tiled=True),
-        lax.all_gather(prefix_values, "req", axis=1, tiled=True),
-    )
+    req_count = lax.axis_size("req")
+    local_kv = jnp.stack([prefix_keys, prefix_values])
+    partner = [(i, i ^ 1) for i in range(req_count)]
+    partner_kv = lax.ppermute(local_kv, "req", partner)
+    ring_kv = jnp.concatenate(
+        [
+            lax.ppermute(local_kv, "req", [(i, (i + 2 * s) % req_count) for i in range(req_count)])
+            for s in range(1, req_count // 2)
+        ],
+        axis=2,
+    )
+    forwarded_kv = lax.ppermute(ring_kv, "req", partner)
+    prefix_part = None
+    for chunk in (
+        jnp.concatenate([local_kv, ring_kv], axis=2),
+        jnp.concatenate([partner_kv, forwarded_kv], axis=2),
+    ):
+        part = attend_prefix_local(queries, tok_group, chunk[0], chunk[1])
+        prefix_part = part if prefix_part is None else combine(prefix_part, part)
     suffix_part = attend_suffix(queries, keys, values, request, position)
     weighted, maxima, totals = combine(prefix_part, suffix_part)
     attended = (

time: 249 us -> 234 us (0.940)
  waiting for transfers between devices: 93.9 us -> 51.5 us
  local copies, waits for them, and re-layouts: 7.22 us -> 22.2 us
  starting transfers between devices: 7.03 us -> 13.7 us
  other arithmetic: 5.76 us -> 10.4 us
    all_gather x2 -> x0, waiting for transfers between devices: 58.3 us -> none  [the longest x1 33.8 us: per_device(): lax.all_gather(prefix_values, 'req', axis=1, tiled=True)]
    ppermute x0 -> x5, waiting for transfers between devices: none -> 42.2 us  [the longest x3 42.2 us: per_device(): lax.ppermute(local_kv, 'req', [(i, (i + 2 * s) % req_count) for i in rang...]
    all_gather x1, waiting for transfers between devices: 22.8 us -> 0.01 us  [per_device(): full_proj = lax.all_gather(out_proj, 'exp', axis=0, tiled=True)]
    squeeze x0 -> x2, local copies, waits for them, and re-layouts: none -> 6.79 us  [per_device(): part = attend_prefix_local(queries, tok_group, chunk[0], chunk[1])]
    ppermute x0 -> x5, starting transfers between devices: none -> 5.74 us  [the longest x3 5.74 us: per_device(): lax.ppermute(local_kv, 'req', [(i, (i + 2 * s) % req_count) for i in rang...]
    concatenate x0 -> x1, local copies, waits for them, and re-layouts: none -> 4.05 us  [per_device(): jnp.concatenate([partner_kv, forwarded_kv], axis=2)]
    concatenate x0 -> x2, other arithmetic: none -> 3.2 us  [the longest x1 1.81 us: per_device(): jnp.concatenate([lax.ppermute(local_kv, 'req', [(i, (i + 2 * s) % req_cou...]
    unnamed x15 -> x32, local copies, waits for them, and re-layouts: 2.75 us -> 5.19 us
  transfers between devices with their start and end apart: 4 -> 7, of which waited for: 4 -> 3; matrix products, arithmetic and copies ran while one was open for 6% -> 15% of each run, Pallas kernels for 11% -> 12%
where the time goes in v5:
time: 234 us; the launch traced here: 233 us
  blocking collectives  64.2 us (27%)
  waiting for transfers between devices  51.5 us (22%)
  matrix products  28.7 us (12%)
  Pallas kernels  28.2 us (12%)
  local copies, waits for them, and re-layouts  22.2 us (9%)
  starting transfers between devices  13.7 us (6%)
  between operations  13.7 us (6%)
  other arithmetic  10.4 us (4%)
    ppermute x3, waiting for transfers between devices, per_device(): lax.ppermute(local_kv, 'req', [(i, (i + 2 * s) % req_count) for i in rang...  42.2 us
    all_to_all x1, blocking collectives, per_device(): lax.all_to_all(buffer, 'exp', split_axis=0, concat_axis=0, tiled=True)  32.9 us
    all_to_all x1, blocking collectives, per_device(): lax.all_to_all(expert_out.astype(jnp.bfloat16).reshape(EXPERTS, slots, re...  31.3 us
    pallas_call x2, Pallas kernels, attend_prefix_local(): pl.pallas_call(prefix_kernel, grid_spec=pltpu.PrefetchScalarGridSpec(num_...  28.2 us
    dot_general x1, matrix products, per_device(): jnp.einsum('secf,efd->secd', hidden, w_down, preferred_element_type=jnp.f...  9.73 us
    all_to_all x1, waiting for transfers between devices, per_device(): lax.all_to_all(attended, 'exp', split_axis=0, concat_axis=1, tiled=True)  8.61 us
    all_to_all x1, starting transfers between devices, per_device(): lax.all_to_all(attended, 'exp', split_axis=0, concat_axis=1, tiled=True)  7.99 us
    squeeze x2, local copies, waits for them, and re-layouts, per_device(): part = attend_prefix_local(queries, tok_group, chunk[0], chunk[1])  6.79 us
  transfers between devices with their start and end apart: 7, of which 3 were waited for; matrix products, arithmetic and copies ran while one was open for 15% of the time, Pallas kernels for 12%

profile of v5, /device:TPU:0, one launch (start us, length us, event | category | flops | bytes accessed | tf_op | source)
XLA Modules:
  0.0 232.7 jit_solution(16133506355638052192)
XLA Ops:
  6.5 0.7 all-gather.2.cloned.1.call-update
  7.3 0.0 copy-start.13
  7.3 2.4 %pad_maximum_fusion.2 = bf16[2,4,512,128]{3,2,1,0:T(8,128)(2,1)} fusion(bf16[1,4,512,128]{3,2,1,0:T(8,128)(2,1)} %bitcast.105, bf16[1,4,512,128]{3,2,1,0:T(8,128)(2,1)} %bitcast.107), kind=kLoop, calls=%fused_computation.37 | loop fusion | flops 524288 | bytes 2097152 | tf_op jit(solution)/shard_map/stack | solution.py:263
  9.6 1.6 collective-permute-start
  11.2 2.7 %collective-permute-start.1 = (bf16[2,4,512,128]{3,2,1,0:T(8,128)(2,1)}, bf16[2,4,512,128]{3,2,1,0:T(8,128)(2,1)S(1)}, u32[]{:S(2)}, u32[]{:S(2)}) collective-permute-start(bf16[2,4,512,128]{3,2,1,0:T(8,128)(2,1)} %pad_maximum_fusion.2), channel_id=1, source_target_pairs={{0,64},{16,80},{32,96},{48,112},{64,0},{80,16},{96,32},{112,48},{1... | collective-permute-start | bytes 3145736 | tf_op jit(solution)/shard_map/ppermute | solution.py:268
  13.9 1.4 collective-permute-start.2
  15.4 0.0 collective-permute-start.3
  15.4 0.8 copy.62
  16.2 0.1 eq.120
  16.3 0.1 eq.116
  16.4 0.8 reduce_window_sum.24
  17.2 0.1 convert_reduce_fusion.1
  17.3 18.6 %collective-permute-done = bf16[2,4,512,128]{3,2,1,0:T(8,128)(2,1)S(1)} collective-permute-done((bf16[2,4,512,128]{3,2,1,0:T(8,128)(2,1)}, bf16[2,4,512,128]{3,2,1,0:T(8,128)(2,1)S(1)}, u32[]{:S(2)}, u32[]{:S(2)}) %collective-permute-start) | collective-permute-done | bytes 1048608 | tf_op jit(solution)/shard_map/ppermute | solution.py:268
  35.8 23.6 %collective-permute-done.1 = bf16[2,4,512,128]{3,2,1,0:T(8,128)(2,1)S(1)} collective-permute-done((bf16[2,4,512,128]{3,2,1,0:T(8,128)(2,1)}, bf16[2,4,512,128]{3,2,1,0:T(8,128)(2,1)S(1)}, u32[]{:S(2)}, u32[]{:S(2)}) %collective-permute-start.1) | collective-permute-done | bytes 1048608 | tf_op jit(solution)/shard_map/ppermute | solution.py:268
  59.5 0.0 collective-permute-done.2
  59.5 1.8 pad_maximum_fusion.1
  61.3 0.0 collective-permute-start.4
  61.3 0.1 select_reduce_fusion.2
  61.4 0.1 fusion.60
  61.6 0.1 copy.57
  61.7 0.6 reshape.333.present_ref
  62.3 0.0 copy-done
  62.3 2.0 fusion.62
  64.3 0.0 copy-start.2
  64.3 0.0 copy-start.10
  64.3 0.0 copy-start.9
  64.3 1.9 copy-done.2
  66.3 0.6 fusion.6
  66.9 1.1 copy.60
  68.0 1.0 copy.58
  69.0 0.6 reduce-window.6
  69.6 0.2 slice_reduce_fusion
  69.8 0.1 fusion.58
  69.9 0.1 reduce_sum.80
  70.1 0.1 copy.65
  70.1 0.0 copy-done.9
  70.2 0.0 collective-permute-done.3
  70.2 2.4 %constant_dynamic-update-slice_fusion.1 = bf16[2,4,2048,128]{3,2,1,0:T(8,128)(2,1)} fusion(bf16[2,4,512,128]{3,2,1,0:T(8,128)(2,1)} %collective-permute-done.3), kind=kLoop, calls=%fused_computation.78 | loop fusion | bytes 2097152
  72.6 1.4 pad_maximum_fusion
  74.0 2.3 %slice_bitcast_fusion.2 = (bf16[4,2048,128]{2,1,0:T(8,128)(2,1)}, bf16[4,2048,128]{2,1,0:T(8,128)(2,1)}) fusion(bf16[2,4,2048,128]{3,2,1,0:T(8,128)(2,1)S(1)} %pad_maximum_fusion), kind=kLoop, calls=%fused_computation.21 | loop fusion | bytes 8388608 | tf_op jit(solution)/shard_map/squeeze | solution.py:279
  76.3 1.1 broadcast_in_dim.74.grp_ref
  77.4 14.0 %shard_map.145 = (f32[1024,128]{1,0:T(8,128)}, f32[1024,128]{1,0:T(8,128)}, f32[1024,128]{1,0:T(8,128)}) custom-call(s32[32]{0:T(128)} %reshape.333.present_ref, bf16[1024,128]{1,0:T(8,128)(2,1)} %q_ref.3, s32[1024,128]{1,0:T(8,128)} %broadcast_in_dim.74.grp_ref, bf16[4,2048,128]{2,1,0:T(8,128)(2,1)} %get-tuple-element.54.k_ref, ...), custom_call_target="tpu_custom_call" | custom-call | flops 2147483648 | bytes 6029312 | tf_op jit(solution)/shard_map/pallas_call | solution.py:152
  91.4 0.0 collective-permute-done.4
  91.4 4.1 %constant_dynamic-update-slice_fusion = bf16[2,4,2048,128]{3,2,1,0:T(8,128)(2,1)} fusion(bf16[2,4,2048,128]{3,2,1,0:T(8,128)(2,1)} %constant_dynamic-update-slice_fusion.1, bf16[2,4,1536,128]{3,2,1,0:T(8,128)(2,1)} %collective-permute-done.4), kind=kLoop, calls=%fused_computation.77 | loop fusion | bytes 6291456 | tf_op jit(solution)/shard_map/concatenate | solution.py:277
  95.4 4.4 %slice_bitcast_fusion = (bf16[4,2048,128]{2,1,0:T(8,128)(2,1)}, bf16[4,2048,128]{2,1,0:T(8,128)(2,1)}) fusion(bf16[2,4,2048,128]{3,2,1,0:T(8,128)(2,1)} %constant_dynamic-update-slice_fusion), kind=kLoop, calls=%fused_computation.19 | loop fusion | bytes 8388608 | tf_op jit(solution)/shard_map/squeeze | solution.py:279
  99.9 0.0 copy-start.12
  99.9 14.2 %shard_map.146 = (f32[1024,128]{1,0:T(8,128)}, f32[1024,128]{1,0:T(8,128)}, f32[1024,128]{1,0:T(8,128)}) custom-call(s32[32]{0:T(128)} %reshape.333.present_ref, bf16[1024,128]{1,0:T(8,128)(2,1)} %q_ref.3, s32[1024,128]{1,0:T(8,128)} %broadcast_in_dim.74.grp_ref, bf16[4,2048,128]{2,1,0:T(8,128)(2,1)} %get-tuple-element.56.k_ref, ...), custom_call_target="tpu_custom_call" | custom-call | flops 2147483648 | bytes 6029312 | tf_op jit(solution)/shard_map/pallas_call | solution.py:152
  114.1 0.0 copy-done.3
  114.1 0.0 copy-start.8
  114.1 0.0 copy-start.7
  114.1 2.2 fusion.51
  116.3 4.3 %fusion.41 = bf16[1024,128]{1,0:T(8,128)(2,1)} fusion(bf16[1024,128]{1,0:T(8,128)(2,1)S(1)} %copy-done.12, f32[1024,1024]{0,1:T(8,128)} %copy-done.2, f32[1024]{0:T(1024)S(1)} %get-tuple-element.57, f32[1024,128]{1,0:T(8,128)} %get-tuple-element.41, f32[1024,128]{1,0:T(8,128)S(1)} %copy-done.14, f32[1024]{0:T(1024)S(1)} %get-tuple-element.45, ...), kind=kOutput, calls=%fused_computation.36 | convolution fusion | flops 271581184 | bytes 5791744 | tf_op jit(solution)/shard_map/while/body/eval_jaxpr/hqk,khd->qhd/dot_general | solution.py:199
  120.7 8.0 %all-to-all-start = ((bf16[16,64,128]{2,1,0:T(8,128)(2,1)}), bf16[16,64,128]{2,1,0:T(8,128)(2,1)S(1)}, u32[]{:S(2)}, u32[]{:S(2)}) async-start(bf16[16,64,128]{2,1,0:T(8,128)(2,1)} %bitcast.12), calls=%async_computation | async-start | bytes 524288 | tf_op jit(solution)/shard_map/all_to_all | solution.py:290
  128.7 0.0 copy-done.8
  128.7 0.2 select_reduce_fusion
  128.9 8.6 %all-to-all-done = bf16[16,64,128]{2,1,0:T(8,128)(2,1)S(1)} async-done(((bf16[16,64,128]{2,1,0:T(8,128)(2,1)}), bf16[16,64,128]{2,1,0:T(8,128)(2,1)S(1)}, u32[]{:S(2)}, u32[]{:S(2)}) %all-to-all-start) | async-done | bytes 262176 | tf_op jit(solution)/shard_map/all_to_all | solution.py:290
  137.5 5.1 %multiply_reduce_fusion = (f32[64]{0:T(128)S(1)}, f32[64,2048]{1,0:T(8,128)S(1)}) fusion(bf16[2048,2048]{1,0:T(8,128)(2,1)} %all-gather.2.cloned.1.call-done, bf16[64,2048]{1,0:T(8,128)(2,1)S(1)} %copy-done.7, bf16[16,64,128]{2,1,0:T(8,128)(2,1)S(1)} %all-to-all-done), kind=kOutput, calls=%fused_computation.44 | convolution fusion | flops 537395136 | bytes 9437440 | tf_op jit(solution)/shard_map/dot_general | solution.py:291
  142.6 0.8 convolution_convert_fusion
  143.4 32.9 %all_to_all.26 = bf16[32,16,2048]{2,1,0:T(8,128)(2,1)S(1)} all-to-all(bf16[32,16,2048]{2,1,0:T(8,128)(2,1)S(1)} %bitcast.101), channel_id=1, replica_groups=mesh['req'=8,'exp'=16] {'exp'}, dimensions={0} | all-to-all | bytes 4194304 | tf_op jit(solution)/shard_map/all_to_all | solution.py:309
  176.2 5.6 %fusion.4 = f32[2,16,16,704]{3,2,1,0:T(8,128)} fusion(bf16[2,2048,704]{1,2,0:T(8,128)(2,1)} %param.27, bf16[16,2,16,2048]{3,2,1,0:T(8,128)(2,1)S(1)} %bitcast.103), kind=kOutput, calls=%fused_computation.4 | convolution fusion | flops 1476395008 | bytes 9306112 | tf_op jit(solution)/shard_map/secd,edf->secf/dot_general | solution.py:312
  181.8 9.7 %fusion.11 = bf16[16,2,16,2048]{3,2,0,1:T(8,128)(2,1)} fusion(bf16[2,704,2048]{2,1,0:T(8,128)(2,1)} %param.29, f32[2,16,16,704]{3,2,1,0:T(8,128)} %fusion.4, bf16[2,2048,704]{1,2,0:T(8,128)(2,1)} %param.28, bf16[16,2,16,2048]{3,2,1,0:T(8,128)(2,1)S(1)} %bitcast.104), kind=kOutput, calls=%fused_computation.14 | convolution fusion | flops 2956001280 | bytes 17170432 | tf_op jit(solution)/shard_map/secf,efd->secd/dot_general | solution.py:315
  191.6 1.8 copy.68
  193.3 31.3 %all_to_all.27 = bf16[32,16,2048]{2,1,0:T(8,128)(2,1)S(1)} all-to-all(bf16[32,16,2048]{2,1,0:T(8,128)(2,1)S(1)} %bitcast.102), channel_id=1, replica_groups=mesh['req'=8,'exp'=16] {'exp'}, dimensions={0} | all-to-all | bytes 4194304 | tf_op jit(solution)/shard_map/all_to_all | solution.py:316
  224.7 1.2 fusion.14
  (30 shorter events, 0.1 us)
Async XLA Ops:
  6.5 55.7 %copy-start = (bf16[1024,128]{1,0:T(8,128)(2,1)S(1)}, bf16[1024,128]{1,0:T(8,128)(2,1)}, u32[]{:S(2)}) copy-start(bf16[1024,128]{1,0:T(8,128)(2,1)} %param.16) | copy-start | bytes 786436
  6.5 130.9 %all-gather.2.cloned.1.call-start = ((), (), s32[]{:S(2)}) async-start(), calls=%async_computation.3 | async-start | bytes 8912896 | tf_op jit(solution)/shard_map/all_gather | solution.py:289
  7.3 54.1 %copy-start.13 = (s32[1,8]{1,0:T(1,128)S(1)}, s32[1,8]{1,0:T(1,128)}, u32[]{:S(2)}) copy-start(s32[1,8]{1,0:T(1,128)} %param.20) | copy-start | bytes 100
  7.3 54.1 %copy-start.11 = (s32[1,8]{1,0:T(1,128)S(1)}, s32[1,8]{1,0:T(1,128)}, u32[]{:S(2)}) copy-start(s32[1,8]{1,0:T(1,128)} %param.21) | copy-start | bytes 100
  9.6 26.2 %collective-permute-start = (bf16[2,4,512,128]{3,2,1,0:T(8,128)(2,1)}, bf16[2,4,512,128]{3,2,1,0:T(8,128)(2,1)S(1)}, u32[]{:S(2)}, u32[]{:S(2)}) collective-permute-start(bf16[2,4,512,128]{3,2,1,0:T(8,128)(2,1)} %pad_maximum_fusion.2), channel_id=1, source_target_pairs={{0,32},{16,48},{32,64},{48,80},{64,96},{80,112},{96,0},{112,16},{1... | collective-permute-start | bytes 3145736 | tf_op jit(solution)/shard_map/ppermute | solution.py:268
  11.2 48.3 %collective-permute-start.1 = (bf16[2,4,512,128]{3,2,1,0:T(8,128)(2,1)}, bf16[2,4,512,128]{3,2,1,0:T(8,128)(2,1)S(1)}, u32[]{:S(2)}, u32[]{:S(2)}) collective-permute-start(bf16[2,4,512,128]{3,2,1,0:T(8,128)(2,1)} %pad_maximum_fusion.2), channel_id=1, source_target_pairs={{0,64},{16,80},{32,96},{48,112},{64,0},{80,16},{96,32},{112,48},{1... | collective-permute-start | bytes 3145736 | tf_op jit(solution)/shard_map/ppermute | solution.py:268
  13.9 45.6 %collective-permute-start.2 = (bf16[2,4,512,128]{3,2,1,0:T(8,128)(2,1)}, bf16[2,4,512,128]{3,2,1,0:T(8,128)(2,1)S(1)}, u32[]{:S(2)}, u32[]{:S(2)}) collective-permute-start(bf16[2,4,512,128]{3,2,1,0:T(8,128)(2,1)} %pad_maximum_fusion.2), channel_id=1, source_target_pairs={{0,96},{16,112},{32,0},{48,16},{64,32},{80,48},{96,64},{112,80},{1... | collective-permute-start | bytes 3145736 | tf_op jit(solution)/shard_map/ppermute | solution.py:268
  15.4 54.8 %collective-permute-start.3 = (bf16[2,4,512,128]{3,2,1,0:T(8,128)(2,1)}, bf16[2,4,512,128]{3,2,1,0:T(8,128)(2,1)}, u32[]{:S(2)}, u32[]{:S(2)}) collective-permute-start(bf16[2,4,512,128]{3,2,1,0:T(8,128)(2,1)} %pad_maximum_fusion.2), channel_id=1, source_target_pairs={{0,16},{16,0},{32,48},{48,32},{64,80},{80,64},{96,112},{112,96},{1... | collective-permute-start | bytes 3145736 | tf_op jit(solution)/shard_map/ppermute | solution.py:265
  61.3 30.1 %collective-permute-start.4 = (bf16[2,4,1536,128]{3,2,1,0:T(8,128)(2,1)}, bf16[2,4,1536,128]{3,2,1,0:T(8,128)(2,1)}, u32[]{:S(2)}, u32[]{:S(2)}) collective-permute-start(bf16[2,4,1536,128]{3,2,1,0:T(8,128)(2,1)} %pad_maximum_fusion.1), channel_id=1, source_target_pairs={{0,16},{16,0},{32,48},{48,32},{64,80},{80,64},{96,112},{112,96},{1... | collective-permute-start | bytes 9437192 | tf_op jit(solution)/shard_map/ppermute | solution.py:273
  64.3 2.0 copy-start.2
  64.3 5.8 %copy-start.10 = (bf16[64,4]{0,1:T(4,128)(2,1)S(1)}, bf16[64,4]{0,1:T(4,128)(2,1)}, u32[]{:S(2)}) copy-start(bf16[64,4]{0,1:T(4,128)(2,1)} %param.26) | copy-start | bytes 1540
  64.3 5.8 %copy-start.9 = (bf16[2048]{0:T(1024)(128)(2,1)S(1)}, bf16[2048]{0:T(1024)(128)(2,1)}, u32[]{:S(2)}) copy-start(bf16[2048]{0:T(1024)(128)(2,1)} %param.24) | copy-start | bytes 12292
  99.9 14.2 %copy-start.3 = (f32[1024,1]{1,0:T(8,128)S(1)}, f32[1024,1]{1,0:T(8,128)}, u32[]{:S(2)}) copy-start(f32[1024,1]{1,0:T(8,128)} %copy.60) | copy-start | bytes 12292
  99.9 14.2 %copy-start.4 = (f32[1024,1]{1,0:T(8,128)S(1)}, f32[1024,1]{1,0:T(8,128)}, u32[]{:S(2)}) copy-start(f32[1024,1]{1,0:T(8,128)} %copy.58) | copy-start | bytes 12292
  99.9 14.2 %copy-start.5 = (f32[1024,128]{1,0:T(8,128)S(1)}, f32[1024,128]{1,0:T(8,128)}, u32[]{:S(2)}) copy-start(f32[1024,128]{1,0:T(8,128)} %get-tuple-element.38) | copy-start | bytes 1572868
  99.9 14.2 %copy-start.6 = (f32[1024,128]{1,0:T(8,128)S(1)}, f32[1024,128]{1,0:T(8,128)}, u32[]{:S(2)}) copy-start(f32[1024,128]{1,0:T(8,128)} %get-tuple-element.42) | copy-start | bytes 1572868
  99.9 16.4 %copy-start.12 = (bf16[1024,128]{1,0:T(8,128)(2,1)S(1)}, bf16[1024,128]{1,0:T(8,128)(2,1)}, u32[]{:S(2)}) copy-start(bf16[1024,128]{1,0:T(8,128)(2,1)} %param.17) | copy-start | bytes 786436
  99.9 16.4 %copy-start.14 = (f32[1024,128]{1,0:T(8,128)S(1)}, f32[1024,128]{1,0:T(8,128)}, u32[]{:S(2)}) copy-start(f32[1024,128]{1,0:T(8,128)} %get-tuple-element.36) | copy-start | bytes 1572868
  114.1 14.6 %copy-start.8 = (s32[64,4]{0,1:T(4,128)S(1)}, s32[64,4]{0,1:T(4,128)}, u32[]{:S(2)}) copy-start(s32[64,4]{0,1:T(4,128)} %param.25) | copy-start | bytes 3076
  114.1 23.4 %copy-start.7 = (bf16[64,2048]{1,0:T(8,128)(2,1)S(1)}, bf16[64,2048]{1,0:T(8,128)(2,1)}, u32[]{:S(2)}) copy-start(bf16[64,2048]{1,0:T(8,128)(2,1)} %param.22) | copy-start | bytes 786436
  120.7 16.8 %all-to-all-start = ((bf16[16,64,128]{2,1,0:T(8,128)(2,1)}), bf16[16,64,128]{2,1,0:T(8,128)(2,1)S(1)}, u32[]{:S(2)}, u32[]{:S(2)}) async-start(bf16[16,64,128]{2,1,0:T(8,128)(2,1)} %bitcast.12), calls=%async_computation | async-start | bytes 524288 | tf_op jit(solution)/shard_map/all_to_all | solution.py:290
  191.6 34.3 %copy-start.1 = (bf16[1024,128]{1,0:T(8,128)(2,1)S(1)}, bf16[1024,128]{1,0:T(8,128)(2,1)}, u32[]{:S(2)}) copy-start(bf16[1024,128]{1,0:T(8,128)(2,1)} %param.16) | copy-start | bytes 786436
Sparse Core Ops, SparseCore 0:
  9.5 73.3 all-gather.1

commit v6 on v5

--- a/solution.py
+++ b/solution.py
@@ -306,20 +306,28 @@
         select.T.astype(jnp.bfloat16), normed, preferred_element_type=jnp.float32
     ).astype(jnp.bfloat16).reshape(EXPERTS, capacity, normed.shape[1])
     exp_dev = w_gate.shape[0]
-    received = lax.all_to_all(buffer, "exp", split_axis=0, concat_axis=0, tiled=True)
-    slots = received.shape[1]
-    grid_in = received.reshape(exp_count, exp_dev, slots, received.shape[2])
-    gate_h = jnp.einsum("secd,edf->secf", grid_in, w_gate, preferred_element_type=jnp.float32)
-    up_h = jnp.einsum("secd,edf->secf", grid_in, w_up, preferred_element_type=jnp.float32)
-    hidden = (jax.nn.silu(gate_h) * up_h).astype(jnp.bfloat16)
-    expert_out = jnp.einsum("secf,efd->secd", hidden, w_down, preferred_element_type=jnp.float32)
-    returned = lax.all_to_all(
-        expert_out.astype(jnp.bfloat16).reshape(EXPERTS, slots, received.shape[2]),
-        "exp",
-        split_axis=0,
-        concat_axis=0,
-        tiled=True,
-    )
+    halves = 2
+    piece = capacity // halves
+    returned_parts = []
+    for half in range(halves):
+        received = lax.all_to_all(
+            buffer[:, half * piece : (half + 1) * piece], "exp", split_axis=0, concat_axis=0, tiled=True
+        )
+        grid_in = received.reshape(exp_count, exp_dev, piece, received.shape[2])
+        gate_h = jnp.einsum("secd,edf->secf", grid_in, w_gate, preferred_element_type=jnp.float32)
+        up_h = jnp.einsum("secd,edf->secf", grid_in, w_up, preferred_element_type=jnp.float32)
+        hidden = (jax.nn.silu(gate_h) * up_h).astype(jnp.bfloat16)
+        expert_out = jnp.einsum("secf,efd->secd", hidden, w_down, preferred_element_type=jnp.float32)
+        returned_parts.append(
+            lax.all_to_all(
+                expert_out.astype(jnp.bfloat16).reshape(EXPERTS, piece, received.shape[2]),
+                "exp",
+                split_axis=0,
+                concat_axis=0,
+                tiled=True,
+            )
+        )
+    returned = jnp.concatenate(returned_parts, axis=1)
     gates = expert_gates.astype(jnp.float32).reshape(tok_dev, TOPK, 1)
     weights = jnp.sum(dest_hot.reshape(tok_dev, TOPK, slot_count).astype(jnp.float32) * gates, axis=1)
     mixture = jnp.dot(

time: 234 us -> 244 us (1.043); the launches traced: 233 us -> 240 us
  blocking collectives: 64.2 us -> 41.6 us
  matrix products: 28.7 us -> 40.8 us
  starting transfers between devices: 13.7 us -> 24.5 us
  Pallas kernels: 28.2 us -> 31.6 us
  local copies, waits for them, and re-layouts: 22.2 us -> 25.3 us
    all_to_all x2, blocking collectives: 64.2 us -> 41.6 us  [the longest x1 21.4 us: per_device(): lax.all_to_all(expert_out.astype(jnp.bfloat16).reshape(EXPERTS, piece, re...]
    all_to_all x0 -> x2, starting transfers between devices: none -> 10.8 us  [the longest x1 7.15 us: per_device(): lax.all_to_all(expert_out.astype(jnp.bfloat16).reshape(EXPERTS, piece, re...]
    dot_general x1 -> x2, matrix products: 9.73 us -> 16.6 us  [per_device(): jnp.einsum('secf,efd->secd', hidden, w_down, preferred_element_type=jnp.f...]
    dot_general x1 -> x2, matrix products: 5.61 us -> 10.8 us  [per_device(): jnp.einsum('secd,edf->secf', grid_in, w_gate, preferred_element_type=jnp....]
    pallas_call x2, Pallas kernels: 28.2 us -> 31.6 us  [attend_prefix_local(): pl.pallas_call(prefix_kernel, grid_spec=pltpu.PrefetchScalarGridSpec(num_...]
  transfers between devices with their start and end apart: 7 -> 9, of which waited for: 3 -> 3; matrix products, arithmetic and copies ran while one was open for 15% -> 28% of each run, Pallas kernels for 12% -> 13%
where the time goes in v6:
time: 244 us; the launch traced here: 240 us
  waiting for transfers between devices  51.9 us (21%)
  blocking collectives  41.6 us (17%)
  matrix products  40.8 us (17%)
  Pallas kernels  31.6 us (13%)
  local copies, waits for them, and re-layouts  25.3 us (10%)
  starting transfers between devices  24.5 us (10%)
  between operations  13.7 us (6%)
  other arithmetic  10.6 us (4%)
    ppermute x3, waiting for transfers between devices, per_device(): lax.ppermute(local_kv, 'req', [(i, (i + 2 * s) % req_count) for i in rang...  42.2 us
    pallas_call x2, Pallas kernels, attend_prefix_local(): pl.pallas_call(prefix_kernel, grid_spec=pltpu.PrefetchScalarGridSpec(num_...  31.6 us
    all_to_all x1, blocking collectives, per_device(): lax.all_to_all(expert_out.astype(jnp.bfloat16).reshape(EXPERTS, piece, re...  21.4 us
    all_to_all x1, blocking collectives, per_device(): lax.all_to_all(buffer[:, half * piece:(half + 1) * piece], 'exp', split_a...  20.1 us
    dot_general x2, matrix products, per_device(): jnp.einsum('secf,efd->secd', hidden, w_down, preferred_element_type=jnp.f...  16.6 us
    dot_general x2, matrix products, per_device(): jnp.einsum('secd,edf->secf', grid_in, w_gate, preferred_element_type=jnp....  10.8 us
    all_to_all x1, waiting for transfers between devices, per_device(): lax.all_to_all(attended, 'exp', split_axis=0, concat_axis=1, tiled=True)  9.01 us
    all_to_all x1, starting transfers between devices, per_device(): lax.all_to_all(attended, 'exp', split_axis=0, concat_axis=1, tiled=True)  8 us
  transfers between devices with their start and end apart: 9, of which 3 were waited for; matrix products, arithmetic and copies ran while one was open for 28% of the time, Pallas kernels for 13%

profile of v6, /device:TPU:0, one launch (start us, length us, event | category | flops | bytes accessed | tf_op | source)
XLA Modules:
  0.0 240.1 jit_solution(2323865554689093625)
XLA Ops:
  6.5 0.7 all-gather.2.cloned.1.call-update
  7.3 0.0 copy-start.13
  7.3 2.4 pad_maximum_fusion.3
  9.6 1.6 collective-permute-start
  11.2 2.7 %collective-permute-start.1 = (bf16[2,4,512,128]{3,2,1,0:T(8,128)(2,1)}, bf16[2,4,512,128]{3,2,1,0:T(8,128)(2,1)S(1)}, u32[]{:S(2)}, u32[]{:S(2)}) collective-permute-start(bf16[2,4,512,128]{3,2,1,0:T(8,128)(2,1)} %pad_maximum_fusion.3), channel_id=1, source_target_pairs={{0,64},{16,80},{32,96},{48,112},{64,0},{80,16},{96,32},{112,48},{1... | collective-permute-start | bytes 3145736 | tf_op jit(solution)/shard_map/ppermute | solution.py:268
  13.9 1.4 collective-permute-start.2
  15.4 0.0 collective-permute-start.3
  15.4 0.8 copy.70
  16.2 0.1 eq.120
  16.3 0.1 eq.116
  16.4 0.8 reduce_window_sum.24
  17.2 0.1 convert_reduce_fusion.1
  17.3 18.6 %collective-permute-done = bf16[2,4,512,128]{3,2,1,0:T(8,128)(2,1)S(1)} collective-permute-done((bf16[2,4,512,128]{3,2,1,0:T(8,128)(2,1)}, bf16[2,4,512,128]{3,2,1,0:T(8,128)(2,1)S(1)}, u32[]{:S(2)}, u32[]{:S(2)}) %collective-permute-start) | collective-permute-done | bytes 1048608 | tf_op jit(solution)/shard_map/ppermute | solution.py:268
  35.8 23.6 %collective-permute-done.1 = bf16[2,4,512,128]{3,2,1,0:T(8,128)(2,1)S(1)} collective-permute-done((bf16[2,4,512,128]{3,2,1,0:T(8,128)(2,1)}, bf16[2,4,512,128]{3,2,1,0:T(8,128)(2,1)S(1)}, u32[]{:S(2)}, u32[]{:S(2)}) %collective-permute-start.1) | collective-permute-done | bytes 1048608 | tf_op jit(solution)/shard_map/ppermute | solution.py:268
  59.5 1.8 pad_maximum_fusion.1
  61.3 0.1 select_reduce_fusion.2
  61.4 0.1 fusion.95
  61.6 0.1 copy.65
  61.7 0.6 reshape.341.present_ref
  62.3 2.0 fusion.99
  64.3 0.0 copy-start.10
  64.3 0.0 copy-start.9
  64.3 1.9 copy-done.2
  66.3 0.6 fusion.12
  66.9 1.1 copy.68
  68.0 1.0 copy.66
  69.0 0.6 reduce-window.6
  69.6 0.2 slice_reduce_fusion
  69.8 0.1 fusion.93
  69.9 0.1 reduce_sum.80
  70.1 0.1 copy.73
  70.1 0.0 copy-done.9
  70.2 2.4 %constant_dynamic-update-slice_fusion.1 = bf16[2,4,2048,128]{3,2,1,0:T(8,128)(2,1)} fusion(bf16[2,4,512,128]{3,2,1,0:T(8,128)(2,1)} %collective-permute-done.3), kind=kLoop, calls=%fused_computation.91 | loop fusion | bytes 2097152
  72.6 1.4 pad_maximum_fusion
  74.0 2.3 slice_bitcast_fusion.2
  76.3 1.1 broadcast_in_dim.74.grp_ref
  77.4 15.7 %shard_map.145 = (f32[1024,128]{1,0:T(8,128)}, f32[1024,128]{1,0:T(8,128)}, f32[1024,128]{1,0:T(8,128)}) custom-call(s32[32]{0:T(128)} %reshape.341.present_ref, bf16[1024,128]{1,0:T(8,128)(2,1)} %q_ref.3, s32[1024,128]{1,0:T(8,128)} %broadcast_in_dim.74.grp_ref, bf16[4,2048,128]{2,1,0:T(8,128)(2,1)} %get-tuple-element.54.k_ref, ...), custom_call_target="tpu_custom_call" | custom-call | flops 2147483648 | bytes 6029312 | tf_op jit(solution)/shard_map/pallas_call | solution.py:152
  93.1 4.1 %constant_dynamic-update-slice_fusion = bf16[2,4,2048,128]{3,2,1,0:T(8,128)(2,1)} fusion(bf16[2,4,2048,128]{3,2,1,0:T(8,128)(2,1)} %constant_dynamic-update-slice_fusion.1, bf16[2,4,1536,128]{3,2,1,0:T(8,128)(2,1)} %collective-permute-done.4), kind=kLoop, calls=%fused_computation.90 | loop fusion | bytes 6291456 | tf_op jit(solution)/shard_map/concatenate | solution.py:277
  97.2 4.4 %slice_bitcast_fusion = (bf16[4,2048,128]{2,1,0:T(8,128)(2,1)}, bf16[4,2048,128]{2,1,0:T(8,128)(2,1)}) fusion(bf16[2,4,2048,128]{3,2,1,0:T(8,128)(2,1)} %constant_dynamic-update-slice_fusion), kind=kLoop, calls=%fused_computation.27 | loop fusion | bytes 8388608 | tf_op jit(solution)/shard_map/squeeze | solution.py:279
  101.6 0.0 copy-start.12
  101.6 15.9 %shard_map.146 = (f32[1024,128]{1,0:T(8,128)}, f32[1024,128]{1,0:T(8,128)}, f32[1024,128]{1,0:T(8,128)}) custom-call(s32[32]{0:T(128)} %reshape.341.present_ref, bf16[1024,128]{1,0:T(8,128)(2,1)} %q_ref.3, s32[1024,128]{1,0:T(8,128)} %broadcast_in_dim.74.grp_ref, bf16[4,2048,128]{2,1,0:T(8,128)(2,1)} %get-tuple-element.56.k_ref, ...), custom_call_target="tpu_custom_call" | custom-call | flops 2147483648 | bytes 6029312 | tf_op jit(solution)/shard_map/pallas_call | solution.py:152
  117.6 0.0 copy-start.8
  117.6 0.0 copy-start.7
  117.6 2.2 fusion.86
  119.8 4.3 %fusion.63 = bf16[1024,128]{1,0:T(8,128)(2,1)} fusion(bf16[1024,128]{1,0:T(8,128)(2,1)S(1)} %copy-done.12, f32[1024,1024]{0,1:T(8,128)} %copy-done.2, f32[1024]{0:T(1024)S(1)} %get-tuple-element.59, f32[1024,128]{1,0:T(8,128)} %get-tuple-element.41, f32[1024,128]{1,0:T(8,128)S(1)} %copy-done.14, f32[1024]{0:T(1024)S(1)} %get-tuple-element.45, ...), kind=kOutput, calls=%fused_computation.44 | convolution fusion | flops 271581184 | bytes 5791744 | tf_op jit(solution)/shard_map/while/body/eval_jaxpr/hqk,khd->qhd/dot_general | solution.py:199
  124.1 8.0 %all-to-all-start = ((bf16[16,64,128]{2,1,0:T(8,128)(2,1)}), bf16[16,64,128]{2,1,0:T(8,128)(2,1)S(1)}, u32[]{:S(2)}, u32[]{:S(2)}) async-start(bf16[16,64,128]{2,1,0:T(8,128)(2,1)} %bitcast.12), calls=%async_computation | async-start | bytes 524288 | tf_op jit(solution)/shard_map/all_to_all | solution.py:290
  132.2 0.2 select_reduce_fusion
  132.3 9.0 %all-to-all-done = bf16[16,64,128]{2,1,0:T(8,128)(2,1)S(1)} async-done(((bf16[16,64,128]{2,1,0:T(8,128)(2,1)}), bf16[16,64,128]{2,1,0:T(8,128)(2,1)S(1)}, u32[]{:S(2)}, u32[]{:S(2)}) %all-to-all-start) | async-done | bytes 262176 | tf_op jit(solution)/shard_map/all_to_all | solution.py:290
  141.4 5.1 %multiply_reduce_fusion = (f32[64]{0:T(128)S(1)}, f32[64,2048]{1,0:T(8,128)S(1)}) fusion(bf16[2048,2048]{1,0:T(8,128)(2,1)} %all-gather.2.cloned.1.call-done, bf16[64,2048]{1,0:T(8,128)(2,1)S(1)} %copy-done.7, bf16[16,64,128]{2,1,0:T(8,128)(2,1)S(1)} %all-to-all-done), kind=kOutput, calls=%fused_computation.55 | convolution fusion | flops 537395136 | bytes 9437440 | tf_op jit(solution)/shard_map/dot_general | solution.py:291
  146.4 0.8 convolution_convert_fusion
  147.2 1.2 fusion.98
  148.5 20.1 %all_to_all.36 = bf16[32,8,2048]{2,1,0:T(8,128)(2,1)S(1)} all-to-all(bf16[32,8,2048]{2,1,0:T(8,128)(2,1)S(1)} %get-tuple-element.57), channel_id=1, replica_groups=mesh['req'=8,'exp'=16] {'exp'}, dimensions={0} | all-to-all | bytes 2097152 | tf_op jit(solution)/shard_map/all_to_all | solution.py:313
  168.6 3.7 %all-to-all-start.3 = ((bf16[32,8,2048]{2,1,0:T(8,128)(2,1)}), bf16[32,8,2048]{2,1,0:T(8,128)(2,1)S(1)}, u32[]{:S(2)}, u32[]{:S(2)}) async-start(bf16[32,8,2048]{2,1,0:T(8,128)(2,1)} %get-tuple-element.58), calls=%async_computation.3 | async-start | bytes 2097152 | tf_op jit(solution)/shard_map/all_to_all | solution.py:313
  172.2 5.4 %fusion.30 = f32[16,2,8,704]{3,2,0,1:T(8,128)} fusion(bf16[2,2048,704]{1,2,0:T(8,128)(2,1)} %param.27, bf16[16,2,8,2048]{3,2,1,0:T(8,128)(2,1)S(1)} %bitcast.134), kind=kOutput, calls=%fused_computation.33 | convolution fusion | flops 738197504 | bytes 7536640 | tf_op jit(solution)/shard_map/secd,edf->secf/dot_general | solution.py:317
  177.6 8.3 %fusion.23 = bf16[16,2,8,2048]{3,2,0,1:T(8,128)(2,1)} fusion(bf16[2,704,2048]{2,1,0:T(8,128)(2,1)} %param.29, bf16[2,2048,704]{1,2,0:T(8,128)(2,1)} %param.28, bf16[16,2,8,2048]{3,2,1,0:T(8,128)(2,1)S(1)} %bitcast.135, f32[16,2,8,704]{3,2,0,1:T(8,128)} %fusion.30), kind=kOutput, calls=%fused_computation.22 | convolution fusion | flops 1478000640 | bytes 14352384 | tf_op jit(solution)/shard_map/secf,efd->secd/dot_general | solution.py:320
  185.9 2.3 copy.76
  188.2 7.2 %all-to-all-start.2 = ((bf16[32,8,2048]{2,1,0:T(8,128)(2,1)}), bf16[32,8,2048]{2,1,0:T(8,128)(2,1)S(1)}, u32[]{:S(2)}, u32[]{:S(2)}) async-start(bf16[32,8,2048]{2,1,0:T(8,128)(2,1)} %bitcast.26), calls=%async_computation.2 | async-start | bytes 2097152 | tf_op jit(solution)/shard_map/all_to_all | solution.py:322
  195.4 5.4 %fusion.33 = f32[16,2,8,704]{3,2,0,1:T(8,128)} fusion(bf16[2,2048,704]{1,2,0:T(8,128)(2,1)} %param.27, bf16[16,2,8,2048]{3,2,1,0:T(8,128)(2,1)S(1)} %bitcast.132), kind=kOutput, calls=%fused_computation.34 | convolution fusion | flops 738197504 | bytes 7536640 | tf_op jit(solution)/shard_map/secd,edf->secf/dot_general | solution.py:317
  200.8 8.3 %fusion.20 = bf16[16,2,8,2048]{3,2,0,1:T(8,128)(2,1)} fusion(bf16[2,704,2048]{2,1,0:T(8,128)(2,1)} %param.29, bf16[2,2048,704]{1,2,0:T(8,128)(2,1)} %param.28, bf16[16,2,8,2048]{3,2,1,0:T(8,128)(2,1)S(1)} %bitcast.133, f32[16,2,8,704]{3,2,0,1:T(8,128)} %fusion.33), kind=kOutput, calls=%fused_computation.21 | convolution fusion | flops 1478000640 | bytes 14352384 | tf_op jit(solution)/shard_map/secf,efd->secd/dot_general | solution.py:320
  209.1 1.3 copy.79
  210.4 0.0 copy-start.1
  210.4 21.4 %all_to_all.37 = bf16[32,8,2048]{2,1,0:T(8,128)(2,1)S(1)} all-to-all(bf16[32,8,2048]{2,1,0:T(8,128)(2,1)S(1)} %bitcast.131), channel_id=1, replica_groups=mesh['req'=8,'exp'=16] {'exp'}, dimensions={0} | all-to-all | bytes 2097152 | tf_op jit(solution)/shard_map/all_to_all | solution.py:322
  231.8 0.2 pad_maximum_fusion.2
  232.0 1.2 fusion.26
  (39 shorter events, 0.1 us)
Async XLA Ops:
  6.5 55.7 %copy-start = (bf16[1024,128]{1,0:T(8,128)(2,1)S(1)}, bf16[1024,128]{1,0:T(8,128)(2,1)}, u32[]{:S(2)}) copy-start(bf16[1024,128]{1,0:T(8,128)(2,1)} %param.16) | copy-start | bytes 786436
  6.5 134.8 %all-gather.2.cloned.1.call-start = ((), (), s32[]{:S(2)}) async-start(), calls=%async_computation.5 | async-start | bytes 8912896 | tf_op jit(solution)/shard_map/all_gather | solution.py:289
  7.3 54.1 %copy-start.13 = (s32[1,8]{1,0:T(1,128)S(1)}, s32[1,8]{1,0:T(1,128)}, u32[]{:S(2)}) copy-start(s32[1,8]{1,0:T(1,128)} %param.20) | copy-start | bytes 100
  7.3 54.1 %copy-start.11 = (s32[1,8]{1,0:T(1,128)S(1)}, s32[1,8]{1,0:T(1,128)}, u32[]{:S(2)}) copy-start(s32[1,8]{1,0:T(1,128)} %param.21) | copy-start | bytes 100
  9.6 26.2 %collective-permute-start = (bf16[2,4,512,128]{3,2,1,0:T(8,128)(2,1)}, bf16[2,4,512,128]{3,2,1,0:T(8,128)(2,1)S(1)}, u32[]{:S(2)}, u32[]{:S(2)}) collective-permute-start(bf16[2,4,512,128]{3,2,1,0:T(8,128)(2,1)} %pad_maximum_fusion.3), channel_id=1, source_target_pairs={{0,32},{16,48},{32,64},{48,80},{64,96},{80,112},{96,0},{112,16},{1... | collective-permute-start | bytes 3145736 | tf_op jit(solution)/shard_map/ppermute | solution.py:268
  11.2 48.3 %collective-permute-start.1 = (bf16[2,4,512,128]{3,2,1,0:T(8,128)(2,1)}, bf16[2,4,512,128]{3,2,1,0:T(8,128)(2,1)S(1)}, u32[]{:S(2)}, u32[]{:S(2)}) collective-permute-start(bf16[2,4,512,128]{3,2,1,0:T(8,128)(2,1)} %pad_maximum_fusion.3), channel_id=1, source_target_pairs={{0,64},{16,80},{32,96},{48,112},{64,0},{80,16},{96,32},{112,48},{1... | collective-permute-start | bytes 3145736 | tf_op jit(solution)/shard_map/ppermute | solution.py:268
  13.9 45.6 %collective-permute-start.2 = (bf16[2,4,512,128]{3,2,1,0:T(8,128)(2,1)}, bf16[2,4,512,128]{3,2,1,0:T(8,128)(2,1)S(1)}, u32[]{:S(2)}, u32[]{:S(2)}) collective-permute-start(bf16[2,4,512,128]{3,2,1,0:T(8,128)(2,1)} %pad_maximum_fusion.3), channel_id=1, source_target_pairs={{0,96},{16,112},{32,0},{48,16},{64,32},{80,48},{96,64},{112,80},{1... | collective-permute-start | bytes 3145736 | tf_op jit(solution)/shard_map/ppermute | solution.py:268
  15.4 54.8 %collective-permute-start.3 = (bf16[2,4,512,128]{3,2,1,0:T(8,128)(2,1)}, bf16[2,4,512,128]{3,2,1,0:T(8,128)(2,1)}, u32[]{:S(2)}, u32[]{:S(2)}) collective-permute-start(bf16[2,4,512,128]{3,2,1,0:T(8,128)(2,1)} %pad_maximum_fusion.3), channel_id=1, source_target_pairs={{0,16},{16,0},{32,48},{48,32},{64,80},{80,64},{96,112},{112,96},{1... | collective-permute-start | bytes 3145736 | tf_op jit(solution)/shard_map/ppermute | solution.py:265
  61.3 31.8 %collective-permute-start.4 = (bf16[2,4,1536,128]{3,2,1,0:T(8,128)(2,1)}, bf16[2,4,1536,128]{3,2,1,0:T(8,128)(2,1)}, u32[]{:S(2)}, u32[]{:S(2)}) collective-permute-start(bf16[2,4,1536,128]{3,2,1,0:T(8,128)(2,1)} %pad_maximum_fusion.1), channel_id=1, source_target_pairs={{0,16},{16,0},{32,48},{48,32},{64,80},{80,64},{96,112},{112,96},{1... | collective-permute-start | bytes 9437192 | tf_op jit(solution)/shard_map/ppermute | solution.py:273
  64.3 2.0 copy-start.2
  64.3 5.8 %copy-start.10 = (bf16[64,4]{0,1:T(4,128)(2,1)S(1)}, bf16[64,4]{0,1:T(4,128)(2,1)}, u32[]{:S(2)}) copy-start(bf16[64,4]{0,1:T(4,128)(2,1)} %param.26) | copy-start | bytes 1540
  64.3 5.8 %copy-start.9 = (bf16[2048]{0:T(1024)(128)(2,1)S(1)}, bf16[2048]{0:T(1024)(128)(2,1)}, u32[]{:S(2)}) copy-start(bf16[2048]{0:T(1024)(128)(2,1)} %param.24) | copy-start | bytes 12292
  101.6 16.0 %copy-start.3 = (f32[1024,1]{1,0:T(8,128)S(1)}, f32[1024,1]{1,0:T(8,128)}, u32[]{:S(2)}) copy-start(f32[1024,1]{1,0:T(8,128)} %copy.68) | copy-start | bytes 12292
  101.6 16.0 %copy-start.4 = (f32[1024,1]{1,0:T(8,128)S(1)}, f32[1024,1]{1,0:T(8,128)}, u32[]{:S(2)}) copy-start(f32[1024,1]{1,0:T(8,128)} %copy.66) | copy-start | bytes 12292
  101.6 16.0 %copy-start.5 = (f32[1024,128]{1,0:T(8,128)S(1)}, f32[1024,128]{1,0:T(8,128)}, u32[]{:S(2)}) copy-start(f32[1024,128]{1,0:T(8,128)} %get-tuple-element.38) | copy-start | bytes 1572868
  101.6 16.0 %copy-start.6 = (f32[1024,128]{1,0:T(8,128)S(1)}, f32[1024,128]{1,0:T(8,128)}, u32[]{:S(2)}) copy-start(f32[1024,128]{1,0:T(8,128)} %get-tuple-element.42) | copy-start | bytes 1572868
  101.6 18.2 %copy-start.12 = (bf16[1024,128]{1,0:T(8,128)(2,1)S(1)}, bf16[1024,128]{1,0:T(8,128)(2,1)}, u32[]{:S(2)}) copy-start(bf16[1024,128]{1,0:T(8,128)(2,1)} %param.17) | copy-start | bytes 786436
  101.6 18.2 %copy-start.14 = (f32[1024,128]{1,0:T(8,128)S(1)}, f32[1024,128]{1,0:T(8,128)}, u32[]{:S(2)}) copy-start(f32[1024,128]{1,0:T(8,128)} %get-tuple-element.36) | copy-start | bytes 1572868
  117.6 14.6 %copy-start.8 = (s32[64,4]{0,1:T(4,128)S(1)}, s32[64,4]{0,1:T(4,128)}, u32[]{:S(2)}) copy-start(s32[64,4]{0,1:T(4,128)} %param.25) | copy-start | bytes 3076
  117.6 23.8 %copy-start.7 = (bf16[64,2048]{1,0:T(8,128)(2,1)S(1)}, bf16[64,2048]{1,0:T(8,128)(2,1)}, u32[]{:S(2)}) copy-start(bf16[64,2048]{1,0:T(8,128)(2,1)} %param.22) | copy-start | bytes 786436
  124.1 17.2 %all-to-all-start = ((bf16[16,64,128]{2,1,0:T(8,128)(2,1)}), bf16[16,64,128]{2,1,0:T(8,128)(2,1)S(1)}, u32[]{:S(2)}, u32[]{:S(2)}) async-start(bf16[16,64,128]{2,1,0:T(8,128)(2,1)} %bitcast.12), calls=%async_computation | async-start | bytes 524288 | tf_op jit(solution)/shard_map/all_to_all | solution.py:290
  168.6 19.6 %all-to-all-start.3 = ((bf16[32,8,2048]{2,1,0:T(8,128)(2,1)}), bf16[32,8,2048]{2,1,0:T(8,128)(2,1)S(1)}, u32[]{:S(2)}, u32[]{:S(2)}) async-start(bf16[32,8,2048]{2,1,0:T(8,128)(2,1)} %get-tuple-element.58), calls=%async_computation.3 | async-start | bytes 2097152 | tf_op jit(solution)/shard_map/all_to_all | solution.py:313
  188.2 22.2 %all-to-all-start.2 = ((bf16[32,8,2048]{2,1,0:T(8,128)(2,1)}), bf16[32,8,2048]{2,1,0:T(8,128)(2,1)S(1)}, u32[]{:S(2)}, u32[]{:S(2)}) async-start(bf16[32,8,2048]{2,1,0:T(8,128)(2,1)} %bitcast.26), calls=%async_computation.2 | async-start | bytes 2097152 | tf_op jit(solution)/shard_map/all_to_all | solution.py:322
  210.4 22.8 %copy-start.1 = (bf16[1024,128]{1,0:T(8,128)(2,1)S(1)}, bf16[1024,128]{1,0:T(8,128)(2,1)}, u32[]{:S(2)}) copy-start(bf16[1024,128]{1,0:T(8,128)(2,1)} %param.16) | copy-start | bytes 786436
Sparse Core Ops, SparseCore 0:
  9.5 73.3 all-gather.1

commit v7 on v6

--- a/solution.py
+++ b/solution.py
@@ -171,6 +171,39 @@
         ),
     )(present, query_rows, grp, prefix_k, prefix_v)
     return (acc, maxima[:, :1], totals[:, :1])
+
+
+def expert_kernel(x_ref, wg_ref, wu_ref, wd_ref, o_ref):
+    x = x_ref[0]
+    gate_h = jnp.dot(x, wg_ref[0], preferred_element_type=jnp.float32)
+    up_h = jnp.dot(x, wu_ref[0], preferred_element_type=jnp.float32)
+    hidden = (gate_h / (1.0 + jnp.exp(-gate_h)) * up_h).astype(jnp.bfloat16)
+    o_ref[0] = jnp.dot(hidden, wd_ref[0], preferred_element_type=jnp.float32).astype(o_ref.dtype)
+
+
+def expert_ffn(rows, w_gate, w_up, w_down):
+    exp_dev, row_count, width = rows.shape
+    inner = w_gate.shape[2]
+    return pl.pallas_call(
+        expert_kernel,
+        grid=(exp_dev,),
+        in_specs=[
+            pl.BlockSpec((1, row_count, width), lambda e: (e, 0, 0)),
+            pl.BlockSpec((1, width, inner), lambda e: (e, 0, 0)),
+            pl.BlockSpec((1, width, inner), lambda e: (e, 0, 0)),
+            pl.BlockSpec((1, inner, width), lambda e: (e, 0, 0)),
+        ],
+        out_specs=pl.BlockSpec((1, row_count, width), lambda e: (e, 0, 0)),
+        out_shape=jax.ShapeDtypeStruct((exp_dev, row_count, width), jnp.bfloat16),
+        compiler_params=pltpu.CompilerParams(
+            dimension_semantics=("arbitrary",), vmem_limit_bytes=56 * 1024 * 1024
+        ),
+        cost_estimate=pl.CostEstimate(
+            flops=6 * exp_dev * row_count * width * inner,
+            transcendentals=exp_dev * row_count * inner,
+            bytes_accessed=exp_dev * (3 * width * inner + 2 * row_count * width) * 2,
+        ),
+    )(rows, w_gate, w_up, w_down)
 
 
 def attend_suffix(queries, keys, values, request, position):
@@ -313,14 +346,13 @@
         received = lax.all_to_all(
             buffer[:, half * piece : (half + 1) * piece], "exp", split_axis=0, concat_axis=0, tiled=True
         )
-        grid_in = received.reshape(exp_count, exp_dev, piece, received.shape[2])
-        gate_h = jnp.einsum("secd,edf->secf", grid_in, w_gate, preferred_element_type=jnp.float32)
-        up_h = jnp.einsum("secd,edf->secf", grid_in, w_up, preferred_element_type=jnp.float32)
-        hidden = (jax.nn.silu(gate_h) * up_h).astype(jnp.bfloat16)
-        expert_out = jnp.einsum("secf,efd->secd", hidden, w_down, preferred_element_type=jnp.float32)
+        width = received.shape[2]
+        rows = jnp.swapaxes(received.reshape(exp_count, exp_dev, piece, width), 0, 1)
+        expert_out = expert_ffn(rows.reshape(exp_dev, exp_count * piece, width), w_gate, w_up, w_down)
+        expert_out = jnp.swapaxes(expert_out.reshape(exp_dev, exp_count, piece, width), 0, 1)
         returned_parts.append(
             lax.all_to_all(
-                expert_out.astype(jnp.bfloat16).reshape(EXPERTS, piece, received.shape[2]),
+                expert_out.reshape(EXPERTS, piece, width),
                 "exp",
                 split_axis=0,
                 concat_axis=0,

time: 244 us -> 255 us (1.045)
  matrix products: 40.8 us -> 13.4 us
  local copies, waits for them, and re-layouts: 25.3 us -> 44.4 us
  Pallas kernels: 31.6 us -> 49.9 us
  waiting for transfers between devices: 51.9 us -> 56.4 us
    dot_general x4 -> x0, matrix products: 27.4 us -> none  [the longest x2 16.6 us: per_device(): jnp.einsum('secf,efd->secd', hidden, w_down, preferred_element_type=jnp.f...]
    pallas_call x0 -> x2, Pallas kernels: none -> 18.1 us  [expert_ffn(): pl.pallas_call(expert_kernel, grid=(exp_dev,), in_specs=[pl.BlockSpec((1,...]
    unnamed x32 -> x34, local copies, waits for them, and re-layouts: 5.2 us -> 22.2 us
    all_to_all x1, waiting for transfers between devices: 0.01 us -> 4.72 us  [per_device(): lax.all_to_all(expert_out.reshape(EXPERTS, piece, width), 'exp', split_ax...]
    reshape x0 -> x2, local copies, waits for them, and re-layouts: none -> 3.68 us  [per_device(): expert_out.reshape(exp_dev, exp_count, piece, width)]
    convert_element_type x2 -> x0, local copies, waits for them, and re-layouts: 3.62 us -> none  [per_device(): expert_out.astype(jnp.bfloat16).reshape(EXPERTS, piece, received.shape[2])]
  transfers between devices with their start and end apart: 9 -> 9, of which waited for: 3 -> 4; matrix products, arithmetic and copies ran while one was open for 28% -> 23% of each run, Pallas kernels for 13% -> 20%
where the time goes in v7:
time: 255 us; the launch traced here: 254 us
  waiting for transfers between devices  56.4 us (22%)
  Pallas kernels  49.9 us (20%)
  local copies, waits for them, and re-layouts  44.4 us (17%)
  blocking collectives  40.7 us (16%)
  starting transfers between devices  24.5 us (10%)
  between operations  13.7 us (5%)
  matrix products  13.4 us (5%)
  other arithmetic  10.6 us (4%)
    ppermute x3, waiting for transfers between devices, per_device(): lax.ppermute(local_kv, 'req', [(i, (i + 2 * s) % req_count) for i in rang...  42.2 us
    pallas_call x2, Pallas kernels, attend_prefix_local(): pl.pallas_call(prefix_kernel, grid_spec=pltpu.PrefetchScalarGridSpec(num_...  31.7 us
    unnamed x34, local copies, waits for them, and re-layouts  22.2 us
    all_to_all x1, blocking collectives, per_device(): lax.all_to_all(buffer[:, half * piece:(half + 1) * piece], 'exp', split_a...  21.5 us
    all_to_all x1, blocking collectives, per_device(): lax.all_to_all(expert_out.reshape(EXPERTS, piece, width), 'exp', split_ax...  19.2 us
    pallas_call x2, Pallas kernels, expert_ffn(): pl.pallas_call(expert_kernel, grid=(exp_dev,), in_specs=[pl.BlockSpec((1,...  18.1 us
    all_to_all x1, waiting for transfers between devices, per_device(): lax.all_to_all(attended, 'exp', split_axis=0, concat_axis=1, tiled=True)  8.7 us
    all_to_all x1, starting transfers between devices, per_device(): lax.all_to_all(attended, 'exp', split_axis=0, concat_axis=1, tiled=True)  7.96 us
  transfers between devices with their start and end apart: 9, of which 4 were waited for; matrix products, arithmetic and copies ran while one was open for 23% of the time, Pallas kernels for 20%

profile of v7, /device:TPU:0, one launch (start us, length us, event | category | flops | bytes accessed | tf_op | source)
XLA Modules:
  0.0 253.6 jit_solution(14453768961254649189)
XLA Ops:
  6.5 0.7 all-gather.2.cloned.1.call-update
  7.3 0.0 copy-start.13
  7.3 2.4 pad_maximum_fusion.3
  9.6 1.6 collective-permute-start
  11.2 2.7 %collective-permute-start.1 = (bf16[2,4,512,128]{3,2,1,0:T(8,128)(2,1)}, bf16[2,4,512,128]{3,2,1,0:T(8,128)(2,1)S(1)}, u32[]{:S(2)}, u32[]{:S(2)}) collective-permute-start(bf16[2,4,512,128]{3,2,1,0:T(8,128)(2,1)} %pad_maximum_fusion.3), channel_id=1, source_target_pairs={{0,64},{16,80},{32,96},{48,112},{64,0},{80,16},{96,32},{112,48},{1... | collective-permute-start | bytes 3145736 | tf_op jit(solution)/shard_map/ppermute | solution.py:301
  13.9 1.4 collective-permute-start.2
  15.4 0.8 copy.82
  16.2 0.1 eq.120
  16.3 0.1 eq.116
  16.4 0.8 reduce_window_sum.24
  17.2 0.1 convert_reduce_fusion.1
  17.3 18.6 %collective-permute-done = bf16[2,4,512,128]{3,2,1,0:T(8,128)(2,1)S(1)} collective-permute-done((bf16[2,4,512,128]{3,2,1,0:T(8,128)(2,1)}, bf16[2,4,512,128]{3,2,1,0:T(8,128)(2,1)S(1)}, u32[]{:S(2)}, u32[]{:S(2)}) %collective-permute-start) | collective-permute-done | bytes 1048608 | tf_op jit(solution)/shard_map/ppermute | solution.py:301
  35.8 23.6 %collective-permute-done.1 = bf16[2,4,512,128]{3,2,1,0:T(8,128)(2,1)S(1)} collective-permute-done((bf16[2,4,512,128]{3,2,1,0:T(8,128)(2,1)}, bf16[2,4,512,128]{3,2,1,0:T(8,128)(2,1)S(1)}, u32[]{:S(2)}, u32[]{:S(2)}) %collective-permute-start.1) | collective-permute-done | bytes 1048608 | tf_op jit(solution)/shard_map/ppermute | solution.py:301
  59.5 1.8 pad_maximum_fusion.1
  61.3 0.1 select_reduce_fusion.2
  61.4 0.1 fusion.33
  61.6 0.1 copy.77
  61.7 0.6 reshape.357.present_ref
  62.3 2.0 fusion.35
  64.3 0.0 copy-start.10
  64.3 1.9 copy-done.2
  66.3 0.6 fusion
  66.9 1.1 copy.80
  68.0 1.0 copy.78
  69.0 0.6 reduce-window.6
  69.6 0.2 slice_reduce_fusion
  69.8 0.1 fusion.31
  69.9 0.1 reduce_sum.80
  70.1 0.1 copy.85
  70.1 0.0 copy-done.9
  70.2 2.4 constant_dynamic-update-slice_fusion.1
  72.6 1.4 pad_maximum_fusion
  74.0 2.3 slice_bitcast_fusion.2
  76.3 1.1 broadcast_in_dim.74.grp_ref
  77.4 15.8 %shard_map.145 = (f32[1024,128]{1,0:T(8,128)}, f32[1024,128]{1,0:T(8,128)}, f32[1024,128]{1,0:T(8,128)}) custom-call(s32[32]{0:T(128)} %reshape.357.present_ref, bf16[1024,128]{1,0:T(8,128)(2,1)} %q_ref.3, s32[1024,128]{1,0:T(8,128)} %broadcast_in_dim.74.grp_ref, bf16[4,2048,128]{2,1,0:T(8,128)(2,1)} %get-tuple-element.54.k_ref, ...), custom_call_target="tpu_custom_call" | custom-call | flops 2147483648 | bytes 6029312 | tf_op jit(solution)/shard_map/pallas_call | solution.py:152
  93.1 4.1 %constant_dynamic-update-slice_fusion = bf16[2,4,2048,128]{3,2,1,0:T(8,128)(2,1)} fusion(bf16[2,4,2048,128]{3,2,1,0:T(8,128)(2,1)} %constant_dynamic-update-slice_fusion.1, bf16[2,4,1536,128]{3,2,1,0:T(8,128)(2,1)} %collective-permute-done.4), kind=kLoop, calls=%fused_computation.62 | loop fusion | bytes 6291456 | tf_op jit(solution)/shard_map/concatenate | solution.py:310
  97.2 4.4 %slice_bitcast_fusion = (bf16[4,2048,128]{2,1,0:T(8,128)(2,1)}, bf16[4,2048,128]{2,1,0:T(8,128)(2,1)}) fusion(bf16[2,4,2048,128]{3,2,1,0:T(8,128)(2,1)} %constant_dynamic-update-slice_fusion), kind=kLoop, calls=%fused_computation.11 | loop fusion | bytes 8388608 | tf_op jit(solution)/shard_map/squeeze | solution.py:312
  101.7 0.0 copy-start.12
  101.7 16.0 %shard_map.146 = (f32[1024,128]{1,0:T(8,128)}, f32[1024,128]{1,0:T(8,128)}, f32[1024,128]{1,0:T(8,128)}) custom-call(s32[32]{0:T(128)} %reshape.357.present_ref, bf16[1024,128]{1,0:T(8,128)(2,1)} %q_ref.3, s32[1024,128]{1,0:T(8,128)} %broadcast_in_dim.74.grp_ref, bf16[4,2048,128]{2,1,0:T(8,128)(2,1)} %get-tuple-element.56.k_ref, ...), custom_call_target="tpu_custom_call" | custom-call | flops 2147483648 | bytes 6029312 | tf_op jit(solution)/shard_map/pallas_call | solution.py:152
  117.7 0.0 copy-start.8
  117.7 0.0 copy-start.7
  117.7 2.2 fusion.24
  119.9 4.3 %fusion.15 = bf16[1024,128]{1,0:T(8,128)(2,1)} fusion(bf16[1024,128]{1,0:T(8,128)(2,1)S(1)} %copy-done.12, f32[1024,1024]{0,1:T(8,128)} %copy-done.2, f32[1024]{0:T(1024)S(1)} %get-tuple-element.59, f32[1024,128]{1,0:T(8,128)} %get-tuple-element.41, f32[1024,128]{1,0:T(8,128)S(1)} %copy-done.14, f32[1024]{0:T(1024)S(1)} %get-tuple-element.45, ...), kind=kOutput, calls=%fused_computation.20 | convolution fusion | flops 271581184 | bytes 5791744 | tf_op jit(solution)/shard_map/while/body/eval_jaxpr/hqk,khd->qhd/dot_general | solution.py:232
  124.2 8.0 %all-to-all-start = ((bf16[16,64,128]{2,1,0:T(8,128)(2,1)}), bf16[16,64,128]{2,1,0:T(8,128)(2,1)S(1)}, u32[]{:S(2)}, u32[]{:S(2)}) async-start(bf16[16,64,128]{2,1,0:T(8,128)(2,1)} %bitcast.12), calls=%async_computation | async-start | bytes 524288 | tf_op jit(solution)/shard_map/all_to_all | solution.py:323
  132.2 0.2 select_reduce_fusion
  132.4 8.7 %all-to-all-done = bf16[16,64,128]{2,1,0:T(8,128)(2,1)S(1)} async-done(((bf16[16,64,128]{2,1,0:T(8,128)(2,1)}), bf16[16,64,128]{2,1,0:T(8,128)(2,1)S(1)}, u32[]{:S(2)}, u32[]{:S(2)}) %all-to-all-start) | async-done | bytes 262176 | tf_op jit(solution)/shard_map/all_to_all | solution.py:323
  141.1 5.1 %multiply_reduce_fusion = (f32[64]{0:T(128)S(1)}, f32[64,2048]{1,0:T(8,128)S(1)}) fusion(bf16[2048,2048]{1,0:T(8,128)(2,1)} %all-gather.2.cloned.1.call-done, bf16[64,2048]{1,0:T(8,128)(2,1)S(1)} %copy-done.7, bf16[16,64,128]{2,1,0:T(8,128)(2,1)S(1)} %all-to-all-done), kind=kOutput, calls=%fused_computation.29 | convolution fusion | flops 537395136 | bytes 9437440 | tf_op jit(solution)/shard_map/dot_general | solution.py:324
  146.2 0.8 convolution_convert_fusion
  147.0 1.1 fusion.34
  148.1 21.5 %all_to_all.36 = bf16[32,8,2048]{2,1,0:T(8,128)(2,1)S(1)} all-to-all(bf16[32,8,2048]{2,1,0:T(8,128)(2,1)S(1)} %get-tuple-element.57), channel_id=1, replica_groups=mesh['req'=8,'exp'=16] {'exp'}, dimensions={0} | all-to-all | bytes 2097152 | tf_op jit(solution)/shard_map/all_to_all | solution.py:346
  169.6 3.7 %all-to-all-start.3 = ((bf16[32,8,2048]{2,1,0:T(8,128)(2,1)}), bf16[32,8,2048]{2,1,0:T(8,128)(2,1)S(1)}, u32[]{:S(2)}, u32[]{:S(2)}) async-start(bf16[32,8,2048]{2,1,0:T(8,128)(2,1)} %get-tuple-element.58), calls=%async_computation.3 | async-start | bytes 2097152 | tf_op jit(solution)/shard_map/all_to_all | solution.py:346
  173.3 8.5 %copy.87.wg_ref = bf16[2,2048,704]{2,1,0:T(8,128)(2,1)} copy(bf16[2,2048,704]{1,2,0:T(8,128)(2,1)} %param.27) | data formatting | bytes 11534336 | tf_op args[12]
  181.8 8.5 %copy.88.wu_ref = bf16[2,2048,704]{2,1,0:T(8,128)(2,1)} copy(bf16[2,2048,704]{1,2,0:T(8,128)(2,1)} %param.28) | data formatting | bytes 11534336 | tf_op args[13]
  190.3 1.1 copy.106
  191.4 9.1 %shard_map.147 = bf16[2,128,2048]{2,1,0:T(8,128)(2,1)} custom-call(bf16[2,128,2048]{2,1,0:T(8,128)(2,1)} %bitcast.76, bf16[2,2048,704]{2,1,0:T(8,128)(2,1)} %copy.87.wg_ref, bf16[2,2048,704]{2,1,0:T(8,128)(2,1)} %copy.88.wu_ref, bf16[2,704,2048]{2,1,0:T(8,128)(2,1)} %wd_ref.3), custom_call_target="tpu_custom_call" | custom-call | flops 2214592512 | bytes 19398656 | tf_op jit(solution)/shard_map/pallas_call | solution.py:187
  200.5 2.4 copy.89
  202.9 7.2 %all-to-all-start.2 = ((bf16[32,8,2048]{2,1,0:T(8,128)(2,1)}), bf16[32,8,2048]{2,1,0:T(8,128)(2,1)S(1)}, u32[]{:S(2)}, u32[]{:S(2)}) async-start(bf16[32,8,2048]{2,1,0:T(8,128)(2,1)} %bitcast.21), calls=%async_computation.2 | async-start | bytes 2097152 | tf_op jit(solution)/shard_map/all_to_all | solution.py:354
  210.0 1.0 copy.105
  211.1 9.1 %shard_map.148 = bf16[2,128,2048]{2,1,0:T(8,128)(2,1)} custom-call(bf16[2,128,2048]{2,1,0:T(8,128)(2,1)} %bitcast.74, bf16[2,2048,704]{2,1,0:T(8,128)(2,1)} %copy.87.wg_ref, bf16[2,2048,704]{2,1,0:T(8,128)(2,1)} %copy.88.wu_ref, bf16[2,704,2048]{2,1,0:T(8,128)(2,1)} %wd_ref.3), custom_call_target="tpu_custom_call" | custom-call | flops 2214592512 | bytes 19398656 | tf_op jit(solution)/shard_map/pallas_call | solution.py:187
  220.1 1.3 copy.93
  221.4 4.7 %all-to-all-done.2 = bf16[32,8,2048]{2,1,0:T(8,128)(2,1)S(1)} async-done(((bf16[32,8,2048]{2,1,0:T(8,128)(2,1)}), bf16[32,8,2048]{2,1,0:T(8,128)(2,1)S(1)}, u32[]{:S(2)}, u32[]{:S(2)}) %all-to-all-start.2) | async-done | bytes 1048608 | tf_op jit(solution)/shard_map/all_to_all | solution.py:354
  226.2 19.2 %all_to_all.37 = bf16[32,8,2048]{2,1,0:T(8,128)(2,1)S(1)} all-to-all(bf16[32,8,2048]{2,1,0:T(8,128)(2,1)S(1)} %bitcast.80), channel_id=1, replica_groups=mesh['req'=8,'exp'=16] {'exp'}, dimensions={0} | all-to-all | bytes 2097152 | tf_op jit(solution)/shard_map/all_to_all | solution.py:354
  245.4 0.2 pad_maximum_fusion.2
  245.6 1.2 fusion.2
  (41 shorter events, 0.1 us)
Async XLA Ops:
  6.5 55.7 %copy-start = (bf16[1024,128]{1,0:T(8,128)(2,1)S(1)}, bf16[1024,128]{1,0:T(8,128)(2,1)}, u32[]{:S(2)}) copy-start(bf16[1024,128]{1,0:T(8,128)(2,1)} %param.16) | copy-start | bytes 786436
  6.5 134.5 %all-gather.2.cloned.1.call-start = ((), (), s32[]{:S(2)}) async-start(), calls=%async_computation.5 | async-start | bytes 8912896 | tf_op jit(solution)/shard_map/all_gather | solution.py:322
  7.3 54.1 %copy-start.13 = (s32[1,8]{1,0:T(1,128)S(1)}, s32[1,8]{1,0:T(1,128)}, u32[]{:S(2)}) copy-start(s32[1,8]{1,0:T(1,128)} %param.20) | copy-start | bytes 100
  7.3 54.1 %copy-start.11 = (s32[1,8]{1,0:T(1,128)S(1)}, s32[1,8]{1,0:T(1,128)}, u32[]{:S(2)}) copy-start(s32[1,8]{1,0:T(1,128)} %param.21) | copy-start | bytes 100
  9.6 26.2 %collective-permute-start = (bf16[2,4,512,128]{3,2,1,0:T(8,128)(2,1)}, bf16[2,4,512,128]{3,2,1,0:T(8,128)(2,1)S(1)}, u32[]{:S(2)}, u32[]{:S(2)}) collective-permute-start(bf16[2,4,512,128]{3,2,1,0:T(8,128)(2,1)} %pad_maximum_fusion.3), channel_id=1, source_target_pairs={{0,32},{16,48},{32,64},{48,80},{64,96},{80,112},{96,0},{112,16},{1... | collective-permute-start | bytes 3145736 | tf_op jit(solution)/shard_map/ppermute | solution.py:301
  11.2 48.3 %collective-permute-start.1 = (bf16[2,4,512,128]{3,2,1,0:T(8,128)(2,1)}, bf16[2,4,512,128]{3,2,1,0:T(8,128)(2,1)S(1)}, u32[]{:S(2)}, u32[]{:S(2)}) collective-permute-start(bf16[2,4,512,128]{3,2,1,0:T(8,128)(2,1)} %pad_maximum_fusion.3), channel_id=1, source_target_pairs={{0,64},{16,80},{32,96},{48,112},{64,0},{80,16},{96,32},{112,48},{1... | collective-permute-start | bytes 3145736 | tf_op jit(solution)/shard_map/ppermute | solution.py:301
  13.9 45.6 %collective-permute-start.2 = (bf16[2,4,512,128]{3,2,1,0:T(8,128)(2,1)}, bf16[2,4,512,128]{3,2,1,0:T(8,128)(2,1)S(1)}, u32[]{:S(2)}, u32[]{:S(2)}) collective-permute-start(bf16[2,4,512,128]{3,2,1,0:T(8,128)(2,1)} %pad_maximum_fusion.3), channel_id=1, source_target_pairs={{0,96},{16,112},{32,0},{48,16},{64,32},{80,48},{96,64},{112,80},{1... | collective-permute-start | bytes 3145736 | tf_op jit(solution)/shard_map/ppermute | solution.py:301
  15.4 54.8 %collective-permute-start.3 = (bf16[2,4,512,128]{3,2,1,0:T(8,128)(2,1)}, bf16[2,4,512,128]{3,2,1,0:T(8,128)(2,1)}, u32[]{:S(2)}, u32[]{:S(2)}) collective-permute-start(bf16[2,4,512,128]{3,2,1,0:T(8,128)(2,1)} %pad_maximum_fusion.3), channel_id=1, source_target_pairs={{0,16},{16,0},{32,48},{48,32},{64,80},{80,64},{96,112},{112,96},{1... | collective-permute-start | bytes 3145736 | tf_op jit(solution)/shard_map/ppermute | solution.py:298
  61.3 31.8 %collective-permute-start.4 = (bf16[2,4,1536,128]{3,2,1,0:T(8,128)(2,1)}, bf16[2,4,1536,128]{3,2,1,0:T(8,128)(2,1)}, u32[]{:S(2)}, u32[]{:S(2)}) collective-permute-start(bf16[2,4,1536,128]{3,2,1,0:T(8,128)(2,1)} %pad_maximum_fusion.1), channel_id=1, source_target_pairs={{0,16},{16,0},{32,48},{48,32},{64,80},{80,64},{96,112},{112,96},{1... | collective-permute-start | bytes 9437192 | tf_op jit(solution)/shard_map/ppermute | solution.py:306
  64.3 2.0 copy-start.2
  64.3 5.8 %copy-start.10 = (bf16[64,4]{0,1:T(4,128)(2,1)S(1)}, bf16[64,4]{0,1:T(4,128)(2,1)}, u32[]{:S(2)}) copy-start(bf16[64,4]{0,1:T(4,128)(2,1)} %param.26) | copy-start | bytes 1540
  64.3 5.8 %copy-start.9 = (bf16[2048]{0:T(1024)(128)(2,1)S(1)}, bf16[2048]{0:T(1024)(128)(2,1)}, u32[]{:S(2)}) copy-start(bf16[2048]{0:T(1024)(128)(2,1)} %param.24) | copy-start | bytes 12292
  101.6 16.0 %copy-start.3 = (f32[1024,1]{1,0:T(8,128)S(1)}, f32[1024,1]{1,0:T(8,128)}, u32[]{:S(2)}) copy-start(f32[1024,1]{1,0:T(8,128)} %copy.80) | copy-start | bytes 12292
  101.6 16.0 %copy-start.4 = (f32[1024,1]{1,0:T(8,128)S(1)}, f32[1024,1]{1,0:T(8,128)}, u32[]{:S(2)}) copy-start(f32[1024,1]{1,0:T(8,128)} %copy.78) | copy-start | bytes 12292
  101.6 16.0 %copy-start.5 = (f32[1024,128]{1,0:T(8,128)S(1)}, f32[1024,128]{1,0:T(8,128)}, u32[]{:S(2)}) copy-start(f32[1024,128]{1,0:T(8,128)} %get-tuple-element.38) | copy-start | bytes 1572868
  101.6 16.0 %copy-start.6 = (f32[1024,128]{1,0:T(8,128)S(1)}, f32[1024,128]{1,0:T(8,128)}, u32[]{:S(2)}) copy-start(f32[1024,128]{1,0:T(8,128)} %get-tuple-element.42) | copy-start | bytes 1572868
  101.7 18.2 %copy-start.12 = (bf16[1024,128]{1,0:T(8,128)(2,1)S(1)}, bf16[1024,128]{1,0:T(8,128)(2,1)}, u32[]{:S(2)}) copy-start(bf16[1024,128]{1,0:T(8,128)(2,1)} %param.17) | copy-start | bytes 786436
  101.7 18.2 %copy-start.14 = (f32[1024,128]{1,0:T(8,128)S(1)}, f32[1024,128]{1,0:T(8,128)}, u32[]{:S(2)}) copy-start(f32[1024,128]{1,0:T(8,128)} %get-tuple-element.36) | copy-start | bytes 1572868
  117.7 14.5 %copy-start.8 = (s32[64,4]{0,1:T(4,128)S(1)}, s32[64,4]{0,1:T(4,128)}, u32[]{:S(2)}) copy-start(s32[64,4]{0,1:T(4,128)} %param.25) | copy-start | bytes 3076
  117.7 23.4 %copy-start.7 = (bf16[64,2048]{1,0:T(8,128)(2,1)S(1)}, bf16[64,2048]{1,0:T(8,128)(2,1)}, u32[]{:S(2)}) copy-start(bf16[64,2048]{1,0:T(8,128)(2,1)} %param.22) | copy-start | bytes 786436
  124.2 16.9 %all-to-all-start = ((bf16[16,64,128]{2,1,0:T(8,128)(2,1)}), bf16[16,64,128]{2,1,0:T(8,128)(2,1)S(1)}, u32[]{:S(2)}, u32[]{:S(2)}) async-start(bf16[16,64,128]{2,1,0:T(8,128)(2,1)} %bitcast.12), calls=%async_computation | async-start | bytes 524288 | tf_op jit(solution)/shard_map/all_to_all | solution.py:323
  169.6 33.3 %all-to-all-start.3 = ((bf16[32,8,2048]{2,1,0:T(8,128)(2,1)}), bf16[32,8,2048]{2,1,0:T(8,128)(2,1)S(1)}, u32[]{:S(2)}, u32[]{:S(2)}) async-start(bf16[32,8,2048]{2,1,0:T(8,128)(2,1)} %get-tuple-element.58), calls=%async_computation.3 | async-start | bytes 2097152 | tf_op jit(solution)/shard_map/all_to_all | solution.py:346
  202.9 23.3 %all-to-all-start.2 = ((bf16[32,8,2048]{2,1,0:T(8,128)(2,1)}), bf16[32,8,2048]{2,1,0:T(8,128)(2,1)S(1)}, u32[]{:S(2)}, u32[]{:S(2)}) async-start(bf16[32,8,2048]{2,1,0:T(8,128)(2,1)} %bitcast.21), calls=%async_computation.2 | async-start | bytes 2097152 | tf_op jit(solution)/shard_map/all_to_all | solution.py:354
  226.2 20.6 %copy-start.1 = (bf16[1024,128]{1,0:T(8,128)(2,1)S(1)}, bf16[1024,128]{1,0:T(8,128)(2,1)}, u32[]{:S(2)}) copy-start(bf16[1024,128]{1,0:T(8,128)(2,1)} %param.16) | copy-start | bytes 786436
Sparse Core Ops, SparseCore 0:
  9.5 73.3 all-gather.1

commit v8 on v7

--- a/solution.py
+++ b/solution.py
@@ -173,37 +173,53 @@
     return (acc, maxima[:, :1], totals[:, :1])
 
 
-def expert_kernel(x_ref, wg_ref, wu_ref, wd_ref, o_ref):
+def expert_kernel(x_ref, wg_ref, wu_ref, wd_ref, o_ref, total):
+    f = pl.program_id(1)
+
+    @pl.when(f == 0)
+    def _():
+        total[...] = jnp.zeros_like(total)
+
     x = x_ref[0]
-    gate_h = jnp.dot(x, wg_ref[0], preferred_element_type=jnp.float32)
-    up_h = jnp.dot(x, wu_ref[0], preferred_element_type=jnp.float32)
+    contract = (((1,), (1,)), ((), ()))
+    gate_h = lax.dot_general(x, wg_ref[0], contract, preferred_element_type=jnp.float32)
+    up_h = lax.dot_general(x, wu_ref[0], contract, preferred_element_type=jnp.float32)
     hidden = (gate_h / (1.0 + jnp.exp(-gate_h)) * up_h).astype(jnp.bfloat16)
-    o_ref[0] = jnp.dot(hidden, wd_ref[0], preferred_element_type=jnp.float32).astype(o_ref.dtype)
+    total[...] += jnp.dot(hidden, wd_ref[0], preferred_element_type=jnp.float32)
+
+    @pl.when(f == pl.num_programs(1) - 1)
+    def _():
+        o_ref[0] = total[...].astype(o_ref.dtype)
+
+
+FE_CHUNK = 176
 
 
 def expert_ffn(rows, w_gate, w_up, w_down):
     exp_dev, row_count, width = rows.shape
     inner = w_gate.shape[2]
+    chunk = FE_CHUNK if inner % FE_CHUNK == 0 else inner
+    gate_t = jnp.swapaxes(w_gate, 1, 2)
+    up_t = jnp.swapaxes(w_up, 1, 2)
     return pl.pallas_call(
         expert_kernel,
-        grid=(exp_dev,),
+        grid=(exp_dev, inner // chunk),
         in_specs=[
-            pl.BlockSpec((1, row_count, width), lambda e: (e, 0, 0)),
-            pl.BlockSpec((1, width, inner), lambda e: (e, 0, 0)),
-            pl.BlockSpec((1, width, inner), lambda e: (e, 0, 0)),
-            pl.BlockSpec((1, inner, width), lambda e: (e, 0, 0)),
+            pl.BlockSpec((1, row_count, width), lambda e, f: (e, 0, 0)),
+            pl.BlockSpec((1, chunk, width), lambda e, f: (e, f, 0)),
+            pl.BlockSpec((1, chunk, width), lambda e, f: (e, f, 0)),
+            pl.BlockSpec((1, chunk, width), lambda e, f: (e, f, 0)),
         ],
-        out_specs=pl.BlockSpec((1, row_count, width), lambda e: (e, 0, 0)),
+        out_specs=pl.BlockSpec((1, row_count, width), lambda e, f: (e, 0, 0)),
         out_shape=jax.ShapeDtypeStruct((exp_dev, row_count, width), jnp.bfloat16),
-        compiler_params=pltpu.CompilerParams(
-            dimension_semantics=("arbitrary",), vmem_limit_bytes=56 * 1024 * 1024
-        ),
+        scratch_shapes=[pltpu.VMEM((row_count, width), jnp.float32)],
+        compiler_params=pltpu.CompilerParams(dimension_semantics=("arbitrary", "arbitrary")),
         cost_estimate=pl.CostEstimate(
             flops=6 * exp_dev * row_count * width * inner,
             transcendentals=exp_dev * row_count * inner,
             bytes_accessed=exp_dev * (3 * width * inner + 2 * row_count * width) * 2,
         ),
-    )(rows, w_gate, w_up, w_down)
+    )(rows, gate_t, up_t, w_down)
 
 
 def attend_suffix(queries, keys, values, request, position):

time: 255 us -> 241 us (0.945)
  the two profiles are of different devices: /device:TPU:0 before, /device:TPU:2 now
where the time goes in v8:
time: 241 us; the launch traced here: 240 us
  waiting for transfers between devices  59.1 us (25%)
  Pallas kernels  54.6 us (23%)
  blocking collectives  40.8 us (17%)
  local copies, waits for them, and re-layouts  27.4 us (11%)
  starting transfers between devices  20.5 us (9%)
  between operations  13.7 us (6%)
  matrix products  13.4 us (6%)
  other arithmetic  10.6 us (4%)
    ppermute x3, waiting for transfers between devices, per_device(): lax.ppermute(local_kv, 'req', [(i, (i + 2 * s) % req_count) for i in rang...  42.8 us
    pallas_call x2, Pallas kernels, attend_prefix_local(): pl.pallas_call(prefix_kernel, grid_spec=pltpu.PrefetchScalarGridSpec(num_...  30 us
    pallas_call x2, Pallas kernels, expert_ffn(): pl.pallas_call(expert_kernel, grid=(exp_dev, inner // chunk), in_specs=[p...  24.6 us
    all_to_all x1, blocking collectives, per_device(): lax.all_to_all(buffer[:, half * piece:(half + 1) * piece], 'exp', split_a...  20.5 us
    all_to_all x1, blocking collectives, per_device(): lax.all_to_all(expert_out.reshape(EXPERTS, piece, width), 'exp', split_ax...  20.3 us
    all_to_all x1, waiting for transfers between devices, per_device(): lax.all_to_all(attended, 'exp', split_axis=0, concat_axis=1, tiled=True)  8.32 us
    all_to_all x1, starting transfers between devices, per_device(): lax.all_to_all(attended, 'exp', split_axis=0, concat_axis=1, tiled=True)  8.17 us
    squeeze x2, local copies, waits for them, and re-layouts, per_device(): part = attend_prefix_local(queries, tok_group, chunk[0], chunk[1])  6.79 us
  transfers between devices with their start and end apart: 9, of which 6 were waited for; matrix products, arithmetic and copies ran while one was open for 17% of the time, Pallas kernels for 23%

profile of v8, /device:TPU:2, one launch (start us, length us, event | category | flops | bytes accessed | tf_op | source)
XLA Modules:
  0.0 240.1 jit_solution(15463287715629998293)
XLA Ops:
  6.5 0.7 all-gather.2.cloned.1.call-update
  7.3 0.0 copy-start.13
  7.3 2.4 pad_maximum_fusion.3
  9.6 1.5 collective-permute-start
  11.1 1.0 collective-permute-start.1
  12.2 2.2 collective-permute-start.2
  14.4 0.8 copy.66
  15.2 0.1 eq.120
  15.3 0.1 eq.116
  15.4 0.8 reduce_window_sum.24
  16.2 0.1 convert_reduce_fusion.1
  16.3 19.6 %collective-permute-done = bf16[2,4,512,128]{3,2,1,0:T(8,128)(2,1)S(1)} collective-permute-done((bf16[2,4,512,128]{3,2,1,0:T(8,128)(2,1)}, bf16[2,4,512,128]{3,2,1,0:T(8,128)(2,1)S(1)}, u32[]{:S(2)}, u32[]{:S(2)}) %collective-permute-start) | collective-permute-done | bytes 1048608 | tf_op jit(solution)/shard_map/ppermute | solution.py:317
  35.9 3.0 %collective-permute-done.1 = bf16[2,4,512,128]{3,2,1,0:T(8,128)(2,1)S(1)} collective-permute-done((bf16[2,4,512,128]{3,2,1,0:T(8,128)(2,1)}, bf16[2,4,512,128]{3,2,1,0:T(8,128)(2,1)S(1)}, u32[]{:S(2)}, u32[]{:S(2)}) %collective-permute-start.1) | collective-permute-done | bytes 1048608 | tf_op jit(solution)/shard_map/ppermute | solution.py:317
  38.9 20.1 %collective-permute-done.2 = bf16[2,4,512,128]{3,2,1,0:T(8,128)(2,1)S(1)} collective-permute-done((bf16[2,4,512,128]{3,2,1,0:T(8,128)(2,1)}, bf16[2,4,512,128]{3,2,1,0:T(8,128)(2,1)S(1)}, u32[]{:S(2)}, u32[]{:S(2)}) %collective-permute-start.2) | collective-permute-done | bytes 1048608 | tf_op jit(solution)/shard_map/ppermute | solution.py:317
  59.1 1.8 pad_maximum_fusion.1
  60.9 0.1 select_reduce_fusion.2
  61.0 0.1 fusion.33
  61.1 0.1 copy.61
  61.2 0.6 reshape.357.present_ref
  61.8 2.0 fusion.35
  63.9 0.0 copy-start.10
  63.9 0.0 copy-start.9
  63.9 1.9 copy-done.2
  65.8 0.6 fusion
  66.5 1.1 copy.64
  67.5 1.0 copy.62
  68.6 0.6 reduce-window.6
  69.2 0.2 slice_reduce_fusion
  69.4 0.1 fusion.31
  69.5 0.1 reduce_sum.80
  69.6 0.1 copy.69
  69.7 0.0 copy-done.9
  69.7 2.4 %constant_dynamic-update-slice_fusion.1 = bf16[2,4,2048,128]{3,2,1,0:T(8,128)(2,1)} fusion(bf16[2,4,512,128]{3,2,1,0:T(8,128)(2,1)} %collective-permute-done.3), kind=kLoop, calls=%fused_computation.63 | loop fusion | bytes 2097152
  72.2 1.4 pad_maximum_fusion
  73.6 2.3 slice_bitcast_fusion.2
  75.9 1.1 broadcast_in_dim.74.grp_ref
  77.0 14.9 %shard_map.145 = (f32[1024,128]{1,0:T(8,128)}, f32[1024,128]{1,0:T(8,128)}, f32[1024,128]{1,0:T(8,128)}) custom-call(s32[32]{0:T(128)} %reshape.357.present_ref, bf16[1024,128]{1,0:T(8,128)(2,1)} %q_ref.3, s32[1024,128]{1,0:T(8,128)} %broadcast_in_dim.74.grp_ref, bf16[4,2048,128]{2,1,0:T(8,128)(2,1)} %get-tuple-element.54.k_ref, ...), custom_call_target="tpu_custom_call" | custom-call | flops 2147483648 | bytes 6029312 | tf_op jit(solution)/shard_map/pallas_call | solution.py:152
  91.9 4.1 %constant_dynamic-update-slice_fusion = bf16[2,4,2048,128]{3,2,1,0:T(8,128)(2,1)} fusion(bf16[2,4,2048,128]{3,2,1,0:T(8,128)(2,1)} %constant_dynamic-update-slice_fusion.1, bf16[2,4,1536,128]{3,2,1,0:T(8,128)(2,1)} %collective-permute-done.4), kind=kLoop, calls=%fused_computation.62 | loop fusion | bytes 6291456 | tf_op jit(solution)/shard_map/concatenate | solution.py:326
  95.9 4.4 %slice_bitcast_fusion = (bf16[4,2048,128]{2,1,0:T(8,128)(2,1)}, bf16[4,2048,128]{2,1,0:T(8,128)(2,1)}) fusion(bf16[2,4,2048,128]{3,2,1,0:T(8,128)(2,1)} %constant_dynamic-update-slice_fusion), kind=kLoop, calls=%fused_computation.11 | loop fusion | bytes 8388608 | tf_op jit(solution)/shard_map/squeeze | solution.py:328
  100.4 0.0 copy-start.12
  100.4 15.1 %shard_map.146 = (f32[1024,128]{1,0:T(8,128)}, f32[1024,128]{1,0:T(8,128)}, f32[1024,128]{1,0:T(8,128)}) custom-call(s32[32]{0:T(128)} %reshape.357.present_ref, bf16[1024,128]{1,0:T(8,128)(2,1)} %q_ref.3, s32[1024,128]{1,0:T(8,128)} %broadcast_in_dim.74.grp_ref, bf16[4,2048,128]{2,1,0:T(8,128)(2,1)} %get-tuple-element.56.k_ref, ...), custom_call_target="tpu_custom_call" | custom-call | flops 2147483648 | bytes 6029312 | tf_op jit(solution)/shard_map/pallas_call | solution.py:152
  115.5 0.0 copy-start.8
  115.5 2.2 fusion.24
  117.7 4.3 %fusion.15 = bf16[1024,128]{1,0:T(8,128)(2,1)} fusion(bf16[1024,128]{1,0:T(8,128)(2,1)S(1)} %copy-done.12, f32[1024,1024]{0,1:T(8,128)} %copy-done.2, f32[1024]{0:T(1024)S(1)} %get-tuple-element.59, f32[1024,128]{1,0:T(8,128)} %get-tuple-element.41, f32[1024,128]{1,0:T(8,128)S(1)} %copy-done.14, f32[1024]{0:T(1024)S(1)} %get-tuple-element.45, ...), kind=kOutput, calls=%fused_computation.20 | convolution fusion | flops 271581184 | bytes 5791744 | tf_op jit(solution)/shard_map/while/body/eval_jaxpr/hqk,khd->qhd/dot_general | solution.py:248
  122.1 8.2 %all-to-all-start = ((bf16[16,64,128]{2,1,0:T(8,128)(2,1)}), bf16[16,64,128]{2,1,0:T(8,128)(2,1)S(1)}, u32[]{:S(2)}, u32[]{:S(2)}) async-start(bf16[16,64,128]{2,1,0:T(8,128)(2,1)} %bitcast.12), calls=%async_computation | async-start | bytes 524288 | tf_op jit(solution)/shard_map/all_to_all | solution.py:339
  130.3 0.2 select_reduce_fusion
  130.4 8.3 %all-to-all-done = bf16[16,64,128]{2,1,0:T(8,128)(2,1)S(1)} async-done(((bf16[16,64,128]{2,1,0:T(8,128)(2,1)}), bf16[16,64,128]{2,1,0:T(8,128)(2,1)S(1)}, u32[]{:S(2)}, u32[]{:S(2)}) %all-to-all-start) | async-done | bytes 262176 | tf_op jit(solution)/shard_map/all_to_all | solution.py:339
  138.8 5.1 %multiply_reduce_fusion = (f32[64]{0:T(128)S(1)}, f32[64,2048]{1,0:T(8,128)S(1)}) fusion(bf16[2048,2048]{1,0:T(8,128)(2,1)} %all-gather.2.cloned.1.call-done, bf16[64,2048]{1,0:T(8,128)(2,1)S(1)} %copy-done.7, bf16[16,64,128]{2,1,0:T(8,128)(2,1)S(1)} %all-to-all-done), kind=kOutput, calls=%fused_computation.29 | convolution fusion | flops 537395136 | bytes 9437440 | tf_op jit(solution)/shard_map/dot_general | solution.py:340
  143.8 0.8 convolution_convert_fusion
  144.6 1.2 fusion.34
  145.8 20.5 %all_to_all.36 = bf16[32,8,2048]{2,1,0:T(8,128)(2,1)S(1)} all-to-all(bf16[32,8,2048]{2,1,0:T(8,128)(2,1)S(1)} %get-tuple-element.57), channel_id=1, replica_groups=mesh['req'=8,'exp'=16] {'exp'}, dimensions={0} | all-to-all | bytes 2097152 | tf_op jit(solution)/shard_map/all_to_all | solution.py:362
  166.3 3.9 %all-to-all-start.3 = ((bf16[32,8,2048]{2,1,0:T(8,128)(2,1)}), bf16[32,8,2048]{2,1,0:T(8,128)(2,1)S(1)}, u32[]{:S(2)}, u32[]{:S(2)}) async-start(bf16[32,8,2048]{2,1,0:T(8,128)(2,1)} %get-tuple-element.58), calls=%async_computation.3 | async-start | bytes 2097152 | tf_op jit(solution)/shard_map/all_to_all | solution.py:362
  170.2 1.1 copy.86
  171.3 12.3 %shard_map.147 = bf16[2,128,2048]{2,1,0:T(8,128)(2,1)} custom-call(bf16[2,128,2048]{2,1,0:T(8,128)(2,1)} %bitcast.80, bf16[2,704,2048]{2,1,0:T(8,128)(2,1)} %bitcast.74, bf16[2,704,2048]{2,1,0:T(8,128)(2,1)} %bitcast.76, bf16[2,704,2048]{2,1,0:T(8,128)(2,1)} %wd_ref.3), custom_call_target="tpu_custom_call" | custom-call | flops 2214592512 | bytes 19398656 | tf_op jit(solution)/shard_map/pallas_call | solution.py:204
  183.6 2.3 copy.71
  185.9 3.6 %all-to-all-done.3 = bf16[32,8,2048]{2,1,0:T(8,128)(2,1)S(1)} async-done(((bf16[32,8,2048]{2,1,0:T(8,128)(2,1)}), bf16[32,8,2048]{2,1,0:T(8,128)(2,1)S(1)}, u32[]{:S(2)}, u32[]{:S(2)}) %all-to-all-start.3) | async-done | bytes 1048608 | tf_op jit(solution)/shard_map/all_to_all | solution.py:362
  189.5 3.7 %all-to-all-start.2 = ((bf16[32,8,2048]{2,1,0:T(8,128)(2,1)}), bf16[32,8,2048]{2,1,0:T(8,128)(2,1)S(1)}, u32[]{:S(2)}, u32[]{:S(2)}) async-start(bf16[32,8,2048]{2,1,0:T(8,128)(2,1)} %bitcast.23), calls=%async_computation.2 | async-start | bytes 2097152 | tf_op jit(solution)/shard_map/all_to_all | solution.py:370
  193.2 1.1 copy.85
  194.3 12.3 %shard_map.148 = bf16[2,128,2048]{2,1,0:T(8,128)(2,1)} custom-call(bf16[2,128,2048]{2,1,0:T(8,128)(2,1)} %bitcast.82, bf16[2,704,2048]{2,1,0:T(8,128)(2,1)} %bitcast.75, bf16[2,704,2048]{2,1,0:T(8,128)(2,1)} %bitcast.77, bf16[2,704,2048]{2,1,0:T(8,128)(2,1)} %wd_ref.3), custom_call_target="tpu_custom_call" | custom-call | flops 2214592512 | bytes 19398656 | tf_op jit(solution)/shard_map/pallas_call | solution.py:204
  206.6 1.3 copy.73
  207.9 3.6 %all-to-all-done.2 = bf16[32,8,2048]{2,1,0:T(8,128)(2,1)S(1)} async-done(((bf16[32,8,2048]{2,1,0:T(8,128)(2,1)}), bf16[32,8,2048]{2,1,0:T(8,128)(2,1)S(1)}, u32[]{:S(2)}, u32[]{:S(2)}) %all-to-all-start.2) | async-done | bytes 1048608 | tf_op jit(solution)/shard_map/all_to_all | solution.py:370
  211.5 20.3 %all_to_all.37 = bf16[32,8,2048]{2,1,0:T(8,128)(2,1)S(1)} all-to-all(bf16[32,8,2048]{2,1,0:T(8,128)(2,1)S(1)} %bitcast.86), channel_id=1, replica_groups=mesh['req'=8,'exp'=16] {'exp'}, dimensions={0} | all-to-all | bytes 2097152 | tf_op jit(solution)/shard_map/all_to_all | solution.py:370
  231.8 0.2 pad_maximum_fusion.2
  232.0 1.2 fusion.2
  (39 shorter events, 0.1 us)
Async XLA Ops:
  6.5 55.3 %copy-start = (bf16[1024,128]{1,0:T(8,128)(2,1)S(1)}, bf16[1024,128]{1,0:T(8,128)(2,1)}, u32[]{:S(2)}) copy-start(bf16[1024,128]{1,0:T(8,128)(2,1)} %param.16) | copy-start | bytes 786436
  6.5 132.2 %all-gather.2.cloned.1.call-start = ((), (), s32[]{:S(2)}) async-start(), calls=%async_computation.5 | async-start | bytes 8912896 | tf_op jit(solution)/shard_map/all_gather | solution.py:338
  7.3 53.6 %copy-start.13 = (s32[1,8]{1,0:T(1,128)S(1)}, s32[1,8]{1,0:T(1,128)}, u32[]{:S(2)}) copy-start(s32[1,8]{1,0:T(1,128)} %param.20) | copy-start | bytes 100
  7.3 53.6 %copy-start.11 = (s32[1,8]{1,0:T(1,128)S(1)}, s32[1,8]{1,0:T(1,128)}, u32[]{:S(2)}) copy-start(s32[1,8]{1,0:T(1,128)} %param.21) | copy-start | bytes 100
  9.6 26.3 %collective-permute-start = (bf16[2,4,512,128]{3,2,1,0:T(8,128)(2,1)}, bf16[2,4,512,128]{3,2,1,0:T(8,128)(2,1)S(1)}, u32[]{:S(2)}, u32[]{:S(2)}) collective-permute-start(bf16[2,4,512,128]{3,2,1,0:T(8,128)(2,1)} %pad_maximum_fusion.3), channel_id=1, source_target_pairs={{0,32},{16,48},{32,64},{48,80},{64,96},{80,112},{96,0},{112,16},{1... | collective-permute-start | bytes 3145736 | tf_op jit(solution)/shard_map/ppermute | solution.py:317
  11.1 27.8 %collective-permute-start.1 = (bf16[2,4,512,128]{3,2,1,0:T(8,128)(2,1)}, bf16[2,4,512,128]{3,2,1,0:T(8,128)(2,1)S(1)}, u32[]{:S(2)}, u32[]{:S(2)}) collective-permute-start(bf16[2,4,512,128]{3,2,1,0:T(8,128)(2,1)} %pad_maximum_fusion.3), channel_id=1, source_target_pairs={{0,64},{16,80},{32,96},{48,112},{64,0},{80,16},{96,32},{112,48},{1... | collective-permute-start | bytes 3145736 | tf_op jit(solution)/shard_map/ppermute | solution.py:317
  12.2 46.9 %collective-permute-start.2 = (bf16[2,4,512,128]{3,2,1,0:T(8,128)(2,1)}, bf16[2,4,512,128]{3,2,1,0:T(8,128)(2,1)S(1)}, u32[]{:S(2)}, u32[]{:S(2)}) collective-permute-start(bf16[2,4,512,128]{3,2,1,0:T(8,128)(2,1)} %pad_maximum_fusion.3), channel_id=1, source_target_pairs={{0,96},{16,112},{32,0},{48,16},{64,32},{80,48},{96,64},{112,80},{1... | collective-permute-start | bytes 3145736 | tf_op jit(solution)/shard_map/ppermute | solution.py:317
  14.4 55.3 %collective-permute-start.3 = (bf16[2,4,512,128]{3,2,1,0:T(8,128)(2,1)}, bf16[2,4,512,128]{3,2,1,0:T(8,128)(2,1)}, u32[]{:S(2)}, u32[]{:S(2)}) collective-permute-start(bf16[2,4,512,128]{3,2,1,0:T(8,128)(2,1)} %pad_maximum_fusion.3), channel_id=1, source_target_pairs={{0,16},{16,0},{32,48},{48,32},{64,80},{80,64},{96,112},{112,96},{1... | collective-permute-start | bytes 3145736 | tf_op jit(solution)/shard_map/ppermute | solution.py:314
  60.9 31.0 %collective-permute-start.4 = (bf16[2,4,1536,128]{3,2,1,0:T(8,128)(2,1)}, bf16[2,4,1536,128]{3,2,1,0:T(8,128)(2,1)}, u32[]{:S(2)}, u32[]{:S(2)}) collective-permute-start(bf16[2,4,1536,128]{3,2,1,0:T(8,128)(2,1)} %pad_maximum_fusion.1), channel_id=1, source_target_pairs={{0,16},{16,0},{32,48},{48,32},{64,80},{80,64},{96,112},{112,96},{1... | collective-permute-start | bytes 9437192 | tf_op jit(solution)/shard_map/ppermute | solution.py:322
  63.9 2.0 copy-start.2
  63.9 5.8 %copy-start.10 = (bf16[64,4]{0,1:T(4,128)(2,1)S(1)}, bf16[64,4]{0,1:T(4,128)(2,1)}, u32[]{:S(2)}) copy-start(bf16[64,4]{0,1:T(4,128)(2,1)} %param.26) | copy-start | bytes 1540
  63.9 5.8 %copy-start.9 = (bf16[2048]{0:T(1024)(128)(2,1)S(1)}, bf16[2048]{0:T(1024)(128)(2,1)}, u32[]{:S(2)}) copy-start(bf16[2048]{0:T(1024)(128)(2,1)} %param.24) | copy-start | bytes 12292
  100.4 15.1 %copy-start.3 = (f32[1024,1]{1,0:T(8,128)S(1)}, f32[1024,1]{1,0:T(8,128)}, u32[]{:S(2)}) copy-start(f32[1024,1]{1,0:T(8,128)} %copy.64) | copy-start | bytes 12292
  100.4 15.1 %copy-start.4 = (f32[1024,1]{1,0:T(8,128)S(1)}, f32[1024,1]{1,0:T(8,128)}, u32[]{:S(2)}) copy-start(f32[1024,1]{1,0:T(8,128)} %copy.62) | copy-start | bytes 12292
  100.4 15.1 %copy-start.5 = (f32[1024,128]{1,0:T(8,128)S(1)}, f32[1024,128]{1,0:T(8,128)}, u32[]{:S(2)}) copy-start(f32[1024,128]{1,0:T(8,128)} %get-tuple-element.38) | copy-start | bytes 1572868
  100.4 15.1 %copy-start.6 = (f32[1024,128]{1,0:T(8,128)S(1)}, f32[1024,128]{1,0:T(8,128)}, u32[]{:S(2)}) copy-start(f32[1024,128]{1,0:T(8,128)} %get-tuple-element.42) | copy-start | bytes 1572868
  100.4 17.3 %copy-start.12 = (bf16[1024,128]{1,0:T(8,128)(2,1)S(1)}, bf16[1024,128]{1,0:T(8,128)(2,1)}, u32[]{:S(2)}) copy-start(bf16[1024,128]{1,0:T(8,128)(2,1)} %param.17) | copy-start | bytes 786436
  100.4 17.3 %copy-start.14 = (f32[1024,128]{1,0:T(8,128)S(1)}, f32[1024,128]{1,0:T(8,128)}, u32[]{:S(2)}) copy-start(f32[1024,128]{1,0:T(8,128)} %get-tuple-element.36) | copy-start | bytes 1572868
  115.5 14.7 %copy-start.8 = (s32[64,4]{0,1:T(4,128)S(1)}, s32[64,4]{0,1:T(4,128)}, u32[]{:S(2)}) copy-start(s32[64,4]{0,1:T(4,128)} %param.25) | copy-start | bytes 3076
  115.5 23.2 %copy-start.7 = (bf16[64,2048]{1,0:T(8,128)(2,1)S(1)}, bf16[64,2048]{1,0:T(8,128)(2,1)}, u32[]{:S(2)}) copy-start(bf16[64,2048]{1,0:T(8,128)(2,1)} %param.22) | copy-start | bytes 786436
  122.1 16.7 %all-to-all-start = ((bf16[16,64,128]{2,1,0:T(8,128)(2,1)}), bf16[16,64,128]{2,1,0:T(8,128)(2,1)S(1)}, u32[]{:S(2)}, u32[]{:S(2)}) async-start(bf16[16,64,128]{2,1,0:T(8,128)(2,1)} %bitcast.12), calls=%async_computation | async-start | bytes 524288 | tf_op jit(solution)/shard_map/all_to_all | solution.py:339
  166.3 23.3 %all-to-all-start.3 = ((bf16[32,8,2048]{2,1,0:T(8,128)(2,1)}), bf16[32,8,2048]{2,1,0:T(8,128)(2,1)S(1)}, u32[]{:S(2)}, u32[]{:S(2)}) async-start(bf16[32,8,2048]{2,1,0:T(8,128)(2,1)} %get-tuple-element.58), calls=%async_computation.3 | async-start | bytes 2097152 | tf_op jit(solution)/shard_map/all_to_all | solution.py:362
  189.5 22.0 %all-to-all-start.2 = ((bf16[32,8,2048]{2,1,0:T(8,128)(2,1)}), bf16[32,8,2048]{2,1,0:T(8,128)(2,1)S(1)}, u32[]{:S(2)}, u32[]{:S(2)}) async-start(bf16[32,8,2048]{2,1,0:T(8,128)(2,1)} %bitcast.23), calls=%async_computation.2 | async-start | bytes 2097152 | tf_op jit(solution)/shard_map/all_to_all | solution.py:370
  211.5 21.7 %copy-start.1 = (bf16[1024,128]{1,0:T(8,128)(2,1)S(1)}, bf16[1024,128]{1,0:T(8,128)(2,1)}, u32[]{:S(2)}) copy-start(bf16[1024,128]{1,0:T(8,128)(2,1)} %param.16) | copy-start | bytes 786436
Sparse Core Ops, SparseCore 0:
  9.5 73.2 all-gather.1

commit v9 on v8

--- a/solution.py
+++ b/solution.py
@@ -180,11 +180,10 @@
     def _():
         total[...] = jnp.zeros_like(total)
 
-    x = x_ref[0]
-    contract = (((1,), (1,)), ((), ()))
-    gate_h = lax.dot_general(x, wg_ref[0], contract, preferred_element_type=jnp.float32)
-    up_h = lax.dot_general(x, wu_ref[0], contract, preferred_element_type=jnp.float32)
-    hidden = (gate_h / (1.0 + jnp.exp(-gate_h)) * up_h).astype(jnp.bfloat16)
+    x_t = x_ref[0]
+    gate_t = jnp.dot(wg_ref[0], x_t, preferred_element_type=jnp.float32)
+    up_t = jnp.dot(wu_ref[0], x_t, preferred_element_type=jnp.float32)
+    hidden = (gate_t / (1.0 + jnp.exp(-gate_t)) * up_t).T.astype(jnp.bfloat16)
     total[...] += jnp.dot(hidden, wd_ref[0], preferred_element_type=jnp.float32)
 
     @pl.when(f == pl.num_programs(1) - 1)
@@ -205,7 +204,7 @@
         expert_kernel,
         grid=(exp_dev, inner // chunk),
         in_specs=[
-            pl.BlockSpec((1, row_count, width), lambda e, f: (e, 0, 0)),
+            pl.BlockSpec((1, width, row_count), lambda e, f: (e, 0, 0)),
             pl.BlockSpec((1, chunk, width), lambda e, f: (e, f, 0)),
             pl.BlockSpec((1, chunk, width), lambda e, f: (e, f, 0)),
             pl.BlockSpec((1, chunk, width), lambda e, f: (e, f, 0)),
@@ -219,7 +218,7 @@
             transcendentals=exp_dev * row_count * inner,
             bytes_accessed=exp_dev * (3 * width * inner + 2 * row_count * width) * 2,
         ),
-    )(rows, gate_t, up_t, w_down)
+    )(jnp.swapaxes(rows, 1, 2), gate_t, up_t, w_down)
 
 
 def attend_suffix(queries, keys, values, request, position):

time: 241 us -> 245 us (1.017)
  the two profiles are of different devices: /device:TPU:2 before, /device:TPU:0 now
where the time goes in v9:
time: 245 us; the launch traced here: 244 us
  Pallas kernels  54.5 us (22%)
  waiting for transfers between devices  53.3 us (22%)
  blocking collectives  42.9 us (18%)
  local copies, waits for them, and re-layouts  30 us (12%)
  starting transfers between devices  24.6 us (10%)
  between operations  13.7 us (6%)
  matrix products  13.4 us (5%)
  other arithmetic  11.8 us (5%)
    ppermute x3, waiting for transfers between devices, per_device(): lax.ppermute(local_kv, 'req', [(i, (i + 2 * s) % req_count) for i in rang...  42.2 us
    pallas_call x2, Pallas kernels, attend_prefix_local(): pl.pallas_call(prefix_kernel, grid_spec=pltpu.PrefetchScalarGridSpec(num_...  29.9 us
    pallas_call x2, Pallas kernels, expert_ffn(): pl.pallas_call(expert_kernel, grid=(exp_dev, inner // chunk), in_specs=[p...  24.6 us
    all_to_all x1, blocking collectives, per_device(): lax.all_to_all(buffer[:, half * piece:(half + 1) * piece], 'exp', split_a...  21.7 us
    all_to_all x1, blocking collectives, per_device(): lax.all_to_all(expert_out.reshape(EXPERTS, piece, width), 'exp', split_ax...  21.2 us
    all_to_all x1, waiting for transfers between devices, per_device(): lax.all_to_all(attended, 'exp', split_axis=0, concat_axis=1, tiled=True)  8.55 us
    all_to_all x1, starting transfers between devices, per_device(): lax.all_to_all(attended, 'exp', split_axis=0, concat_axis=1, tiled=True)  8 us
    all_to_all x1, starting transfers between devices, per_device(): lax.all_to_all(expert_out.reshape(EXPERTS, piece, width), 'exp', split_ax...  7.2 us
  transfers between devices with their start and end apart: 9, of which 4 were waited for; matrix products, arithmetic and copies ran while one was open for 18% of the time, Pallas kernels for 22%

profile of v9, /device:TPU:0, one launch (start us, length us, event | category | flops | bytes accessed | tf_op | source)
XLA Modules:
  0.0 244.3 jit_solution(17318114032237940709)
XLA Ops:
  6.5 0.7 all-gather.2.cloned.1.call-update
  7.3 0.0 copy-start.13
  7.3 2.4 pad_maximum_fusion.3
  9.6 1.6 collective-permute-start
  11.2 2.7 %collective-permute-start.1 = (bf16[2,4,512,128]{3,2,1,0:T(8,128)(2,1)}, bf16[2,4,512,128]{3,2,1,0:T(8,128)(2,1)S(1)}, u32[]{:S(2)}, u32[]{:S(2)}) collective-permute-start(bf16[2,4,512,128]{3,2,1,0:T(8,128)(2,1)} %pad_maximum_fusion.3), channel_id=1, source_target_pairs={{0,64},{16,80},{32,96},{48,112},{64,0},{80,16},{96,32},{112,48},{1... | collective-permute-start | bytes 3145736 | tf_op jit(solution)/shard_map/ppermute | solution.py:316
  13.9 1.4 collective-permute-start.2
  15.4 0.8 copy.72
  16.2 0.1 eq.120
  16.3 0.1 eq.116
  16.4 0.8 reduce_window_sum.24
  17.2 0.1 convert_reduce_fusion.1
  17.3 18.6 %collective-permute-done = bf16[2,4,512,128]{3,2,1,0:T(8,128)(2,1)S(1)} collective-permute-done((bf16[2,4,512,128]{3,2,1,0:T(8,128)(2,1)}, bf16[2,4,512,128]{3,2,1,0:T(8,128)(2,1)S(1)}, u32[]{:S(2)}, u32[]{:S(2)}) %collective-permute-start) | collective-permute-done | bytes 1048608 | tf_op jit(solution)/shard_map/ppermute | solution.py:316
  35.8 23.6 %collective-permute-done.1 = bf16[2,4,512,128]{3,2,1,0:T(8,128)(2,1)S(1)} collective-permute-done((bf16[2,4,512,128]{3,2,1,0:T(8,128)(2,1)}, bf16[2,4,512,128]{3,2,1,0:T(8,128)(2,1)S(1)}, u32[]{:S(2)}, u32[]{:S(2)}) %collective-permute-start.1) | collective-permute-done | bytes 1048608 | tf_op jit(solution)/shard_map/ppermute | solution.py:316
  59.5 1.8 pad_maximum_fusion.1
  61.3 0.1 select_reduce_fusion.2
  61.4 0.1 fusion.33
  61.6 0.1 copy.67
  61.7 0.6 reshape.357.present_ref
  62.3 2.0 fusion.35
  64.3 0.0 copy-start.10
  64.3 0.0 copy-start.9
  64.3 1.9 copy-done.2
  66.3 0.6 fusion
  66.9 1.1 copy.70
  68.0 1.0 copy.68
  69.0 0.6 reduce-window.6
  69.6 0.2 slice_reduce_fusion
  69.8 0.1 fusion.31
  69.9 0.1 reduce_sum.80
  70.1 0.1 copy.75
  70.1 0.0 copy-done.9
  70.2 2.4 constant_dynamic-update-slice_fusion.1
  72.6 1.4 pad_maximum_fusion
  74.0 2.3 slice_bitcast_fusion.2
  76.3 1.1 broadcast_in_dim.74.grp_ref
  77.4 14.9 %shard_map.145 = (f32[1024,128]{1,0:T(8,128)}, f32[1024,128]{1,0:T(8,128)}, f32[1024,128]{1,0:T(8,128)}) custom-call(s32[32]{0:T(128)} %reshape.357.present_ref, bf16[1024,128]{1,0:T(8,128)(2,1)} %q_ref.3, s32[1024,128]{1,0:T(8,128)} %broadcast_in_dim.74.grp_ref, bf16[4,2048,128]{2,1,0:T(8,128)(2,1)} %get-tuple-element.54.k_ref, ...), custom_call_target="tpu_custom_call" | custom-call | flops 2147483648 | bytes 6029312 | tf_op jit(solution)/shard_map/pallas_call | solution.py:152
  92.2 4.1 %constant_dynamic-update-slice_fusion = bf16[2,4,2048,128]{3,2,1,0:T(8,128)(2,1)} fusion(bf16[2,4,2048,128]{3,2,1,0:T(8,128)(2,1)} %constant_dynamic-update-slice_fusion.1, bf16[2,4,1536,128]{3,2,1,0:T(8,128)(2,1)} %collective-permute-done.4), kind=kLoop, calls=%fused_computation.62 | loop fusion | bytes 6291456 | tf_op jit(solution)/shard_map/concatenate | solution.py:325
  96.3 4.4 %slice_bitcast_fusion = (bf16[4,2048,128]{2,1,0:T(8,128)(2,1)}, bf16[4,2048,128]{2,1,0:T(8,128)(2,1)}) fusion(bf16[2,4,2048,128]{3,2,1,0:T(8,128)(2,1)} %constant_dynamic-update-slice_fusion), kind=kLoop, calls=%fused_computation.11 | loop fusion | bytes 8388608 | tf_op jit(solution)/shard_map/squeeze | solution.py:327
  100.7 0.0 copy-start.12
  100.8 15.0 %shard_map.146 = (f32[1024,128]{1,0:T(8,128)}, f32[1024,128]{1,0:T(8,128)}, f32[1024,128]{1,0:T(8,128)}) custom-call(s32[32]{0:T(128)} %reshape.357.present_ref, bf16[1024,128]{1,0:T(8,128)(2,1)} %q_ref.3, s32[1024,128]{1,0:T(8,128)} %broadcast_in_dim.74.grp_ref, bf16[4,2048,128]{2,1,0:T(8,128)(2,1)} %get-tuple-element.56.k_ref, ...), custom_call_target="tpu_custom_call" | custom-call | flops 2147483648 | bytes 6029312 | tf_op jit(solution)/shard_map/pallas_call | solution.py:152
  115.8 0.0 copy-start.8
  115.8 2.2 fusion.24
  118.0 4.3 %fusion.15 = bf16[1024,128]{1,0:T(8,128)(2,1)} fusion(bf16[1024,128]{1,0:T(8,128)(2,1)S(1)} %copy-done.12, f32[1024,1024]{0,1:T(8,128)} %copy-done.2, f32[1024]{0:T(1024)S(1)} %get-tuple-element.59, f32[1024,128]{1,0:T(8,128)} %get-tuple-element.41, f32[1024,128]{1,0:T(8,128)S(1)} %copy-done.14, f32[1024]{0:T(1024)S(1)} %get-tuple-element.45, ...), kind=kOutput, calls=%fused_computation.20 | convolution fusion | flops 271581184 | bytes 5791744 | tf_op jit(solution)/shard_map/while/body/eval_jaxpr/hqk,khd->qhd/dot_general | solution.py:247
  122.4 8.0 %all-to-all-start = ((bf16[16,64,128]{2,1,0:T(8,128)(2,1)}), bf16[16,64,128]{2,1,0:T(8,128)(2,1)S(1)}, u32[]{:S(2)}, u32[]{:S(2)}) async-start(bf16[16,64,128]{2,1,0:T(8,128)(2,1)} %bitcast.12), calls=%async_computation | async-start | bytes 524288 | tf_op jit(solution)/shard_map/all_to_all | solution.py:338
  130.4 0.2 select_reduce_fusion
  130.6 8.5 %all-to-all-done = bf16[16,64,128]{2,1,0:T(8,128)(2,1)S(1)} async-done(((bf16[16,64,128]{2,1,0:T(8,128)(2,1)}), bf16[16,64,128]{2,1,0:T(8,128)(2,1)S(1)}, u32[]{:S(2)}, u32[]{:S(2)}) %all-to-all-start) | async-done | bytes 262176 | tf_op jit(solution)/shard_map/all_to_all | solution.py:338
  139.1 5.1 %multiply_reduce_fusion = (f32[64]{0:T(128)S(1)}, f32[64,2048]{1,0:T(8,128)S(1)}) fusion(bf16[2048,2048]{1,0:T(8,128)(2,1)} %all-gather.2.cloned.1.call-done, bf16[64,2048]{1,0:T(8,128)(2,1)S(1)} %copy-done.7, bf16[16,64,128]{2,1,0:T(8,128)(2,1)S(1)} %all-to-all-done), kind=kOutput, calls=%fused_computation.29 | convolution fusion | flops 537395136 | bytes 9437440 | tf_op jit(solution)/shard_map/dot_general | solution.py:339
  144.2 0.8 convolution_convert_fusion
  145.0 1.1 fusion.34
  146.1 21.7 %all_to_all.36 = bf16[32,8,2048]{2,1,0:T(8,128)(2,1)S(1)} all-to-all(bf16[32,8,2048]{2,1,0:T(8,128)(2,1)S(1)} %get-tuple-element.57), channel_id=1, replica_groups=mesh['req'=8,'exp'=16] {'exp'}, dimensions={0} | all-to-all | bytes 2097152 | tf_op jit(solution)/shard_map/all_to_all | solution.py:361
  167.8 3.7 %all-to-all-start.3 = ((bf16[32,8,2048]{2,1,0:T(8,128)(2,1)}), bf16[32,8,2048]{2,1,0:T(8,128)(2,1)S(1)}, u32[]{:S(2)}, u32[]{:S(2)}) async-start(bf16[32,8,2048]{2,1,0:T(8,128)(2,1)} %get-tuple-element.58), calls=%async_computation.3 | async-start | bytes 2097152 | tf_op jit(solution)/shard_map/all_to_all | solution.py:361
  171.5 1.1 copy.94
  172.5 2.3 copy.77
  174.8 12.3 %shard_map.147 = bf16[2,128,2048]{2,1,0:T(8,128)(2,1)} custom-call(bf16[2,2048,128]{2,1,0:T(8,128)(2,1)} %bitcast.82, bf16[2,704,2048]{2,1,0:T(8,128)(2,1)} %bitcast.76, bf16[2,704,2048]{2,1,0:T(8,128)(2,1)} %bitcast.78, bf16[2,704,2048]{2,1,0:T(8,128)(2,1)} %wd_ref.3), custom_call_target="tpu_custom_call" | custom-call | flops 2214592512 | bytes 19398656 | tf_op jit(solution)/shard_map/pallas_call | solution.py:203
  187.1 2.4 copy.78
  189.5 7.2 %all-to-all-start.2 = ((bf16[32,8,2048]{2,1,0:T(8,128)(2,1)}), bf16[32,8,2048]{2,1,0:T(8,128)(2,1)}, u32[]{:S(2)}, u32[]{:S(2)}) async-start(bf16[32,8,2048]{2,1,0:T(8,128)(2,1)} %bitcast.24), calls=%async_computation.2 | async-start | bytes 2097152 | tf_op jit(solution)/shard_map/all_to_all | solution.py:369
  196.7 0.1 copy.93
  196.8 1.3 copy.80
  198.1 12.3 %shard_map.148 = bf16[2,128,2048]{2,1,0:T(8,128)(2,1)} custom-call(bf16[2,2048,128]{2,1,0:T(8,128)(2,1)} %bitcast.84, bf16[2,704,2048]{2,1,0:T(8,128)(2,1)} %bitcast.77, bf16[2,704,2048]{2,1,0:T(8,128)(2,1)} %bitcast.79, bf16[2,704,2048]{2,1,0:T(8,128)(2,1)} %wd_ref.3), custom_call_target="tpu_custom_call" | custom-call | flops 2214592512 | bytes 19398656 | tf_op jit(solution)/shard_map/pallas_call | solution.py:203
  210.4 1.3 copy.81
  211.7 1.8 all-to-all-done.2
  213.5 21.2 %all_to_all.37 = bf16[32,8,2048]{2,1,0:T(8,128)(2,1)S(1)} all-to-all(bf16[32,8,2048]{2,1,0:T(8,128)(2,1)S(1)} %bitcast.88), channel_id=1, replica_groups=mesh['req'=8,'exp'=16] {'exp'}, dimensions={0} | all-to-all | bytes 2097152 | tf_op jit(solution)/shard_map/all_to_all | solution.py:369
  234.8 1.4 pad_maximum_fusion.2
  236.2 1.2 fusion.2
  (41 shorter events, 0.1 us)
Async XLA Ops:
  6.5 55.7 %copy-start = (bf16[1024,128]{1,0:T(8,128)(2,1)S(1)}, bf16[1024,128]{1,0:T(8,128)(2,1)}, u32[]{:S(2)}) copy-start(bf16[1024,128]{1,0:T(8,128)(2,1)} %param.16) | copy-start | bytes 786436
  6.5 132.6 %all-gather.2.cloned.1.call-start = ((), (), s32[]{:S(2)}) async-start(), calls=%async_computation.5 | async-start | bytes 8912896 | tf_op jit(solution)/shard_map/all_gather | solution.py:337
  7.3 54.1 %copy-start.13 = (s32[1,8]{1,0:T(1,128)S(1)}, s32[1,8]{1,0:T(1,128)}, u32[]{:S(2)}) copy-start(s32[1,8]{1,0:T(1,128)} %param.20) | copy-start | bytes 100
  7.3 54.1 %copy-start.11 = (s32[1,8]{1,0:T(1,128)S(1)}, s32[1,8]{1,0:T(1,128)}, u32[]{:S(2)}) copy-start(s32[1,8]{1,0:T(1,128)} %param.21) | copy-start | bytes 100
  9.6 26.2 %collective-permute-start = (bf16[2,4,512,128]{3,2,1,0:T(8,128)(2,1)}, bf16[2,4,512,128]{3,2,1,0:T(8,128)(2,1)S(1)}, u32[]{:S(2)}, u32[]{:S(2)}) collective-permute-start(bf16[2,4,512,128]{3,2,1,0:T(8,128)(2,1)} %pad_maximum_fusion.3), channel_id=1, source_target_pairs={{0,32},{16,48},{32,64},{48,80},{64,96},{80,112},{96,0},{112,16},{1... | collective-permute-start | bytes 3145736 | tf_op jit(solution)/shard_map/ppermute | solution.py:316
  11.2 48.3 %collective-permute-start.1 = (bf16[2,4,512,128]{3,2,1,0:T(8,128)(2,1)}, bf16[2,4,512,128]{3,2,1,0:T(8,128)(2,1)S(1)}, u32[]{:S(2)}, u32[]{:S(2)}) collective-permute-start(bf16[2,4,512,128]{3,2,1,0:T(8,128)(2,1)} %pad_maximum_fusion.3), channel_id=1, source_target_pairs={{0,64},{16,80},{32,96},{48,112},{64,0},{80,16},{96,32},{112,48},{1... | collective-permute-start | bytes 3145736 | tf_op jit(solution)/shard_map/ppermute | solution.py:316
  13.9 45.6 %collective-permute-start.2 = (bf16[2,4,512,128]{3,2,1,0:T(8,128)(2,1)}, bf16[2,4,512,128]{3,2,1,0:T(8,128)(2,1)S(1)}, u32[]{:S(2)}, u32[]{:S(2)}) collective-permute-start(bf16[2,4,512,128]{3,2,1,0:T(8,128)(2,1)} %pad_maximum_fusion.3), channel_id=1, source_target_pairs={{0,96},{16,112},{32,0},{48,16},{64,32},{80,48},{96,64},{112,80},{1... | collective-permute-start | bytes 3145736 | tf_op jit(solution)/shard_map/ppermute | solution.py:316
  15.4 54.8 %collective-permute-start.3 = (bf16[2,4,512,128]{3,2,1,0:T(8,128)(2,1)}, bf16[2,4,512,128]{3,2,1,0:T(8,128)(2,1)}, u32[]{:S(2)}, u32[]{:S(2)}) collective-permute-start(bf16[2,4,512,128]{3,2,1,0:T(8,128)(2,1)} %pad_maximum_fusion.3), channel_id=1, source_target_pairs={{0,16},{16,0},{32,48},{48,32},{64,80},{80,64},{96,112},{112,96},{1... | collective-permute-start | bytes 3145736 | tf_op jit(solution)/shard_map/ppermute | solution.py:313
  61.3 30.9 %collective-permute-start.4 = (bf16[2,4,1536,128]{3,2,1,0:T(8,128)(2,1)}, bf16[2,4,1536,128]{3,2,1,0:T(8,128)(2,1)}, u32[]{:S(2)}, u32[]{:S(2)}) collective-permute-start(bf16[2,4,1536,128]{3,2,1,0:T(8,128)(2,1)} %pad_maximum_fusion.1), channel_id=1, source_target_pairs={{0,16},{16,0},{32,48},{48,32},{64,80},{80,64},{96,112},{112,96},{1... | collective-permute-start | bytes 9437192 | tf_op jit(solution)/shard_map/ppermute | solution.py:321
  64.3 2.0 copy-start.2
  64.3 5.8 %copy-start.10 = (bf16[64,4]{0,1:T(4,128)(2,1)S(1)}, bf16[64,4]{0,1:T(4,128)(2,1)}, u32[]{:S(2)}) copy-start(bf16[64,4]{0,1:T(4,128)(2,1)} %param.26) | copy-start | bytes 1540
  64.3 5.8 %copy-start.9 = (bf16[2048]{0:T(1024)(128)(2,1)S(1)}, bf16[2048]{0:T(1024)(128)(2,1)}, u32[]{:S(2)}) copy-start(bf16[2048]{0:T(1024)(128)(2,1)} %param.24) | copy-start | bytes 12292
  100.7 15.1 %copy-start.3 = (f32[1024,1]{1,0:T(8,128)S(1)}, f32[1024,1]{1,0:T(8,128)}, u32[]{:S(2)}) copy-start(f32[1024,1]{1,0:T(8,128)} %copy.70) | copy-start | bytes 12292
  100.7 15.1 %copy-start.4 = (f32[1024,1]{1,0:T(8,128)S(1)}, f32[1024,1]{1,0:T(8,128)}, u32[]{:S(2)}) copy-start(f32[1024,1]{1,0:T(8,128)} %copy.68) | copy-start | bytes 12292
  100.7 15.1 %copy-start.5 = (f32[1024,128]{1,0:T(8,128)S(1)}, f32[1024,128]{1,0:T(8,128)}, u32[]{:S(2)}) copy-start(f32[1024,128]{1,0:T(8,128)} %get-tuple-element.38) | copy-start | bytes 1572868
  100.7 15.1 %copy-start.6 = (f32[1024,128]{1,0:T(8,128)S(1)}, f32[1024,128]{1,0:T(8,128)}, u32[]{:S(2)}) copy-start(f32[1024,128]{1,0:T(8,128)} %get-tuple-element.42) | copy-start | bytes 1572868
  100.7 17.3 %copy-start.12 = (bf16[1024,128]{1,0:T(8,128)(2,1)S(1)}, bf16[1024,128]{1,0:T(8,128)(2,1)}, u32[]{:S(2)}) copy-start(bf16[1024,128]{1,0:T(8,128)(2,1)} %param.17) | copy-start | bytes 786436
  100.7 17.3 %copy-start.14 = (f32[1024,128]{1,0:T(8,128)S(1)}, f32[1024,128]{1,0:T(8,128)}, u32[]{:S(2)}) copy-start(f32[1024,128]{1,0:T(8,128)} %get-tuple-element.36) | copy-start | bytes 1572868
  115.8 14.6 %copy-start.8 = (s32[64,4]{0,1:T(4,128)S(1)}, s32[64,4]{0,1:T(4,128)}, u32[]{:S(2)}) copy-start(s32[64,4]{0,1:T(4,128)} %param.25) | copy-start | bytes 3076
  115.8 23.3 %copy-start.7 = (bf16[64,2048]{1,0:T(8,128)(2,1)S(1)}, bf16[64,2048]{1,0:T(8,128)(2,1)}, u32[]{:S(2)}) copy-start(bf16[64,2048]{1,0:T(8,128)(2,1)} %param.22) | copy-start | bytes 786436
  122.4 16.7 %all-to-all-start = ((bf16[16,64,128]{2,1,0:T(8,128)(2,1)}), bf16[16,64,128]{2,1,0:T(8,128)(2,1)S(1)}, u32[]{:S(2)}, u32[]{:S(2)}) async-start(bf16[16,64,128]{2,1,0:T(8,128)(2,1)} %bitcast.12), calls=%async_computation | async-start | bytes 524288 | tf_op jit(solution)/shard_map/all_to_all | solution.py:338
  167.8 21.7 %all-to-all-start.3 = ((bf16[32,8,2048]{2,1,0:T(8,128)(2,1)}), bf16[32,8,2048]{2,1,0:T(8,128)(2,1)S(1)}, u32[]{:S(2)}, u32[]{:S(2)}) async-start(bf16[32,8,2048]{2,1,0:T(8,128)(2,1)} %get-tuple-element.58), calls=%async_computation.3 | async-start | bytes 2097152 | tf_op jit(solution)/shard_map/all_to_all | solution.py:361
  189.5 24.0 %all-to-all-start.2 = ((bf16[32,8,2048]{2,1,0:T(8,128)(2,1)}), bf16[32,8,2048]{2,1,0:T(8,128)(2,1)}, u32[]{:S(2)}, u32[]{:S(2)}) async-start(bf16[32,8,2048]{2,1,0:T(8,128)(2,1)} %bitcast.24), calls=%async_computation.2 | async-start | bytes 2097152 | tf_op jit(solution)/shard_map/all_to_all | solution.py:369
  213.5 23.9 %copy-start.1 = (bf16[1024,128]{1,0:T(8,128)(2,1)S(1)}, bf16[1024,128]{1,0:T(8,128)(2,1)}, u32[]{:S(2)}) copy-start(bf16[1024,128]{1,0:T(8,128)(2,1)} %param.16) | copy-start | bytes 786436
Sparse Core Ops, SparseCore 0:
  9.5 73.3 all-gather.1

commit v10 on v9

--- a/solution.py
+++ b/solution.py
@@ -354,27 +354,19 @@
         select.T.astype(jnp.bfloat16), normed, preferred_element_type=jnp.float32
     ).astype(jnp.bfloat16).reshape(EXPERTS, capacity, normed.shape[1])
     exp_dev = w_gate.shape[0]
-    halves = 2
-    piece = capacity // halves
-    returned_parts = []
-    for half in range(halves):
-        received = lax.all_to_all(
-            buffer[:, half * piece : (half + 1) * piece], "exp", split_axis=0, concat_axis=0, tiled=True
-        )
-        width = received.shape[2]
-        rows = jnp.swapaxes(received.reshape(exp_count, exp_dev, piece, width), 0, 1)
-        expert_out = expert_ffn(rows.reshape(exp_dev, exp_count * piece, width), w_gate, w_up, w_down)
-        expert_out = jnp.swapaxes(expert_out.reshape(exp_dev, exp_count, piece, width), 0, 1)
-        returned_parts.append(
-            lax.all_to_all(
-                expert_out.reshape(EXPERTS, piece, width),
-                "exp",
-                split_axis=0,
-                concat_axis=0,
-                tiled=True,
-            )
-        )
-    returned = jnp.concatenate(returned_parts, axis=1)
+    received = lax.all_to_all(buffer, "exp", split_axis=0, concat_axis=0, tiled=True)
+    slots = received.shape[1]
+    width = received.shape[2]
+    rows = jnp.swapaxes(received.reshape(exp_count, exp_dev, slots, width), 0, 1)
+    expert_out = expert_ffn(rows.reshape(exp_dev, exp_count * slots, width), w_gate, w_up, w_down)
+    expert_out = jnp.swapaxes(expert_out.reshape(exp_dev, exp_count, slots, width), 0, 1)
+    returned = lax.all_to_all(
+        expert_out.reshape(EXPERTS, slots, width),
+        "exp",
+        split_axis=0,
+        concat_axis=0,
+        tiled=True,
+    )
     gates = expert_gates.astype(jnp.float32).reshape(tok_dev, TOPK, 1)
     weights = jnp.sum(dest_hot.reshape(tok_dev, TOPK, slot_count).astype(jnp.float32) * gates, axis=1)
     mixture = jnp.dot(

time: 245 us -> 238 us (0.971)
  blocking collectives: 42.9 us -> 64.2 us
  starting transfers between devices: 24.6 us -> 13.7 us
  Pallas kernels: 54.5 us -> 45.5 us
  local copies, waits for them, and re-layouts: 30 us -> 24.9 us
    all_to_all x2, blocking collectives: 42.9 us -> 64.2 us  [the longest x1 32.9 us: per_device(): lax.all_to_all(buffer, 'exp', split_axis=0, concat_axis=0, tiled=True)]
    all_to_all x2 -> x0, starting transfers between devices: 10.9 us -> none  [the longest x1 7.2 us: per_device(): lax.all_to_all(expert_out.reshape(EXPERTS, piece, width), 'exp', split_ax...]
    pallas_call x2 -> x1, Pallas kernels: 24.6 us -> 13.9 us  [expert_ffn(): pl.pallas_call(expert_kernel, grid=(exp_dev, inner // chunk), in_specs=[p...]
    reshape x4 -> x2, local copies, waits for them, and re-layouts: 7.27 us -> 4.29 us  [the longest x1 2.52 us: per_device(): rows.reshape(exp_dev, exp_count * slots, width)]
  transfers between devices with their start and end apart: 9 -> 7, of which waited for: 4 -> 3; matrix products, arithmetic and copies ran while one was open for 18% -> 15% of each run, Pallas kernels for 22% -> 13%
where the time goes in v10:
time: 238 us; the launch traced here: 237 us
  blocking collectives  64.2 us (27%)
  waiting for transfers between devices  51.5 us (22%)
  Pallas kernels  45.5 us (19%)
  local copies, waits for them, and re-layouts  24.9 us (10%)
  starting transfers between devices  13.7 us (6%)
  between operations  13.7 us (6%)
  matrix products  13.4 us (6%)
  other arithmetic  10.4 us (4%)
    ppermute x3, waiting for transfers between devices, per_device(): lax.ppermute(local_kv, 'req', [(i, (i + 2 * s) % req_count) for i in rang...  42.2 us
    all_to_all x1, blocking collectives, per_device(): lax.all_to_all(buffer, 'exp', split_axis=0, concat_axis=0, tiled=True)  32.9 us
    pallas_call x2, Pallas kernels, attend_prefix_local(): pl.pallas_call(prefix_kernel, grid_spec=pltpu.PrefetchScalarGridSpec(num_...  31.7 us
    all_to_all x1, blocking collectives, per_device(): lax.all_to_all(expert_out.reshape(EXPERTS, slots, width), 'exp', split_ax...  31.3 us
    pallas_call x1, Pallas kernels, expert_ffn(): pl.pallas_call(expert_kernel, grid=(exp_dev, inner // chunk), in_specs=[p...  13.9 us
    all_to_all x1, waiting for transfers between devices, per_device(): lax.all_to_all(attended, 'exp', split_axis=0, concat_axis=1, tiled=True)  8.6 us
    all_to_all x1, starting transfers between devices, per_device(): lax.all_to_all(attended, 'exp', split_axis=0, concat_axis=1, tiled=True)  7.99 us
    squeeze x2, local copies, waits for them, and re-layouts, per_device(): part = attend_prefix_local(queries, tok_group, chunk[0], chunk[1])  6.79 us
  transfers between devices with their start and end apart: 7, of which 3 were waited for; matrix products, arithmetic and copies ran while one was open for 15% of the time, Pallas kernels for 13%

profile of v10, /device:TPU:0, one launch (start us, length us, event | category | flops | bytes accessed | tf_op | source)
XLA Modules:
  0.0 237.4 jit_solution(14090300851418701165)
XLA Ops:
  6.5 0.7 all-gather.2.cloned.1.call-update
  7.3 0.0 copy-start.13
  7.3 2.4 pad_maximum_fusion.2
  9.6 1.6 collective-permute-start
  11.2 2.7 %collective-permute-start.1 = (bf16[2,4,512,128]{3,2,1,0:T(8,128)(2,1)}, bf16[2,4,512,128]{3,2,1,0:T(8,128)(2,1)S(1)}, u32[]{:S(2)}, u32[]{:S(2)}) collective-permute-start(bf16[2,4,512,128]{3,2,1,0:T(8,128)(2,1)} %pad_maximum_fusion.2), channel_id=1, source_target_pairs={{0,64},{16,80},{32,96},{48,112},{64,0},{80,16},{96,32},{112,48},{1... | collective-permute-start | bytes 3145736 | tf_op jit(solution)/shard_map/ppermute | solution.py:316
  13.9 1.4 collective-permute-start.2
  15.4 0.0 collective-permute-start.3
  15.4 0.8 copy.63
  16.2 0.1 eq.120
  16.3 0.1 eq.116
  16.4 0.8 reduce_window_sum.24
  17.2 0.1 convert_reduce_fusion.1
  17.3 18.6 %collective-permute-done = bf16[2,4,512,128]{3,2,1,0:T(8,128)(2,1)S(1)} collective-permute-done((bf16[2,4,512,128]{3,2,1,0:T(8,128)(2,1)}, bf16[2,4,512,128]{3,2,1,0:T(8,128)(2,1)S(1)}, u32[]{:S(2)}, u32[]{:S(2)}) %collective-permute-start) | collective-permute-done | bytes 1048608 | tf_op jit(solution)/shard_map/ppermute | solution.py:316
  35.8 23.6 %collective-permute-done.1 = bf16[2,4,512,128]{3,2,1,0:T(8,128)(2,1)S(1)} collective-permute-done((bf16[2,4,512,128]{3,2,1,0:T(8,128)(2,1)}, bf16[2,4,512,128]{3,2,1,0:T(8,128)(2,1)S(1)}, u32[]{:S(2)}, u32[]{:S(2)}) %collective-permute-start.1) | collective-permute-done | bytes 1048608 | tf_op jit(solution)/shard_map/ppermute | solution.py:316
  59.5 0.0 collective-permute-done.2
  59.5 1.8 pad_maximum_fusion.1
  61.3 0.0 collective-permute-start.4
  61.3 0.1 select_reduce_fusion.2
  61.4 0.1 fusion.33
  61.6 0.1 copy.58
  61.7 0.6 reshape.341.present_ref
  62.3 0.0 copy-done
  62.3 2.0 fusion.34
  64.3 0.0 copy-start.2
  64.3 0.0 copy-start.10
  64.3 0.0 copy-start.9
  64.3 1.9 copy-done.2
  66.3 0.6 fusion
  66.9 1.1 copy.61
  68.0 1.0 copy.59
  69.0 0.6 reduce-window.6
  69.6 0.2 slice_reduce_fusion
  69.8 0.1 fusion.31
  69.9 0.1 reduce_sum.80
  70.1 0.1 copy.66
  70.1 0.0 copy-done.9
  70.2 0.0 collective-permute-done.3
  70.2 2.4 %constant_dynamic-update-slice_fusion.1 = bf16[2,4,2048,128]{3,2,1,0:T(8,128)(2,1)} fusion(bf16[2,4,512,128]{3,2,1,0:T(8,128)(2,1)} %collective-permute-done.3), kind=kLoop, calls=%fused_computation.60 | loop fusion | bytes 2097152
  72.6 1.4 pad_maximum_fusion
  74.0 2.3 slice_bitcast_fusion.2
  76.3 1.1 broadcast_in_dim.74.grp_ref
  77.4 15.7 %shard_map.145 = (f32[1024,128]{1,0:T(8,128)}, f32[1024,128]{1,0:T(8,128)}, f32[1024,128]{1,0:T(8,128)}) custom-call(s32[32]{0:T(128)} %reshape.341.present_ref, bf16[1024,128]{1,0:T(8,128)(2,1)} %q_ref.3, s32[1024,128]{1,0:T(8,128)} %broadcast_in_dim.74.grp_ref, bf16[4,2048,128]{2,1,0:T(8,128)(2,1)} %get-tuple-element.54.k_ref, ...), custom_call_target="tpu_custom_call" | custom-call | flops 2147483648 | bytes 6029312 | tf_op jit(solution)/shard_map/pallas_call | solution.py:152
  93.1 0.0 collective-permute-done.4
  93.1 4.1 %constant_dynamic-update-slice_fusion = bf16[2,4,2048,128]{3,2,1,0:T(8,128)(2,1)} fusion(bf16[2,4,2048,128]{3,2,1,0:T(8,128)(2,1)} %constant_dynamic-update-slice_fusion.1, bf16[2,4,1536,128]{3,2,1,0:T(8,128)(2,1)} %collective-permute-done.4), kind=kLoop, calls=%fused_computation.59 | loop fusion | bytes 6291456 | tf_op jit(solution)/shard_map/concatenate | solution.py:325
  97.2 4.4 %slice_bitcast_fusion = (bf16[4,2048,128]{2,1,0:T(8,128)(2,1)}, bf16[4,2048,128]{2,1,0:T(8,128)(2,1)}) fusion(bf16[2,4,2048,128]{3,2,1,0:T(8,128)(2,1)} %constant_dynamic-update-slice_fusion), kind=kLoop, calls=%fused_computation.11 | loop fusion | bytes 8388608 | tf_op jit(solution)/shard_map/squeeze | solution.py:327
  101.6 0.0 copy-start.12
  101.6 0.0 copy-start.14
  101.6 15.9 %shard_map.146 = (f32[1024,128]{1,0:T(8,128)}, f32[1024,128]{1,0:T(8,128)}, f32[1024,128]{1,0:T(8,128)}) custom-call(s32[32]{0:T(128)} %reshape.341.present_ref, bf16[1024,128]{1,0:T(8,128)(2,1)} %q_ref.3, s32[1024,128]{1,0:T(8,128)} %broadcast_in_dim.74.grp_ref, bf16[4,2048,128]{2,1,0:T(8,128)(2,1)} %get-tuple-element.56.k_ref, ...), custom_call_target="tpu_custom_call" | custom-call | flops 2147483648 | bytes 6029312 | tf_op jit(solution)/shard_map/pallas_call | solution.py:152
  117.6 0.0 copy-start.8
  117.6 0.0 copy-start.7
  117.6 2.2 fusion.24
  119.8 4.3 %fusion.15 = bf16[1024,128]{1,0:T(8,128)(2,1)} fusion(bf16[1024,128]{1,0:T(8,128)(2,1)S(1)} %copy-done.12, f32[1024,1024]{0,1:T(8,128)} %copy-done.2, f32[1024]{0:T(1024)S(1)} %get-tuple-element.57, f32[1024,128]{1,0:T(8,128)} %get-tuple-element.41, f32[1024,128]{1,0:T(8,128)S(1)} %copy-done.14, f32[1024]{0:T(1024)S(1)} %get-tuple-element.45, ...), kind=kOutput, calls=%fused_computation.19 | convolution fusion | flops 271581184 | bytes 5791744 | tf_op jit(solution)/shard_map/while/body/eval_jaxpr/hqk,khd->qhd/dot_general | solution.py:247
  124.2 8.0 %all-to-all-start = ((bf16[16,64,128]{2,1,0:T(8,128)(2,1)}), bf16[16,64,128]{2,1,0:T(8,128)(2,1)S(1)}, u32[]{:S(2)}, u32[]{:S(2)}) async-start(bf16[16,64,128]{2,1,0:T(8,128)(2,1)} %bitcast.12), calls=%async_computation | async-start | bytes 524288 | tf_op jit(solution)/shard_map/all_to_all | solution.py:338
  132.2 0.2 select_reduce_fusion
  132.4 8.6 %all-to-all-done = bf16[16,64,128]{2,1,0:T(8,128)(2,1)S(1)} async-done(((bf16[16,64,128]{2,1,0:T(8,128)(2,1)}), bf16[16,64,128]{2,1,0:T(8,128)(2,1)S(1)}, u32[]{:S(2)}, u32[]{:S(2)}) %all-to-all-start) | async-done | bytes 262176 | tf_op jit(solution)/shard_map/all_to_all | solution.py:338
  141.0 5.1 %multiply_reduce_fusion = (f32[64]{0:T(128)S(1)}, f32[64,2048]{1,0:T(8,128)S(1)}) fusion(bf16[2048,2048]{1,0:T(8,128)(2,1)} %all-gather.2.cloned.1.call-done, bf16[64,2048]{1,0:T(8,128)(2,1)S(1)} %copy-done.7, bf16[16,64,128]{2,1,0:T(8,128)(2,1)S(1)} %all-to-all-done), kind=kOutput, calls=%fused_computation.26 | convolution fusion | flops 537395136 | bytes 9437440 | tf_op jit(solution)/shard_map/dot_general | solution.py:339
  146.0 0.8 convolution_convert_fusion
  146.8 32.9 %all_to_all.26 = bf16[32,16,2048]{2,1,0:T(8,128)(2,1)S(1)} all-to-all(bf16[32,16,2048]{2,1,0:T(8,128)(2,1)S(1)} %bitcast.64), channel_id=1, replica_groups=mesh['req'=8,'exp'=16] {'exp'}, dimensions={0} | all-to-all | bytes 4194304 | tf_op jit(solution)/shard_map/all_to_all | solution.py:357
  179.7 0.1 copy.67
  179.9 2.5 %copy.68 = bf16[2,256,2048]{1,2,0:T(8,128)(2,1)} copy(bf16[2,256,2048]{2,1,0:T(8,128)(2,1)S(1)} %bitcast.66) | data formatting | bytes 4194304 | tf_op jit(solution)/shard_map/reshape | solution.py:361
  182.4 13.9 %shard_map.147 = bf16[2,256,2048]{2,1,0:T(8,128)(2,1)} custom-call(bf16[2,2048,256]{2,1,0:T(8,128)(2,1)} %bitcast.68, bf16[2,704,2048]{2,1,0:T(8,128)(2,1)} %bitcast.70, bf16[2,704,2048]{2,1,0:T(8,128)(2,1)} %bitcast.71, bf16[2,704,2048]{2,1,0:T(8,128)(2,1)} %wd_ref.1), custom_call_target="tpu_custom_call" | custom-call | flops 4429185024 | bytes 21495808 | tf_op jit(solution)/shard_map/pallas_call | solution.py:203
  196.2 1.8 copy.69
  198.0 31.3 %all_to_all.27 = bf16[32,16,2048]{2,1,0:T(8,128)(2,1)S(1)} all-to-all(bf16[32,16,2048]{2,1,0:T(8,128)(2,1)S(1)} %bitcast.67), channel_id=1, replica_groups=mesh['req'=8,'exp'=16] {'exp'}, dimensions={0} | all-to-all | bytes 4194304 | tf_op jit(solution)/shard_map/all_to_all | solution.py:363
  229.3 1.2 fusion.2
  (31 shorter events, 0.1 us)
Async XLA Ops:
  6.5 55.7 %copy-start = (bf16[1024,128]{1,0:T(8,128)(2,1)S(1)}, bf16[1024,128]{1,0:T(8,128)(2,1)}, u32[]{:S(2)}) copy-start(bf16[1024,128]{1,0:T(8,128)(2,1)} %param.16) | copy-start | bytes 786436
  6.5 134.4 %all-gather.2.cloned.1.call-start = ((), (), s32[]{:S(2)}) async-start(), calls=%async_computation.3 | async-start | bytes 8912896 | tf_op jit(solution)/shard_map/all_gather | solution.py:337
  7.3 54.1 %copy-start.13 = (s32[1,8]{1,0:T(1,128)S(1)}, s32[1,8]{1,0:T(1,128)}, u32[]{:S(2)}) copy-start(s32[1,8]{1,0:T(1,128)} %param.20) | copy-start | bytes 100
  7.3 54.1 %copy-start.11 = (s32[1,8]{1,0:T(1,128)S(1)}, s32[1,8]{1,0:T(1,128)}, u32[]{:S(2)}) copy-start(s32[1,8]{1,0:T(1,128)} %param.21) | copy-start | bytes 100
  9.6 26.2 %collective-permute-start = (bf16[2,4,512,128]{3,2,1,0:T(8,128)(2,1)}, bf16[2,4,512,128]{3,2,1,0:T(8,128)(2,1)S(1)}, u32[]{:S(2)}, u32[]{:S(2)}) collective-permute-start(bf16[2,4,512,128]{3,2,1,0:T(8,128)(2,1)} %pad_maximum_fusion.2), channel_id=1, source_target_pairs={{0,32},{16,48},{32,64},{48,80},{64,96},{80,112},{96,0},{112,16},{1... | collective-permute-start | bytes 3145736 | tf_op jit(solution)/shard_map/ppermute | solution.py:316
  11.2 48.3 %collective-permute-start.1 = (bf16[2,4,512,128]{3,2,1,0:T(8,128)(2,1)}, bf16[2,4,512,128]{3,2,1,0:T(8,128)(2,1)S(1)}, u32[]{:S(2)}, u32[]{:S(2)}) collective-permute-start(bf16[2,4,512,128]{3,2,1,0:T(8,128)(2,1)} %pad_maximum_fusion.2), channel_id=1, source_target_pairs={{0,64},{16,80},{32,96},{48,112},{64,0},{80,16},{96,32},{112,48},{1... | collective-permute-start | bytes 3145736 | tf_op jit(solution)/shard_map/ppermute | solution.py:316
  13.9 45.6 %collective-permute-start.2 = (bf16[2,4,512,128]{3,2,1,0:T(8,128)(2,1)}, bf16[2,4,512,128]{3,2,1,0:T(8,128)(2,1)S(1)}, u32[]{:S(2)}, u32[]{:S(2)}) collective-permute-start(bf16[2,4,512,128]{3,2,1,0:T(8,128)(2,1)} %pad_maximum_fusion.2), channel_id=1, source_target_pairs={{0,96},{16,112},{32,0},{48,16},{64,32},{80,48},{96,64},{112,80},{1... | collective-permute-start | bytes 3145736 | tf_op jit(solution)/shard_map/ppermute | solution.py:316
  15.4 54.8 %collective-permute-start.3 = (bf16[2,4,512,128]{3,2,1,0:T(8,128)(2,1)}, bf16[2,4,512,128]{3,2,1,0:T(8,128)(2,1)}, u32[]{:S(2)}, u32[]{:S(2)}) collective-permute-start(bf16[2,4,512,128]{3,2,1,0:T(8,128)(2,1)} %pad_maximum_fusion.2), channel_id=1, source_target_pairs={{0,16},{16,0},{32,48},{48,32},{64,80},{80,64},{96,112},{112,96},{1... | collective-permute-start | bytes 3145736 | tf_op jit(solution)/shard_map/ppermute | solution.py:313
  61.3 31.8 %collective-permute-start.4 = (bf16[2,4,1536,128]{3,2,1,0:T(8,128)(2,1)}, bf16[2,4,1536,128]{3,2,1,0:T(8,128)(2,1)}, u32[]{:S(2)}, u32[]{:S(2)}) collective-permute-start(bf16[2,4,1536,128]{3,2,1,0:T(8,128)(2,1)} %pad_maximum_fusion.1), channel_id=1, source_target_pairs={{0,16},{16,0},{32,48},{48,32},{64,80},{80,64},{96,112},{112,96},{1... | collective-permute-start | bytes 9437192 | tf_op jit(solution)/shard_map/ppermute | solution.py:321
  64.3 2.0 copy-start.2
  64.3 5.8 %copy-start.10 = (bf16[64,4]{0,1:T(4,128)(2,1)S(1)}, bf16[64,4]{0,1:T(4,128)(2,1)}, u32[]{:S(2)}) copy-start(bf16[64,4]{0,1:T(4,128)(2,1)} %param.26) | copy-start | bytes 1540
  64.3 5.8 %copy-start.9 = (bf16[2048]{0:T(1024)(128)(2,1)S(1)}, bf16[2048]{0:T(1024)(128)(2,1)}, u32[]{:S(2)}) copy-start(bf16[2048]{0:T(1024)(128)(2,1)} %param.24) | copy-start | bytes 12292
  101.6 16.0 %copy-start.3 = (f32[1024,1]{1,0:T(8,128)S(1)}, f32[1024,1]{1,0:T(8,128)}, u32[]{:S(2)}) copy-start(f32[1024,1]{1,0:T(8,128)} %copy.61) | copy-start | bytes 12292
  101.6 16.0 %copy-start.4 = (f32[1024,1]{1,0:T(8,128)S(1)}, f32[1024,1]{1,0:T(8,128)}, u32[]{:S(2)}) copy-start(f32[1024,1]{1,0:T(8,128)} %copy.59) | copy-start | bytes 12292
  101.6 16.0 %copy-start.5 = (f32[1024,128]{1,0:T(8,128)S(1)}, f32[1024,128]{1,0:T(8,128)}, u32[]{:S(2)}) copy-start(f32[1024,128]{1,0:T(8,128)} %get-tuple-element.38) | copy-start | bytes 1572868
  101.6 16.0 %copy-start.6 = (f32[1024,128]{1,0:T(8,128)S(1)}, f32[1024,128]{1,0:T(8,128)}, u32[]{:S(2)}) copy-start(f32[1024,128]{1,0:T(8,128)} %get-tuple-element.42) | copy-start | bytes 1572868
  101.6 18.2 %copy-start.12 = (bf16[1024,128]{1,0:T(8,128)(2,1)S(1)}, bf16[1024,128]{1,0:T(8,128)(2,1)}, u32[]{:S(2)}) copy-start(bf16[1024,128]{1,0:T(8,128)(2,1)} %param.17) | copy-start | bytes 786436
  101.6 18.2 %copy-start.14 = (f32[1024,128]{1,0:T(8,128)S(1)}, f32[1024,128]{1,0:T(8,128)}, u32[]{:S(2)}) copy-start(f32[1024,128]{1,0:T(8,128)} %get-tuple-element.36) | copy-start | bytes 1572868
  117.6 14.6 %copy-start.8 = (s32[64,4]{0,1:T(4,128)S(1)}, s32[64,4]{0,1:T(4,128)}, u32[]{:S(2)}) copy-start(s32[64,4]{0,1:T(4,128)} %param.25) | copy-start | bytes 3076
  117.6 23.3 %copy-start.7 = (bf16[64,2048]{1,0:T(8,128)(2,1)S(1)}, bf16[64,2048]{1,0:T(8,128)(2,1)}, u32[]{:S(2)}) copy-start(bf16[64,2048]{1,0:T(8,128)(2,1)} %param.22) | copy-start | bytes 786436
  124.2 16.8 %all-to-all-start = ((bf16[16,64,128]{2,1,0:T(8,128)(2,1)}), bf16[16,64,128]{2,1,0:T(8,128)(2,1)S(1)}, u32[]{:S(2)}, u32[]{:S(2)}) async-start(bf16[16,64,128]{2,1,0:T(8,128)(2,1)} %bitcast.12), calls=%async_computation | async-start | bytes 524288 | tf_op jit(solution)/shard_map/all_to_all | solution.py:338
  196.2 34.3 %copy-start.1 = (bf16[1024,128]{1,0:T(8,128)(2,1)S(1)}, bf16[1024,128]{1,0:T(8,128)(2,1)}, u32[]{:S(2)}) copy-start(bf16[1024,128]{1,0:T(8,128)(2,1)} %param.16) | copy-start | bytes 786436
Sparse Core Ops, SparseCore 0:
  9.5 73.3 all-gather.1

commit v11 on v10

--- a/solution.py
+++ b/solution.py
@@ -93,83 +93,60 @@
 KEY_BLOCK = 2048
 
 
-def prefix_kernel(present_ref, q_ref, grp_ref, k_ref, v_ref, acc_ref, m_ref, l_ref):
-    g = pl.program_id(0)
-    kb = pl.program_id(1)
+def prefix_kernel(block_group_ref, q_ref, k_ref, v_ref, acc_ref, m_ref, l_ref):
     scaling = 1.0 / math.sqrt(HEAD)
-
-    @pl.when((g == 0) & (kb == 0))
-    def _():
-        acc_ref[...] = jnp.zeros_like(acc_ref)
-        m_ref[...] = jnp.full_like(m_ref, NEG)
-        l_ref[...] = jnp.zeros_like(l_ref)
-
-    k = k_ref[0]
-    v = v_ref[0]
-    block_count = q_ref.shape[0] // QUERY_BLOCK
-
-    def body(qb, carry):
-        @pl.when(present_ref[qb * G + g] > 0)
-        def _():
-            rows = pl.ds(pl.multiple_of(qb * QUERY_BLOCK, QUERY_BLOCK), QUERY_BLOCK)
-            s = lax.dot_general(
-                q_ref[rows, :], k, (((1,), (1,)), ((), ())), preferred_element_type=jnp.float32
-            ) * scaling
-            mask = grp_ref[rows, :] == g
-            m_prev = m_ref[rows, :]
-            m_cand = jnp.maximum(m_prev, jnp.max(s, axis=1, keepdims=True))
-            p = jnp.exp(s - m_cand[:, :1])
-            alpha = jnp.exp(m_prev - m_cand)
-            l_ref[rows, :] = jnp.where(
-                mask, alpha * l_ref[rows, :] + jnp.sum(p, axis=1, keepdims=True), l_ref[rows, :]
-            )
-            acc_ref[rows, :] = jnp.where(
-                mask,
-                alpha * acc_ref[rows, :]
-                + jnp.dot(p.astype(jnp.bfloat16), v, preferred_element_type=jnp.float32),
-                acc_ref[rows, :],
-            )
-            m_ref[rows, :] = jnp.where(mask, m_cand, m_prev)
-
-        return carry
-
-    lax.fori_loop(0, block_count, body, 0)
-
-
-def attend_prefix_local(query_rows, query_group, prefix_k, prefix_v):
-    row_count = query_rows.shape[0]
+    s = lax.dot_general(
+        q_ref[...], k_ref[0], (((1,), (1,)), ((), ())), preferred_element_type=jnp.float32
+    ) * scaling
+    m = jnp.max(s, axis=1, keepdims=True)
+    p = jnp.exp(s - m)
+    acc_ref[...] = jnp.dot(p.astype(jnp.bfloat16), v_ref[0], preferred_element_type=jnp.float32)
+    m_ref[...] = jnp.broadcast_to(m, m_ref.shape)
+    l_ref[...] = jnp.broadcast_to(jnp.sum(p, axis=1, keepdims=True), l_ref.shape)
+
+
+def group_layout(query_group):
+    row_count = query_group.shape[0]
+    block_count = row_count // QUERY_BLOCK + G - 1
+    member = query_group[:, None] == jnp.arange(G, dtype=jnp.int32)[None, :]
+    counts = jnp.sum(member.astype(jnp.int32), axis=0)
+    blocks = (counts + QUERY_BLOCK - 1) // QUERY_BLOCK
+    first_block = jnp.cumsum(blocks) - blocks
+    rank = jnp.sum(jnp.where(member, jnp.cumsum(member.astype(jnp.int32), axis=0) - 1, 0), axis=1)
+    padded_index = jnp.sum(jnp.where(member, first_block[None, :], 0), axis=1) * QUERY_BLOCK + rank
+    source = jnp.zeros((block_count * QUERY_BLOCK,), jnp.int32).at[padded_index].set(
+        jnp.arange(row_count, dtype=jnp.int32)
+    )
+    block_group = jnp.sum(
+        (jnp.arange(block_count, dtype=jnp.int32)[:, None] >= first_block[None, 1:]).astype(jnp.int32),
+        axis=1,
+    )
+    return padded_index, source, block_group
+
+
+def attend_prefix_grouped(padded_rows, block_group, prefix_k, prefix_v):
+    padded_count = padded_rows.shape[0]
     span = prefix_k.shape[1]
-    block_count = row_count // QUERY_BLOCK
-    present = jnp.any(
-        query_group.reshape(block_count, QUERY_BLOCK, 1)
-        == jnp.arange(G, dtype=jnp.int32)[None, None, :],
-        axis=1,
-    ).astype(jnp.int32).reshape(-1)
-    grp = jnp.broadcast_to(query_group[:, None], (row_count, HEAD))
-    full = lambda g, kb, pr: (0, 0)
-    kv_spec = pl.BlockSpec((1, KEY_BLOCK, HEAD), lambda g, kb, pr: (g, kb, 0))
-    out_shape = jax.ShapeDtypeStruct((row_count, HEAD), jnp.float32)
+    block_count = padded_count // QUERY_BLOCK
+    row_spec = pl.BlockSpec((QUERY_BLOCK, HEAD), lambda b, bg: (b, 0))
+    kv_spec = pl.BlockSpec((1, span, HEAD), lambda b, bg: (bg[b], 0, 0))
+    out_shape = jax.ShapeDtypeStruct((padded_count, HEAD), jnp.float32)
     acc, maxima, totals = pl.pallas_call(
         prefix_kernel,
         grid_spec=pltpu.PrefetchScalarGridSpec(
             num_scalar_prefetch=1,
-            grid=(G, span // KEY_BLOCK),
-            in_specs=[
-                pl.BlockSpec((row_count, HEAD), full),
-                pl.BlockSpec((row_count, HEAD), full),
-                kv_spec,
-                kv_spec,
-            ],
-            out_specs=[pl.BlockSpec((row_count, HEAD), full)] * 3,
+            grid=(block_count,),
+            in_specs=[row_spec, kv_spec, kv_spec],
+            out_specs=[row_spec] * 3,
         ),
         out_shape=[out_shape] * 3,
-        compiler_params=pltpu.CompilerParams(dimension_semantics=("arbitrary", "arbitrary")),
+        compiler_params=pltpu.CompilerParams(dimension_semantics=("arbitrary",)),
         cost_estimate=pl.CostEstimate(
-            flops=4 * row_count * span * HEAD * 2,
-            transcendentals=row_count * span * 2,
-            bytes_accessed=2 * G * span * HEAD * 2 + row_count * HEAD * 14,
+            flops=4 * padded_count * span * HEAD,
+            transcendentals=padded_count * span,
+            bytes_accessed=2 * G * span * HEAD * 2 + padded_count * HEAD * 14,
         ),
-    )(present, query_rows, grp, prefix_k, prefix_v)
+    )(block_group, padded_rows, prefix_k, prefix_v)
     return (acc, maxima[:, :1], totals[:, :1])
 
 
@@ -319,13 +296,16 @@
         axis=2,
     )
     forwarded_kv = lax.ppermute(ring_kv, "req", partner)
+    padded_index, source, block_group = group_layout(tok_group)
+    padded_rows = jnp.take(queries, source, axis=0)
     prefix_part = None
     for chunk in (
         jnp.concatenate([local_kv, ring_kv], axis=2),
         jnp.concatenate([partner_kv, forwarded_kv], axis=2),
     ):
-        part = attend_prefix_local(queries, tok_group, chunk[0], chunk[1])
+        part = attend_prefix_grouped(padded_rows, block_group, chunk[0], chunk[1])
         prefix_part = part if prefix_part is None else combine(prefix_part, part)
+    prefix_part = tuple(jnp.take(piece, padded_index, axis=0) for piece in prefix_part)
     suffix_part = attend_suffix(queries, keys, values, request, position)
     weighted, maxima, totals = combine(prefix_part, suffix_part)
     attended = (

time: 238 us -> 233 us (0.979); the launches traced: 237 us -> 229 us
  waiting for transfers between devices: 51.5 us -> 36.2 us
  local copies, waits for them, and re-layouts: 24.9 us -> 39.1 us
  Pallas kernels: 45.5 us -> 38.3 us
  other arithmetic: 10.4 us -> 15.8 us
  blocking collectives: 64.2 us -> 60 us
    gather x0 -> x4, local copies, waits for them, and re-layouts: none -> 19.1 us  [the longest x3 15.1 us: per_device(): jnp.take(piece, padded_index, axis=0)]
    ppermute x3, waiting for transfers between devices: 42.2 us -> 27.2 us  [per_device(): lax.ppermute(local_kv, 'req', [(i, (i + 2 * s) % req_count) for i in rang...]
    pallas_call x2, Pallas kernels: 31.7 us -> 24.5 us  [attend_prefix_grouped(): pl.pallas_call(prefix_kernel, grid_spec=pltpu.PrefetchScalarGridSpec(num_...]
    scatter x0 -> x1, local copies, waits for them, and re-layouts: none -> 4.32 us  [group_layout(): jnp.zeros((block_count * QUERY_BLOCK,), jnp.int32).at[padded_index]]
    add x0 -> x3, other arithmetic: none -> 2.7 us  [the longest x2 2.26 us: combine(): totals_a * factor_a + totals_b * factor_b]
    unnamed x32 -> x30, local copies, waits for them, and re-layouts: 5.19 us -> 3.45 us
  transfers between devices with their start and end apart: 7 -> 7, of which waited for: 3 -> 3; matrix products, arithmetic and copies ran while one was open for 15% -> 24% of each run, Pallas kernels for 13% -> 11%
where the time goes in v11:
time: 233 us; the launch traced here: 229 us
  blocking collectives  60 us (26%)
  local copies, waits for them, and re-layouts  39.1 us (17%)
  Pallas kernels  38.3 us (16%)
  waiting for transfers between devices  36.2 us (16%)
  other arithmetic  15.8 us (7%)
  starting transfers between devices  13.8 us (6%)
  between operations  13.8 us (6%)
  matrix products  12.2 us (5%)
    all_to_all x1, blocking collectives, per_device(): lax.all_to_all(buffer, 'exp', split_axis=0, concat_axis=0, tiled=True)  30.6 us
    all_to_all x1, blocking collectives, per_device(): lax.all_to_all(expert_out.reshape(EXPERTS, slots, width), 'exp', split_ax...  29.4 us
    ppermute x3, waiting for transfers between devices, per_device(): lax.ppermute(local_kv, 'req', [(i, (i + 2 * s) % req_count) for i in rang...  27.2 us
    pallas_call x2, Pallas kernels, attend_prefix_grouped(): pl.pallas_call(prefix_kernel, grid_spec=pltpu.PrefetchScalarGridSpec(num_...  24.5 us
    gather x3, local copies, waits for them, and re-layouts, per_device(): jnp.take(piece, padded_index, axis=0)  15.1 us
    pallas_call x1, Pallas kernels, expert_ffn(): pl.pallas_call(expert_kernel, grid=(exp_dev, inner // chunk), in_specs=[p...  13.9 us
    all_to_all x1, waiting for transfers between devices, per_device(): lax.all_to_all(attended, 'exp', split_axis=0, concat_axis=1, tiled=True)  8.33 us
    all_to_all x1, starting transfers between devices, per_device(): lax.all_to_all(attended, 'exp', split_axis=0, concat_axis=1, tiled=True)  8.08 us
  transfers between devices with their start and end apart: 7, of which 3 were waited for; matrix products, arithmetic and copies ran while one was open for 24% of the time, Pallas kernels for 11%

profile of v11, /device:TPU:0, one launch (start us, length us, event | category | flops | bytes accessed | tf_op | source)
XLA Modules:
  0.0 229.3 jit_solution(14166544599752568661)
XLA Ops:
  6.5 0.7 all-gather.2.cloned.1.call-update
  7.3 2.3 %pad_maximum_fusion.2 = bf16[2,4,512,128]{3,2,1,0:T(8,128)(2,1)} fusion(bf16[1,4,512,128]{3,2,1,0:T(8,128)(2,1)} %bitcast.132, bf16[1,4,512,128]{3,2,1,0:T(8,128)(2,1)} %bitcast.134), kind=kLoop, calls=%fused_computation.27 | loop fusion | flops 524288 | bytes 2097152 | tf_op jit(solution)/shard_map/stack | solution.py:288
  9.6 1.6 collective-permute-start
  11.1 2.7 %collective-permute-start.1 = (bf16[2,4,512,128]{3,2,1,0:T(8,128)(2,1)}, bf16[2,4,512,128]{3,2,1,0:T(8,128)(2,1)S(1)}, u32[]{:S(2)}, u32[]{:S(2)}) collective-permute-start(bf16[2,4,512,128]{3,2,1,0:T(8,128)(2,1)} %pad_maximum_fusion.2), channel_id=1, source_target_pairs={{0,64},{16,80},{32,96},{48,112},{64,0},{80,16},{96,32},{112,48},{1... | collective-permute-start | bytes 3145736 | tf_op jit(solution)/shard_map/ppermute | solution.py:293
  13.9 1.4 collective-permute-start.2
  15.3 0.8 copy.49
  16.1 0.1 eq.124
  16.2 0.1 eq.120
  16.3 0.8 reduce_window_sum.44
  17.1 0.1 convert_reduce_fusion.1
  17.2 0.7 subtract_bitcast_fusion
  17.9 0.7 select_reduce_fusion.2
  18.6 0.1 convert_reduce_fusion.2
  18.8 0.2 reduce-window.20
  18.9 1.1 reduce-window.21
  20.1 0.2 slice_reduce_fusion.1
  20.3 0.2 reduce-window.24
  20.5 0.6 reduce-window.30
  21.1 0.2 slice_reduce_fusion
  21.3 0.1 add_bitcast_fusion.1
  21.4 0.1 fusion.34
  21.5 0.1 slice.41
  21.6 0.1 reduce_sum.120
  21.7 0.1 copy.52
  21.7 0.7 convert_element_type.77
  22.4 0.7 convert_element_type.81
  23.1 0.1 select_reduce_fusion.3
  23.3 4.3 %scatter_custom_fusion = s32[1408]{0:T(1024)S(1)} fusion(s32[1024]{0:T(1024)S(1)} %bitcast.140, s32[1024]{0:T(1024)S(1)} %iota.55, s32[]{:T(128)} %constant.103.clone.1), kind=kCustom, calls=%fused_computation.85 | custom fusion | bytes 5636 | tf_op jit(solution)/shard_map/scatter | solution.py:117
  27.6 4.0 %gather_fusion = bf16[1408,128]{1,0:T(8,128)(2,1)} fusion(bf16[1024,128]{1,0:T(8,128)(2,1)S(1)} %copy-done, s32[2048]{0:T(1024)S(1)} %pad_clamp_fusion), kind=kCustom, calls=%fused_computation.2 | custom fusion | bytes 726528 | tf_op jit(solution)/shard_map/jit(_take)/gather | solution.py:300
  31.6 0.6 convert_reduce_fusion.3.block_group_ref
  32.2 3.5 %collective-permute-done = bf16[2,4,512,128]{3,2,1,0:T(8,128)(2,1)S(1)} collective-permute-done((bf16[2,4,512,128]{3,2,1,0:T(8,128)(2,1)}, bf16[2,4,512,128]{3,2,1,0:T(8,128)(2,1)S(1)}, u32[]{:S(2)}, u32[]{:S(2)}) %collective-permute-start) | collective-permute-done | bytes 1048608 | tf_op jit(solution)/shard_map/ppermute | solution.py:293
  35.8 23.6 %collective-permute-done.1 = bf16[2,4,512,128]{3,2,1,0:T(8,128)(2,1)S(1)} collective-permute-done((bf16[2,4,512,128]{3,2,1,0:T(8,128)(2,1)}, bf16[2,4,512,128]{3,2,1,0:T(8,128)(2,1)S(1)}, u32[]{:S(2)}, u32[]{:S(2)}) %collective-permute-start.1) | collective-permute-done | bytes 1048608 | tf_op jit(solution)/shard_map/ppermute | solution.py:293
  59.4 1.8 pad_maximum_fusion.1
  61.3 1.1 fusion.46
  62.4 0.0 copy-start.3
  62.4 0.6 fusion
  63.0 1.3 copy-done.2
  64.3 1.0 broadcast_select_fusion.q_ref
  65.3 0.3 pad_maximum_fusion
  65.6 2.3 %slice_bitcast_fusion.2 = (bf16[4,2048,128]{2,1,0:T(8,128)(2,1)}, bf16[4,2048,128]{2,1,0:T(8,128)(2,1)}) fusion(bf16[2,4,2048,128]{3,2,1,0:T(8,128)(2,1)S(1)} %pad_maximum_fusion), kind=kLoop, calls=%fused_computation.18 | loop fusion | bytes 8388608 | tf_op jit(solution)/shard_map/squeeze | solution.py:306
  68.0 12.2 %shard_map.145 = (f32[1408,128]{1,0:T(8,128)}, f32[1408,128]{1,0:T(8,128)}, f32[1408,128]{1,0:T(8,128)}) custom-call(s32[11]{0:T(128)} %convert_reduce_fusion.3.block_group_ref, bf16[1408,128]{1,0:T(8,128)(2,1)} %broadcast_select_fusion.q_ref, bf16[4,2048,128]{2,1,0:T(8,128)(2,1)} %get-tuple-element.63.k_ref, bf16[4,2048,128]{2,1,0:T(8,128)(2,1)} %get-tuple-element.62.v_ref), custom_call_target="tpu_custom_call" | custom-call | flops 1476395008 | bytes 6717440 | tf_op jit(solution)/shard_map/pallas_call | solution.py:134
  80.1 1.3 constant_dynamic-update-slice_fusion.1
  81.5 2.3 %constant_dynamic-update-slice_fusion = bf16[2,4,2048,128]{3,2,1,0:T(8,128)(2,1)S(1)} fusion(bf16[2,4,2048,128]{3,2,1,0:T(8,128)(2,1)S(1)} %constant_dynamic-update-slice_fusion.1, bf16[2,4,1536,128]{3,2,1,0:T(8,128)(2,1)} %collective-permute-done.4), kind=kLoop, calls=%fused_computation.81 | loop fusion | bytes 6291456 | tf_op jit(solution)/shard_map/concatenate | solution.py:304
  83.8 2.3 slice_bitcast_fusion
  86.1 12.3 %shard_map.146 = (f32[1408,128]{1,0:T(8,128)}, f32[1408,128]{1,0:T(8,128)}, f32[1408,128]{1,0:T(8,128)}) custom-call(s32[11]{0:T(128)} %convert_reduce_fusion.3.block_group_ref, bf16[1408,128]{1,0:T(8,128)(2,1)} %broadcast_select_fusion.q_ref, bf16[4,2048,128]{2,1,0:T(8,128)(2,1)} %get-tuple-element.65.k_ref, bf16[4,2048,128]{2,1,0:T(8,128)(2,1)} %get-tuple-element.64.v_ref), custom_call_target="tpu_custom_call" | custom-call | flops 1476395008 | bytes 6717440 | tf_op jit(solution)/shard_map/pallas_call | solution.py:134
  98.4 2.2 add_reduce_fusion
  100.6 6.2 %gather_fusion.3 = f32[1024]{0:T(1024)S(1)} fusion(f32[1408]{0:T(1024)S(1)} %get-tuple-element.45, s32[1024]{0:T(1024)S(1)} %get-tuple-element.60), kind=kCustom, calls=%fused_computation.1.clone | custom fusion | bytes 12288 | tf_op jit(solution)/shard_map/jit(_take)/gather | solution.py:308
  106.8 6.2 %gather_fusion.2 = f32[1024]{0:T(1024)S(1)} fusion(f32[1408]{0:T(1024)S(1)} %get-tuple-element.48, s32[1024]{0:T(1024)S(1)} %get-tuple-element.60), kind=kCustom, calls=%fused_computation.clone | custom fusion | bytes 12288 | tf_op jit(solution)/shard_map/jit(_take)/gather | solution.py:308
  113.0 0.4 multiply_add_fusion
  113.4 2.8 %gather_fusion.1 = f32[1024,128]{1,0:T(8,128)S(1)} fusion(f32[1408,128]{1,0:T(8,128)S(1)} %multiply_add_fusion, s32[1024]{0:T(1024)S(1)} %broadcast_clamp_fusion), kind=kCustom, calls=%fused_computation.3 | custom fusion | bytes 1052672 | tf_op jit(solution)/shard_map/jit(_take)/gather | solution.py:308
  116.3 0.0 copy-start.11
  116.3 4.1 %fusion.21 = bf16[1024,1,128]{2,0,1:T(8,128)(2,1)} fusion(bf16[1024,128]{1,0:T(8,128)(2,1)S(1)} %copy-done.13, f32[1024,1024]{0,1:T(8,128)} %copy-done.2, f32[1024]{0:T(1024)S(1)} %get-tuple-element.66, f32[1024,128]{1,0:T(8,128)S(1)} %gather_fusion.1, f32[1024]{0:T(1024)S(1)} %bitcast.145, f32[1024]{0:T(1024)S(1)} %bitcast.147, f32[1024]{0:T(1024)S(1)} %bitcast.146, ...), kind=kOutput, calls=%fused_computation.26 | convolution fusion | flops 271319040 | bytes 5260288 | tf_op jit(solution)/shard_map/while/body/eval_jaxpr/hqk,khd->qhd/dot_general | solution.py:224
  120.4 8.1 %all-to-all-start = ((bf16[16,64,128]{2,1,0:T(8,128)(2,1)}), bf16[16,64,128]{2,1,0:T(8,128)(2,1)S(1)}, u32[]{:S(2)}, u32[]{:S(2)}) async-start(bf16[16,64,128]{2,1,0:T(8,128)(2,1)} %bitcast.26), calls=%async_computation | async-start | bytes 524288 | tf_op jit(solution)/shard_map/all_to_all | solution.py:318
  128.6 0.2 select_reduce_fusion
  128.7 8.3 %all-to-all-done = bf16[16,64,128]{2,1,0:T(8,128)(2,1)S(1)} async-done(((bf16[16,64,128]{2,1,0:T(8,128)(2,1)}), bf16[16,64,128]{2,1,0:T(8,128)(2,1)S(1)}, u32[]{:S(2)}, u32[]{:S(2)}) %all-to-all-start) | async-done | bytes 262176 | tf_op jit(solution)/shard_map/all_to_all | solution.py:318
  137.1 5.1 %multiply_reduce_fusion = (f32[64]{0:T(128)S(1)}, f32[64,2048]{1,0:T(8,128)S(1)}) fusion(bf16[2048,2048]{1,0:T(8,128)(2,1)} %all-gather.2.cloned.1.call-done, bf16[64,2048]{1,0:T(8,128)(2,1)S(1)} %copy-done.10, bf16[16,64,128]{2,1,0:T(8,128)(2,1)S(1)} %all-to-all-done), kind=kOutput, calls=%fused_computation.36 | convolution fusion | flops 537395136 | bytes 9437440 | tf_op jit(solution)/shard_map/dot_general | solution.py:319
  142.1 0.8 convolution_convert_fusion
  142.9 30.6 %all_to_all.26 = bf16[32,16,2048]{2,1,0:T(8,128)(2,1)S(1)} all-to-all(bf16[32,16,2048]{2,1,0:T(8,128)(2,1)S(1)} %bitcast.124), channel_id=1, replica_groups=mesh['req'=8,'exp'=16] {'exp'}, dimensions={0} | all-to-all | bytes 4194304 | tf_op jit(solution)/shard_map/all_to_all | solution.py:337
  173.6 0.1 copy.53
  173.7 2.5 %copy.54 = bf16[2,256,2048]{1,2,0:T(8,128)(2,1)} copy(bf16[2,256,2048]{2,1,0:T(8,128)(2,1)S(1)} %bitcast.126) | data formatting | bytes 4194304 | tf_op jit(solution)/shard_map/reshape | solution.py:341
  176.2 13.9 %shard_map.147 = bf16[2,256,2048]{2,1,0:T(8,128)(2,1)} custom-call(bf16[2,2048,256]{2,1,0:T(8,128)(2,1)} %bitcast.128, bf16[2,704,2048]{2,1,0:T(8,128)(2,1)} %bitcast.130, bf16[2,704,2048]{2,1,0:T(8,128)(2,1)} %bitcast.131, bf16[2,704,2048]{2,1,0:T(8,128)(2,1)} %wd_ref.1), custom_call_target="tpu_custom_call" | custom-call | flops 4429185024 | bytes 21495808 | tf_op jit(solution)/shard_map/pallas_call | solution.py:180
  190.1 1.8 copy.55
  191.9 29.4 %all_to_all.27 = bf16[32,16,2048]{2,1,0:T(8,128)(2,1)S(1)} all-to-all(bf16[32,16,2048]{2,1,0:T(8,128)(2,1)S(1)} %bitcast.127), channel_id=1, replica_groups=mesh['req'=8,'exp'=16] {'exp'}, dimensions={0} | all-to-all | bytes 4194304 | tf_op jit(solution)/shard_map/all_to_all | solution.py:343
  221.3 1.2 fusion.2
  (51 shorter events, 0.2 us)
Async XLA Ops:
  6.5 21.1 %copy-start = (bf16[1024,128]{1,0:T(8,128)(2,1)S(1)}, bf16[1024,128]{1,0:T(8,128)(2,1)}, u32[]{:S(2)}) copy-start(bf16[1024,128]{1,0:T(8,128)(2,1)} %param.17) | copy-start | bytes 786436
  6.5 130.5 %all-gather.2.cloned.1.call-start = ((), (), s32[]{:S(2)}) async-start(), calls=%async_computation.3 | async-start | bytes 8912896 | tf_op jit(solution)/shard_map/all_gather | solution.py:317
  9.6 26.2 %collective-permute-start = (bf16[2,4,512,128]{3,2,1,0:T(8,128)(2,1)}, bf16[2,4,512,128]{3,2,1,0:T(8,128)(2,1)S(1)}, u32[]{:S(2)}, u32[]{:S(2)}) collective-permute-start(bf16[2,4,512,128]{3,2,1,0:T(8,128)(2,1)} %pad_maximum_fusion.2), channel_id=1, source_target_pairs={{0,32},{16,48},{32,64},{48,80},{64,96},{80,112},{96,0},{112,16},{1... | collective-permute-start | bytes 3145736 | tf_op jit(solution)/shard_map/ppermute | solution.py:293
  11.1 48.3 %collective-permute-start.1 = (bf16[2,4,512,128]{3,2,1,0:T(8,128)(2,1)}, bf16[2,4,512,128]{3,2,1,0:T(8,128)(2,1)S(1)}, u32[]{:S(2)}, u32[]{:S(2)}) collective-permute-start(bf16[2,4,512,128]{3,2,1,0:T(8,128)(2,1)} %pad_maximum_fusion.2), channel_id=1, source_target_pairs={{0,64},{16,80},{32,96},{48,112},{64,0},{80,16},{96,32},{112,48},{1... | collective-permute-start | bytes 3145736 | tf_op jit(solution)/shard_map/ppermute | solution.py:293
  13.9 45.6 %collective-permute-start.2 = (bf16[2,4,512,128]{3,2,1,0:T(8,128)(2,1)}, bf16[2,4,512,128]{3,2,1,0:T(8,128)(2,1)S(1)}, u32[]{:S(2)}, u32[]{:S(2)}) collective-permute-start(bf16[2,4,512,128]{3,2,1,0:T(8,128)(2,1)} %pad_maximum_fusion.2), channel_id=1, source_target_pairs={{0,96},{16,112},{32,0},{48,16},{64,32},{80,48},{96,64},{112,80},{1... | collective-permute-start | bytes 3145736 | tf_op jit(solution)/shard_map/ppermute | solution.py:293
  15.3 64.8 %collective-permute-start.3 = (bf16[2,4,512,128]{3,2,1,0:T(8,128)(2,1)}, bf16[2,4,512,128]{3,2,1,0:T(8,128)(2,1)}, u32[]{:S(2)}, u32[]{:S(2)}) collective-permute-start(bf16[2,4,512,128]{3,2,1,0:T(8,128)(2,1)} %pad_maximum_fusion.2), channel_id=1, source_target_pairs={{0,16},{16,0},{32,48},{48,32},{64,80},{80,64},{96,112},{112,96},{1... | collective-permute-start | bytes 3145736 | tf_op jit(solution)/shard_map/ppermute | solution.py:290
  31.6 29.6 %copy-start.12 = (bf16[1024,128]{1,0:T(8,128)(2,1)S(1)}, bf16[1024,128]{1,0:T(8,128)(2,1)}, u32[]{:S(2)}) copy-start(bf16[1024,128]{1,0:T(8,128)(2,1)} %param.18) | copy-start | bytes 786436
  61.2 20.3 %collective-permute-start.4 = (bf16[2,4,1536,128]{3,2,1,0:T(8,128)(2,1)}, bf16[2,4,1536,128]{3,2,1,0:T(8,128)(2,1)}, u32[]{:S(2)}, u32[]{:S(2)}) collective-permute-start(bf16[2,4,1536,128]{3,2,1,0:T(8,128)(2,1)} %pad_maximum_fusion.1), channel_id=1, source_target_pairs={{0,16},{16,0},{32,48},{48,32},{64,80},{80,64},{96,112},{112,96},{1... | collective-permute-start | bytes 9437192 | tf_op jit(solution)/shard_map/ppermute | solution.py:298
  61.2 3.1 %copy-start.5 = (bf16[1408,128]{1,0:T(8,128)(2,1)S(1)}, bf16[1408,128]{1,0:T(8,128)(2,1)}, u32[]{:S(2)}) copy-start(bf16[1408,128]{1,0:T(8,128)(2,1)} %gather_fusion) | copy-start | bytes 1081348
  62.3 2.0 copy-start.2
  62.4 3.0 %copy-start.3 = (bf16[4,512,128]{2,1,0:T(8,128)(2,1)S(1)}, bf16[4,512,128]{2,1,0:T(8,128)(2,1)}, u32[]{:S(2)}) copy-start(bf16[4,512,128]{2,1,0:T(8,128)(2,1)} %param.21) | copy-start | bytes 1572868
  62.4 3.0 %copy-start.4 = (bf16[4,512,128]{2,1,0:T(8,128)(2,1)S(1)}, bf16[4,512,128]{2,1,0:T(8,128)(2,1)}, u32[]{:S(2)}) copy-start(bf16[4,512,128]{2,1,0:T(8,128)(2,1)} %param.20) | copy-start | bytes 1572868
  86.0 12.3 %copy-start.8 = (f32[1408,128]{1,0:T(8,128)S(1)}, f32[1408,128]{1,0:T(8,128)}, u32[]{:S(2)}) copy-start(f32[1408,128]{1,0:T(8,128)} %get-tuple-element.40) | copy-start | bytes 2162692
  86.1 12.3 %copy-start.9 = (f32[1408,128]{1,0:T(8,128)S(1)}, f32[1408,128]{1,0:T(8,128)}, u32[]{:S(2)}) copy-start(f32[1408,128]{1,0:T(8,128)} %get-tuple-element.43) | copy-start | bytes 2162692
  100.6 12.4 %copy-start.6 = (f32[1408,128]{1,0:T(8,128)S(1)}, f32[1408,128]{1,0:T(8,128)}, u32[]{:S(2)}) copy-start(f32[1408,128]{1,0:T(8,128)} %get-tuple-element.38) | copy-start | bytes 2162692
  100.6 12.4 %copy-start.7 = (f32[1408,128]{1,0:T(8,128)S(1)}, f32[1408,128]{1,0:T(8,128)}, u32[]{:S(2)}) copy-start(f32[1408,128]{1,0:T(8,128)} %get-tuple-element.42) | copy-start | bytes 2162692
  113.0 3.4 %copy-start.13 = (bf16[1024,128]{1,0:T(8,128)(2,1)S(1)}, bf16[1024,128]{1,0:T(8,128)(2,1)}, u32[]{:S(2)}) copy-start(bf16[1024,128]{1,0:T(8,128)(2,1)} %param.19) | copy-start | bytes 786436
  116.3 12.3 %copy-start.11 = (s32[64,4]{0,1:T(4,128)S(1)}, s32[64,4]{0,1:T(4,128)}, u32[]{:S(2)}) copy-start(s32[64,4]{0,1:T(4,128)} %param.27) | copy-start | bytes 3076
  116.3 20.8 %copy-start.10 = (bf16[64,2048]{1,0:T(8,128)(2,1)S(1)}, bf16[64,2048]{1,0:T(8,128)(2,1)}, u32[]{:S(2)}) copy-start(bf16[64,2048]{1,0:T(8,128)(2,1)} %param.24) | copy-start | bytes 786436
  120.4 16.6 %all-to-all-start = ((bf16[16,64,128]{2,1,0:T(8,128)(2,1)}), bf16[16,64,128]{2,1,0:T(8,128)(2,1)S(1)}, u32[]{:S(2)}, u32[]{:S(2)}) async-start(bf16[16,64,128]{2,1,0:T(8,128)(2,1)} %bitcast.26), calls=%async_computation | async-start | bytes 524288 | tf_op jit(solution)/shard_map/all_to_all | solution.py:318
  190.1 32.4 %copy-start.1 = (bf16[1024,128]{1,0:T(8,128)(2,1)S(1)}, bf16[1024,128]{1,0:T(8,128)(2,1)}, u32[]{:S(2)}) copy-start(bf16[1024,128]{1,0:T(8,128)(2,1)} %param.17) | copy-start | bytes 786436
Sparse Core Ops, SparseCore 0:
  9.5 73.4 all-gather.1

commit v12 on v11

--- a/solution.py
+++ b/solution.py
@@ -242,6 +242,18 @@
         maxima.reshape(row_count, head_count),
         totals.reshape(row_count, head_count),
     )
+
+
+def attend_suffix_rows(query_rows, query_req, query_pos, keys, values, request, position):
+    scaling = 1.0 / math.sqrt(HEAD)
+    scores = jnp.dot(query_rows, keys.T, preferred_element_type=jnp.float32) * scaling
+    allowed = (request[None, :] == query_req[:, None]) & (position[None, :] <= query_pos[:, None])
+    scores = jnp.where(allowed, scores, NEG)
+    maxima = jnp.max(scores, axis=1, keepdims=True)
+    exp_terms = jnp.exp(scores - maxima)
+    totals = jnp.sum(exp_terms, axis=1, keepdims=True)
+    weighted = jnp.dot(exp_terms.astype(jnp.bfloat16), values, preferred_element_type=jnp.float32)
+    return (weighted, maxima, totals)
 
 
 def combine(former, latter):
@@ -305,14 +317,21 @@
     ):
         part = attend_prefix_grouped(padded_rows, block_group, chunk[0], chunk[1])
         prefix_part = part if prefix_part is None else combine(prefix_part, part)
-    prefix_part = tuple(jnp.take(piece, padded_index, axis=0) for piece in prefix_part)
-    suffix_part = attend_suffix(queries, keys, values, request, position)
+    suffix_part = attend_suffix_rows(
+        padded_rows,
+        jnp.take(request, source, axis=0),
+        jnp.take(position, source, axis=0),
+        keys,
+        values,
+        request,
+        position,
+    )
     weighted, maxima, totals = combine(prefix_part, suffix_part)
-    attended = (
-        (weighted.reshape(row_tok, head_count, HEAD) / totals[:, :, None])
-        .reshape(row_tok, columns)
-        .astype(jnp.bfloat16)
-    )
+    padded_attended = (weighted / totals).astype(jnp.bfloat16)
+    back = (padded_index[:, None] == jnp.arange(padded_rows.shape[0], dtype=jnp.int32)[None, :])
+    attended = jnp.dot(
+        back.astype(jnp.bfloat16), padded_attended, preferred_element_type=jnp.float32
+    ).astype(jnp.bfloat16)
     exp_count = lax.axis_size("exp")
     full_proj = lax.all_gather(out_proj, "exp", axis=0, tiled=True)
     token_rows = lax.all_to_all(attended, "exp", split_axis=0, concat_axis=1, tiled=True)

time: 233 us -> 226 us (0.970)
  waiting for transfers between devices: 36.2 us -> 28.7 us
  local copies, waits for them, and re-layouts: 39.1 us -> 35.4 us
  matrix products: 12.2 us -> 15.1 us
    ppermute x3, waiting for transfers between devices: 27.2 us -> 18.8 us  [per_device(): lax.ppermute(local_kv, 'req', [(i, (i + 2 * s) % req_count) for i in rang...]
    gather x3 -> x2, local copies, waits for them, and re-layouts: 15.1 us -> 10.9 us  [the longest x1 5.45 us: per_device(): jnp.take(position, source, axis=0)]
    dot_general x2, matrix products: 5.18 us -> 8.11 us  [the longest x1 6.56 us: per_device(): jnp.dot(back.astype(jnp.bfloat16), padded_attended, preferred_element_typ...]
    exp x0 -> x1, other arithmetic: none -> 2.84 us  [combine(): factor_a = jnp.exp(maxima_a - maxima)]
    add x3 -> x1, other arithmetic: 2.7 us -> 0.01 us  [group_layout(): jnp.sum(jnp.where(member, first_block[None, :], 0), axis=1) * QUERY_BLOCK]
  transfers between devices with their start and end apart: 7 -> 7, of which waited for: 3 -> 2; matrix products, arithmetic and copies ran while one was open for 24% -> 24% of each run, Pallas kernels for 11% -> 11%
where the time goes in v12:
time: 226 us; the launch traced here: 223 us
  blocking collectives  61.7 us (27%)
  Pallas kernels  38.4 us (17%)
  local copies, waits for them, and re-layouts  35.4 us (16%)
  waiting for transfers between devices  28.7 us (13%)
  other arithmetic  16.2 us (7%)
  matrix products  15.1 us (7%)
  starting transfers between devices  13.8 us (6%)
  between operations  13.8 us (6%)
    all_to_all x1, blocking collectives, per_device(): lax.all_to_all(buffer, 'exp', split_axis=0, concat_axis=0, tiled=True)  31.5 us
    all_to_all x1, blocking collectives, per_device(): lax.all_to_all(expert_out.reshape(EXPERTS, slots, width), 'exp', split_ax...  30.2 us
    pallas_call x2, Pallas kernels, attend_prefix_grouped(): pl.pallas_call(prefix_kernel, grid_spec=pltpu.PrefetchScalarGridSpec(num_...  24.5 us
    ppermute x3, waiting for transfers between devices, per_device(): lax.ppermute(local_kv, 'req', [(i, (i + 2 * s) % req_count) for i in rang...  18.8 us
    pallas_call x1, Pallas kernels, expert_ffn(): pl.pallas_call(expert_kernel, grid=(exp_dev, inner // chunk), in_specs=[p...  13.8 us
    all_to_all x1, waiting for transfers between devices, per_device(): lax.all_to_all(attended, 'exp', split_axis=0, concat_axis=1, tiled=True)  9.16 us
    all_to_all x1, starting transfers between devices, per_device(): lax.all_to_all(attended, 'exp', split_axis=0, concat_axis=1, tiled=True)  8.01 us
    dot_general x1, matrix products, per_device(): jnp.dot(back.astype(jnp.bfloat16), padded_attended, preferred_element_typ...  6.56 us
  transfers between devices with their start and end apart: 7, of which 2 were waited for; matrix products, arithmetic and copies ran while one was open for 24% of the time, Pallas kernels for 11%

profile of v12, /device:TPU:0, one launch (start us, length us, event | category | flops | bytes accessed | tf_op | source)
XLA Modules:
  0.0 223.0 jit_solution(2140962289365192815)
XLA Ops:
  6.5 0.7 all-gather.2.cloned.1.call-update
  7.3 2.4 %pad_maximum_fusion.2 = bf16[2,4,512,128]{3,2,1,0:T(8,128)(2,1)} fusion(bf16[1,4,512,128]{3,2,1,0:T(8,128)(2,1)} %bitcast.97, bf16[1,4,512,128]{3,2,1,0:T(8,128)(2,1)} %bitcast.99), kind=kLoop, calls=%fused_computation.30 | loop fusion | flops 524288 | bytes 2097152 | tf_op jit(solution)/shard_map/stack | solution.py:300
  9.6 1.6 collective-permute-start
  11.2 2.7 %collective-permute-start.1 = (bf16[2,4,512,128]{3,2,1,0:T(8,128)(2,1)}, bf16[2,4,512,128]{3,2,1,0:T(8,128)(2,1)S(1)}, u32[]{:S(2)}, u32[]{:S(2)}) collective-permute-start(bf16[2,4,512,128]{3,2,1,0:T(8,128)(2,1)} %pad_maximum_fusion.2), channel_id=1, source_target_pairs={{0,64},{16,80},{32,96},{48,112},{64,0},{80,16},{96,32},{112,48},{1... | collective-permute-start | bytes 3145736 | tf_op jit(solution)/shard_map/ppermute | solution.py:305
  13.9 1.4 collective-permute-start.2
  15.4 0.8 reduce_window_sum.44
  16.2 0.1 convert_reduce_fusion.1
  16.3 0.7 subtract_bitcast_fusion
  17.0 0.7 select_reduce_fusion.1
  17.7 0.1 convert_reduce_fusion.2
  17.8 0.2 reduce-window.20
  18.0 1.1 reduce-window.21
  19.2 0.2 slice_reduce_fusion.1
  19.4 0.2 reduce-window.24
  19.6 0.1 add_bitcast_fusion.1
  19.6 0.1 select_reduce_fusion.3
  19.8 0.1 slice.41
  19.8 0.8 copy.61
  20.6 0.1 eq.133
  20.7 0.1 eq.129
  20.8 4.3 %scatter_custom_fusion = s32[1408]{0:T(1024)S(1)} fusion(s32[1024]{0:T(1024)S(1)} %bitcast.104, s32[1024]{0:T(1024)S(1)} %iota.58, s32[]{:T(128)} %constant.70.clone.1), kind=kCustom, calls=%fused_computation.97 | custom fusion | bytes 5636 | tf_op jit(solution)/shard_map/scatter | solution.py:117
  25.2 0.0 copy-start.2
  25.2 5.4 %gather_fusion.1 = s32[1408]{0:T(1024)S(1)} fusion(s32[1024]{0:T(1024)S(1)} %convert_reduce_fusion.1, s32[2048]{0:T(1024)S(1)} %pad_clamp_fusion), kind=kCustom, calls=%fused_computation.clone | custom fusion | bytes 16896 | tf_op jit(solution)/shard_map/jit(_take)/gather | solution.py:322
  30.7 3.3 %gather_fusion = bf16[1408,128]{1,0:T(8,128)(2,1)S(1)} fusion(bf16[1024,128]{1,0:T(8,128)(2,1)S(1)} %copy-done.2, s32[2048]{0:T(1024)S(1)} %pad_clamp_fusion), kind=kCustom, calls=%fused_computation.2 | custom fusion | bytes 726528 | tf_op jit(solution)/shard_map/jit(_take)/gather | solution.py:312
  34.0 0.0 copy-start.12
  34.0 0.0 copy-start.11
  34.1 5.4 %gather_fusion.2 = s32[1408]{0:T(1024)S(1)} fusion(s32[1024]{0:T(1024)S(1)} %iota_subtract_fusion, s32[2048]{0:T(1024)S(1)} %pad_clamp_fusion), kind=kCustom, calls=%fused_computation.1.clone | custom fusion | bytes 16896 | tf_op jit(solution)/shard_map/jit(_take)/gather | solution.py:323
  39.5 0.6 reduce-window.30
  40.1 0.2 slice_reduce_fusion
  40.4 0.1 fusion.48
  40.5 0.1 reduce_sum.119
  40.6 0.1 copy.64
  40.7 18.8 %collective-permute-done.1 = bf16[2,4,512,128]{3,2,1,0:T(8,128)(2,1)S(1)} collective-permute-done((bf16[2,4,512,128]{3,2,1,0:T(8,128)(2,1)}, bf16[2,4,512,128]{3,2,1,0:T(8,128)(2,1)S(1)}, u32[]{:S(2)}, u32[]{:S(2)}) %collective-permute-start.1) | collective-permute-done | bytes 1048608 | tf_op jit(solution)/shard_map/ppermute | solution.py:305
  59.5 2.8 %pad_maximum_fusion.1 = bf16[2,4,1536,128]{3,2,1,0:T(8,128)(2,1)} fusion(bf16[2,4,512,128]{3,2,1,0:T(8,128)(2,1)} %collective-permute-done.2, bf16[2,4,512,128]{3,2,1,0:T(8,128)(2,1)S(1)} %collective-permute-done.1, bf16[2,4,512,128]{3,2,1,0:T(8,128)(2,1)S(1)} %collective-permute-done), kind=kLoop, calls=%fused_computation.11 | loop fusion | flops 9437184 | bytes 6291456 | tf_op jit(solution)/shard_map/concatenate | solution.py:303
  62.3 0.6 convert_reduce_fusion.3.block_group_ref
  62.9 0.3 broadcast_select_fusion.q_ref
  63.2 1.5 fusion.55
  64.8 0.0 copy-start.4
  64.8 0.0 copy-start.5
  64.8 2.5 %copy-done.3 = f32[1408,1024]{0,1:T(8,128)} copy-done((f32[1408,1024]{0,1:T(8,128)}, f32[1408,1024]{0,1:T(8,128)S(1)}, u32[]{:S(2)}) %copy-start.3) | copy-done | bytes 5767192
  67.3 0.8 fusion.1
  68.2 1.4 pad_maximum_fusion
  69.5 2.3 %slice_bitcast_fusion.2 = (bf16[4,2048,128]{2,1,0:T(8,128)(2,1)}, bf16[4,2048,128]{2,1,0:T(8,128)(2,1)}) fusion(bf16[2,4,2048,128]{3,2,1,0:T(8,128)(2,1)S(1)} %pad_maximum_fusion), kind=kLoop, calls=%fused_computation.25 | loop fusion | bytes 8388608 | tf_op jit(solution)/shard_map/squeeze | solution.py:318
  71.9 12.2 %shard_map.145 = (f32[1408,128]{1,0:T(8,128)}, f32[1408,128]{1,0:T(8,128)}, f32[1408,128]{1,0:T(8,128)}) custom-call(s32[11]{0:T(128)} %convert_reduce_fusion.3.block_group_ref, bf16[1408,128]{1,0:T(8,128)(2,1)} %copy-done.8, bf16[4,2048,128]{2,1,0:T(8,128)(2,1)} %get-tuple-element.32.k_ref, bf16[4,2048,128]{2,1,0:T(8,128)(2,1)} %get-tuple-element.31.v_ref), custom_call_target="tpu_custom_call" | custom-call | flops 1476395008 | bytes 6717440 | tf_op jit(solution)/shard_map/pallas_call | solution.py:134
  84.1 1.3 constant_dynamic-update-slice_fusion.1
  85.4 2.3 %constant_dynamic-update-slice_fusion = bf16[2,4,2048,128]{3,2,1,0:T(8,128)(2,1)S(1)} fusion(bf16[2,4,2048,128]{3,2,1,0:T(8,128)(2,1)S(1)} %constant_dynamic-update-slice_fusion.1, bf16[2,4,1536,128]{3,2,1,0:T(8,128)(2,1)} %collective-permute-done.4), kind=kLoop, calls=%fused_computation.92 | loop fusion | bytes 6291456 | tf_op jit(solution)/shard_map/concatenate | solution.py:316
  87.7 2.2 %slice_bitcast_fusion = (bf16[4,2048,128]{2,1,0:T(8,128)(2,1)}, bf16[4,2048,128]{2,1,0:T(8,128)(2,1)}) fusion(bf16[2,4,2048,128]{3,2,1,0:T(8,128)(2,1)S(1)} %constant_dynamic-update-slice_fusion), kind=kLoop, calls=%fused_computation.23 | loop fusion | bytes 8388608 | tf_op jit(solution)/shard_map/squeeze | solution.py:318
  90.0 12.3 %shard_map.146 = (f32[1408,128]{1,0:T(8,128)}, f32[1408,128]{1,0:T(8,128)}, f32[1408,128]{1,0:T(8,128)}) custom-call(s32[11]{0:T(128)} %convert_reduce_fusion.3.block_group_ref, bf16[1408,128]{1,0:T(8,128)(2,1)} %copy-done.8, bf16[4,2048,128]{2,1,0:T(8,128)(2,1)} %get-tuple-element.34.k_ref, bf16[4,2048,128]{2,1,0:T(8,128)(2,1)} %get-tuple-element.33.v_ref), custom_call_target="tpu_custom_call" | custom-call | flops 1476395008 | bytes 6717440 | tf_op jit(solution)/shard_map/pallas_call | solution.py:134
  102.3 2.8 %fusion.43 = (f32[1408]{0:T(1024)S(1)}, f32[1408]{0:T(1024)S(1)}, f32[1408]{0:T(1024)S(1)}, f32[1408]{0:T(1024)S(1)}, f32[1408]{0:T(1024)S(1)}) fusion(f32[1408,128]{1,0:T(8,128)S(1)} %copy-done.6, f32[1408]{0:T(1024)S(1)} %fusion.1, f32[1408]{0:T(1024)S(1)} %get-tuple-element.35, f32[1408,128]{1,0:T(8,128)} %get-tuple-element.14, ...), kind=kLoop, calls=%fused_computation.61 | loop fusion | flops 16896 | bytes 61952 | tf_op jit(solution)/shard_map/exp | solution.py:264
  105.2 0.0 copy-start.10
  105.2 0.0 copy-start.9
  105.2 6.6 %fusion.20 = bf16[1024,128]{1,0:T(8,128)(2,1)} fusion(s32[1024]{0:T(1024)S(1)} %multiply_add_fusion, bf16[1024,128]{1,0:T(8,128)(2,1)S(1)} %copy-done.13, f32[1408,1024]{0,1:T(8,128)} %copy-done.3, f32[1408]{0:T(1024)S(1)} %get-tuple-element.35, f32[1408,128]{1,0:T(8,128)} %get-tuple-element.15, f32[1408,128]{1,0:T(8,128)S(1)} %copy-done.14, ...), kind=kOutput, calls=%fused_computation.27 | convolution fusion | flops 744095744 | bytes 7771136 | tf_op jit(solution)/shard_map/dot_general | solution.py:332
  111.7 8.0 %all-to-all-start = ((bf16[16,64,128]{2,1,0:T(8,128)(2,1)}), bf16[16,64,128]{2,1,0:T(8,128)(2,1)S(1)}, u32[]{:S(2)}, u32[]{:S(2)}) async-start(bf16[16,64,128]{2,1,0:T(8,128)(2,1)} %bitcast.15), calls=%async_computation | async-start | bytes 524288 | tf_op jit(solution)/shard_map/all_to_all | solution.py:337
  119.8 0.2 select_reduce_fusion
  119.9 9.2 %all-to-all-done = bf16[16,64,128]{2,1,0:T(8,128)(2,1)S(1)} async-done(((bf16[16,64,128]{2,1,0:T(8,128)(2,1)}), bf16[16,64,128]{2,1,0:T(8,128)(2,1)S(1)}, u32[]{:S(2)}, u32[]{:S(2)}) %all-to-all-start) | async-done | bytes 262176 | tf_op jit(solution)/shard_map/all_to_all | solution.py:337
  129.1 5.1 %multiply_reduce_fusion = (f32[64]{0:T(128)S(1)}, f32[64,2048]{1,0:T(8,128)S(1)}) fusion(bf16[2048,2048]{1,0:T(8,128)(2,1)} %all-gather.2.cloned.1.call-done, bf16[64,2048]{1,0:T(8,128)(2,1)S(1)} %copy-done.9, bf16[16,64,128]{2,1,0:T(8,128)(2,1)S(1)} %all-to-all-done), kind=kOutput, calls=%fused_computation.47 | convolution fusion | flops 537395136 | bytes 9437440 | tf_op jit(solution)/shard_map/dot_general | solution.py:338
  134.2 0.8 convolution_convert_fusion
  135.0 31.5 %all_to_all.29 = bf16[32,16,2048]{2,1,0:T(8,128)(2,1)S(1)} all-to-all(bf16[32,16,2048]{2,1,0:T(8,128)(2,1)S(1)} %bitcast.89), channel_id=1, replica_groups=mesh['req'=8,'exp'=16] {'exp'}, dimensions={0} | all-to-all | bytes 4194304 | tf_op jit(solution)/shard_map/all_to_all | solution.py:356
  166.4 0.1 copy.65
  166.6 2.5 %copy.66 = bf16[2,256,2048]{1,2,0:T(8,128)(2,1)} copy(bf16[2,256,2048]{2,1,0:T(8,128)(2,1)S(1)} %bitcast.91) | data formatting | bytes 4194304 | tf_op jit(solution)/shard_map/reshape | solution.py:360
  169.1 13.8 %shard_map.147 = bf16[2,256,2048]{2,1,0:T(8,128)(2,1)} custom-call(bf16[2,2048,256]{2,1,0:T(8,128)(2,1)} %bitcast.93, bf16[2,704,2048]{2,1,0:T(8,128)(2,1)} %bitcast.95, bf16[2,704,2048]{2,1,0:T(8,128)(2,1)} %bitcast.96, bf16[2,704,2048]{2,1,0:T(8,128)(2,1)} %wd_ref.1), custom_call_target="tpu_custom_call" | custom-call | flops 4429185024 | bytes 21495808 | tf_op jit(solution)/shard_map/pallas_call | solution.py:180
  183.0 1.8 copy.67
  184.7 30.2 %all_to_all.30 = bf16[32,16,2048]{2,1,0:T(8,128)(2,1)S(1)} all-to-all(bf16[32,16,2048]{2,1,0:T(8,128)(2,1)S(1)} %bitcast.92), channel_id=1, replica_groups=mesh['req'=8,'exp'=16] {'exp'}, dimensions={0} | all-to-all | bytes 4194304 | tf_op jit(solution)/shard_map/all_to_all | solution.py:362
  215.0 1.2 fusion.19
  (48 shorter events, 0.2 us)
Async XLA Ops:
  6.5 56.7 %copy-start = (bf16[1024,128]{1,0:T(8,128)(2,1)S(1)}, bf16[1024,128]{1,0:T(8,128)(2,1)}, u32[]{:S(2)}) copy-start(bf16[1024,128]{1,0:T(8,128)(2,1)} %param.18) | copy-start | bytes 786436
  6.5 122.6 %all-gather.2.cloned.1.call-start = ((), (), s32[]{:S(2)}) async-start(), calls=%async_computation.3 | async-start | bytes 8912896 | tf_op jit(solution)/shard_map/all_gather | solution.py:336
  9.6 31.0 %collective-permute-start = (bf16[2,4,512,128]{3,2,1,0:T(8,128)(2,1)}, bf16[2,4,512,128]{3,2,1,0:T(8,128)(2,1)S(1)}, u32[]{:S(2)}, u32[]{:S(2)}) collective-permute-start(bf16[2,4,512,128]{3,2,1,0:T(8,128)(2,1)} %pad_maximum_fusion.2), channel_id=1, source_target_pairs={{0,32},{16,48},{32,64},{48,80},{64,96},{80,112},{96,0},{112,16},{1... | collective-permute-start | bytes 3145736 | tf_op jit(solution)/shard_map/ppermute | solution.py:305
  11.2 48.3 %collective-permute-start.1 = (bf16[2,4,512,128]{3,2,1,0:T(8,128)(2,1)}, bf16[2,4,512,128]{3,2,1,0:T(8,128)(2,1)S(1)}, u32[]{:S(2)}, u32[]{:S(2)}) collective-permute-start(bf16[2,4,512,128]{3,2,1,0:T(8,128)(2,1)} %pad_maximum_fusion.2), channel_id=1, source_target_pairs={{0,64},{16,80},{32,96},{48,112},{64,0},{80,16},{96,32},{112,48},{1... | collective-permute-start | bytes 3145736 | tf_op jit(solution)/shard_map/ppermute | solution.py:305
  13.9 45.6 %collective-permute-start.2 = (bf16[2,4,512,128]{3,2,1,0:T(8,128)(2,1)}, bf16[2,4,512,128]{3,2,1,0:T(8,128)(2,1)}, u32[]{:S(2)}, u32[]{:S(2)}) collective-permute-start(bf16[2,4,512,128]{3,2,1,0:T(8,128)(2,1)} %pad_maximum_fusion.2), channel_id=1, source_target_pairs={{0,96},{16,112},{32,0},{48,16},{64,32},{80,48},{96,64},{112,80},{1... | collective-permute-start | bytes 3145736 | tf_op jit(solution)/shard_map/ppermute | solution.py:305
  15.4 68.7 %collective-permute-start.3 = (bf16[2,4,512,128]{3,2,1,0:T(8,128)(2,1)}, bf16[2,4,512,128]{3,2,1,0:T(8,128)(2,1)}, u32[]{:S(2)}, u32[]{:S(2)}) collective-permute-start(bf16[2,4,512,128]{3,2,1,0:T(8,128)(2,1)} %pad_maximum_fusion.2), channel_id=1, source_target_pairs={{0,16},{16,0},{32,48},{48,32},{64,80},{80,64},{96,112},{112,96},{1... | collective-permute-start | bytes 3145736 | tf_op jit(solution)/shard_map/ppermute | solution.py:302
  25.2 5.5 %copy-start.2 = (bf16[1024,128]{1,0:T(8,128)(2,1)S(1)}, bf16[1024,128]{1,0:T(8,128)(2,1)}, u32[]{:S(2)}) copy-start(bf16[1024,128]{1,0:T(8,128)(2,1)} %param.17) | copy-start | bytes 786436
  34.0 6.6 %copy-start.12 = (bf16[64,4]{0,1:T(4,128)(2,1)S(1)}, bf16[64,4]{0,1:T(4,128)(2,1)}, u32[]{:S(2)}) copy-start(bf16[64,4]{0,1:T(4,128)(2,1)} %param.28) | copy-start | bytes 1540
  34.0 6.6 %copy-start.11 = (bf16[2048]{0:T(1024)(128)(2,1)S(1)}, bf16[2048]{0:T(1024)(128)(2,1)}, u32[]{:S(2)}) copy-start(bf16[2048]{0:T(1024)(128)(2,1)} %param.26) | copy-start | bytes 12292
  62.3 23.1 %collective-permute-start.4 = (bf16[2,4,1536,128]{3,2,1,0:T(8,128)(2,1)}, bf16[2,4,1536,128]{3,2,1,0:T(8,128)(2,1)}, u32[]{:S(2)}, u32[]{:S(2)}) collective-permute-start(bf16[2,4,1536,128]{3,2,1,0:T(8,128)(2,1)} %pad_maximum_fusion.1), channel_id=1, source_target_pairs={{0,16},{16,0},{32,48},{48,32},{64,80},{80,64},{96,112},{112,96},{1... | collective-permute-start | bytes 9437192 | tf_op jit(solution)/shard_map/ppermute | solution.py:310
  63.2 1.6 copy-start.8
  64.8 2.5 %copy-start.3 = (f32[1408,1024]{0,1:T(8,128)}, f32[1408,1024]{0,1:T(8,128)S(1)}, u32[]{:S(2)}) copy-start(f32[1408,1024]{0,1:T(8,128)S(1)} %get-tuple-element.36) | copy-start | bytes 17301508
  64.8 3.4 %copy-start.4 = (bf16[4,512,128]{2,1,0:T(8,128)(2,1)S(1)}, bf16[4,512,128]{2,1,0:T(8,128)(2,1)}, u32[]{:S(2)}) copy-start(bf16[4,512,128]{2,1,0:T(8,128)(2,1)} %param.21) | copy-start | bytes 1572868
  64.8 3.4 %copy-start.5 = (bf16[4,512,128]{2,1,0:T(8,128)(2,1)S(1)}, bf16[4,512,128]{2,1,0:T(8,128)(2,1)}, u32[]{:S(2)}) copy-start(bf16[4,512,128]{2,1,0:T(8,128)(2,1)} %param.20) | copy-start | bytes 1572868
  90.0 12.3 %copy-start.6 = (f32[1408,128]{1,0:T(8,128)S(1)}, f32[1408,128]{1,0:T(8,128)}, u32[]{:S(2)}) copy-start(f32[1408,128]{1,0:T(8,128)} %get-tuple-element.13) | copy-start | bytes 2162692
  90.0 12.3 %copy-start.7 = (f32[1408,128]{1,0:T(8,128)S(1)}, f32[1408,128]{1,0:T(8,128)}, u32[]{:S(2)}) copy-start(f32[1408,128]{1,0:T(8,128)} %get-tuple-element.16) | copy-start | bytes 2162692
  90.0 15.2 %copy-start.13 = (bf16[1024,128]{1,0:T(8,128)(2,1)S(1)}, bf16[1024,128]{1,0:T(8,128)(2,1)}, u32[]{:S(2)}) copy-start(bf16[1024,128]{1,0:T(8,128)(2,1)} %param.19) | copy-start | bytes 786436
  90.0 15.2 %copy-start.14 = (f32[1408,128]{1,0:T(8,128)S(1)}, f32[1408,128]{1,0:T(8,128)}, u32[]{:S(2)}) copy-start(f32[1408,128]{1,0:T(8,128)} %get-tuple-element.12) | copy-start | bytes 2162692
  105.2 14.6 %copy-start.10 = (s32[64,4]{0,1:T(4,128)S(1)}, s32[64,4]{0,1:T(4,128)}, u32[]{:S(2)}) copy-start(s32[64,4]{0,1:T(4,128)} %param.27) | copy-start | bytes 3076
  105.2 23.9 %copy-start.9 = (bf16[64,2048]{1,0:T(8,128)(2,1)S(1)}, bf16[64,2048]{1,0:T(8,128)(2,1)}, u32[]{:S(2)}) copy-start(bf16[64,2048]{1,0:T(8,128)(2,1)} %param.24) | copy-start | bytes 786436
  111.7 17.4 %all-to-all-start = ((bf16[16,64,128]{2,1,0:T(8,128)(2,1)}), bf16[16,64,128]{2,1,0:T(8,128)(2,1)S(1)}, u32[]{:S(2)}, u32[]{:S(2)}) async-start(bf16[16,64,128]{2,1,0:T(8,128)(2,1)} %bitcast.15), calls=%async_computation | async-start | bytes 524288 | tf_op jit(solution)/shard_map/all_to_all | solution.py:337
  182.9 33.2 %copy-start.1 = (bf16[1024,128]{1,0:T(8,128)(2,1)S(1)}, bf16[1024,128]{1,0:T(8,128)(2,1)}, u32[]{:S(2)}) copy-start(bf16[1024,128]{1,0:T(8,128)(2,1)} %param.18) | copy-start | bytes 786436
Sparse Core Ops, SparseCore 0:
  9.5 73.3 all-gather.1

commit v13 on v12

--- a/solution.py
+++ b/solution.py
@@ -93,16 +93,22 @@
 KEY_BLOCK = 2048
 
 
-def prefix_kernel(block_group_ref, q_ref, k_ref, v_ref, acc_ref, m_ref, l_ref):
+def prefix_kernel(block_group_ref, q_ref, ka_ref, va_ref, kb_ref, vb_ref, acc_ref, m_ref, l_ref):
     scaling = 1.0 / math.sqrt(HEAD)
-    s = lax.dot_general(
-        q_ref[...], k_ref[0], (((1,), (1,)), ((), ())), preferred_element_type=jnp.float32
-    ) * scaling
-    m = jnp.max(s, axis=1, keepdims=True)
-    p = jnp.exp(s - m)
-    acc_ref[...] = jnp.dot(p.astype(jnp.bfloat16), v_ref[0], preferred_element_type=jnp.float32)
+    q = q_ref[...]
+    contract = (((1,), (1,)), ((), ()))
+    s_a = lax.dot_general(q, ka_ref[0, 0], contract, preferred_element_type=jnp.float32) * scaling
+    s_b = lax.dot_general(q, kb_ref[0, 0], contract, preferred_element_type=jnp.float32) * scaling
+    m = jnp.maximum(jnp.max(s_a, axis=1, keepdims=True), jnp.max(s_b, axis=1, keepdims=True))
+    p_a = jnp.exp(s_a - m)
+    p_b = jnp.exp(s_b - m)
+    acc_ref[...] = jnp.dot(
+        p_a.astype(jnp.bfloat16), va_ref[0, 0], preferred_element_type=jnp.float32
+    ) + jnp.dot(p_b.astype(jnp.bfloat16), vb_ref[0, 0], preferred_element_type=jnp.float32)
     m_ref[...] = jnp.broadcast_to(m, m_ref.shape)
-    l_ref[...] = jnp.broadcast_to(jnp.sum(p, axis=1, keepdims=True), l_ref.shape)
+    l_ref[...] = jnp.broadcast_to(
+        jnp.sum(p_a, axis=1, keepdims=True) + jnp.sum(p_b, axis=1, keepdims=True), l_ref.shape
+    )
 
 
 def group_layout(query_group):
@@ -124,19 +130,26 @@
     return padded_index, source, block_group
 
 
-def attend_prefix_grouped(padded_rows, block_group, prefix_k, prefix_v):
+def attend_prefix_grouped(padded_rows, block_group, kv_a, kv_b):
     padded_count = padded_rows.shape[0]
-    span = prefix_k.shape[1]
     block_count = padded_count // QUERY_BLOCK
     row_spec = pl.BlockSpec((QUERY_BLOCK, HEAD), lambda b, bg: (b, 0))
-    kv_spec = pl.BlockSpec((1, span, HEAD), lambda b, bg: (bg[b], 0, 0))
+
+    def piece_specs(kv):
+        span = kv.shape[2]
+        return [
+            pl.BlockSpec((1, 1, span, HEAD), lambda b, bg: (0, bg[b], 0, 0)),
+            pl.BlockSpec((1, 1, span, HEAD), lambda b, bg: (1, bg[b], 0, 0)),
+        ]
+
+    span = kv_a.shape[2] + kv_b.shape[2]
     out_shape = jax.ShapeDtypeStruct((padded_count, HEAD), jnp.float32)
     acc, maxima, totals = pl.pallas_call(
         prefix_kernel,
         grid_spec=pltpu.PrefetchScalarGridSpec(
             num_scalar_prefetch=1,
             grid=(block_count,),
-            in_specs=[row_spec, kv_spec, kv_spec],
+            in_specs=[row_spec] + piece_specs(kv_a) + piece_specs(kv_b),
             out_specs=[row_spec] * 3,
         ),
         out_shape=[out_shape] * 3,
@@ -146,7 +159,7 @@
             transcendentals=padded_count * span,
             bytes_accessed=2 * G * span * HEAD * 2 + padded_count * HEAD * 14,
         ),
-    )(block_group, padded_rows, prefix_k, prefix_v)
+    )(block_group, padded_rows, kv_a, kv_a, kv_b, kv_b)
     return (acc, maxima[:, :1], totals[:, :1])
 
 
@@ -300,23 +313,18 @@
     local_kv = jnp.stack([prefix_keys, prefix_values])
     partner = [(i, i ^ 1) for i in range(req_count)]
     partner_kv = lax.ppermute(local_kv, "req", partner)
-    ring_kv = jnp.concatenate(
-        [
-            lax.ppermute(local_kv, "req", [(i, (i + 2 * s) % req_count) for i in range(req_count)])
-            for s in range(1, req_count // 2)
-        ],
-        axis=2,
-    )
+    ring_parts = [
+        lax.ppermute(local_kv, "req", [(i, (i + 2 * s) % req_count) for i in range(req_count)])
+        for s in range(1, req_count // 2)
+    ]
+    ring_kv = jnp.concatenate(ring_parts, axis=2)
     forwarded_kv = lax.ppermute(ring_kv, "req", partner)
     padded_index, source, block_group = group_layout(tok_group)
     padded_rows = jnp.take(queries, source, axis=0)
-    prefix_part = None
-    for chunk in (
-        jnp.concatenate([local_kv, ring_kv], axis=2),
-        jnp.concatenate([partner_kv, forwarded_kv], axis=2),
-    ):
-        part = attend_prefix_grouped(padded_rows, block_group, chunk[0], chunk[1])
-        prefix_part = part if prefix_part is None else combine(prefix_part, part)
+    prefix_part = combine(
+        attend_prefix_grouped(padded_rows, block_group, local_kv, ring_kv),
+        attend_prefix_grouped(padded_rows, block_group, partner_kv, forwarded_kv),
+    )
     suffix_part = attend_suffix_rows(
         padded_rows,
         jnp.take(request, source, axis=0),

time: 226 us -> 236 us (1.044); the launches traced: 223 us -> 235 us
  waiting for transfers between devices: 28.7 us -> 45.9 us
  other arithmetic: 16.2 us -> 10.9 us
    ppermute x3, waiting for transfers between devices: 18.8 us -> 36.2 us  [per_device(): lax.ppermute(local_kv, 'req', [(i, (i + 2 * s) % req_count) for i in rang...]
    squeeze x2 -> x0, local copies, waits for them, and re-layouts: 4.56 us -> none  [per_device(): part = attend_prefix_grouped(padded_rows, block_group, chunk[0], chunk[1])]
    unnamed x32 -> x31, local copies, waits for them, and re-layouts: 4.65 us -> 9.16 us
    concatenate x2 -> x0, other arithmetic: 4.19 us -> none  [the longest x1 2.81 us: per_device(): jnp.concatenate([lax.ppermute(local_kv, 'req', [(i, (i + 2 * s) % req_cou...]
  transfers between devices with their start and end apart: 7 -> 7, of which waited for: 2 -> 3; matrix products, arithmetic and copies ran while one was open for 24% -> 20% of each run, Pallas kernels for 11% -> 11%
where the time goes in v13:
time: 236 us; the launch traced here: 235 us
  blocking collectives  61.4 us (26%)
  waiting for transfers between devices  45.9 us (19%)
  Pallas kernels  38.8 us (16%)
  local copies, waits for them, and re-layouts  35.6 us (15%)
  matrix products  15.3 us (6%)
  starting transfers between devices  13.9 us (6%)
  between operations  13.8 us (6%)
  other arithmetic  10.9 us (5%)
    ppermute x3, waiting for transfers between devices, per_device(): lax.ppermute(local_kv, 'req', [(i, (i + 2 * s) % req_count) for i in rang...  36.2 us
    all_to_all x1, blocking collectives, per_device(): lax.all_to_all(buffer, 'exp', split_axis=0, concat_axis=0, tiled=True)  31.3 us
    all_to_all x1, blocking collectives, per_device(): lax.all_to_all(expert_out.reshape(EXPERTS, slots, width), 'exp', split_ax...  30.1 us
    pallas_call x2, Pallas kernels, attend_prefix_grouped(): pl.pallas_call(prefix_kernel, grid_spec=pltpu.PrefetchScalarGridSpec(num_...  24.9 us
    pallas_call x1, Pallas kernels, expert_ffn(): pl.pallas_call(expert_kernel, grid=(exp_dev, inner // chunk), in_specs=[p...  13.9 us
    unnamed x31, local copies, waits for them, and re-layouts  9.16 us
    all_to_all x1, waiting for transfers between devices, per_device(): lax.all_to_all(attended, 'exp', split_axis=0, concat_axis=1, tiled=True)  8.91 us
    all_to_all x1, starting transfers between devices, per_device(): lax.all_to_all(attended, 'exp', split_axis=0, concat_axis=1, tiled=True)  8.04 us
  transfers between devices with their start and end apart: 7, of which 3 were waited for; matrix products, arithmetic and copies ran while one was open for 20% of the time, Pallas kernels for 11%

profile of v13, /device:TPU:0, one launch (start us, length us, event | category | flops | bytes accessed | tf_op | source)
XLA Modules:
  0.0 235.4 jit_solution(10900939468428743343)
XLA Ops:
  6.5 0.7 all-gather.2.cloned.1.call-update
  7.3 1.3 pad_maximum_fusion.ka_ref.va_ref
  8.6 1.6 collective-permute-start
  10.2 2.7 %collective-permute-start.1 = (bf16[2,4,512,128]{3,2,1,0:T(8,128)(2,1)S(1)}, bf16[2,4,512,128]{3,2,1,0:T(8,128)(2,1)}, u32[]{:S(2)}, u32[]{:S(2)}) collective-permute-start(bf16[2,4,512,128]{3,2,1,0:T(8,128)(2,1)S(1)} %pad_maximum_fusion.ka_ref.va_ref), channel_id=1, source_target_pairs={{0,64},{16,80},{32,96},{48,112},{64,0},{80,16},{96,32},{112,48},{1... | collective-permute-start | bytes 3145736 | tf_op jit(solution)/shard_map/ppermute | solution.py:317
  12.9 1.4 collective-permute-start.2
  14.4 0.0 collective-permute-start.3
  14.4 0.8 reduce_window_sum.44
  15.2 0.1 convert_reduce_fusion.1
  15.3 0.7 subtract_bitcast_fusion
  16.0 0.7 select_reduce_fusion.1
  16.7 0.1 convert_reduce_fusion.2
  16.9 0.8 copy.61
  17.6 0.1 eq.133
  17.7 0.1 eq.129
  17.8 0.2 reduce-window.20
  18.0 1.1 reduce-window.21
  19.1 0.2 slice_reduce_fusion.1
  19.4 0.2 reduce-window.24
  19.6 0.1 add_bitcast_fusion.1
  19.6 0.1 select_reduce_fusion.3
  19.7 15.0 %collective-permute-done = bf16[2,4,512,128]{3,2,1,0:T(8,128)(2,1)} collective-permute-done((bf16[2,4,512,128]{3,2,1,0:T(8,128)(2,1)S(1)}, bf16[2,4,512,128]{3,2,1,0:T(8,128)(2,1)}, u32[]{:S(2)}, u32[]{:S(2)}) %collective-permute-start) | collective-permute-done | bytes 1048608 | tf_op jit(solution)/shard_map/ppermute | solution.py:317
  34.7 2.4 %constant_dynamic-update-slice_fusion.2 = bf16[2,4,1536,128]{3,2,1,0:T(8,128)(2,1)} fusion(bf16[2,4,512,128]{3,2,1,0:T(8,128)(2,1)} %collective-permute-done), kind=kLoop, calls=%fused_computation.80 | loop fusion | bytes 2097152
  37.2 21.2 %collective-permute-done.1 = bf16[2,4,512,128]{3,2,1,0:T(8,128)(2,1)} collective-permute-done((bf16[2,4,512,128]{3,2,1,0:T(8,128)(2,1)S(1)}, bf16[2,4,512,128]{3,2,1,0:T(8,128)(2,1)}, u32[]{:S(2)}, u32[]{:S(2)}) %collective-permute-start.1) | collective-permute-done | bytes 1048608 | tf_op jit(solution)/shard_map/ppermute | solution.py:317
  58.4 2.4 %constant_dynamic-update-slice_fusion.1 = bf16[2,4,1536,128]{3,2,1,0:T(8,128)(2,1)} fusion(bf16[2,4,1536,128]{3,2,1,0:T(8,128)(2,1)} %constant_dynamic-update-slice_fusion.2, bf16[2,4,512,128]{3,2,1,0:T(8,128)(2,1)} %collective-permute-done.1), kind=kLoop, calls=%fused_computation.79 | loop fusion | bytes 2097152
  60.8 0.0 collective-permute-done.2
  60.8 2.5 %constant_dynamic-update-slice_fusion.kb_ref.vb_ref = bf16[2,4,1536,128]{3,2,1,0:T(8,128)(2,1)} fusion(bf16[2,4,1536,128]{3,2,1,0:T(8,128)(2,1)} %constant_dynamic-update-slice_fusion.1, bf16[2,4,512,128]{3,2,1,0:T(8,128)(2,1)} %collective-permute-done.2), kind=kLoop, calls=%fused_computation.78 | loop fusion | bytes 2097152 | tf_op jit(solution)/shard_map/concatenate | solution.py:320
  63.3 4.5 %scatter_custom_fusion = s32[1408]{0:T(1024)S(1)} fusion(s32[1024]{0:T(1024)S(1)} %bitcast.94, s32[1024]{0:T(1024)S(1)} %iota.58, s32[]{:T(128)} %constant.70.clone.1), kind=kCustom, calls=%fused_computation.84 | custom fusion | bytes 5636 | tf_op jit(solution)/shard_map/scatter | solution.py:123
  67.9 5.4 %gather_fusion.1 = s32[1408]{0:T(1024)S(1)} fusion(s32[1024]{0:T(1024)S(1)} %convert_reduce_fusion.1, s32[2048]{0:T(1024)S(1)} %pad_clamp_fusion), kind=kCustom, calls=%fused_computation.clone | custom fusion | bytes 16896 | tf_op jit(solution)/shard_map/jit(_take)/gather | solution.py:330
  73.4 0.0 copy-start.12
  73.4 0.0 copy-start.11
  73.4 3.3 %gather_fusion = bf16[1408,128]{1,0:T(8,128)(2,1)S(1)} fusion(bf16[1024,128]{1,0:T(8,128)(2,1)S(1)} %copy-done.2, s32[2048]{0:T(1024)S(1)} %pad_clamp_fusion), kind=kCustom, calls=%fused_computation.2 | custom fusion | bytes 726528 | tf_op jit(solution)/shard_map/jit(_take)/gather | solution.py:323
  76.7 5.4 %gather_fusion.2 = s32[1408]{0:T(1024)S(1)} fusion(s32[1024]{0:T(1024)S(1)} %iota_subtract_fusion, s32[2048]{0:T(1024)S(1)} %pad_clamp_fusion), kind=kCustom, calls=%fused_computation.1.clone | custom fusion | bytes 16896 | tf_op jit(solution)/shard_map/jit(_take)/gather | solution.py:331
  82.2 0.6 reduce-window.30
  82.8 0.2 slice_reduce_fusion
  83.1 0.3 broadcast_select_fusion.q_ref
  83.3 0.1 fusion.35
  83.4 0.1 slice.29
  83.5 0.1 reduce_sum.119
  83.6 0.1 copy.64
  83.7 0.0 copy-done.11
  83.7 0.6 convert_reduce_fusion.3.block_group_ref
  84.3 1.6 fusion.42
  85.9 2.5 %copy-done.4 = f32[1408,1024]{0,1:T(8,128)} copy-done((f32[1408,1024]{0,1:T(8,128)}, f32[1408,1024]{0,1:T(8,128)S(1)}, u32[]{:S(2)}) %copy-start.4) | copy-done | bytes 5767192
  88.4 0.8 fusion.1
  89.3 12.4 %shard_map.145 = (f32[1408,128]{1,0:T(8,128)}, f32[1408,128]{1,0:T(8,128)}, f32[1408,128]{1,0:T(8,128)}) custom-call(s32[11]{0:T(128)} %convert_reduce_fusion.3.block_group_ref, bf16[1408,128]{1,0:T(8,128)(2,1)} %copy-done.6, bf16[2,4,512,128]{3,2,1,0:T(8,128)(2,1)} %copy-done.3, bf16[2,4,512,128]{3,2,1,0:T(8,128)(2,1)} %copy-done.3, ...), custom_call_target="tpu_custom_call" | custom-call | flops 1476395008 | bytes 6717440 | tf_op jit(solution)/shard_map/pallas_call | solution.py:147
  101.7 0.0 copy-start.13
  101.7 0.9 copy-done.5
  102.7 12.4 %shard_map.146 = (f32[1408,128]{1,0:T(8,128)}, f32[1408,128]{1,0:T(8,128)}, f32[1408,128]{1,0:T(8,128)}) custom-call(s32[11]{0:T(128)} %convert_reduce_fusion.3.block_group_ref, bf16[1408,128]{1,0:T(8,128)(2,1)} %copy-done.6, bf16[2,4,512,128]{3,2,1,0:T(8,128)(2,1)} %copy-done.5, bf16[2,4,512,128]{3,2,1,0:T(8,128)(2,1)} %copy-done.5, ...), custom_call_target="tpu_custom_call" | custom-call | flops 1476395008 | bytes 6717440 | tf_op jit(solution)/shard_map/pallas_call | solution.py:147
  115.1 2.8 %fusion.30 = (f32[1408]{0:T(1024)S(1)}, f32[1408]{0:T(1024)S(1)}, f32[1408]{0:T(1024)S(1)}, f32[1408]{0:T(1024)S(1)}, f32[1408]{0:T(1024)S(1)}) fusion(f32[1408,128]{1,0:T(8,128)S(1)} %copy-done.7, f32[1408]{0:T(1024)S(1)} %fusion.1, f32[1408]{0:T(1024)S(1)} %get-tuple-element.31, f32[1408,128]{1,0:T(8,128)} %get-tuple-element.14, ...), kind=kLoop, calls=%fused_computation.47 | loop fusion | flops 16896 | bytes 61952 | tf_op jit(solution)/shard_map/exp | solution.py:277
  117.9 0.0 copy-start.10
  118.0 0.0 copy-start.9
  118.0 6.8 %fusion.11 = bf16[1024,128]{1,0:T(8,128)(2,1)} fusion(s32[1024]{0:T(1024)S(1)} %multiply_add_fusion, f32[1408,128]{1,0:T(8,128)} %get-tuple-element.15, f32[1408,128]{1,0:T(8,128)} %get-tuple-element.12, f32[1408]{0:T(1024)S(1)} %get-tuple-element.19, f32[1408]{0:T(1024)S(1)} %get-tuple-element.22, bf16[1024,128]{1,0:T(8,128)(2,1)S(1)} %copy-done.13, ...), kind=kOutput, calls=%fused_computation.18 | convolution fusion | flops 744095744 | bytes 7771136 | tf_op jit(solution)/shard_map/dot_general | solution.py:340
  124.7 8.0 %all-to-all-start = ((bf16[16,64,128]{2,1,0:T(8,128)(2,1)}), bf16[16,64,128]{2,1,0:T(8,128)(2,1)S(1)}, u32[]{:S(2)}, u32[]{:S(2)}) async-start(bf16[16,64,128]{2,1,0:T(8,128)(2,1)} %bitcast.11), calls=%async_computation | async-start | bytes 524288 | tf_op jit(solution)/shard_map/all_to_all | solution.py:345
  132.8 0.2 select_reduce_fusion
  133.0 8.9 %all-to-all-done = bf16[16,64,128]{2,1,0:T(8,128)(2,1)S(1)} async-done(((bf16[16,64,128]{2,1,0:T(8,128)(2,1)}), bf16[16,64,128]{2,1,0:T(8,128)(2,1)S(1)}, u32[]{:S(2)}, u32[]{:S(2)}) %all-to-all-start) | async-done | bytes 262176 | tf_op jit(solution)/shard_map/all_to_all | solution.py:345
  141.9 5.1 %multiply_reduce_fusion = (f32[64]{0:T(128)S(1)}, f32[64,2048]{1,0:T(8,128)S(1)}) fusion(bf16[2048,2048]{1,0:T(8,128)(2,1)} %all-gather.2.cloned.1.call-done, bf16[64,2048]{1,0:T(8,128)(2,1)S(1)} %copy-done.9, bf16[16,64,128]{2,1,0:T(8,128)(2,1)S(1)} %all-to-all-done), kind=kOutput, calls=%fused_computation.35 | convolution fusion | flops 537395136 | bytes 9437440 | tf_op jit(solution)/shard_map/dot_general | solution.py:346
  146.9 0.8 convolution_convert_fusion
  147.7 31.3 %all_to_all.29 = bf16[32,16,2048]{2,1,0:T(8,128)(2,1)S(1)} all-to-all(bf16[32,16,2048]{2,1,0:T(8,128)(2,1)S(1)} %bitcast.81), channel_id=1, replica_groups=mesh['req'=8,'exp'=16] {'exp'}, dimensions={0} | all-to-all | bytes 4194304 | tf_op jit(solution)/shard_map/all_to_all | solution.py:364
  179.0 0.1 copy.65
  179.1 2.5 %copy.66 = bf16[2,256,2048]{1,2,0:T(8,128)(2,1)} copy(bf16[2,256,2048]{2,1,0:T(8,128)(2,1)S(1)} %bitcast.83) | data formatting | bytes 4194304 | tf_op jit(solution)/shard_map/reshape | solution.py:368
  181.6 13.9 %shard_map.147 = bf16[2,256,2048]{2,1,0:T(8,128)(2,1)} custom-call(bf16[2,2048,256]{2,1,0:T(8,128)(2,1)} %bitcast.85, bf16[2,704,2048]{2,1,0:T(8,128)(2,1)} %bitcast.87, bf16[2,704,2048]{2,1,0:T(8,128)(2,1)} %bitcast.88, bf16[2,704,2048]{2,1,0:T(8,128)(2,1)} %wd_ref.1), custom_call_target="tpu_custom_call" | custom-call | flops 4429185024 | bytes 21495808 | tf_op jit(solution)/shard_map/pallas_call | solution.py:193
  195.5 1.7 copy.67
  197.3 30.1 %all_to_all.30 = bf16[32,16,2048]{2,1,0:T(8,128)(2,1)S(1)} all-to-all(bf16[32,16,2048]{2,1,0:T(8,128)(2,1)S(1)} %bitcast.84), channel_id=1, replica_groups=mesh['req'=8,'exp'=16] {'exp'}, dimensions={0} | all-to-all | bytes 4194304 | tf_op jit(solution)/shard_map/all_to_all | solution.py:370
  227.4 1.2 fusion.10
  (43 shorter events, 0.2 us)
Async XLA Ops:
  6.5 77.8 %copy-start = (bf16[1024,128]{1,0:T(8,128)(2,1)S(1)}, bf16[1024,128]{1,0:T(8,128)(2,1)}, u32[]{:S(2)}) copy-start(bf16[1024,128]{1,0:T(8,128)(2,1)} %param.18) | copy-start | bytes 786436
  6.5 135.3 %all-gather.2.cloned.1.call-start = ((), (), s32[]{:S(2)}) async-start(), calls=%async_computation.3 | async-start | bytes 8912896 | tf_op jit(solution)/shard_map/all_gather | solution.py:344
  8.6 64.8 %copy-start.3 = (bf16[2,4,512,128]{3,2,1,0:T(8,128)(2,1)}, bf16[2,4,512,128]{3,2,1,0:T(8,128)(2,1)S(1)}, u32[]{:S(2)}) copy-start(bf16[2,4,512,128]{3,2,1,0:T(8,128)(2,1)S(1)} %pad_maximum_fusion.ka_ref.va_ref) | copy-start | bytes 3145732
  8.6 26.2 %collective-permute-start = (bf16[2,4,512,128]{3,2,1,0:T(8,128)(2,1)S(1)}, bf16[2,4,512,128]{3,2,1,0:T(8,128)(2,1)}, u32[]{:S(2)}, u32[]{:S(2)}) collective-permute-start(bf16[2,4,512,128]{3,2,1,0:T(8,128)(2,1)S(1)} %pad_maximum_fusion.ka_ref.va_ref), channel_id=1, source_target_pairs={{0,32},{16,48},{32,64},{48,80},{64,96},{80,112},{96,0},{112,16},{1... | collective-permute-start | bytes 3145736 | tf_op jit(solution)/shard_map/ppermute | solution.py:317
  10.2 48.2 %collective-permute-start.1 = (bf16[2,4,512,128]{3,2,1,0:T(8,128)(2,1)S(1)}, bf16[2,4,512,128]{3,2,1,0:T(8,128)(2,1)}, u32[]{:S(2)}, u32[]{:S(2)}) collective-permute-start(bf16[2,4,512,128]{3,2,1,0:T(8,128)(2,1)S(1)} %pad_maximum_fusion.ka_ref.va_ref), channel_id=1, source_target_pairs={{0,64},{16,80},{32,96},{48,112},{64,0},{80,16},{96,32},{112,48},{1... | collective-permute-start | bytes 3145736 | tf_op jit(solution)/shard_map/ppermute | solution.py:317
  12.9 47.9 %collective-permute-start.2 = (bf16[2,4,512,128]{3,2,1,0:T(8,128)(2,1)S(1)}, bf16[2,4,512,128]{3,2,1,0:T(8,128)(2,1)}, u32[]{:S(2)}, u32[]{:S(2)}) collective-permute-start(bf16[2,4,512,128]{3,2,1,0:T(8,128)(2,1)S(1)} %pad_maximum_fusion.ka_ref.va_ref), channel_id=1, source_target_pairs={{0,96},{16,112},{32,0},{48,16},{64,32},{80,48},{96,64},{112,80},{1... | collective-permute-start | bytes 3145736 | tf_op jit(solution)/shard_map/ppermute | solution.py:317
  14.4 87.3 %collective-permute-start.3 = (bf16[2,4,512,128]{3,2,1,0:T(8,128)(2,1)S(1)}, bf16[2,4,512,128]{3,2,1,0:T(8,128)(2,1)S(1)}, u32[]{:S(2)}, u32[]{:S(2)}) collective-permute-start(bf16[2,4,512,128]{3,2,1,0:T(8,128)(2,1)S(1)} %pad_maximum_fusion.ka_ref.va_ref), channel_id=1, source_target_pairs={{0,16},{16,0},{32,48},{48,32},{64,80},{80,64},{96,112},{112,96},{1... | collective-permute-start | bytes 3145736 | tf_op jit(solution)/shard_map/ppermute | solution.py:315
  60.8 12.5 %copy-start.2 = (bf16[1024,128]{1,0:T(8,128)(2,1)S(1)}, bf16[1024,128]{1,0:T(8,128)(2,1)}, u32[]{:S(2)}) copy-start(bf16[1024,128]{1,0:T(8,128)(2,1)} %param.17) | copy-start | bytes 786436
  63.3 38.4 %collective-permute-start.4 = (bf16[2,4,1536,128]{3,2,1,0:T(8,128)(2,1)}, bf16[2,4,1536,128]{3,2,1,0:T(8,128)(2,1)}, u32[]{:S(2)}, u32[]{:S(2)}) collective-permute-start(bf16[2,4,1536,128]{3,2,1,0:T(8,128)(2,1)} %constant_dynamic-update-slice_fusion.kb_ref.vb_ref), channel_id=1, source_target_pairs={{0,16},{16,0},{32,48},{48,32},{64,80},{80,64},{96,112},{112,96},{1... | collective-permute-start | bytes 9437192 | tf_op jit(solution)/shard_map/ppermute | solution.py:321
  73.4 10.3 %copy-start.12 = (bf16[64,4]{0,1:T(4,128)(2,1)S(1)}, bf16[64,4]{0,1:T(4,128)(2,1)}, u32[]{:S(2)}) copy-start(bf16[64,4]{0,1:T(4,128)(2,1)} %param.28) | copy-start | bytes 1540
  73.4 10.3 %copy-start.11 = (bf16[2048]{0:T(1024)(128)(2,1)S(1)}, bf16[2048]{0:T(1024)(128)(2,1)}, u32[]{:S(2)}) copy-start(bf16[2048]{0:T(1024)(128)(2,1)} %param.26) | copy-start | bytes 12292
  83.3 2.5 %copy-start.6 = (bf16[1408,128]{1,0:T(8,128)(2,1)}, bf16[1408,128]{1,0:T(8,128)(2,1)S(1)}, u32[]{:S(2)}) copy-start(bf16[1408,128]{1,0:T(8,128)(2,1)S(1)} %broadcast_select_fusion.q_ref) | copy-start | bytes 1081348
  85.9 2.5 %copy-start.4 = (f32[1408,1024]{0,1:T(8,128)}, f32[1408,1024]{0,1:T(8,128)S(1)}, u32[]{:S(2)}) copy-start(f32[1408,1024]{0,1:T(8,128)S(1)} %get-tuple-element.32) | copy-start | bytes 17301508
  101.7 13.4 %copy-start.7 = (f32[1408,128]{1,0:T(8,128)S(1)}, f32[1408,128]{1,0:T(8,128)}, u32[]{:S(2)}) copy-start(f32[1408,128]{1,0:T(8,128)} %get-tuple-element.13) | copy-start | bytes 2162692
  101.7 16.3 %copy-start.13 = (bf16[1024,128]{1,0:T(8,128)(2,1)S(1)}, bf16[1024,128]{1,0:T(8,128)(2,1)}, u32[]{:S(2)}) copy-start(bf16[1024,128]{1,0:T(8,128)(2,1)} %param.19) | copy-start | bytes 786436
  101.7 1.0 copy-start.5
  101.7 13.4 %copy-start.8 = (f32[1408,128]{1,0:T(8,128)S(1)}, f32[1408,128]{1,0:T(8,128)}, u32[]{:S(2)}) copy-start(f32[1408,128]{1,0:T(8,128)} %get-tuple-element.16) | copy-start | bytes 2162692
  117.9 14.8 %copy-start.10 = (s32[64,4]{0,1:T(4,128)S(1)}, s32[64,4]{0,1:T(4,128)}, u32[]{:S(2)}) copy-start(s32[64,4]{0,1:T(4,128)} %param.27) | copy-start | bytes 3076
  118.0 23.9 %copy-start.9 = (bf16[64,2048]{1,0:T(8,128)(2,1)S(1)}, bf16[64,2048]{1,0:T(8,128)(2,1)}, u32[]{:S(2)}) copy-start(bf16[64,2048]{1,0:T(8,128)(2,1)} %param.24) | copy-start | bytes 786436
  124.7 17.1 %all-to-all-start = ((bf16[16,64,128]{2,1,0:T(8,128)(2,1)}), bf16[16,64,128]{2,1,0:T(8,128)(2,1)S(1)}, u32[]{:S(2)}, u32[]{:S(2)}) async-start(bf16[16,64,128]{2,1,0:T(8,128)(2,1)} %bitcast.11), calls=%async_computation | async-start | bytes 524288 | tf_op jit(solution)/shard_map/all_to_all | solution.py:345
  181.6 46.9 %copy-start.1 = (bf16[1024,128]{1,0:T(8,128)(2,1)S(1)}, bf16[1024,128]{1,0:T(8,128)(2,1)}, u32[]{:S(2)}) copy-start(bf16[1024,128]{1,0:T(8,128)(2,1)} %param.18) | copy-start | bytes 786436
Sparse Core Ops, SparseCore 0:
  9.5 73.3 all-gather.1

commit v14 on v13

--- a/solution.py
+++ b/solution.py
@@ -120,9 +120,7 @@
     first_block = jnp.cumsum(blocks) - blocks
     rank = jnp.sum(jnp.where(member, jnp.cumsum(member.astype(jnp.int32), axis=0) - 1, 0), axis=1)
     padded_index = jnp.sum(jnp.where(member, first_block[None, :], 0), axis=1) * QUERY_BLOCK + rank
-    source = jnp.zeros((block_count * QUERY_BLOCK,), jnp.int32).at[padded_index].set(
-        jnp.arange(row_count, dtype=jnp.int32)
-    )
+    source = jnp.arange(block_count * QUERY_BLOCK, dtype=jnp.int32)[:, None] == padded_index[None, :]
     block_group = jnp.sum(
         (jnp.arange(block_count, dtype=jnp.int32)[:, None] >= first_block[None, 1:]).astype(jnp.int32),
         axis=1,
@@ -320,15 +318,17 @@
     ring_kv = jnp.concatenate(ring_parts, axis=2)
     forwarded_kv = lax.ppermute(ring_kv, "req", partner)
     padded_index, source, block_group = group_layout(tok_group)
-    padded_rows = jnp.take(queries, source, axis=0)
+    padded_rows = jnp.dot(
+        source.astype(jnp.bfloat16), queries, preferred_element_type=jnp.float32
+    ).astype(jnp.bfloat16)
     prefix_part = combine(
         attend_prefix_grouped(padded_rows, block_group, local_kv, ring_kv),
         attend_prefix_grouped(padded_rows, block_group, partner_kv, forwarded_kv),
     )
     suffix_part = attend_suffix_rows(
         padded_rows,
-        jnp.take(request, source, axis=0),
-        jnp.take(position, source, axis=0),
+        jnp.sum(jnp.where(source, request[None, :], 0), axis=1),
+        jnp.sum(jnp.where(source, position[None, :], 0), axis=1),
         keys,
         values,
         request,

time: 236 us -> 221 us (0.936)
  local copies, waits for them, and re-layouts: 35.6 us -> 12.7 us
  matrix products: 15.3 us -> 19.7 us
    gather x3 -> x0, local copies, waits for them, and re-layouts: 14.2 us -> none  [the longest x1 5.45 us: per_device(): jnp.take(request, source, axis=0)]
    scatter x1 -> x0, local copies, waits for them, and re-layouts: 4.5 us -> none  [group_layout(): jnp.zeros((block_count * QUERY_BLOCK,), jnp.int32).at[padded_index]]
    dot_general x0 -> x1, matrix products: none -> 3.53 us  [per_device(): jnp.dot(source.astype(jnp.bfloat16), queries, preferred_element_type=jnp....]
    unnamed x31 -> x25, local copies, waits for them, and re-layouts: 9.16 us -> 6.02 us
  transfers between devices with their start and end apart: 7 -> 7, of which waited for: 3 -> 3; matrix products, arithmetic and copies ran while one was open for 20% -> 14% of each run, Pallas kernels for 11% -> 11%
where the time goes in v14:
time: 221 us; the launch traced here: 220 us
  blocking collectives  61.3 us (28%)
  waiting for transfers between devices  47.7 us (22%)
  Pallas kernels  38.1 us (17%)
  matrix products  19.7 us (9%)
  starting transfers between devices  14.1 us (6%)
  between operations  13.7 us (6%)
  other arithmetic  12.9 us (6%)
  local copies, waits for them, and re-layouts  12.7 us (6%)
    ppermute x3, waiting for transfers between devices, per_device(): lax.ppermute(local_kv, 'req', [(i, (i + 2 * s) % req_count) for i in rang...  38.2 us
    all_to_all x1, blocking collectives, per_device(): lax.all_to_all(buffer, 'exp', split_axis=0, concat_axis=0, tiled=True)  31.2 us
    all_to_all x1, blocking collectives, per_device(): lax.all_to_all(expert_out.reshape(EXPERTS, slots, width), 'exp', split_ax...  30.2 us
    pallas_call x2, Pallas kernels, attend_prefix_grouped(): pl.pallas_call(prefix_kernel, grid_spec=pltpu.PrefetchScalarGridSpec(num_...  24.2 us
    pallas_call x1, Pallas kernels, expert_ffn(): pl.pallas_call(expert_kernel, grid=(exp_dev, inner // chunk), in_specs=[p...  13.9 us
    all_to_all x1, waiting for transfers between devices, per_device(): lax.all_to_all(attended, 'exp', split_axis=0, concat_axis=1, tiled=True)  8.84 us
    all_to_all x1, starting transfers between devices, per_device(): lax.all_to_all(attended, 'exp', split_axis=0, concat_axis=1, tiled=True)  8.08 us
    dot_general x1, matrix products, per_device(): jnp.dot(back.astype(jnp.bfloat16), padded_attended, preferred_element_typ...  6.57 us
  transfers between devices with their start and end apart: 7, of which 3 were waited for; matrix products, arithmetic and copies ran while one was open for 14% of the time, Pallas kernels for 11%

profile of v14, /device:TPU:0, one launch (start us, length us, event | category | flops | bytes accessed | tf_op | source)
XLA Modules:
  0.0 220.2 jit_solution(12864772118472391880)
XLA Ops:
  6.5 0.7 all-gather.2.cloned.1.call-update
  7.3 2.3 %pad_maximum_fusion.ka_ref.va_ref = bf16[2,4,512,128]{3,2,1,0:T(8,128)(2,1)} fusion(bf16[1,4,512,128]{3,2,1,0:T(8,128)(2,1)} %bitcast.88, bf16[1,4,512,128]{3,2,1,0:T(8,128)(2,1)} %bitcast.89), kind=kLoop, calls=%fused_computation.23 | loop fusion | flops 524288 | bytes 2097152 | tf_op jit(solution)/shard_map/stack | solution.py:311
  9.5 1.6 collective-permute-start
  11.1 2.7 %collective-permute-start.1 = (bf16[2,4,512,128]{3,2,1,0:T(8,128)(2,1)}, bf16[2,4,512,128]{3,2,1,0:T(8,128)(2,1)}, u32[]{:S(2)}, u32[]{:S(2)}) collective-permute-start(bf16[2,4,512,128]{3,2,1,0:T(8,128)(2,1)} %pad_maximum_fusion.ka_ref.va_ref), channel_id=1, source_target_pairs={{0,64},{16,80},{32,96},{48,112},{64,0},{80,16},{96,32},{112,48},{1... | collective-permute-start | bytes 3145736 | tf_op jit(solution)/shard_map/ppermute | solution.py:315
  13.8 1.4 collective-permute-start.2
  15.3 0.0 collective-permute-start.3
  15.3 0.8 copy.61
  16.0 0.1 eq.149
  16.1 0.1 eq.145
  16.2 0.8 reduce_window_sum.44
  17.1 0.7 subtract_bitcast_fusion
  17.7 0.1 convert_reduce_fusion.1
  17.8 0.8 select_reduce_fusion.3
  18.6 0.1 convert_reduce_fusion.2
  18.7 0.2 reduce-window.20
  18.9 1.1 reduce-window.21
  20.0 15.8 %collective-permute-done = bf16[2,4,512,128]{3,2,1,0:T(8,128)(2,1)} collective-permute-done((bf16[2,4,512,128]{3,2,1,0:T(8,128)(2,1)}, bf16[2,4,512,128]{3,2,1,0:T(8,128)(2,1)}, u32[]{:S(2)}, u32[]{:S(2)}) %collective-permute-start) | collective-permute-done | bytes 1048608 | tf_op jit(solution)/shard_map/ppermute | solution.py:315
  35.8 1.3 constant_dynamic-update-slice_fusion.2
  37.1 22.3 %collective-permute-done.1 = bf16[2,4,512,128]{3,2,1,0:T(8,128)(2,1)} collective-permute-done((bf16[2,4,512,128]{3,2,1,0:T(8,128)(2,1)}, bf16[2,4,512,128]{3,2,1,0:T(8,128)(2,1)}, u32[]{:S(2)}, u32[]{:S(2)}) %collective-permute-start.1) | collective-permute-done | bytes 1048608 | tf_op jit(solution)/shard_map/ppermute | solution.py:315
  59.5 1.4 constant_dynamic-update-slice_fusion.1
  60.8 0.0 collective-permute-done.2
  60.9 1.4 constant_dynamic-update-slice_fusion.kb_ref.vb_ref
  62.3 0.0 copy-start.1
  62.3 0.3 collective-permute-start.4
  62.6 0.2 slice_reduce_fusion.1
  62.8 0.2 reduce-window.24
  63.0 0.6 reduce-window.30
  63.6 0.2 slice_reduce_fusion
  63.8 0.1 add_bitcast_fusion.1
  63.9 0.1 select_reduce_fusion.5
  64.0 3.5 %fusion.12.q_ref = bf16[1408,128]{1,0:T(8,128)(2,1)} fusion(bf16[1024,128]{1,0:T(8,128)(2,1)} %param.15, s32[1024]{0:T(1024)S(1)} %multiply_add_fusion), kind=kOutput, calls=%fused_computation.16 | convolution fusion | flops 370720768 | bytes 626688 | tf_op jit(solution)/shard_map/dot_general | solution.py:321
  67.5 1.3 select_reduce_fusion.1
  68.9 0.1 fusion.38
  69.0 0.1 slice.29
  69.0 0.1 reduce_sum.139
  69.1 0.1 copy.64
  69.2 0.0 copy-done.7
  69.2 0.6 convert_reduce_fusion.3.block_group_ref
  69.8 2.5 %fusion.43 = (f32[1408]{0:T(1024)S(1)}, f32[1408,1024]{0,1:T(8,128)S(1)}) fusion(bf16[1408,128]{1,0:T(8,128)(2,1)} %fusion.12.q_ref, bf16[1024,128]{1,0:T(8,128)(2,1)S(1)} %copy-done, s32[1408]{0:T(1024)S(1)} %get-tuple-element.23, s32[1024]{0:T(1024)S(1)} %iota_subtract_fusion, s32[1408]{0:T(1024)S(1)} %get-tuple-element.22, s32[1024]{0:T(1024)S(1)} %convert_reduce_fusion.1), kind=kOutput, calls=%fused_computation.95 | convolution fusion | flops 377748096 | bytes 6414848 | tf_op jit(solution)/shard_map/dot_general | solution.py:260
  72.4 0.0 copy-done.1
  72.4 0.0 copy-start.2
  72.4 2.5 %copy-done.2 = f32[1408,1024]{0,1:T(8,128)} copy-done((f32[1408,1024]{0,1:T(8,128)}, f32[1408,1024]{0,1:T(8,128)S(1)}, u32[]{:S(2)}) %copy-start.2) | copy-done | bytes 5767192
  74.9 0.8 fusion.2
  75.7 12.1 %shard_map.145 = (f32[1408,128]{1,0:T(8,128)}, f32[1408,128]{1,0:T(8,128)}, f32[1408,128]{1,0:T(8,128)}) custom-call(s32[11]{0:T(128)} %convert_reduce_fusion.3.block_group_ref, bf16[1408,128]{1,0:T(8,128)(2,1)} %fusion.12.q_ref, bf16[2,4,512,128]{3,2,1,0:T(8,128)(2,1)} %pad_maximum_fusion.ka_ref.va_ref, ...), custom_call_target="tpu_custom_call" | custom-call | flops 1476395008 | bytes 6717440 | tf_op jit(solution)/shard_map/pallas_call | solution.py:145
  87.8 0.0 collective-permute-done.3.ka_ref.va_ref
  87.8 0.0 collective-permute-done.4.kb_ref.vb_ref
  87.8 0.0 copy-start.10
  87.9 12.2 %shard_map.146 = (f32[1408,128]{1,0:T(8,128)}, f32[1408,128]{1,0:T(8,128)}, f32[1408,128]{1,0:T(8,128)}) custom-call(s32[11]{0:T(128)} %convert_reduce_fusion.3.block_group_ref, bf16[1408,128]{1,0:T(8,128)(2,1)} %fusion.12.q_ref, bf16[2,4,512,128]{3,2,1,0:T(8,128)(2,1)} %collective-permute-done.3.ka_ref.va_ref, ...), custom_call_target="tpu_custom_call" | custom-call | flops 1476395008 | bytes 6717440 | tf_op jit(solution)/shard_map/pallas_call | solution.py:145
  100.1 2.9 %fusion.33 = (f32[1408]{0:T(1024)S(1)}, f32[1408]{0:T(1024)S(1)}, f32[1408]{0:T(1024)S(1)}, f32[1408]{0:T(1024)S(1)}, f32[1408]{0:T(1024)S(1)}) fusion(f32[1408,128]{1,0:T(8,128)S(1)} %copy-done.3, f32[1408]{0:T(1024)S(1)} %fusion.2, f32[1408]{0:T(1024)S(1)} %get-tuple-element.30, f32[1408,128]{1,0:T(8,128)} %get-tuple-element.13, ...), kind=kLoop, calls=%fused_computation.48 | loop fusion | flops 16896 | bytes 61952 | tf_op jit(solution)/shard_map/exp | solution.py:275
  102.9 0.0 copy-start.6
  103.0 0.0 copy-start.5
  103.0 6.6 %fusion.14 = bf16[1024,128]{1,0:T(8,128)(2,1)} fusion(s32[1024]{0:T(1024)S(1)} %multiply_add_fusion, f32[1408,128]{1,0:T(8,128)} %get-tuple-element.14, f32[1408,128]{1,0:T(8,128)S(1)} %copy-done.9, f32[1408]{0:T(1024)S(1)} %get-tuple-element.18, f32[1408]{0:T(1024)S(1)} %get-tuple-element.21, bf16[1024,128]{1,0:T(8,128)(2,1)S(1)} %copy-done.10, ...), kind=kOutput, calls=%fused_computation.20 | convolution fusion | flops 744095744 | bytes 7771136 | tf_op jit(solution)/shard_map/dot_general | solution.py:340
  109.6 8.1 %all-to-all-start = ((bf16[16,64,128]{2,1,0:T(8,128)(2,1)}), bf16[16,64,128]{2,1,0:T(8,128)(2,1)S(1)}, u32[]{:S(2)}, u32[]{:S(2)}) async-start(bf16[16,64,128]{2,1,0:T(8,128)(2,1)} %bitcast.9), calls=%async_computation | async-start | bytes 524288 | tf_op jit(solution)/shard_map/all_to_all | solution.py:345
  117.7 0.2 select_reduce_fusion.2
  117.8 8.8 %all-to-all-done = bf16[16,64,128]{2,1,0:T(8,128)(2,1)S(1)} async-done(((bf16[16,64,128]{2,1,0:T(8,128)(2,1)}), bf16[16,64,128]{2,1,0:T(8,128)(2,1)S(1)}, u32[]{:S(2)}, u32[]{:S(2)}) %all-to-all-start) | async-done | bytes 262176 | tf_op jit(solution)/shard_map/all_to_all | solution.py:345
  126.7 5.1 %multiply_reduce_fusion = (f32[64]{0:T(128)S(1)}, f32[64,2048]{1,0:T(8,128)S(1)}) fusion(bf16[2048,2048]{1,0:T(8,128)(2,1)} %all-gather.2.cloned.1.call-done, bf16[64,2048]{1,0:T(8,128)(2,1)S(1)} %copy-done.5, bf16[16,64,128]{2,1,0:T(8,128)(2,1)S(1)} %all-to-all-done), kind=kOutput, calls=%fused_computation.37 | convolution fusion | flops 537395136 | bytes 9437440 | tf_op jit(solution)/shard_map/dot_general | solution.py:346
  131.8 0.8 convolution_convert_fusion
  132.6 31.2 %all_to_all.29 = bf16[32,16,2048]{2,1,0:T(8,128)(2,1)S(1)} all-to-all(bf16[32,16,2048]{2,1,0:T(8,128)(2,1)S(1)} %bitcast.80), channel_id=1, replica_groups=mesh['req'=8,'exp'=16] {'exp'}, dimensions={0} | all-to-all | bytes 4194304 | tf_op jit(solution)/shard_map/all_to_all | solution.py:364
  163.8 0.1 copy.65
  163.9 2.5 %copy.66 = bf16[2,256,2048]{1,2,0:T(8,128)(2,1)} copy(bf16[2,256,2048]{2,1,0:T(8,128)(2,1)S(1)} %bitcast.82) | data formatting | bytes 4194304 | tf_op jit(solution)/shard_map/reshape | solution.py:368
  166.4 13.9 %shard_map.147 = bf16[2,256,2048]{2,1,0:T(8,128)(2,1)} custom-call(bf16[2,2048,256]{2,1,0:T(8,128)(2,1)} %bitcast.84, bf16[2,704,2048]{2,1,0:T(8,128)(2,1)} %bitcast.86, bf16[2,704,2048]{2,1,0:T(8,128)(2,1)} %bitcast.87, bf16[2,704,2048]{2,1,0:T(8,128)(2,1)} %wd_ref.1), custom_call_target="tpu_custom_call" | custom-call | flops 4429185024 | bytes 21495808 | tf_op jit(solution)/shard_map/pallas_call | solution.py:191
  180.3 1.7 copy.67
  182.0 30.2 %all_to_all.30 = bf16[32,16,2048]{2,1,0:T(8,128)(2,1)S(1)} all-to-all(bf16[32,16,2048]{2,1,0:T(8,128)(2,1)S(1)} %bitcast.83), channel_id=1, replica_groups=mesh['req'=8,'exp'=16] {'exp'}, dimensions={0} | all-to-all | bytes 4194304 | tf_op jit(solution)/shard_map/all_to_all | solution.py:370
  212.2 1.2 fusion.13
  (28 shorter events, 0.1 us)
Async XLA Ops:
  6.5 63.3 %copy-start = (bf16[1024,128]{1,0:T(8,128)(2,1)S(1)}, bf16[1024,128]{1,0:T(8,128)(2,1)}, u32[]{:S(2)}) copy-start(bf16[1024,128]{1,0:T(8,128)(2,1)} %param.16) | copy-start | bytes 786436
  6.5 120.1 %all-gather.2.cloned.1.call-start = ((), (), s32[]{:S(2)}) async-start(), calls=%async_computation.3 | async-start | bytes 8912896 | tf_op jit(solution)/shard_map/all_gather | solution.py:344
  9.5 26.3 %collective-permute-start = (bf16[2,4,512,128]{3,2,1,0:T(8,128)(2,1)}, bf16[2,4,512,128]{3,2,1,0:T(8,128)(2,1)}, u32[]{:S(2)}, u32[]{:S(2)}) collective-permute-start(bf16[2,4,512,128]{3,2,1,0:T(8,128)(2,1)} %pad_maximum_fusion.ka_ref.va_ref), channel_id=1, source_target_pairs={{0,32},{16,48},{32,64},{48,80},{64,96},{80,112},{96,0},{112,16},{1... | collective-permute-start | bytes 3145736 | tf_op jit(solution)/shard_map/ppermute | solution.py:315
  11.1 48.4 %collective-permute-start.1 = (bf16[2,4,512,128]{3,2,1,0:T(8,128)(2,1)}, bf16[2,4,512,128]{3,2,1,0:T(8,128)(2,1)}, u32[]{:S(2)}, u32[]{:S(2)}) collective-permute-start(bf16[2,4,512,128]{3,2,1,0:T(8,128)(2,1)} %pad_maximum_fusion.ka_ref.va_ref), channel_id=1, source_target_pairs={{0,64},{16,80},{32,96},{48,112},{64,0},{80,16},{96,32},{112,48},{1... | collective-permute-start | bytes 3145736 | tf_op jit(solution)/shard_map/ppermute | solution.py:315
  13.8 47.0 %collective-permute-start.2 = (bf16[2,4,512,128]{3,2,1,0:T(8,128)(2,1)}, bf16[2,4,512,128]{3,2,1,0:T(8,128)(2,1)}, u32[]{:S(2)}, u32[]{:S(2)}) collective-permute-start(bf16[2,4,512,128]{3,2,1,0:T(8,128)(2,1)} %pad_maximum_fusion.ka_ref.va_ref), channel_id=1, source_target_pairs={{0,96},{16,112},{32,0},{48,16},{64,32},{80,48},{96,64},{112,80},{1... | collective-permute-start | bytes 3145736 | tf_op jit(solution)/shard_map/ppermute | solution.py:315
  15.3 72.5 %collective-permute-start.3 = (bf16[2,4,512,128]{3,2,1,0:T(8,128)(2,1)}, bf16[2,4,512,128]{3,2,1,0:T(8,128)(2,1)}, u32[]{:S(2)}, u32[]{:S(2)}) collective-permute-start(bf16[2,4,512,128]{3,2,1,0:T(8,128)(2,1)} %pad_maximum_fusion.ka_ref.va_ref), channel_id=1, source_target_pairs={{0,16},{16,0},{32,48},{48,32},{64,80},{80,64},{96,112},{112,96},{1... | collective-permute-start | bytes 3145736 | tf_op jit(solution)/shard_map/ppermute | solution.py:313
  20.0 49.2 %copy-start.8 = (bf16[64,4]{0,1:T(4,128)(2,1)S(1)}, bf16[64,4]{0,1:T(4,128)(2,1)}, u32[]{:S(2)}) copy-start(bf16[64,4]{0,1:T(4,128)(2,1)} %param.26) | copy-start | bytes 1540
  20.0 49.2 %copy-start.7 = (bf16[2048]{0:T(1024)(128)(2,1)S(1)}, bf16[2048]{0:T(1024)(128)(2,1)}, u32[]{:S(2)}) copy-start(bf16[2048]{0:T(1024)(128)(2,1)} %param.24) | copy-start | bytes 12292
  62.3 10.1 %copy-start.1 = (bf16[2,4,1536,128]{3,2,1,0:T(8,128)(2,1)}, bf16[2,4,1536,128]{3,2,1,0:T(8,128)(2,1)S(1)}, u32[]{:S(2)}) copy-start(bf16[2,4,1536,128]{3,2,1,0:T(8,128)(2,1)S(1)} %constant_dynamic-update-slice_fusion.kb_ref.vb_ref) | copy-start | bytes 9437188
  62.3 25.5 %collective-permute-start.4 = (bf16[2,4,1536,128]{3,2,1,0:T(8,128)(2,1)S(1)}, bf16[2,4,1536,128]{3,2,1,0:T(8,128)(2,1)}, u32[]{:S(2)}, u32[]{:S(2)}) collective-permute-start(bf16[2,4,1536,128]{3,2,1,0:T(8,128)(2,1)S(1)} %constant_dynamic-update-slice_fusion.kb_ref.vb_ref), channel_id=1, source_target_pairs={{0,16},{16,0},{32,48},{48,32},{64,80},{80,64},{96,112},{112,96},{1... | collective-permute-start | bytes 9437192 | tf_op jit(solution)/shard_map/ppermute | solution.py:319
  72.4 2.5 %copy-start.2 = (f32[1408,1024]{0,1:T(8,128)}, f32[1408,1024]{0,1:T(8,128)S(1)}, u32[]{:S(2)}) copy-start(f32[1408,1024]{0,1:T(8,128)S(1)} %get-tuple-element.31) | copy-start | bytes 17301508
  87.8 12.2 %copy-start.3 = (f32[1408,128]{1,0:T(8,128)S(1)}, f32[1408,128]{1,0:T(8,128)}, u32[]{:S(2)}) copy-start(f32[1408,128]{1,0:T(8,128)} %get-tuple-element.12) | copy-start | bytes 2162692
  87.8 12.2 %copy-start.4 = (f32[1408,128]{1,0:T(8,128)S(1)}, f32[1408,128]{1,0:T(8,128)}, u32[]{:S(2)}) copy-start(f32[1408,128]{1,0:T(8,128)} %get-tuple-element.15) | copy-start | bytes 2162692
  87.8 15.1 %copy-start.9 = (f32[1408,128]{1,0:T(8,128)S(1)}, f32[1408,128]{1,0:T(8,128)}, u32[]{:S(2)}) copy-start(f32[1408,128]{1,0:T(8,128)} %get-tuple-element.11) | copy-start | bytes 2162692
  87.8 15.1 %copy-start.10 = (bf16[1024,128]{1,0:T(8,128)(2,1)S(1)}, bf16[1024,128]{1,0:T(8,128)(2,1)}, u32[]{:S(2)}) copy-start(bf16[1024,128]{1,0:T(8,128)(2,1)} %param.17) | copy-start | bytes 786436
  102.9 14.7 %copy-start.6 = (s32[64,4]{0,1:T(4,128)S(1)}, s32[64,4]{0,1:T(4,128)}, u32[]{:S(2)}) copy-start(s32[64,4]{0,1:T(4,128)} %param.25) | copy-start | bytes 3076
  103.0 23.7 %copy-start.5 = (bf16[64,2048]{1,0:T(8,128)(2,1)S(1)}, bf16[64,2048]{1,0:T(8,128)(2,1)}, u32[]{:S(2)}) copy-start(bf16[64,2048]{1,0:T(8,128)(2,1)} %param.22) | copy-start | bytes 786436
  109.6 17.1 %all-to-all-start = ((bf16[16,64,128]{2,1,0:T(8,128)(2,1)}), bf16[16,64,128]{2,1,0:T(8,128)(2,1)S(1)}, u32[]{:S(2)}, u32[]{:S(2)}) async-start(bf16[16,64,128]{2,1,0:T(8,128)(2,1)} %bitcast.9), calls=%async_computation | async-start | bytes 524288 | tf_op jit(solution)/shard_map/all_to_all | solution.py:345
Sparse Core Ops, SparseCore 0:
  9.5 73.3 all-gather.1

commit v15 on v14

--- a/solution.py
+++ b/solution.py
@@ -315,16 +315,10 @@
         lax.ppermute(local_kv, "req", [(i, (i + 2 * s) % req_count) for i in range(req_count)])
         for s in range(1, req_count // 2)
     ]
-    ring_kv = jnp.concatenate(ring_parts, axis=2)
-    forwarded_kv = lax.ppermute(ring_kv, "req", partner)
     padded_index, source, block_group = group_layout(tok_group)
     padded_rows = jnp.dot(
         source.astype(jnp.bfloat16), queries, preferred_element_type=jnp.float32
     ).astype(jnp.bfloat16)
-    prefix_part = combine(
-        attend_prefix_grouped(padded_rows, block_group, local_kv, ring_kv),
-        attend_prefix_grouped(padded_rows, block_group, partner_kv, forwarded_kv),
-    )
     suffix_part = attend_suffix_rows(
         padded_rows,
         jnp.sum(jnp.where(source, request[None, :], 0), axis=1),
@@ -333,6 +327,13 @@
         values,
         request,
         position,
+    )
+    ring_parts, suffix_part = lax.optimization_barrier((ring_parts, suffix_part))
+    ring_kv = jnp.concatenate(ring_parts, axis=2)
+    forwarded_kv = lax.ppermute(ring_kv, "req", partner)
+    prefix_part = combine(
+        attend_prefix_grouped(padded_rows, block_group, local_kv, ring_kv),
+        attend_prefix_grouped(padded_rows, block_group, partner_kv, forwarded_kv),
     )
     weighted, maxima, totals = combine(prefix_part, suffix_part)
     padded_attended = (weighted / totals).astype(jnp.bfloat16)

time: 221 us -> 212 us (0.959); the launches traced: 220 us -> 209 us
  waiting for transfers between devices: 47.7 us -> 40.2 us
  blocking collectives: 61.3 us -> 58.1 us
  matrix products: 19.7 us -> 16.9 us
    ppermute x3, waiting for transfers between devices: 38.2 us -> 31.1 us  [per_device(): lax.ppermute(local_kv, 'req', [(i, (i + 2 * s) % req_count) for i in rang...]
    dot_general x1, matrix products: 6.57 us -> 3.68 us  [per_device(): jnp.dot(back.astype(jnp.bfloat16), padded_attended, preferred_element_typ...]
    optimization_barrier x0 -> x2, local copies, waits for them, and re-layouts: none -> 2.32 us  [per_device(): lax.optimization_barrier((ring_parts, suffix_part))]
    unnamed x25 -> x33, local copies, waits for them, and re-layouts: 6.02 us -> 3.94 us
  transfers between devices with their start and end apart: 7 -> 7, of which waited for: 3 -> 3; matrix products, arithmetic and copies ran while one was open for 14% -> 14% of each run, Pallas kernels for 11% -> 12%
where the time goes in v15:
time: 212 us; the launch traced here: 209 us
  blocking collectives  58.1 us (27%)
  waiting for transfers between devices  40.2 us (19%)
  Pallas kernels  39.6 us (19%)
  matrix products  16.9 us (8%)
  starting transfers between devices  14.4 us (7%)
  between operations  13.7 us (6%)
  local copies, waits for them, and re-layouts  12.9 us (6%)
  other arithmetic  12.9 us (6%)
    ppermute x3, waiting for transfers between devices, per_device(): lax.ppermute(local_kv, 'req', [(i, (i + 2 * s) % req_count) for i in rang...  31.1 us
    all_to_all x1, blocking collectives, per_device(): lax.all_to_all(buffer, 'exp', split_axis=0, concat_axis=0, tiled=True)  29.7 us
    all_to_all x1, blocking collectives, per_device(): lax.all_to_all(expert_out.reshape(EXPERTS, slots, width), 'exp', split_ax...  28.3 us
    pallas_call x2, Pallas kernels, attend_prefix_grouped(): pl.pallas_call(prefix_kernel, grid_spec=pltpu.PrefetchScalarGridSpec(num_...  25.7 us
    pallas_call x1, Pallas kernels, expert_ffn(): pl.pallas_call(expert_kernel, grid=(exp_dev, inner // chunk), in_specs=[p...  13.9 us
    all_to_all x1, waiting for transfers between devices, per_device(): lax.all_to_all(attended, 'exp', split_axis=0, concat_axis=1, tiled=True)  8.29 us
    all_to_all x1, starting transfers between devices, per_device(): lax.all_to_all(attended, 'exp', split_axis=0, concat_axis=1, tiled=True)  8.04 us
    ppermute x3, starting transfers between devices, per_device(): lax.ppermute(local_kv, 'req', [(i, (i + 2 * s) % req_count) for i in rang...  5.74 us
  transfers between devices with their start and end apart: 7, of which 3 were waited for; matrix products, arithmetic and copies ran while one was open for 14% of the time, Pallas kernels for 12%

profile of v15, /device:TPU:0, one launch (start us, length us, event | category | flops | bytes accessed | tf_op | source)
XLA Modules:
  0.0 208.6 jit_solution(6258212804030511459)
XLA Ops:
  6.5 0.7 all-gather.2.cloned.1.call-update
  7.3 2.3 %pad_maximum_fusion.ka_ref.va_ref = bf16[2,4,512,128]{3,2,1,0:T(8,128)(2,1)} fusion(bf16[1,4,512,128]{3,2,1,0:T(8,128)(2,1)} %bitcast.88, bf16[1,4,512,128]{3,2,1,0:T(8,128)(2,1)} %bitcast.89), kind=kLoop, calls=%fused_computation.20 | loop fusion | flops 524288 | bytes 2097152 | tf_op jit(solution)/shard_map/stack | solution.py:311
  9.5 1.6 collective-permute-start
  11.1 2.7 %collective-permute-start.1 = (bf16[2,4,512,128]{3,2,1,0:T(8,128)(2,1)}, bf16[2,4,512,128]{3,2,1,0:T(8,128)(2,1)S(1)}, u32[]{:S(2)}, u32[]{:S(2)}) collective-permute-start(bf16[2,4,512,128]{3,2,1,0:T(8,128)(2,1)} %pad_maximum_fusion.ka_ref.va_ref), channel_id=1, source_target_pairs={{0,64},{16,80},{32,96},{48,112},{64,0},{80,16},{96,32},{112,48},{1... | collective-permute-start | bytes 3145736 | tf_op jit(solution)/shard_map/ppermute | solution.py:315
  13.8 1.4 collective-permute-start.2
  15.3 0.8 reduce_window_sum.44
  16.1 0.1 convert_reduce_fusion.1
  16.2 0.7 subtract_bitcast_fusion
  16.9 0.7 select_reduce_fusion.3
  17.6 0.1 convert_reduce_fusion.2
  17.7 0.2 reduce-window.20
  17.9 1.1 reduce-window.21
  19.1 0.2 slice_reduce_fusion.1
  19.3 0.2 reduce-window.24
  19.5 0.1 add_bitcast_fusion.1
  19.5 0.1 select_reduce_fusion.5
  19.7 2.8 %fusion.9.q_ref = bf16[1408,128]{1,0:T(8,128)(2,1)S(1)} fusion(bf16[1024,128]{1,0:T(8,128)(2,1)} %param.15, s32[1024]{0:T(1024)S(1)} %multiply_add_fusion), kind=kOutput, calls=%fused_computation.15 | convolution fusion | flops 370720768 | bytes 626688 | tf_op jit(solution)/shard_map/dot_general | solution.py:319
  22.5 1.4 select_reduce_fusion.1
  23.8 1.5 fusion.30
  25.4 0.0 copy-start.11
  25.4 0.8 fusion.2
  26.2 0.1 copy-done.11
  26.3 1.9 fusion.4
  28.2 7.5 %collective-permute-done = bf16[2,4,512,128]{3,2,1,0:T(8,128)(2,1)S(1)} collective-permute-done((bf16[2,4,512,128]{3,2,1,0:T(8,128)(2,1)}, bf16[2,4,512,128]{3,2,1,0:T(8,128)(2,1)S(1)}, u32[]{:S(2)}, u32[]{:S(2)}) %collective-permute-start) | collective-permute-done | bytes 1048608 | tf_op jit(solution)/shard_map/ppermute | solution.py:315
  35.7 23.6 %collective-permute-done.1 = bf16[2,4,512,128]{3,2,1,0:T(8,128)(2,1)S(1)} collective-permute-done((bf16[2,4,512,128]{3,2,1,0:T(8,128)(2,1)}, bf16[2,4,512,128]{3,2,1,0:T(8,128)(2,1)S(1)}, u32[]{:S(2)}, u32[]{:S(2)}) %collective-permute-start.1) | collective-permute-done | bytes 1048608 | tf_op jit(solution)/shard_map/ppermute | solution.py:315
  59.4 1.0 copy-done.7
  60.4 0.0 collective-permute-done.2
  60.4 1.3 constant_dynamic-update-slice_fusion.2
  61.7 1.4 constant_dynamic-update-slice_fusion.1
  63.1 1.4 constant_dynamic-update-slice_fusion.kb_ref.vb_ref
  64.5 0.1 collective-permute-start.4
  64.6 0.5 collective-permute-start.3
  65.1 0.1 slice.29
  65.2 0.1 copy.61
  65.3 0.1 eq.149
  65.4 0.1 eq.145
  65.5 0.6 reduce-window.30
  66.1 0.2 slice_reduce_fusion
  66.3 0.1 fusion.25
  66.4 0.1 reduce_sum.139
  66.5 0.1 copy.64
  66.6 0.0 copy-done.13
  66.6 0.6 convert_reduce_fusion.3.block_group_ref
  67.2 1.2 copy.57
  68.4 1.2 copy.59
  69.6 12.8 %shard_map.145 = (f32[1408,128]{1,0:T(8,128)}, f32[1408,128]{1,0:T(8,128)}, f32[1408,128]{1,0:T(8,128)}) custom-call(s32[11]{0:T(128)} %convert_reduce_fusion.3.block_group_ref, bf16[1408,128]{1,0:T(8,128)(2,1)} %copy-done.5, bf16[2,4,512,128]{3,2,1,0:T(8,128)(2,1)} %pad_maximum_fusion.ka_ref.va_ref, bf16[2,4,512,128]{3,2,1,0:T(8,128)(2,1)} %pad_maximum_fusion.ka_ref.va_ref, ...), custom_call_target="tpu_custom_call" | custom-call | flops 1476395008 | bytes 6717440 | tf_op jit(solution)/shard_map/pallas_call | solution.py:145
  82.3 0.0 collective-permute-done.3.ka_ref.va_ref
  82.3 0.0 collective-permute-done.4.kb_ref.vb_ref
  82.4 12.9 %shard_map.146 = (f32[1408,128]{1,0:T(8,128)}, f32[1408,128]{1,0:T(8,128)}, f32[1408,128]{1,0:T(8,128)}) custom-call(s32[11]{0:T(128)} %convert_reduce_fusion.3.block_group_ref, bf16[1408,128]{1,0:T(8,128)(2,1)} %copy-done.5, bf16[2,4,512,128]{3,2,1,0:T(8,128)(2,1)} %collective-permute-done.3.ka_ref.va_ref, ...), custom_call_target="tpu_custom_call" | custom-call | flops 1476395008 | bytes 6717440 | tf_op jit(solution)/shard_map/pallas_call | solution.py:145
  95.3 2.8 %fusion.18 = (f32[1408]{0:T(1024)S(1)}, f32[1408]{0:T(1024)S(1)}, f32[1408]{0:T(1024)S(1)}, f32[1408]{0:T(1024)S(1)}, f32[1408]{0:T(1024)S(1)}) fusion(f32[1408,128]{1,0:T(8,128)S(1)} %copy-done.9, f32[1408,1]{1,0:T(8,128)S(1)} %copy-done.4, f32[1408,1]{1,0:T(8,128)S(1)} %copy-done.3, f32[1408,128]{1,0:T(8,128)} %get-tuple-element.22, ...), kind=kLoop, calls=%fused_computation.39 | loop fusion | flops 16896 | bytes 61952 | tf_op jit(solution)/shard_map/exp | solution.py:275
  98.2 3.7 %fusion.11 = bf16[1024,128]{1,0:T(8,128)(2,1)} fusion(s32[1024]{0:T(1024)S(1)} %multiply_add_fusion, f32[1408,128]{1,0:T(8,128)S(1)} %copy-done.8, f32[1408,128]{1,0:T(8,128)} %get-tuple-element.23, f32[1408,128]{1,0:T(8,128)} %get-tuple-element.20, f32[1408]{0:T(1024)S(1)} %get-tuple-element.30, f32[1408]{0:T(1024)S(1)} %get-tuple-element.32, ...), kind=kOutput, calls=%fused_computation.19 | convolution fusion | flops 372113408 | bytes 2457088 | tf_op jit(solution)/shard_map/dot_general | solution.py:341
  101.9 8.0 %all-to-all-start = ((bf16[16,64,128]{2,1,0:T(8,128)(2,1)}), bf16[16,64,128]{2,1,0:T(8,128)(2,1)S(1)}, u32[]{:S(2)}, u32[]{:S(2)}) async-start(bf16[16,64,128]{2,1,0:T(8,128)(2,1)} %bitcast.9), calls=%async_computation | async-start | bytes 524288 | tf_op jit(solution)/shard_map/all_to_all | solution.py:346
  109.9 0.2 select_reduce_fusion.2
  110.1 8.3 %all-to-all-done = bf16[16,64,128]{2,1,0:T(8,128)(2,1)S(1)} async-done(((bf16[16,64,128]{2,1,0:T(8,128)(2,1)}), bf16[16,64,128]{2,1,0:T(8,128)(2,1)S(1)}, u32[]{:S(2)}, u32[]{:S(2)}) %all-to-all-start) | async-done | bytes 262176 | tf_op jit(solution)/shard_map/all_to_all | solution.py:346
  118.4 0.0 copy-done.10
  118.4 5.1 %multiply_reduce_fusion = (f32[64]{0:T(128)S(1)}, f32[64,2048]{1,0:T(8,128)S(1)}) fusion(bf16[2048,2048]{1,0:T(8,128)(2,1)} %all-gather.2.cloned.1.call-done, bf16[64,2048]{1,0:T(8,128)(2,1)S(1)} %copy-done.10, bf16[16,64,128]{2,1,0:T(8,128)(2,1)S(1)} %all-to-all-done), kind=kOutput, calls=%fused_computation.31 | convolution fusion | flops 537395136 | bytes 9437440 | tf_op jit(solution)/shard_map/dot_general | solution.py:347
  123.5 0.8 convolution_convert_fusion
  124.3 29.7 %all_to_all.29 = bf16[32,16,2048]{2,1,0:T(8,128)(2,1)S(1)} all-to-all(bf16[32,16,2048]{2,1,0:T(8,128)(2,1)S(1)} %bitcast.80), channel_id=1, replica_groups=mesh['req'=8,'exp'=16] {'exp'}, dimensions={0} | all-to-all | bytes 4194304 | tf_op jit(solution)/shard_map/all_to_all | solution.py:365
  154.0 0.1 copy.65
  154.1 2.5 %copy.66 = bf16[2,256,2048]{1,2,0:T(8,128)(2,1)} copy(bf16[2,256,2048]{2,1,0:T(8,128)(2,1)S(1)} %bitcast.82) | data formatting | bytes 4194304 | tf_op jit(solution)/shard_map/reshape | solution.py:369
  156.7 13.9 %shard_map.147 = bf16[2,256,2048]{2,1,0:T(8,128)(2,1)} custom-call(bf16[2,2048,256]{2,1,0:T(8,128)(2,1)} %bitcast.84, bf16[2,704,2048]{2,1,0:T(8,128)(2,1)} %bitcast.86, bf16[2,704,2048]{2,1,0:T(8,128)(2,1)} %bitcast.87, bf16[2,704,2048]{2,1,0:T(8,128)(2,1)} %wd_ref.1), custom_call_target="tpu_custom_call" | custom-call | flops 4429185024 | bytes 21495808 | tf_op jit(solution)/shard_map/pallas_call | solution.py:191
  170.5 1.7 copy.67
  172.3 28.3 %all_to_all.30 = bf16[32,16,2048]{2,1,0:T(8,128)(2,1)S(1)} all-to-all(bf16[32,16,2048]{2,1,0:T(8,128)(2,1)S(1)} %bitcast.83), channel_id=1, replica_groups=mesh['req'=8,'exp'=16] {'exp'}, dimensions={0} | all-to-all | bytes 4194304 | tf_op jit(solution)/shard_map/all_to_all | solution.py:371
  200.6 1.2 fusion.10
  (41 shorter events, 0.2 us)
Async XLA Ops:
  6.5 17.3 %copy-start = (bf16[1024,128]{1,0:T(8,128)(2,1)S(1)}, bf16[1024,128]{1,0:T(8,128)(2,1)}, u32[]{:S(2)}) copy-start(bf16[1024,128]{1,0:T(8,128)(2,1)} %param.16) | copy-start | bytes 786436
  6.5 111.9 %all-gather.2.cloned.1.call-start = ((), (), s32[]{:S(2)}) async-start(), calls=%async_computation.3 | async-start | bytes 8912896 | tf_op jit(solution)/shard_map/all_gather | solution.py:345
  9.5 26.2 %collective-permute-start = (bf16[2,4,512,128]{3,2,1,0:T(8,128)(2,1)}, bf16[2,4,512,128]{3,2,1,0:T(8,128)(2,1)S(1)}, u32[]{:S(2)}, u32[]{:S(2)}) collective-permute-start(bf16[2,4,512,128]{3,2,1,0:T(8,128)(2,1)} %pad_maximum_fusion.ka_ref.va_ref), channel_id=1, source_target_pairs={{0,32},{16,48},{32,64},{48,80},{64,96},{80,112},{96,0},{112,16},{1... | collective-permute-start | bytes 3145736 | tf_op jit(solution)/shard_map/ppermute | solution.py:315
  11.1 48.3 %collective-permute-start.1 = (bf16[2,4,512,128]{3,2,1,0:T(8,128)(2,1)}, bf16[2,4,512,128]{3,2,1,0:T(8,128)(2,1)S(1)}, u32[]{:S(2)}, u32[]{:S(2)}) collective-permute-start(bf16[2,4,512,128]{3,2,1,0:T(8,128)(2,1)} %pad_maximum_fusion.ka_ref.va_ref), channel_id=1, source_target_pairs={{0,64},{16,80},{32,96},{48,112},{64,0},{80,16},{96,32},{112,48},{1... | collective-permute-start | bytes 3145736 | tf_op jit(solution)/shard_map/ppermute | solution.py:315
  13.8 46.5 %collective-permute-start.2 = (bf16[2,4,512,128]{3,2,1,0:T(8,128)(2,1)}, bf16[2,4,512,128]{3,2,1,0:T(8,128)(2,1)}, u32[]{:S(2)}, u32[]{:S(2)}) collective-permute-start(bf16[2,4,512,128]{3,2,1,0:T(8,128)(2,1)} %pad_maximum_fusion.ka_ref.va_ref), channel_id=1, source_target_pairs={{0,96},{16,112},{32,0},{48,16},{64,32},{80,48},{96,64},{112,80},{1... | collective-permute-start | bytes 3145736 | tf_op jit(solution)/shard_map/ppermute | solution.py:315
  22.4 2.9 %copy-start.5 = (bf16[1408,128]{1,0:T(8,128)(2,1)}, bf16[1408,128]{1,0:T(8,128)(2,1)S(1)}, u32[]{:S(2)}) copy-start(bf16[1408,128]{1,0:T(8,128)(2,1)S(1)} %fusion.9.q_ref) | copy-start | bytes 1081348
  25.4 1.0 copy-start.11
  26.3 38.8 %copy-start.12 = (s32[64,4]{0,1:T(4,128)S(1)}, s32[64,4]{0,1:T(4,128)}, u32[]{:S(2)}) copy-start(s32[64,4]{0,1:T(4,128)} %param.25) | copy-start | bytes 3076
  26.3 40.3 %copy-start.14 = (bf16[64,4]{0,1:T(4,128)(2,1)S(1)}, bf16[64,4]{0,1:T(4,128)(2,1)}, u32[]{:S(2)}) copy-start(bf16[64,4]{0,1:T(4,128)(2,1)} %param.26) | copy-start | bytes 1540
  26.3 40.3 %copy-start.13 = (bf16[2048]{0:T(1024)(128)(2,1)S(1)}, bf16[2048]{0:T(1024)(128)(2,1)}, u32[]{:S(2)}) copy-start(bf16[2048]{0:T(1024)(128)(2,1)} %param.24) | copy-start | bytes 12292
  35.7 23.7 %copy-start.6 = (bf16[2,4,512,128]{3,2,1,0:T(8,128)(2,1)}, bf16[2,4,512,128]{3,2,1,0:T(8,128)(2,1)S(1)}, u32[]{:S(2)}) copy-start(bf16[2,4,512,128]{3,2,1,0:T(8,128)(2,1)S(1)} %collective-permute-done) | copy-start | bytes 3145732
  59.4 1.0 copy-start.7
  64.5 5.1 %copy-start.2 = (bf16[2,4,1536,128]{3,2,1,0:T(8,128)(2,1)}, bf16[2,4,1536,128]{3,2,1,0:T(8,128)(2,1)S(1)}, u32[]{:S(2)}) copy-start(bf16[2,4,1536,128]{3,2,1,0:T(8,128)(2,1)S(1)} %constant_dynamic-update-slice_fusion.kb_ref.vb_ref) | copy-start | bytes 9437188
  64.5 17.8 %collective-permute-start.4 = (bf16[2,4,1536,128]{3,2,1,0:T(8,128)(2,1)S(1)}, bf16[2,4,1536,128]{3,2,1,0:T(8,128)(2,1)}, u32[]{:S(2)}, u32[]{:S(2)}) collective-permute-start(bf16[2,4,1536,128]{3,2,1,0:T(8,128)(2,1)S(1)} %constant_dynamic-update-slice_fusion.kb_ref.vb_ref), channel_id=1, source_target_pairs={{0,16},{16,0},{32,48},{48,32},{64,80},{80,64},{96,112},{112,96},{1... | collective-permute-start | bytes 9437192 | tf_op jit(solution)/shard_map/ppermute | solution.py:333
  64.6 17.7 %collective-permute-start.3 = (bf16[2,4,512,128]{3,2,1,0:T(8,128)(2,1)}, bf16[2,4,512,128]{3,2,1,0:T(8,128)(2,1)}, u32[]{:S(2)}, u32[]{:S(2)}) collective-permute-start(bf16[2,4,512,128]{3,2,1,0:T(8,128)(2,1)} %pad_maximum_fusion.ka_ref.va_ref), channel_id=1, source_target_pairs={{0,16},{16,0},{32,48},{48,32},{64,80},{80,64},{96,112},{112,96},{1... | collective-permute-start | bytes 3145736 | tf_op jit(solution)/shard_map/ppermute | solution.py:313
  82.4 13.0 %copy-start.3 = (f32[1408,1]{1,0:T(8,128)S(1)}, f32[1408,1]{1,0:T(8,128)}, u32[]{:S(2)}) copy-start(f32[1408,1]{1,0:T(8,128)} %copy.57) | copy-start | bytes 16900
  82.4 13.0 %copy-start.4 = (f32[1408,1]{1,0:T(8,128)S(1)}, f32[1408,1]{1,0:T(8,128)}, u32[]{:S(2)}) copy-start(f32[1408,1]{1,0:T(8,128)} %copy.59) | copy-start | bytes 16900
  82.4 13.0 %copy-start.9 = (f32[1408,128]{1,0:T(8,128)S(1)}, f32[1408,128]{1,0:T(8,128)}, u32[]{:S(2)}) copy-start(f32[1408,128]{1,0:T(8,128)} %get-tuple-element.21) | copy-start | bytes 2162692
  82.4 15.8 %copy-start.8 = (f32[1408,128]{1,0:T(8,128)S(1)}, f32[1408,128]{1,0:T(8,128)}, u32[]{:S(2)}) copy-start(f32[1408,128]{1,0:T(8,128)} %fusion.4) | copy-start | bytes 2162692
  95.3 23.1 %copy-start.10 = (bf16[64,2048]{1,0:T(8,128)(2,1)S(1)}, bf16[64,2048]{1,0:T(8,128)(2,1)}, u32[]{:S(2)}) copy-start(bf16[64,2048]{1,0:T(8,128)(2,1)} %param.22) | copy-start | bytes 786436
  101.9 16.5 %all-to-all-start = ((bf16[16,64,128]{2,1,0:T(8,128)(2,1)}), bf16[16,64,128]{2,1,0:T(8,128)(2,1)S(1)}, u32[]{:S(2)}, u32[]{:S(2)}) async-start(bf16[16,64,128]{2,1,0:T(8,128)(2,1)} %bitcast.9), calls=%async_computation | async-start | bytes 524288 | tf_op jit(solution)/shard_map/all_to_all | solution.py:346
  156.7 45.1 %copy-start.1 = (bf16[1024,128]{1,0:T(8,128)(2,1)S(1)}, bf16[1024,128]{1,0:T(8,128)(2,1)}, u32[]{:S(2)}) copy-start(bf16[1024,128]{1,0:T(8,128)(2,1)} %param.16) | copy-start | bytes 786436
Sparse Core Ops, SparseCore 0:
  9.5 73.3 all-gather.1

commit v16 on v15

--- a/solution.py
+++ b/solution.py
@@ -89,7 +89,7 @@
     )
 
 
-QUERY_BLOCK = 128
+QUERY_BLOCK = 64
 KEY_BLOCK = 2048
 
 

time: 212 us -> 221 us (1.042)
  Pallas kernels: 39.6 us -> 48.6 us
    pallas_call x2, Pallas kernels: 25.7 us -> 34.7 us  [attend_prefix_grouped(): pl.pallas_call(prefix_kernel, grid_spec=pltpu.PrefetchScalarGridSpec(num_...]
  transfers between devices with their start and end apart: 7 -> 7, of which waited for: 3 -> 3; matrix products, arithmetic and copies ran while one was open for 14% -> 13% of each run, Pallas kernels for 12% -> 16%
where the time goes in v16:
time: 221 us; the launch traced here: 217 us
  blocking collectives  58.5 us (26%)
  Pallas kernels  48.6 us (22%)
  waiting for transfers between devices  41 us (19%)
  matrix products  15.7 us (7%)
  starting transfers between devices  14.3 us (6%)
  between operations  13.8 us (6%)
  other arithmetic  12.9 us (6%)
  local copies, waits for them, and re-layouts  12.7 us (6%)
    pallas_call x2, Pallas kernels, attend_prefix_grouped(): pl.pallas_call(prefix_kernel, grid_spec=pltpu.PrefetchScalarGridSpec(num_...  34.7 us
    ppermute x3, waiting for transfers between devices, per_device(): lax.ppermute(local_kv, 'req', [(i, (i + 2 * s) % req_count) for i in rang...  32 us
    all_to_all x1, blocking collectives, per_device(): lax.all_to_all(buffer, 'exp', split_axis=0, concat_axis=0, tiled=True)  30 us
    all_to_all x1, blocking collectives, per_device(): lax.all_to_all(expert_out.reshape(EXPERTS, slots, width), 'exp', split_ax...  28.6 us
    pallas_call x1, Pallas kernels, expert_ffn(): pl.pallas_call(expert_kernel, grid=(exp_dev, inner // chunk), in_specs=[p...  13.8 us
    all_to_all x1, waiting for transfers between devices, per_device(): lax.all_to_all(attended, 'exp', split_axis=0, concat_axis=1, tiled=True)  8.34 us
    all_to_all x1, starting transfers between devices, per_device(): lax.all_to_all(attended, 'exp', split_axis=0, concat_axis=1, tiled=True)  7.98 us
    ppermute x3, starting transfers between devices, per_device(): lax.ppermute(local_kv, 'req', [(i, (i + 2 * s) % req_count) for i in rang...  5.74 us
  transfers between devices with their start and end apart: 7, of which 3 were waited for; matrix products, arithmetic and copies ran while one was open for 13% of the time, Pallas kernels for 16%

profile of v16, /device:TPU:0, one launch (start us, length us, event | category | flops | bytes accessed | tf_op | source)
XLA Modules:
  0.0 217.5 jit_solution(37305312203176881)
XLA Ops:
  6.5 0.7 all-gather.2.cloned.1.call-update
  7.3 2.3 %pad_maximum_fusion.ka_ref.va_ref = bf16[2,4,512,128]{3,2,1,0:T(8,128)(2,1)} fusion(bf16[1,4,512,128]{3,2,1,0:T(8,128)(2,1)} %bitcast.88, bf16[1,4,512,128]{3,2,1,0:T(8,128)(2,1)} %bitcast.89), kind=kLoop, calls=%fused_computation.20 | loop fusion | flops 524288 | bytes 2097152 | tf_op jit(solution)/shard_map/stack | solution.py:311
  9.5 1.6 collective-permute-start
  11.1 2.7 %collective-permute-start.1 = (bf16[2,4,512,128]{3,2,1,0:T(8,128)(2,1)}, bf16[2,4,512,128]{3,2,1,0:T(8,128)(2,1)S(1)}, u32[]{:S(2)}, u32[]{:S(2)}) collective-permute-start(bf16[2,4,512,128]{3,2,1,0:T(8,128)(2,1)} %pad_maximum_fusion.ka_ref.va_ref), channel_id=1, source_target_pairs={{0,64},{16,80},{32,96},{48,112},{64,0},{80,16},{96,32},{112,48},{1... | collective-permute-start | bytes 3145736 | tf_op jit(solution)/shard_map/ppermute | solution.py:315
  13.8 1.4 collective-permute-start.2
  15.3 0.8 reduce_window_sum.44
  16.1 0.1 convert_reduce_fusion.1
  16.2 0.7 subtract_bitcast_fusion
  16.9 0.7 select_reduce_fusion.3
  17.6 0.1 convert_reduce_fusion.2
  17.7 0.2 reduce-window.20
  17.9 1.1 reduce-window.21
  19.1 0.2 slice_reduce_fusion.1
  19.3 0.2 reduce-window.24
  19.5 0.1 add_bitcast_fusion.1
  19.5 0.1 select_reduce_fusion.5
  19.7 1.9 fusion.9.q_ref
  21.6 1.5 select_reduce_fusion.1
  23.0 0.0 copy-start.12
  23.1 1.4 fusion.30
  24.5 1.1 fusion.2
  25.6 0.0 copy-start.13
  25.6 0.0 copy-start.15
  25.7 0.0 copy-start.14
  25.7 1.7 fusion.5
  27.4 8.3 %collective-permute-done = bf16[2,4,512,128]{3,2,1,0:T(8,128)(2,1)S(1)} collective-permute-done((bf16[2,4,512,128]{3,2,1,0:T(8,128)(2,1)}, bf16[2,4,512,128]{3,2,1,0:T(8,128)(2,1)S(1)}, u32[]{:S(2)}, u32[]{:S(2)}) %collective-permute-start) | collective-permute-done | bytes 1048608 | tf_op jit(solution)/shard_map/ppermute | solution.py:315
  35.7 23.6 %collective-permute-done.1 = bf16[2,4,512,128]{3,2,1,0:T(8,128)(2,1)S(1)} collective-permute-done((bf16[2,4,512,128]{3,2,1,0:T(8,128)(2,1)}, bf16[2,4,512,128]{3,2,1,0:T(8,128)(2,1)S(1)}, u32[]{:S(2)}, u32[]{:S(2)}) %collective-permute-start.1) | collective-permute-done | bytes 1048608 | tf_op jit(solution)/shard_map/ppermute | solution.py:315
  59.4 1.0 copy-done.7
  60.4 1.3 constant_dynamic-update-slice_fusion.2
  61.7 1.4 constant_dynamic-update-slice_fusion.1
  63.1 1.4 constant_dynamic-update-slice_fusion.kb_ref.vb_ref
  64.5 0.1 collective-permute-start.4
  64.6 0.5 collective-permute-start.3
  65.1 0.1 slice.29
  65.2 0.1 copy.61
  65.3 0.1 eq.149
  65.4 0.1 eq.145
  65.5 0.6 reduce-window.30
  66.1 0.2 slice_reduce_fusion
  66.3 0.1 fusion.25
  66.4 0.1 reduce_sum.139
  66.5 0.1 copy.64
  66.6 0.0 copy-done.14
  66.6 0.6 convert_reduce_fusion.3.block_group_ref
  67.2 1.1 copy.57
  68.3 1.1 copy.59
  69.4 17.3 %shard_map.145 = (f32[1216,128]{1,0:T(8,128)}, f32[1216,128]{1,0:T(8,128)}, f32[1216,128]{1,0:T(8,128)}) custom-call(s32[19]{0:T(128)} %convert_reduce_fusion.3.block_group_ref, bf16[1216,128]{1,0:T(8,128)(2,1)} %copy-done.5, bf16[2,4,512,128]{3,2,1,0:T(8,128)(2,1)} %pad_maximum_fusion.ka_ref.va_ref, bf16[2,4,512,128]{3,2,1,0:T(8,128)(2,1)} %pad_maximum_fusion.ka_ref.va_ref, ...), custom_call_target="tpu_custom_call" | custom-call | flops 1275068416 | bytes 6373376 | tf_op jit(solution)/shard_map/pallas_call | solution.py:145
  86.7 0.0 collective-permute-done.3.ka_ref.va_ref
  86.8 17.4 %shard_map.146 = (f32[1216,128]{1,0:T(8,128)}, f32[1216,128]{1,0:T(8,128)}, f32[1216,128]{1,0:T(8,128)}) custom-call(s32[19]{0:T(128)} %convert_reduce_fusion.3.block_group_ref, bf16[1216,128]{1,0:T(8,128)(2,1)} %copy-done.5, bf16[2,4,512,128]{3,2,1,0:T(8,128)(2,1)} %collective-permute-done.3.ka_ref.va_ref, ...), custom_call_target="tpu_custom_call" | custom-call | flops 1275068416 | bytes 6373376 | tf_op jit(solution)/shard_map/pallas_call | solution.py:145
  104.3 2.4 %fusion.18 = (f32[1216]{0:T(1024)S(1)}, f32[1216]{0:T(1024)S(1)}, f32[1216]{0:T(1024)S(1)}, f32[1216]{0:T(1024)S(1)}, f32[1216]{0:T(1024)S(1)}) fusion(f32[1216,128]{1,0:T(8,128)S(1)} %copy-done.8, f32[1216,1]{1,0:T(8,128)S(1)} %copy-done.4, f32[1216,1]{1,0:T(8,128)S(1)} %copy-done.3, f32[1216,128]{1,0:T(8,128)} %get-tuple-element.22, ...), kind=kLoop, calls=%fused_computation.39 | loop fusion | flops 14592 | bytes 53504 | tf_op jit(solution)/shard_map/exp | solution.py:275
  106.6 0.0 copy-start.11
  106.7 3.6 %fusion.11 = bf16[1024,128]{1,0:T(8,128)(2,1)} fusion(s32[1024]{0:T(1024)S(1)} %multiply_add_fusion, f32[1216,128]{1,0:T(8,128)S(1)} %copy-done.10, f32[1216,128]{1,0:T(8,128)} %get-tuple-element.23, f32[1216,128]{1,0:T(8,128)} %get-tuple-element.20, f32[1216]{0:T(1024)S(1)} %get-tuple-element.30, f32[1216]{0:T(1024)S(1)} %get-tuple-element.32, ...), kind=kOutput, calls=%fused_computation.19 | convolution fusion | flops 321388544 | bytes 2158336 | tf_op jit(solution)/shard_map/dot_general | solution.py:341
  110.2 8.0 %all-to-all-start = ((bf16[16,64,128]{2,1,0:T(8,128)(2,1)}), bf16[16,64,128]{2,1,0:T(8,128)(2,1)S(1)}, u32[]{:S(2)}, u32[]{:S(2)}) async-start(bf16[16,64,128]{2,1,0:T(8,128)(2,1)} %bitcast.9), calls=%async_computation | async-start | bytes 524288 | tf_op jit(solution)/shard_map/all_to_all | solution.py:346
  118.3 0.2 select_reduce_fusion.2
  118.4 8.3 %all-to-all-done = bf16[16,64,128]{2,1,0:T(8,128)(2,1)S(1)} async-done(((bf16[16,64,128]{2,1,0:T(8,128)(2,1)}), bf16[16,64,128]{2,1,0:T(8,128)(2,1)S(1)}, u32[]{:S(2)}, u32[]{:S(2)}) %all-to-all-start) | async-done | bytes 262176 | tf_op jit(solution)/shard_map/all_to_all | solution.py:346
  126.8 5.1 %multiply_reduce_fusion = (f32[64]{0:T(128)S(1)}, f32[64,2048]{1,0:T(8,128)S(1)}) fusion(bf16[2048,2048]{1,0:T(8,128)(2,1)} %all-gather.2.cloned.1.call-done, bf16[64,2048]{1,0:T(8,128)(2,1)S(1)} %copy-done.11, bf16[16,64,128]{2,1,0:T(8,128)(2,1)S(1)} %all-to-all-done), kind=kOutput, calls=%fused_computation.31 | convolution fusion | flops 537395136 | bytes 9437440 | tf_op jit(solution)/shard_map/dot_general | solution.py:347
  131.8 0.8 convolution_convert_fusion
  132.6 30.0 %all_to_all.29 = bf16[32,16,2048]{2,1,0:T(8,128)(2,1)S(1)} all-to-all(bf16[32,16,2048]{2,1,0:T(8,128)(2,1)S(1)} %bitcast.80), channel_id=1, replica_groups=mesh['req'=8,'exp'=16] {'exp'}, dimensions={0} | all-to-all | bytes 4194304 | tf_op jit(solution)/shard_map/all_to_all | solution.py:365
  162.6 0.1 copy.65
  162.7 2.5 %copy.66 = bf16[2,256,2048]{1,2,0:T(8,128)(2,1)} copy(bf16[2,256,2048]{2,1,0:T(8,128)(2,1)S(1)} %bitcast.82) | data formatting | bytes 4194304 | tf_op jit(solution)/shard_map/reshape | solution.py:369
  165.2 13.8 %shard_map.147 = bf16[2,256,2048]{2,1,0:T(8,128)(2,1)} custom-call(bf16[2,2048,256]{2,1,0:T(8,128)(2,1)} %bitcast.84, bf16[2,704,2048]{2,1,0:T(8,128)(2,1)} %bitcast.86, bf16[2,704,2048]{2,1,0:T(8,128)(2,1)} %bitcast.87, bf16[2,704,2048]{2,1,0:T(8,128)(2,1)} %wd_ref.1), custom_call_target="tpu_custom_call" | custom-call | flops 4429185024 | bytes 21495808 | tf_op jit(solution)/shard_map/pallas_call | solution.py:191
  179.1 1.8 copy.67
  180.9 28.6 %all_to_all.30 = bf16[32,16,2048]{2,1,0:T(8,128)(2,1)S(1)} all-to-all(bf16[32,16,2048]{2,1,0:T(8,128)(2,1)S(1)} %bitcast.83), channel_id=1, replica_groups=mesh['req'=8,'exp'=16] {'exp'}, dimensions={0} | all-to-all | bytes 4194304 | tf_op jit(solution)/shard_map/all_to_all | solution.py:371
  209.5 1.2 fusion.10
  (43 shorter events, 0.2 us)
Async XLA Ops:
  6.5 16.5 %copy-start = (bf16[1024,128]{1,0:T(8,128)(2,1)S(1)}, bf16[1024,128]{1,0:T(8,128)(2,1)}, u32[]{:S(2)}) copy-start(bf16[1024,128]{1,0:T(8,128)(2,1)} %param.16) | copy-start | bytes 786436
  6.5 120.2 %all-gather.2.cloned.1.call-start = ((), (), s32[]{:S(2)}) async-start(), calls=%async_computation.3 | async-start | bytes 8912896 | tf_op jit(solution)/shard_map/all_gather | solution.py:345
  9.5 26.2 %collective-permute-start = (bf16[2,4,512,128]{3,2,1,0:T(8,128)(2,1)}, bf16[2,4,512,128]{3,2,1,0:T(8,128)(2,1)S(1)}, u32[]{:S(2)}, u32[]{:S(2)}) collective-permute-start(bf16[2,4,512,128]{3,2,1,0:T(8,128)(2,1)} %pad_maximum_fusion.ka_ref.va_ref), channel_id=1, source_target_pairs={{0,32},{16,48},{32,64},{48,80},{64,96},{80,112},{96,0},{112,16},{1... | collective-permute-start | bytes 3145736 | tf_op jit(solution)/shard_map/ppermute | solution.py:315
  11.1 48.3 %collective-permute-start.1 = (bf16[2,4,512,128]{3,2,1,0:T(8,128)(2,1)}, bf16[2,4,512,128]{3,2,1,0:T(8,128)(2,1)S(1)}, u32[]{:S(2)}, u32[]{:S(2)}) collective-permute-start(bf16[2,4,512,128]{3,2,1,0:T(8,128)(2,1)} %pad_maximum_fusion.ka_ref.va_ref), channel_id=1, source_target_pairs={{0,64},{16,80},{32,96},{48,112},{64,0},{80,16},{96,32},{112,48},{1... | collective-permute-start | bytes 3145736 | tf_op jit(solution)/shard_map/ppermute | solution.py:315
  13.8 46.5 %collective-permute-start.2 = (bf16[2,4,512,128]{3,2,1,0:T(8,128)(2,1)}, bf16[2,4,512,128]{3,2,1,0:T(8,128)(2,1)}, u32[]{:S(2)}, u32[]{:S(2)}) collective-permute-start(bf16[2,4,512,128]{3,2,1,0:T(8,128)(2,1)} %pad_maximum_fusion.ka_ref.va_ref), channel_id=1, source_target_pairs={{0,96},{16,112},{32,0},{48,16},{64,32},{80,48},{96,64},{112,80},{1... | collective-permute-start | bytes 3145736 | tf_op jit(solution)/shard_map/ppermute | solution.py:315
  21.6 1.5 copy-start.5
  23.0 2.6 %copy-start.12 = (bf16[1024,128]{1,0:T(8,128)(2,1)S(1)}, bf16[1024,128]{1,0:T(8,128)(2,1)}, u32[]{:S(2)}) copy-start(bf16[1024,128]{1,0:T(8,128)(2,1)} %param.17) | copy-start | bytes 786436
  25.6 39.5 %copy-start.13 = (s32[64,4]{0,1:T(4,128)S(1)}, s32[64,4]{0,1:T(4,128)}, u32[]{:S(2)}) copy-start(s32[64,4]{0,1:T(4,128)} %param.25) | copy-start | bytes 3076
  25.6 41.0 %copy-start.15 = (bf16[64,4]{0,1:T(4,128)(2,1)S(1)}, bf16[64,4]{0,1:T(4,128)(2,1)}, u32[]{:S(2)}) copy-start(bf16[64,4]{0,1:T(4,128)(2,1)} %param.26) | copy-start | bytes 1540
  25.7 41.0 %copy-start.14 = (bf16[2048]{0:T(1024)(128)(2,1)S(1)}, bf16[2048]{0:T(1024)(128)(2,1)}, u32[]{:S(2)}) copy-start(bf16[2048]{0:T(1024)(128)(2,1)} %param.24) | copy-start | bytes 12292
  35.7 23.7 %copy-start.6 = (bf16[2,4,512,128]{3,2,1,0:T(8,128)(2,1)}, bf16[2,4,512,128]{3,2,1,0:T(8,128)(2,1)S(1)}, u32[]{:S(2)}) copy-start(bf16[2,4,512,128]{3,2,1,0:T(8,128)(2,1)S(1)} %collective-permute-done) | copy-start | bytes 3145732
  59.4 1.0 copy-start.7
  64.5 4.9 %copy-start.2 = (bf16[2,4,1536,128]{3,2,1,0:T(8,128)(2,1)}, bf16[2,4,1536,128]{3,2,1,0:T(8,128)(2,1)S(1)}, u32[]{:S(2)}) copy-start(bf16[2,4,1536,128]{3,2,1,0:T(8,128)(2,1)S(1)} %constant_dynamic-update-slice_fusion.kb_ref.vb_ref) | copy-start | bytes 9437188
  64.5 22.2 %collective-permute-start.4 = (bf16[2,4,1536,128]{3,2,1,0:T(8,128)(2,1)S(1)}, bf16[2,4,1536,128]{3,2,1,0:T(8,128)(2,1)}, u32[]{:S(2)}, u32[]{:S(2)}) collective-permute-start(bf16[2,4,1536,128]{3,2,1,0:T(8,128)(2,1)S(1)} %constant_dynamic-update-slice_fusion.kb_ref.vb_ref), channel_id=1, source_target_pairs={{0,16},{16,0},{32,48},{48,32},{64,80},{80,64},{96,112},{112,96},{1... | collective-permute-start | bytes 9437192 | tf_op jit(solution)/shard_map/ppermute | solution.py:333
  64.6 22.1 %collective-permute-start.3 = (bf16[2,4,512,128]{3,2,1,0:T(8,128)(2,1)}, bf16[2,4,512,128]{3,2,1,0:T(8,128)(2,1)}, u32[]{:S(2)}, u32[]{:S(2)}) collective-permute-start(bf16[2,4,512,128]{3,2,1,0:T(8,128)(2,1)} %pad_maximum_fusion.ka_ref.va_ref), channel_id=1, source_target_pairs={{0,16},{16,0},{32,48},{48,32},{64,80},{80,64},{96,112},{112,96},{1... | collective-permute-start | bytes 3145736 | tf_op jit(solution)/shard_map/ppermute | solution.py:313
  86.8 17.5 %copy-start.3 = (f32[1216,1]{1,0:T(8,128)S(1)}, f32[1216,1]{1,0:T(8,128)}, u32[]{:S(2)}) copy-start(f32[1216,1]{1,0:T(8,128)} %copy.57) | copy-start | bytes 14596
  86.8 17.5 %copy-start.4 = (f32[1216,1]{1,0:T(8,128)S(1)}, f32[1216,1]{1,0:T(8,128)}, u32[]{:S(2)}) copy-start(f32[1216,1]{1,0:T(8,128)} %copy.59) | copy-start | bytes 14596
  86.8 17.5 %copy-start.8 = (f32[1216,128]{1,0:T(8,128)S(1)}, f32[1216,128]{1,0:T(8,128)}, u32[]{:S(2)}) copy-start(f32[1216,128]{1,0:T(8,128)} %get-tuple-element.21) | copy-start | bytes 1867780
  86.8 17.5 %copy-start.9 = (f32[1216,128]{1,0:T(8,128)S(1)}, f32[1216,128]{1,0:T(8,128)}, u32[]{:S(2)}) copy-start(f32[1216,128]{1,0:T(8,128)} %get-tuple-element.26) | copy-start | bytes 1867780
  86.8 19.9 %copy-start.10 = (f32[1216,128]{1,0:T(8,128)S(1)}, f32[1216,128]{1,0:T(8,128)}, u32[]{:S(2)}) copy-start(f32[1216,128]{1,0:T(8,128)} %fusion.5) | copy-start | bytes 1867780
  106.6 20.1 %copy-start.11 = (bf16[64,2048]{1,0:T(8,128)(2,1)S(1)}, bf16[64,2048]{1,0:T(8,128)(2,1)}, u32[]{:S(2)}) copy-start(bf16[64,2048]{1,0:T(8,128)(2,1)} %param.22) | copy-start | bytes 786436
  110.2 16.5 %all-to-all-start = ((bf16[16,64,128]{2,1,0:T(8,128)(2,1)}), bf16[16,64,128]{2,1,0:T(8,128)(2,1)S(1)}, u32[]{:S(2)}, u32[]{:S(2)}) async-start(bf16[16,64,128]{2,1,0:T(8,128)(2,1)} %bitcast.9), calls=%async_computation | async-start | bytes 524288 | tf_op jit(solution)/shard_map/all_to_all | solution.py:346
  179.1 31.6 %copy-start.1 = (bf16[1024,128]{1,0:T(8,128)(2,1)S(1)}, bf16[1024,128]{1,0:T(8,128)(2,1)}, u32[]{:S(2)}) copy-start(bf16[1024,128]{1,0:T(8,128)(2,1)} %param.16) | copy-start | bytes 786436
Sparse Core Ops, SparseCore 0:
  9.5 73.3 all-gather.1

commit v17 on v16

--- a/solution.py
+++ b/solution.py
@@ -89,7 +89,7 @@
     )
 
 
-QUERY_BLOCK = 64
+QUERY_BLOCK = 256
 KEY_BLOCK = 2048
 
 

time: 221 us -> 211 us (0.955); the launches traced: 217 us -> 210 us
  Pallas kernels: 48.6 us -> 36.5 us
  matrix products: 15.7 us -> 18.6 us
  blocking collectives: 58.5 us -> 60.9 us
    pallas_call x2, Pallas kernels: 34.7 us -> 22.6 us  [attend_prefix_grouped(): pl.pallas_call(prefix_kernel, grid_spec=pltpu.PrefetchScalarGridSpec(num_...]
    ppermute x3, waiting for transfers between devices: 32 us -> 29.6 us  [per_device(): lax.ppermute(local_kv, 'req', [(i, (i + 2 * s) % req_count) for i in rang...]
  transfers between devices with their start and end apart: 7 -> 7, of which waited for: 3 -> 3; matrix products, arithmetic and copies ran while one was open for 13% -> 16% of each run, Pallas kernels for 16% -> 11%
where the time goes in v17:
time: 211 us; the launch traced here: 210 us
  blocking collectives  60.9 us (29%)
  waiting for transfers between devices  39 us (18%)
  Pallas kernels  36.5 us (17%)
  matrix products  18.6 us (9%)
  starting transfers between devices  14.4 us (7%)
  other arithmetic  14.3 us (7%)
  between operations  13.7 us (6%)
  local copies, waits for them, and re-layouts  13 us (6%)
    all_to_all x1, blocking collectives, per_device(): lax.all_to_all(buffer, 'exp', split_axis=0, concat_axis=0, tiled=True)  31.1 us
    all_to_all x1, blocking collectives, per_device(): lax.all_to_all(expert_out.reshape(EXPERTS, slots, width), 'exp', split_ax...  29.8 us
    ppermute x3, waiting for transfers between devices, per_device(): lax.ppermute(local_kv, 'req', [(i, (i + 2 * s) % req_count) for i in rang...  29.6 us
    pallas_call x2, Pallas kernels, attend_prefix_grouped(): pl.pallas_call(prefix_kernel, grid_spec=pltpu.PrefetchScalarGridSpec(num_...  22.6 us
    pallas_call x1, Pallas kernels, expert_ffn(): pl.pallas_call(expert_kernel, grid=(exp_dev, inner // chunk), in_specs=[p...  13.9 us
    all_to_all x1, waiting for transfers between devices, per_device(): lax.all_to_all(attended, 'exp', split_axis=0, concat_axis=1, tiled=True)  8.76 us
    all_to_all x1, starting transfers between devices, per_device(): lax.all_to_all(attended, 'exp', split_axis=0, concat_axis=1, tiled=True)  8.06 us
    ppermute x3, starting transfers between devices, per_device(): lax.ppermute(local_kv, 'req', [(i, (i + 2 * s) % req_count) for i in rang...  5.74 us
  transfers between devices with their start and end apart: 7, of which 3 were waited for; matrix products, arithmetic and copies ran while one was open for 16% of the time, Pallas kernels for 11%

profile of v17, /device:TPU:0, one launch (start us, length us, event | category | flops | bytes accessed | tf_op | source)
XLA Modules:
  0.0 210.4 jit_solution(1654762059169924198)
XLA Ops:
  6.5 0.7 all-gather.2.cloned.1.call-update
  7.3 2.3 %pad_maximum_fusion.ka_ref.va_ref = bf16[2,4,512,128]{3,2,1,0:T(8,128)(2,1)} fusion(bf16[1,4,512,128]{3,2,1,0:T(8,128)(2,1)} %bitcast.88, bf16[1,4,512,128]{3,2,1,0:T(8,128)(2,1)} %bitcast.89), kind=kLoop, calls=%fused_computation.22 | loop fusion | flops 524288 | bytes 2097152 | tf_op jit(solution)/shard_map/stack | solution.py:311
  9.5 1.6 collective-permute-start
  11.1 2.7 %collective-permute-start.1 = (bf16[2,4,512,128]{3,2,1,0:T(8,128)(2,1)}, bf16[2,4,512,128]{3,2,1,0:T(8,128)(2,1)S(1)}, u32[]{:S(2)}, u32[]{:S(2)}) collective-permute-start(bf16[2,4,512,128]{3,2,1,0:T(8,128)(2,1)} %pad_maximum_fusion.ka_ref.va_ref), channel_id=1, source_target_pairs={{0,64},{16,80},{32,96},{48,112},{64,0},{80,16},{96,32},{112,48},{1... | collective-permute-start | bytes 3145736 | tf_op jit(solution)/shard_map/ppermute | solution.py:315
  13.8 1.4 collective-permute-start.2
  15.3 0.8 reduce_window_sum.44
  16.1 0.1 convert_reduce_fusion.1
  16.2 0.7 subtract_bitcast_fusion
  16.9 0.7 select_reduce_fusion.3
  17.6 0.1 convert_reduce_fusion.2
  17.7 0.2 reduce-window.20
  17.9 1.1 reduce-window.21
  19.1 0.2 slice_reduce_fusion.1
  19.3 0.2 reduce-window.24
  19.5 0.1 add_bitcast_fusion.1
  19.5 0.1 select_reduce_fusion.5
  19.7 3.2 %fusion.9.q_ref = bf16[1792,128]{1,0:T(8,128)(2,1)S(1)} fusion(bf16[1024,128]{1,0:T(8,128)(2,1)} %param.15, s32[1024]{0:T(1024)S(1)} %multiply_add_fusion), kind=kOutput, calls=%fused_computation.15 | convolution fusion | flops 471826432 | bytes 724992 | tf_op jit(solution)/shard_map/dot_general | solution.py:319
  22.9 1.7 select_reduce_fusion.1
  24.6 1.9 fusion.30
  26.5 0.0 copy-start.9
  26.5 1.0 fusion.2
  27.5 0.0 copy-done.9
  27.6 2.3 %fusion.4 = f32[1792,128]{1,0:T(8,128)} fusion(bf16[1024,128]{1,0:T(8,128)(2,1)S(1)} %copy-done.9, f32[1792,1024]{0,1:T(8,128)S(1)} %get-tuple-element.43, f32[1792]{0:T(1024)S(1)} %get-tuple-element.42), kind=kOutput, calls=%fused_computation.10 | convolution fusion | flops 473432064 | bytes 8526848 | tf_op jit(solution)/shard_map/dot_general | solution.py:266
  29.8 5.9 %collective-permute-done = bf16[2,4,512,128]{3,2,1,0:T(8,128)(2,1)S(1)} collective-permute-done((bf16[2,4,512,128]{3,2,1,0:T(8,128)(2,1)}, bf16[2,4,512,128]{3,2,1,0:T(8,128)(2,1)S(1)}, u32[]{:S(2)}, u32[]{:S(2)}) %collective-permute-start) | collective-permute-done | bytes 1048608 | tf_op jit(solution)/shard_map/ppermute | solution.py:315
  35.7 23.6 %collective-permute-done.1 = bf16[2,4,512,128]{3,2,1,0:T(8,128)(2,1)S(1)} collective-permute-done((bf16[2,4,512,128]{3,2,1,0:T(8,128)(2,1)}, bf16[2,4,512,128]{3,2,1,0:T(8,128)(2,1)S(1)}, u32[]{:S(2)}, u32[]{:S(2)}) %collective-permute-start.1) | collective-permute-done | bytes 1048608 | tf_op jit(solution)/shard_map/ppermute | solution.py:315
  59.4 1.0 copy-done.8
  60.4 0.0 collective-permute-done.2
  60.4 1.3 constant_dynamic-update-slice_fusion.2
  61.7 1.4 constant_dynamic-update-slice_fusion.1
  63.1 1.4 constant_dynamic-update-slice_fusion.kb_ref.vb_ref
  64.5 0.1 collective-permute-start.4
  64.6 0.5 collective-permute-start.3
  65.1 0.1 slice.29
  65.2 0.1 copy.61
  65.3 0.1 eq.149
  65.4 0.1 eq.145
  65.5 0.6 reduce-window.30
  66.1 0.2 slice_reduce_fusion
  66.3 0.1 fusion.25
  66.4 0.1 reduce_sum.139
  66.5 0.1 copy.64
  66.6 0.0 copy-done.12
  66.6 0.6 convert_reduce_fusion.3.block_group_ref
  67.2 1.3 copy.57
  68.5 1.3 copy.59
  69.8 11.3 %shard_map.145 = (f32[1792,128]{1,0:T(8,128)}, f32[1792,128]{1,0:T(8,128)}, f32[1792,128]{1,0:T(8,128)}) custom-call(s32[7]{0:T(128)} %convert_reduce_fusion.3.block_group_ref, bf16[1792,128]{1,0:T(8,128)(2,1)} %copy-done.6, bf16[2,4,512,128]{3,2,1,0:T(8,128)(2,1)} %pad_maximum_fusion.ka_ref.va_ref, bf16[2,4,512,128]{3,2,1,0:T(8,128)(2,1)} %pad_maximum_fusion.ka_ref.va_ref, ...), custom_call_target="tpu_custom_call" | custom-call | flops 1879048192 | bytes 7405568 | tf_op jit(solution)/shard_map/pallas_call | solution.py:145
  81.0 0.0 collective-permute-done.3.ka_ref.va_ref
  81.0 0.0 collective-permute-done.4.kb_ref.vb_ref
  81.1 11.4 %shard_map.146 = (f32[1792,128]{1,0:T(8,128)}, f32[1792,128]{1,0:T(8,128)}, f32[1792,128]{1,0:T(8,128)}) custom-call(s32[7]{0:T(128)} %convert_reduce_fusion.3.block_group_ref, bf16[1792,128]{1,0:T(8,128)(2,1)} %copy-done.6, bf16[2,4,512,128]{3,2,1,0:T(8,128)(2,1)} %collective-permute-done.3.ka_ref.va_ref, ...), custom_call_target="tpu_custom_call" | custom-call | flops 1879048192 | bytes 7405568 | tf_op jit(solution)/shard_map/pallas_call | solution.py:145
  92.5 0.0 copy-start.10
  92.5 3.6 %fusion.14 = (f32[1792]{0:T(1024)S(1)}, f32[1792]{0:T(1024)S(1)}, f32[1792]{0:T(1024)S(1)}, f32[1792]{0:T(1024)S(1)}, f32[1792]{0:T(1024)S(1)}) fusion(f32[1792,128]{1,0:T(8,128)} %get-tuple-element.21, f32[1792,1]{1,0:T(8,128)S(1)} %copy-done.4, f32[1792,1]{1,0:T(8,128)S(1)} %copy-done.3, f32[1792,128]{1,0:T(8,128)} %get-tuple-element.22, ...), kind=kLoop, calls=%fused_computation.35 | loop fusion | flops 21504 | bytes 78848 | tf_op jit(solution)/shard_map/exp | solution.py:275
  96.1 4.2 %fusion.11 = bf16[1024,128]{1,0:T(8,128)(2,1)} fusion(s32[1024]{0:T(1024)S(1)} %multiply_add_fusion, f32[1792,128]{1,0:T(8,128)S(1)} %copy-done.5, f32[1792,128]{1,0:T(8,128)} %get-tuple-element.23, f32[1792,128]{1,0:T(8,128)} %get-tuple-element.20, f32[1792]{0:T(1024)S(1)} %get-tuple-element.30, f32[1792]{0:T(1024)S(1)} %get-tuple-element.32, ...), kind=kOutput, calls=%fused_computation.21 | convolution fusion | flops 473563136 | bytes 3054592 | tf_op jit(solution)/shard_map/dot_general | solution.py:341
  100.3 8.1 %all-to-all-start = ((bf16[16,64,128]{2,1,0:T(8,128)(2,1)}), bf16[16,64,128]{2,1,0:T(8,128)(2,1)S(1)}, u32[]{:S(2)}, u32[]{:S(2)}) async-start(bf16[16,64,128]{2,1,0:T(8,128)(2,1)} %bitcast.9), calls=%async_computation | async-start | bytes 524288 | tf_op jit(solution)/shard_map/all_to_all | solution.py:346
  108.4 0.2 select_reduce_fusion.2
  108.5 8.8 %all-to-all-done = bf16[16,64,128]{2,1,0:T(8,128)(2,1)S(1)} async-done(((bf16[16,64,128]{2,1,0:T(8,128)(2,1)}), bf16[16,64,128]{2,1,0:T(8,128)(2,1)S(1)}, u32[]{:S(2)}, u32[]{:S(2)}) %all-to-all-start) | async-done | bytes 262176 | tf_op jit(solution)/shard_map/all_to_all | solution.py:346
  117.3 5.1 %multiply_reduce_fusion = (f32[64]{0:T(128)S(1)}, f32[64,2048]{1,0:T(8,128)S(1)}) fusion(bf16[2048,2048]{1,0:T(8,128)(2,1)} %all-gather.2.cloned.1.call-done, bf16[64,2048]{1,0:T(8,128)(2,1)S(1)} %copy-done.10, bf16[16,64,128]{2,1,0:T(8,128)(2,1)S(1)} %all-to-all-done), kind=kOutput, calls=%fused_computation.31 | convolution fusion | flops 537395136 | bytes 9437440 | tf_op jit(solution)/shard_map/dot_general | solution.py:347
  122.4 0.8 convolution_convert_fusion
  123.2 31.1 %all_to_all.29 = bf16[32,16,2048]{2,1,0:T(8,128)(2,1)S(1)} all-to-all(bf16[32,16,2048]{2,1,0:T(8,128)(2,1)S(1)} %bitcast.80), channel_id=1, replica_groups=mesh['req'=8,'exp'=16] {'exp'}, dimensions={0} | all-to-all | bytes 4194304 | tf_op jit(solution)/shard_map/all_to_all | solution.py:365
  154.3 0.1 copy.65
  154.4 2.5 %copy.66 = bf16[2,256,2048]{1,2,0:T(8,128)(2,1)} copy(bf16[2,256,2048]{2,1,0:T(8,128)(2,1)S(1)} %bitcast.82) | data formatting | bytes 4194304 | tf_op jit(solution)/shard_map/reshape | solution.py:369
  156.9 13.9 %shard_map.147 = bf16[2,256,2048]{2,1,0:T(8,128)(2,1)} custom-call(bf16[2,2048,256]{2,1,0:T(8,128)(2,1)} %bitcast.84, bf16[2,704,2048]{2,1,0:T(8,128)(2,1)} %bitcast.86, bf16[2,704,2048]{2,1,0:T(8,128)(2,1)} %bitcast.87, bf16[2,704,2048]{2,1,0:T(8,128)(2,1)} %wd_ref.1), custom_call_target="tpu_custom_call" | custom-call | flops 4429185024 | bytes 21495808 | tf_op jit(solution)/shard_map/pallas_call | solution.py:191
  170.8 1.7 copy.67
  172.5 29.8 %all_to_all.30 = bf16[32,16,2048]{2,1,0:T(8,128)(2,1)S(1)} all-to-all(bf16[32,16,2048]{2,1,0:T(8,128)(2,1)S(1)} %bitcast.83), channel_id=1, replica_groups=mesh['req'=8,'exp'=16] {'exp'}, dimensions={0} | all-to-all | bytes 4194304 | tf_op jit(solution)/shard_map/all_to_all | solution.py:371
  202.4 1.2 fusion.10
  (39 shorter events, 0.2 us)
Async XLA Ops:
  6.5 18.0 %copy-start = (bf16[1024,128]{1,0:T(8,128)(2,1)S(1)}, bf16[1024,128]{1,0:T(8,128)(2,1)}, u32[]{:S(2)}) copy-start(bf16[1024,128]{1,0:T(8,128)(2,1)} %param.16) | copy-start | bytes 786436
  6.5 110.8 %all-gather.2.cloned.1.call-start = ((), (), s32[]{:S(2)}) async-start(), calls=%async_computation.3 | async-start | bytes 8912896 | tf_op jit(solution)/shard_map/all_gather | solution.py:345
  9.5 26.2 %collective-permute-start = (bf16[2,4,512,128]{3,2,1,0:T(8,128)(2,1)}, bf16[2,4,512,128]{3,2,1,0:T(8,128)(2,1)S(1)}, u32[]{:S(2)}, u32[]{:S(2)}) collective-permute-start(bf16[2,4,512,128]{3,2,1,0:T(8,128)(2,1)} %pad_maximum_fusion.ka_ref.va_ref), channel_id=1, source_target_pairs={{0,32},{16,48},{32,64},{48,80},{64,96},{80,112},{96,0},{112,16},{1... | collective-permute-start | bytes 3145736 | tf_op jit(solution)/shard_map/ppermute | solution.py:315
  11.1 48.3 %collective-permute-start.1 = (bf16[2,4,512,128]{3,2,1,0:T(8,128)(2,1)}, bf16[2,4,512,128]{3,2,1,0:T(8,128)(2,1)S(1)}, u32[]{:S(2)}, u32[]{:S(2)}) collective-permute-start(bf16[2,4,512,128]{3,2,1,0:T(8,128)(2,1)} %pad_maximum_fusion.ka_ref.va_ref), channel_id=1, source_target_pairs={{0,64},{16,80},{32,96},{48,112},{64,0},{80,16},{96,32},{112,48},{1... | collective-permute-start | bytes 3145736 | tf_op jit(solution)/shard_map/ppermute | solution.py:315
  13.8 46.5 %collective-permute-start.2 = (bf16[2,4,512,128]{3,2,1,0:T(8,128)(2,1)}, bf16[2,4,512,128]{3,2,1,0:T(8,128)(2,1)}, u32[]{:S(2)}, u32[]{:S(2)}) collective-permute-start(bf16[2,4,512,128]{3,2,1,0:T(8,128)(2,1)} %pad_maximum_fusion.ka_ref.va_ref), channel_id=1, source_target_pairs={{0,96},{16,112},{32,0},{48,16},{64,32},{80,48},{96,64},{112,80},{1... | collective-permute-start | bytes 3145736 | tf_op jit(solution)/shard_map/ppermute | solution.py:315
  22.8 3.6 %copy-start.6 = (bf16[1792,128]{1,0:T(8,128)(2,1)}, bf16[1792,128]{1,0:T(8,128)(2,1)S(1)}, u32[]{:S(2)}) copy-start(bf16[1792,128]{1,0:T(8,128)(2,1)S(1)} %fusion.9.q_ref) | copy-start | bytes 1376260
  26.5 1.1 copy-start.9
  29.8 35.3 %copy-start.11 = (s32[64,4]{0,1:T(4,128)S(1)}, s32[64,4]{0,1:T(4,128)}, u32[]{:S(2)}) copy-start(s32[64,4]{0,1:T(4,128)} %param.25) | copy-start | bytes 3076
  29.8 36.8 %copy-start.13 = (bf16[64,4]{0,1:T(4,128)(2,1)S(1)}, bf16[64,4]{0,1:T(4,128)(2,1)}, u32[]{:S(2)}) copy-start(bf16[64,4]{0,1:T(4,128)(2,1)} %param.26) | copy-start | bytes 1540
  29.8 36.8 %copy-start.12 = (bf16[2048]{0:T(1024)(128)(2,1)S(1)}, bf16[2048]{0:T(1024)(128)(2,1)}, u32[]{:S(2)}) copy-start(bf16[2048]{0:T(1024)(128)(2,1)} %param.24) | copy-start | bytes 12292
  35.7 23.7 %copy-start.7 = (bf16[2,4,512,128]{3,2,1,0:T(8,128)(2,1)}, bf16[2,4,512,128]{3,2,1,0:T(8,128)(2,1)S(1)}, u32[]{:S(2)}) copy-start(bf16[2,4,512,128]{3,2,1,0:T(8,128)(2,1)S(1)} %collective-permute-done) | copy-start | bytes 3145732
  59.4 1.0 copy-start.8
  64.5 5.3 %copy-start.2 = (bf16[2,4,1536,128]{3,2,1,0:T(8,128)(2,1)}, bf16[2,4,1536,128]{3,2,1,0:T(8,128)(2,1)S(1)}, u32[]{:S(2)}) copy-start(bf16[2,4,1536,128]{3,2,1,0:T(8,128)(2,1)S(1)} %constant_dynamic-update-slice_fusion.kb_ref.vb_ref) | copy-start | bytes 9437188
  64.5 16.5 %collective-permute-start.4 = (bf16[2,4,1536,128]{3,2,1,0:T(8,128)(2,1)S(1)}, bf16[2,4,1536,128]{3,2,1,0:T(8,128)(2,1)}, u32[]{:S(2)}, u32[]{:S(2)}) collective-permute-start(bf16[2,4,1536,128]{3,2,1,0:T(8,128)(2,1)S(1)} %constant_dynamic-update-slice_fusion.kb_ref.vb_ref), channel_id=1, source_target_pairs={{0,16},{16,0},{32,48},{48,32},{64,80},{80,64},{96,112},{112,96},{1... | collective-permute-start | bytes 9437192 | tf_op jit(solution)/shard_map/ppermute | solution.py:333
  64.6 16.4 %collective-permute-start.3 = (bf16[2,4,512,128]{3,2,1,0:T(8,128)(2,1)}, bf16[2,4,512,128]{3,2,1,0:T(8,128)(2,1)}, u32[]{:S(2)}, u32[]{:S(2)}) collective-permute-start(bf16[2,4,512,128]{3,2,1,0:T(8,128)(2,1)} %pad_maximum_fusion.ka_ref.va_ref), channel_id=1, source_target_pairs={{0,16},{16,0},{32,48},{48,32},{64,80},{80,64},{96,112},{112,96},{1... | collective-permute-start | bytes 3145736 | tf_op jit(solution)/shard_map/ppermute | solution.py:313
  81.0 11.4 %copy-start.3 = (f32[1792,1]{1,0:T(8,128)S(1)}, f32[1792,1]{1,0:T(8,128)}, u32[]{:S(2)}) copy-start(f32[1792,1]{1,0:T(8,128)} %copy.57) | copy-start | bytes 21508
  81.0 11.4 %copy-start.4 = (f32[1792,1]{1,0:T(8,128)S(1)}, f32[1792,1]{1,0:T(8,128)}, u32[]{:S(2)}) copy-start(f32[1792,1]{1,0:T(8,128)} %copy.59) | copy-start | bytes 21508
  81.1 15.0 %copy-start.5 = (f32[1792,128]{1,0:T(8,128)S(1)}, f32[1792,128]{1,0:T(8,128)}, u32[]{:S(2)}) copy-start(f32[1792,128]{1,0:T(8,128)} %fusion.4) | copy-start | bytes 2752516
  92.5 24.9 %copy-start.10 = (bf16[64,2048]{1,0:T(8,128)(2,1)S(1)}, bf16[64,2048]{1,0:T(8,128)(2,1)}, u32[]{:S(2)}) copy-start(bf16[64,2048]{1,0:T(8,128)(2,1)} %param.22) | copy-start | bytes 786436
  100.3 17.0 %all-to-all-start = ((bf16[16,64,128]{2,1,0:T(8,128)(2,1)}), bf16[16,64,128]{2,1,0:T(8,128)(2,1)S(1)}, u32[]{:S(2)}, u32[]{:S(2)}) async-start(bf16[16,64,128]{2,1,0:T(8,128)(2,1)} %bitcast.9), calls=%async_computation | async-start | bytes 524288 | tf_op jit(solution)/shard_map/all_to_all | solution.py:346
  156.9 46.7 %copy-start.1 = (bf16[1024,128]{1,0:T(8,128)(2,1)S(1)}, bf16[1024,128]{1,0:T(8,128)(2,1)}, u32[]{:S(2)}) copy-start(bf16[1024,128]{1,0:T(8,128)(2,1)} %param.16) | copy-start | bytes 786436
Sparse Core Ops, SparseCore 0:
  9.5 73.3 all-gather.1

commit v18 on v17

--- a/solution.py
+++ b/solution.py
@@ -93,22 +93,30 @@
 KEY_BLOCK = 2048
 
 
-def prefix_kernel(block_group_ref, q_ref, ka_ref, va_ref, kb_ref, vb_ref, acc_ref, m_ref, l_ref):
+def prefix_kernel(block_group_ref, q_ref, *refs):
     scaling = 1.0 / math.sqrt(HEAD)
+    acc_ref, m_ref, l_ref = refs[-3:]
+    pieces = refs[:-3]
     q = q_ref[...]
     contract = (((1,), (1,)), ((), ()))
-    s_a = lax.dot_general(q, ka_ref[0, 0], contract, preferred_element_type=jnp.float32) * scaling
-    s_b = lax.dot_general(q, kb_ref[0, 0], contract, preferred_element_type=jnp.float32) * scaling
-    m = jnp.maximum(jnp.max(s_a, axis=1, keepdims=True), jnp.max(s_b, axis=1, keepdims=True))
-    p_a = jnp.exp(s_a - m)
-    p_b = jnp.exp(s_b - m)
-    acc_ref[...] = jnp.dot(
-        p_a.astype(jnp.bfloat16), va_ref[0, 0], preferred_element_type=jnp.float32
-    ) + jnp.dot(p_b.astype(jnp.bfloat16), vb_ref[0, 0], preferred_element_type=jnp.float32)
+    scores = [
+        lax.dot_general(q, pieces[i][0, 0], contract, preferred_element_type=jnp.float32) * scaling
+        for i in range(0, len(pieces), 2)
+    ]
+    m = scores[0].max(axis=1, keepdims=True)
+    for s in scores[1:]:
+        m = jnp.maximum(m, s.max(axis=1, keepdims=True))
+    acc = None
+    total = None
+    for i, s in enumerate(scores):
+        p = jnp.exp(s - m)
+        term = jnp.dot(p.astype(jnp.bfloat16), pieces[2 * i + 1][0, 0], preferred_element_type=jnp.float32)
+        acc = term if acc is None else acc + term
+        row_sum = jnp.sum(p, axis=1, keepdims=True)
+        total = row_sum if total is None else total + row_sum
+    acc_ref[...] = acc
     m_ref[...] = jnp.broadcast_to(m, m_ref.shape)
-    l_ref[...] = jnp.broadcast_to(
-        jnp.sum(p_a, axis=1, keepdims=True) + jnp.sum(p_b, axis=1, keepdims=True), l_ref.shape
-    )
+    l_ref[...] = jnp.broadcast_to(total, l_ref.shape)
 
 
 def group_layout(query_group):
@@ -128,7 +136,7 @@
     return padded_index, source, block_group
 
 
-def attend_prefix_grouped(padded_rows, block_group, kv_a, kv_b):
+def attend_prefix_grouped(padded_rows, block_group, *kv_list):
     padded_count = padded_rows.shape[0]
     block_count = padded_count // QUERY_BLOCK
     row_spec = pl.BlockSpec((QUERY_BLOCK, HEAD), lambda b, bg: (b, 0))
@@ -140,14 +148,14 @@
             pl.BlockSpec((1, 1, span, HEAD), lambda b, bg: (1, bg[b], 0, 0)),
         ]
 
-    span = kv_a.shape[2] + kv_b.shape[2]
+    span = sum(kv.shape[2] for kv in kv_list)
     out_shape = jax.ShapeDtypeStruct((padded_count, HEAD), jnp.float32)
     acc, maxima, totals = pl.pallas_call(
         prefix_kernel,
         grid_spec=pltpu.PrefetchScalarGridSpec(
             num_scalar_prefetch=1,
             grid=(block_count,),
-            in_specs=[row_spec] + piece_specs(kv_a) + piece_specs(kv_b),
+            in_specs=[row_spec] + [spec for kv in kv_list for spec in piece_specs(kv)],
             out_specs=[row_spec] * 3,
         ),
         out_shape=[out_shape] * 3,
@@ -157,7 +165,7 @@
             transcendentals=padded_count * span,
             bytes_accessed=2 * G * span * HEAD * 2 + padded_count * HEAD * 14,
         ),
-    )(block_group, padded_rows, kv_a, kv_a, kv_b, kv_b)
+    )(block_group, padded_rows, *[kv for kv in kv_list for _ in range(2)])
     return (acc, maxima[:, :1], totals[:, :1])
 
 
@@ -331,9 +339,8 @@
     ring_parts, suffix_part = lax.optimization_barrier((ring_parts, suffix_part))
     ring_kv = jnp.concatenate(ring_parts, axis=2)
     forwarded_kv = lax.ppermute(ring_kv, "req", partner)
-    prefix_part = combine(
-        attend_prefix_grouped(padded_rows, block_group, local_kv, ring_kv),
-        attend_prefix_grouped(padded_rows, block_group, partner_kv, forwarded_kv),
+    prefix_part = attend_prefix_grouped(
+        padded_rows, block_group, local_kv, ring_kv, partner_kv, forwarded_kv
     )
     weighted, maxima, totals = combine(prefix_part, suffix_part)
     padded_attended = (weighted / totals).astype(jnp.bfloat16)

time: 211 us -> 209 us (level)
  Pallas kernels: 36.5 us -> 33.5 us
    pallas_call x2 -> x1, Pallas kernels: 22.6 us -> 19.6 us  [attend_prefix_grouped(): pl.pallas_call(prefix_kernel, grid_spec=pltpu.PrefetchScalarGridSpec(num_...]
  transfers between devices with their start and end apart: 7 -> 7, of which waited for: 3 -> 4; matrix products, arithmetic and copies ran while one was open for 16% -> 16% of each run, Pallas kernels for 11% -> 9%
where the time goes in v18:
time: 209 us; the launch traced here: 208 us
  blocking collectives  60.8 us (29%)
  waiting for transfers between devices  41.1 us (20%)
  Pallas kernels  33.5 us (16%)
  matrix products  18.2 us (9%)
  starting transfers between devices  14.3 us (7%)
  between operations  13.7 us (7%)
  other arithmetic  13.5 us (6%)
  local copies, waits for them, and re-layouts  13 us (6%)
    all_to_all x1, blocking collectives, per_device(): lax.all_to_all(buffer, 'exp', split_axis=0, concat_axis=0, tiled=True)  31 us
    all_to_all x1, blocking collectives, per_device(): lax.all_to_all(expert_out.reshape(EXPERTS, slots, width), 'exp', split_ax...  29.8 us
    ppermute x3, waiting for transfers between devices, per_device(): lax.ppermute(local_kv, 'req', [(i, (i + 2 * s) % req_count) for i in rang...  29.6 us
    pallas_call x1, Pallas kernels, attend_prefix_grouped(): pl.pallas_call(prefix_kernel, grid_spec=pltpu.PrefetchScalarGridSpec(num_...  19.6 us
    pallas_call x1, Pallas kernels, expert_ffn(): pl.pallas_call(expert_kernel, grid=(exp_dev, inner // chunk), in_specs=[p...  13.9 us
    all_to_all x1, waiting for transfers between devices, per_device(): lax.all_to_all(attended, 'exp', split_axis=0, concat_axis=1, tiled=True)  8.71 us
    all_to_all x1, starting transfers between devices, per_device(): lax.all_to_all(attended, 'exp', split_axis=0, concat_axis=1, tiled=True)  7.99 us
    ppermute x3, starting transfers between devices, per_device(): lax.ppermute(local_kv, 'req', [(i, (i + 2 * s) % req_count) for i in rang...  5.74 us
  transfers between devices with their start and end apart: 7, of which 4 were waited for; matrix products, arithmetic and copies ran while one was open for 16% of the time, Pallas kernels for 9%

profile of v18, /device:TPU:0, one launch (start us, length us, event | category | flops | bytes accessed | tf_op | source)
XLA Modules:
  0.0 208.1 jit_solution(15299806310394463572)
XLA Ops:
  6.5 0.7 all-gather.2.cloned.1.call-update
  7.3 2.3 %pad_maximum_fusion.refs_0_.refs_1_ = bf16[2,4,512,128]{3,2,1,0:T(8,128)(2,1)} fusion(bf16[1,4,512,128]{3,2,1,0:T(8,128)(2,1)} %bitcast.88, bf16[1,4,512,128]{3,2,1,0:T(8,128)(2,1)} %bitcast.89), kind=kLoop, calls=%fused_computation.22 | loop fusion | flops 524288 | bytes 2097152 | tf_op jit(solution)/shard_map/stack | solution.py:319
  9.5 1.6 collective-permute-start
  11.1 2.7 %collective-permute-start.1 = (bf16[2,4,512,128]{3,2,1,0:T(8,128)(2,1)}, bf16[2,4,512,128]{3,2,1,0:T(8,128)(2,1)S(1)}, u32[]{:S(2)}, u32[]{:S(2)}) collective-permute-start(bf16[2,4,512,128]{3,2,1,0:T(8,128)(2,1)} %pad_maximum_fusion.refs_0_.refs_1_), channel_id=1, source_target_pairs={{0,64},{16,80},{32,96},{48,112},{64,0},{80,16},{96,32},{112,48},{1... | collective-permute-start | bytes 3145736 | tf_op jit(solution)/shard_map/ppermute | solution.py:323
  13.8 1.4 collective-permute-start.2
  15.3 0.8 reduce_window_sum.44
  16.1 0.1 convert_reduce_fusion.1
  16.2 0.7 subtract_bitcast_fusion
  16.9 0.7 select_reduce_fusion.3
  17.6 0.1 convert_reduce_fusion.2
  17.7 0.2 reduce-window.20
  17.9 1.1 reduce-window.21
  19.1 0.2 slice_reduce_fusion.1
  19.3 0.2 reduce-window.24
  19.5 0.1 add_bitcast_fusion.1
  19.5 0.1 select_reduce_fusion.5
  19.7 3.2 %fusion.9.q_ref = bf16[1792,128]{1,0:T(8,128)(2,1)S(1)} fusion(bf16[1024,128]{1,0:T(8,128)(2,1)} %param.15, s32[1024]{0:T(1024)S(1)} %multiply_add_fusion), kind=kOutput, calls=%fused_computation.15 | convolution fusion | flops 471826432 | bytes 724992 | tf_op jit(solution)/shard_map/dot_general | solution.py:327
  22.9 1.7 select_reduce_fusion.1
  24.6 1.9 fusion.28
  26.5 0.0 copy-start.6
  26.5 1.0 fusion.2
  27.5 0.0 copy-done.6
  27.6 2.3 %fusion.4 = f32[1792,128]{1,0:T(8,128)} fusion(bf16[1024,128]{1,0:T(8,128)(2,1)S(1)} %copy-done.6, f32[1792,1024]{0,1:T(8,128)S(1)} %get-tuple-element.35, f32[1792]{0:T(1024)S(1)} %get-tuple-element.34), kind=kOutput, calls=%fused_computation.10 | convolution fusion | flops 473432064 | bytes 8526848 | tf_op jit(solution)/shard_map/dot_general | solution.py:274
  29.8 5.9 %collective-permute-done = bf16[2,4,512,128]{3,2,1,0:T(8,128)(2,1)S(1)} collective-permute-done((bf16[2,4,512,128]{3,2,1,0:T(8,128)(2,1)}, bf16[2,4,512,128]{3,2,1,0:T(8,128)(2,1)S(1)}, u32[]{:S(2)}, u32[]{:S(2)}) %collective-permute-start) | collective-permute-done | bytes 1048608 | tf_op jit(solution)/shard_map/ppermute | solution.py:323
  35.7 23.6 %collective-permute-done.1 = bf16[2,4,512,128]{3,2,1,0:T(8,128)(2,1)S(1)} collective-permute-done((bf16[2,4,512,128]{3,2,1,0:T(8,128)(2,1)}, bf16[2,4,512,128]{3,2,1,0:T(8,128)(2,1)S(1)}, u32[]{:S(2)}, u32[]{:S(2)}) %collective-permute-start.1) | collective-permute-done | bytes 1048608 | tf_op jit(solution)/shard_map/ppermute | solution.py:323
  59.4 1.0 copy-done.4
  60.4 0.0 collective-permute-done.2
  60.4 1.3 constant_dynamic-update-slice_fusion.2
  61.7 1.4 constant_dynamic-update-slice_fusion.1
  63.1 1.4 constant_dynamic-update-slice_fusion.refs_2_.refs_3_
  64.5 0.1 collective-permute-start.4
  64.6 0.5 collective-permute-start.3
  65.1 0.1 slice.23
  65.2 0.0 copy-done.8
  65.2 0.1 copy.61
  65.3 0.1 eq.149
  65.4 0.1 eq.145
  65.5 0.6 reduce-window.30
  66.1 0.2 slice_reduce_fusion
  66.3 0.1 fusion.23
  66.4 0.1 reduce_sum.139
  66.5 0.1 copy.64
  66.6 0.0 copy-done.9
  66.6 0.6 convert_reduce_fusion.3.block_group_ref
  67.2 1.3 copy.57
  68.5 1.3 copy.59
  69.8 2.1 collective-permute-done.3.refs_4_.refs_5_
  71.8 0.0 collective-permute-done.4.refs_6_.refs_7_
  71.9 19.6 %shard_map.145 = (f32[1792,128]{1,0:T(8,128)}, f32[1792,128]{1,0:T(8,128)}, f32[1792,128]{1,0:T(8,128)}) custom-call(s32[7]{0:T(128)} %convert_reduce_fusion.3.block_group_ref, bf16[1792,128]{1,0:T(8,128)(2,1)} %copy-done.5, bf16[2,4,512,128]{3,2,1,0:T(8,128)(2,1)} %pad_maximum_fusion.refs_0_.refs_1_, ...), custom_call_target="tpu_custom_call" | custom-call | flops 3758096384 | bytes 11599872 | tf_op jit(solution)/shard_map/pallas_call | solution.py:153
  91.5 0.0 copy-start.7
  91.5 2.9 %fusion.19 = (f32[1792]{0:T(1024)S(1)}, f32[1792]{0:T(1024)S(1)}, f32[1792]{0:T(1024)S(1)}) fusion(f32[1792,1]{1,0:T(8,128)} %copy.57, f32[1792,128]{1,0:T(8,128)} %get-tuple-element.18, f32[1792,1]{1,0:T(8,128)} %copy.59, f32[1792,128]{1,0:T(8,128)} %get-tuple-element.21), kind=kLoop, calls=%fused_computation.37 | loop fusion | flops 10752 | bytes 50176 | tf_op jit(solution)/shard_map/exp | solution.py:283
  94.3 3.9 %fusion.11 = bf16[1024,128]{1,0:T(8,128)(2,1)} fusion(s32[1024]{0:T(1024)S(1)} %multiply_add_fusion, f32[1792,128]{1,0:T(8,128)} %fusion.4, f32[1792,128]{1,0:T(8,128)} %get-tuple-element.17, f32[1792]{0:T(1024)S(1)} %get-tuple-element.24, f32[1792]{0:T(1024)S(1)} %get-tuple-element.25, f32[1792]{0:T(1024)S(1)} %get-tuple-element.23), kind=kOutput, calls=%fused_computation.21 | convolution fusion | flops 472875008 | bytes 2122752 | tf_op jit(solution)/shard_map/dot_general | solution.py:348
  98.2 8.0 %all-to-all-start = ((bf16[16,64,128]{2,1,0:T(8,128)(2,1)}), bf16[16,64,128]{2,1,0:T(8,128)(2,1)S(1)}, u32[]{:S(2)}, u32[]{:S(2)}) async-start(bf16[16,64,128]{2,1,0:T(8,128)(2,1)} %bitcast.9), calls=%async_computation | async-start | bytes 524288 | tf_op jit(solution)/shard_map/all_to_all | solution.py:353
  106.2 0.2 select_reduce_fusion.2
  106.4 8.7 %all-to-all-done = bf16[16,64,128]{2,1,0:T(8,128)(2,1)S(1)} async-done(((bf16[16,64,128]{2,1,0:T(8,128)(2,1)}), bf16[16,64,128]{2,1,0:T(8,128)(2,1)S(1)}, u32[]{:S(2)}, u32[]{:S(2)}) %all-to-all-start) | async-done | bytes 262176 | tf_op jit(solution)/shard_map/all_to_all | solution.py:353
  115.1 5.1 %multiply_reduce_fusion = (f32[64]{0:T(128)S(1)}, f32[64,2048]{1,0:T(8,128)S(1)}) fusion(bf16[2048,2048]{1,0:T(8,128)(2,1)} %all-gather.2.cloned.1.call-done, bf16[64,2048]{1,0:T(8,128)(2,1)S(1)} %copy-done.7, bf16[16,64,128]{2,1,0:T(8,128)(2,1)S(1)} %all-to-all-done), kind=kOutput, calls=%fused_computation.28 | convolution fusion | flops 537395136 | bytes 9437440 | tf_op jit(solution)/shard_map/dot_general | solution.py:354
  120.2 0.8 convolution_convert_fusion
  121.0 31.0 %all_to_all.29 = bf16[32,16,2048]{2,1,0:T(8,128)(2,1)S(1)} all-to-all(bf16[32,16,2048]{2,1,0:T(8,128)(2,1)S(1)} %bitcast.80), channel_id=1, replica_groups=mesh['req'=8,'exp'=16] {'exp'}, dimensions={0} | all-to-all | bytes 4194304 | tf_op jit(solution)/shard_map/all_to_all | solution.py:372
  152.0 0.1 copy.65
  152.1 2.5 %copy.66 = bf16[2,256,2048]{1,2,0:T(8,128)(2,1)} copy(bf16[2,256,2048]{2,1,0:T(8,128)(2,1)S(1)} %bitcast.82) | data formatting | bytes 4194304 | tf_op jit(solution)/shard_map/reshape | solution.py:376
  154.6 13.9 %shard_map.146 = bf16[2,256,2048]{2,1,0:T(8,128)(2,1)} custom-call(bf16[2,2048,256]{2,1,0:T(8,128)(2,1)} %bitcast.84, bf16[2,704,2048]{2,1,0:T(8,128)(2,1)} %bitcast.86, bf16[2,704,2048]{2,1,0:T(8,128)(2,1)} %bitcast.87, bf16[2,704,2048]{2,1,0:T(8,128)(2,1)} %wd_ref.1), custom_call_target="tpu_custom_call" | custom-call | flops 4429185024 | bytes 21495808 | tf_op jit(solution)/shard_map/pallas_call | solution.py:199
  168.5 1.7 copy.67
  170.3 29.8 %all_to_all.30 = bf16[32,16,2048]{2,1,0:T(8,128)(2,1)S(1)} all-to-all(bf16[32,16,2048]{2,1,0:T(8,128)(2,1)S(1)} %bitcast.83), channel_id=1, replica_groups=mesh['req'=8,'exp'=16] {'exp'}, dimensions={0} | all-to-all | bytes 4194304 | tf_op jit(solution)/shard_map/all_to_all | solution.py:378
  200.1 1.2 fusion.10
  (32 shorter events, 0.1 us)
Async XLA Ops:
  6.5 18.0 %copy-start = (bf16[1024,128]{1,0:T(8,128)(2,1)S(1)}, bf16[1024,128]{1,0:T(8,128)(2,1)}, u32[]{:S(2)}) copy-start(bf16[1024,128]{1,0:T(8,128)(2,1)} %param.16) | copy-start | bytes 786436
  6.5 108.6 %all-gather.2.cloned.1.call-start = ((), (), s32[]{:S(2)}) async-start(), calls=%async_computation.3 | async-start | bytes 8912896 | tf_op jit(solution)/shard_map/all_gather | solution.py:352
  9.5 26.2 %collective-permute-start = (bf16[2,4,512,128]{3,2,1,0:T(8,128)(2,1)}, bf16[2,4,512,128]{3,2,1,0:T(8,128)(2,1)S(1)}, u32[]{:S(2)}, u32[]{:S(2)}) collective-permute-start(bf16[2,4,512,128]{3,2,1,0:T(8,128)(2,1)} %pad_maximum_fusion.refs_0_.refs_1_), channel_id=1, source_target_pairs={{0,32},{16,48},{32,64},{48,80},{64,96},{80,112},{96,0},{112,16},{1... | collective-permute-start | bytes 3145736 | tf_op jit(solution)/shard_map/ppermute | solution.py:323
  11.1 48.3 %collective-permute-start.1 = (bf16[2,4,512,128]{3,2,1,0:T(8,128)(2,1)}, bf16[2,4,512,128]{3,2,1,0:T(8,128)(2,1)S(1)}, u32[]{:S(2)}, u32[]{:S(2)}) collective-permute-start(bf16[2,4,512,128]{3,2,1,0:T(8,128)(2,1)} %pad_maximum_fusion.refs_0_.refs_1_), channel_id=1, source_target_pairs={{0,64},{16,80},{32,96},{48,112},{64,0},{80,16},{96,32},{112,48},{1... | collective-permute-start | bytes 3145736 | tf_op jit(solution)/shard_map/ppermute | solution.py:323
  13.8 46.5 %collective-permute-start.2 = (bf16[2,4,512,128]{3,2,1,0:T(8,128)(2,1)}, bf16[2,4,512,128]{3,2,1,0:T(8,128)(2,1)}, u32[]{:S(2)}, u32[]{:S(2)}) collective-permute-start(bf16[2,4,512,128]{3,2,1,0:T(8,128)(2,1)} %pad_maximum_fusion.refs_0_.refs_1_), channel_id=1, source_target_pairs={{0,96},{16,112},{32,0},{48,16},{64,32},{80,48},{96,64},{112,80},{1... | collective-permute-start | bytes 3145736 | tf_op jit(solution)/shard_map/ppermute | solution.py:323
  22.8 3.6 %copy-start.5 = (bf16[1792,128]{1,0:T(8,128)(2,1)}, bf16[1792,128]{1,0:T(8,128)(2,1)S(1)}, u32[]{:S(2)}) copy-start(bf16[1792,128]{1,0:T(8,128)(2,1)S(1)} %fusion.9.q_ref) | copy-start | bytes 1376260
  26.5 1.1 copy-start.6
  29.8 35.3 %copy-start.8 = (s32[64,4]{0,1:T(4,128)S(1)}, s32[64,4]{0,1:T(4,128)}, u32[]{:S(2)}) copy-start(s32[64,4]{0,1:T(4,128)} %param.25) | copy-start | bytes 3076
  29.8 36.8 %copy-start.10 = (bf16[64,4]{0,1:T(4,128)(2,1)S(1)}, bf16[64,4]{0,1:T(4,128)(2,1)}, u32[]{:S(2)}) copy-start(bf16[64,4]{0,1:T(4,128)(2,1)} %param.26) | copy-start | bytes 1540
  29.8 36.8 %copy-start.9 = (bf16[2048]{0:T(1024)(128)(2,1)S(1)}, bf16[2048]{0:T(1024)(128)(2,1)}, u32[]{:S(2)}) copy-start(bf16[2048]{0:T(1024)(128)(2,1)} %param.24) | copy-start | bytes 12292
  35.7 23.7 %copy-start.3 = (bf16[2,4,512,128]{3,2,1,0:T(8,128)(2,1)}, bf16[2,4,512,128]{3,2,1,0:T(8,128)(2,1)S(1)}, u32[]{:S(2)}) copy-start(bf16[2,4,512,128]{3,2,1,0:T(8,128)(2,1)S(1)} %collective-permute-done) | copy-start | bytes 3145732
  59.4 1.0 copy-start.4
  64.5 7.4 %copy-start.2 = (bf16[2,4,1536,128]{3,2,1,0:T(8,128)(2,1)}, bf16[2,4,1536,128]{3,2,1,0:T(8,128)(2,1)S(1)}, u32[]{:S(2)}) copy-start(bf16[2,4,1536,128]{3,2,1,0:T(8,128)(2,1)S(1)} %constant_dynamic-update-slice_fusion.refs_2_.refs_3_) | copy-start | bytes 9437188
  64.5 7.4 %collective-permute-start.4 = (bf16[2,4,1536,128]{3,2,1,0:T(8,128)(2,1)S(1)}, bf16[2,4,1536,128]{3,2,1,0:T(8,128)(2,1)}, u32[]{:S(2)}, u32[]{:S(2)}) collective-permute-start(bf16[2,4,1536,128]{3,2,1,0:T(8,128)(2,1)S(1)} %constant_dynamic-update-slice_fusion.refs_2_.refs_3_), channel_id=1, source_target_pairs={{0,16},{16,0},{32,48},{48,32},{64,80},{80,64},{96,112},{112,96},{1... | collective-permute-start | bytes 9437192 | tf_op jit(solution)/shard_map/ppermute | solution.py:341
  64.6 7.2 %collective-permute-start.3 = (bf16[2,4,512,128]{3,2,1,0:T(8,128)(2,1)}, bf16[2,4,512,128]{3,2,1,0:T(8,128)(2,1)}, u32[]{:S(2)}, u32[]{:S(2)}) collective-permute-start(bf16[2,4,512,128]{3,2,1,0:T(8,128)(2,1)} %pad_maximum_fusion.refs_0_.refs_1_), channel_id=1, source_target_pairs={{0,16},{16,0},{32,48},{48,32},{64,80},{80,64},{96,112},{112,96},{1... | collective-permute-start | bytes 3145736 | tf_op jit(solution)/shard_map/ppermute | solution.py:321
  91.5 23.6 %copy-start.7 = (bf16[64,2048]{1,0:T(8,128)(2,1)S(1)}, bf16[64,2048]{1,0:T(8,128)(2,1)}, u32[]{:S(2)}) copy-start(bf16[64,2048]{1,0:T(8,128)(2,1)} %param.22) | copy-start | bytes 786436
  98.2 16.9 %all-to-all-start = ((bf16[16,64,128]{2,1,0:T(8,128)(2,1)}), bf16[16,64,128]{2,1,0:T(8,128)(2,1)S(1)}, u32[]{:S(2)}, u32[]{:S(2)}) async-start(bf16[16,64,128]{2,1,0:T(8,128)(2,1)} %bitcast.9), calls=%async_computation | async-start | bytes 524288 | tf_op jit(solution)/shard_map/all_to_all | solution.py:353
  154.6 46.6 %copy-start.1 = (bf16[1024,128]{1,0:T(8,128)(2,1)S(1)}, bf16[1024,128]{1,0:T(8,128)(2,1)}, u32[]{:S(2)}) copy-start(bf16[1024,128]{1,0:T(8,128)(2,1)} %param.16) | copy-start | bytes 786436
Sparse Core Ops, SparseCore 0:
  9.5 73.3 all-gather.1

commit v19 on v18

--- a/solution.py
+++ b/solution.py
@@ -337,10 +337,9 @@
         position,
     )
     ring_parts, suffix_part = lax.optimization_barrier((ring_parts, suffix_part))
-    ring_kv = jnp.concatenate(ring_parts, axis=2)
-    forwarded_kv = lax.ppermute(ring_kv, "req", partner)
+    forwarded_parts = [lax.ppermute(part, "req", partner) for part in ring_parts]
     prefix_part = attend_prefix_grouped(
-        padded_rows, block_group, local_kv, ring_kv, partner_kv, forwarded_kv
+        padded_rows, block_group, local_kv, *ring_parts, partner_kv, *forwarded_parts
     )
     weighted, maxima, totals = combine(prefix_part, suffix_part)
     padded_attended = (weighted / totals).astype(jnp.bfloat16)

time: 209 us -> 201 us (0.962)
  local copies, waits for them, and re-layouts: 13 us -> 7.95 us
    unnamed x25 -> x23, local copies, waits for them, and re-layouts: 3.83 us -> 0.15 us
  transfers between devices with their start and end apart: 7 -> 9, of which waited for: 4 -> 5; matrix products, arithmetic and copies ran while one was open for 16% -> 13% of each run, Pallas kernels for 9% -> 10%
where the time goes in v19:
time: 201 us; the launch traced here: 200 us
  blocking collectives  60.7 us (30%)
  waiting for transfers between devices  39.4 us (20%)
  Pallas kernels  33.4 us (17%)
  matrix products  18.2 us (9%)
  starting transfers between devices  14.5 us (7%)
  between operations  13.7 us (7%)
  other arithmetic  12.2 us (6%)
  local copies, waits for them, and re-layouts  7.95 us (4%)
    all_to_all x1, blocking collectives, per_device(): lax.all_to_all(buffer, 'exp', split_axis=0, concat_axis=0, tiled=True)  31 us
    all_to_all x1, blocking collectives, per_device(): lax.all_to_all(expert_out.reshape(EXPERTS, slots, width), 'exp', split_ax...  29.8 us
    ppermute x3, waiting for transfers between devices, per_device(): lax.ppermute(local_kv, 'req', [(i, (i + 2 * s) % req_count) for i in rang...  29.3 us
    pallas_call x1, Pallas kernels, attend_prefix_grouped(): pl.pallas_call(prefix_kernel, grid_spec=pltpu.PrefetchScalarGridSpec(num_...  19.5 us
    pallas_call x1, Pallas kernels, expert_ffn(): pl.pallas_call(expert_kernel, grid=(exp_dev, inner // chunk), in_specs=[p...  13.9 us
    all_to_all x1, waiting for transfers between devices, per_device(): lax.all_to_all(attended, 'exp', split_axis=0, concat_axis=1, tiled=True)  8.68 us
    all_to_all x1, starting transfers between devices, per_device(): lax.all_to_all(attended, 'exp', split_axis=0, concat_axis=1, tiled=True)  8.08 us
    ppermute x3, starting transfers between devices, per_device(): lax.ppermute(local_kv, 'req', [(i, (i + 2 * s) % req_count) for i in rang...  5.81 us
  transfers between devices with their start and end apart: 9, of which 5 were waited for; matrix products, arithmetic and copies ran while one was open for 13% of the time, Pallas kernels for 10%

profile of v19, /device:TPU:0, one launch (start us, length us, event | category | flops | bytes accessed | tf_op | source)
XLA Modules:
  0.0 200.1 jit_solution(4555057127092990359)
XLA Ops:
  6.5 0.7 all-gather.2.cloned.1.call-update
  7.3 1.3 pad_maximum_fusion.refs_0_.refs_1_
  8.6 1.6 collective-permute-start
  10.2 2.7 %collective-permute-start.1 = (bf16[2,4,512,128]{3,2,1,0:T(8,128)(2,1)S(1)}, bf16[2,4,512,128]{3,2,1,0:T(8,128)(2,1)S(1)}, u32[]{:S(2)}, u32[]{:S(2)}) collective-permute-start(bf16[2,4,512,128]{3,2,1,0:T(8,128)(2,1)S(1)} %pad_maximum_fusion.refs_0_.refs_1_), channel_id=1, source_target_pairs={{0,64},{16,80},{32,96},{48,112},{64,0},{80,16},{96,32},{112,48},{1... | collective-permute-start | bytes 3145736 | tf_op jit(solution)/shard_map/ppermute | solution.py:323
  12.9 1.4 collective-permute-start.2
  14.4 0.0 collective-permute-start.3
  14.4 0.8 reduce_window_sum.44
  15.2 0.1 convert_reduce_fusion.1
  15.3 0.7 subtract_bitcast_fusion
  16.0 0.7 select_reduce_fusion.3
  16.7 0.1 convert_reduce_fusion.2
  16.8 0.2 reduce-window.20
  17.0 1.1 reduce-window.21
  18.2 0.2 slice_reduce_fusion.1
  18.4 0.2 reduce-window.24
  18.6 0.1 add_bitcast_fusion.1
  18.7 0.1 select_reduce_fusion.5
  18.8 3.2 %fusion.9.q_ref = bf16[1792,128]{1,0:T(8,128)(2,1)S(1)} fusion(bf16[1024,128]{1,0:T(8,128)(2,1)} %param.15, s32[1024]{0:T(1024)S(1)} %multiply_add_fusion), kind=kOutput, calls=%fused_computation.15 | convolution fusion | flops 471826432 | bytes 724992 | tf_op jit(solution)/shard_map/dot_general | solution.py:327
  22.0 1.7 select_reduce_fusion.1
  23.7 1.9 fusion.28
  25.6 0.0 copy-start.6
  25.6 1.0 fusion.2
  26.7 0.0 copy-start.10
  26.7 0.0 copy-start.9
  26.7 2.3 %fusion.4 = f32[1792,128]{1,0:T(8,128)} fusion(bf16[1024,128]{1,0:T(8,128)(2,1)S(1)} %copy-done.6, f32[1792,1024]{0,1:T(8,128)S(1)} %get-tuple-element.35, f32[1792]{0:T(1024)S(1)} %get-tuple-element.34), kind=kOutput, calls=%fused_computation.10 | convolution fusion | flops 473432064 | bytes 8526848 | tf_op jit(solution)/shard_map/dot_general | solution.py:274
  29.0 5.7 %collective-permute-done.refs_2_.refs_3_ = bf16[2,4,512,128]{3,2,1,0:T(8,128)(2,1)S(1)} collective-permute-done((bf16[2,4,512,128]{3,2,1,0:T(8,128)(2,1)S(1)}, bf16[2,4,512,128]{3,2,1,0:T(8,128)(2,1)S(1)}, u32[]{:S(2)}, u32[]{:S(2)}) %collective-permute-start) | collective-permute-done | bytes 1048608 | tf_op jit(solution)/shard_map/ppermute | solution.py:323
  34.6 23.6 %collective-permute-done.1.refs_4_.refs_5_ = bf16[2,4,512,128]{3,2,1,0:T(8,128)(2,1)S(1)} collective-permute-done((bf16[2,4,512,128]{3,2,1,0:T(8,128)(2,1)S(1)}, bf16[2,4,512,128]{3,2,1,0:T(8,128)(2,1)S(1)}, u32[]{:S(2)}, u32[]{:S(2)}) %collective-permute-start.1) | collective-permute-done | bytes 1048608 | tf_op jit(solution)/shard_map/ppermute | solution.py:323
  58.3 0.0 collective-permute-done.2.refs_6_.refs_7_
  58.3 0.0 collective-permute-start.4
  58.3 0.5 collective-permute-start.5
  58.8 0.1 collective-permute-start.6
  58.9 0.1 slice.23
  59.0 0.1 copy.61
  59.1 0.1 eq.149
  59.2 0.1 eq.145
  59.3 0.6 reduce-window.30
  59.9 0.2 slice_reduce_fusion
  60.1 0.1 fusion.23
  60.2 0.1 reduce_sum.139
  60.3 0.1 copy.64
  60.4 0.0 copy-done.9
  60.4 0.6 convert_reduce_fusion.3.block_group_ref
  61.0 1.3 copy.57
  62.3 1.3 copy.59
  63.6 0.0 collective-permute-done.3.refs_8_.refs_9_
  63.6 0.0 collective-permute-done.4.refs_10_.refs_11_
  63.6 0.5 collective-permute-done.5.refs_12_.refs_13_
  64.1 0.2 collective-permute-done.6.refs_14_.refs_15_
  64.3 19.5 %shard_map.145 = (f32[1792,128]{1,0:T(8,128)}, f32[1792,128]{1,0:T(8,128)}, f32[1792,128]{1,0:T(8,128)}) custom-call(s32[7]{0:T(128)} %convert_reduce_fusion.3.block_group_ref, bf16[1792,128]{1,0:T(8,128)(2,1)} %copy-done.5, bf16[2,4,512,128]{3,2,1,0:T(8,128)(2,1)} %copy-done.1, bf16[2,4,512,128]{3,2,1,0:T(8,128)(2,1)} %copy-done.1, ...), custom_call_target="tpu_custom_call" | custom-call | flops 3758096384 | bytes 11599872 | tf_op jit(solution)/shard_map/pallas_call | solution.py:153
  83.8 0.0 copy-start.7
  83.9 2.6 %fusion.19 = (f32[1792]{0:T(1024)S(1)}, f32[1792]{0:T(1024)S(1)}, f32[1792]{0:T(1024)S(1)}) fusion(f32[1792,1]{1,0:T(8,128)S(1)} %copy-done.4, f32[1792,128]{1,0:T(8,128)} %get-tuple-element.18, f32[1792,1]{1,0:T(8,128)} %copy.59, f32[1792,128]{1,0:T(8,128)} %get-tuple-element.21), kind=kLoop, calls=%fused_computation.37 | loop fusion | flops 10752 | bytes 50176 | tf_op jit(solution)/shard_map/exp | solution.py:283
  86.4 3.9 %fusion.11 = bf16[1024,128]{1,0:T(8,128)(2,1)} fusion(s32[1024]{0:T(1024)S(1)} %multiply_add_fusion, f32[1792,128]{1,0:T(8,128)} %fusion.4, f32[1792,128]{1,0:T(8,128)} %get-tuple-element.17, f32[1792]{0:T(1024)S(1)} %get-tuple-element.24, f32[1792]{0:T(1024)S(1)} %get-tuple-element.25, f32[1792]{0:T(1024)S(1)} %get-tuple-element.23), kind=kOutput, calls=%fused_computation.21 | convolution fusion | flops 472875008 | bytes 2122752 | tf_op jit(solution)/shard_map/dot_general | solution.py:347
  90.3 8.1 %all-to-all-start = ((bf16[16,64,128]{2,1,0:T(8,128)(2,1)}), bf16[16,64,128]{2,1,0:T(8,128)(2,1)S(1)}, u32[]{:S(2)}, u32[]{:S(2)}) async-start(bf16[16,64,128]{2,1,0:T(8,128)(2,1)} %bitcast.9), calls=%async_computation | async-start | bytes 524288 | tf_op jit(solution)/shard_map/all_to_all | solution.py:352
  98.4 0.2 select_reduce_fusion.2
  98.6 8.7 %all-to-all-done = bf16[16,64,128]{2,1,0:T(8,128)(2,1)S(1)} async-done(((bf16[16,64,128]{2,1,0:T(8,128)(2,1)}), bf16[16,64,128]{2,1,0:T(8,128)(2,1)S(1)}, u32[]{:S(2)}, u32[]{:S(2)}) %all-to-all-start) | async-done | bytes 262176 | tf_op jit(solution)/shard_map/all_to_all | solution.py:352
  107.3 5.1 %multiply_reduce_fusion = (f32[64]{0:T(128)S(1)}, f32[64,2048]{1,0:T(8,128)S(1)}) fusion(bf16[2048,2048]{1,0:T(8,128)(2,1)} %all-gather.2.cloned.1.call-done, bf16[64,2048]{1,0:T(8,128)(2,1)S(1)} %copy-done.7, bf16[16,64,128]{2,1,0:T(8,128)(2,1)S(1)} %all-to-all-done), kind=kOutput, calls=%fused_computation.28 | convolution fusion | flops 537395136 | bytes 9437440 | tf_op jit(solution)/shard_map/dot_general | solution.py:353
  112.3 0.8 convolution_convert_fusion
  113.1 31.0 %all_to_all.29 = bf16[32,16,2048]{2,1,0:T(8,128)(2,1)S(1)} all-to-all(bf16[32,16,2048]{2,1,0:T(8,128)(2,1)S(1)} %bitcast.80), channel_id=1, replica_groups=mesh['req'=8,'exp'=16] {'exp'}, dimensions={0} | all-to-all | bytes 4194304 | tf_op jit(solution)/shard_map/all_to_all | solution.py:371
  144.1 0.1 copy.65
  144.2 2.5 %copy.66 = bf16[2,256,2048]{1,2,0:T(8,128)(2,1)} copy(bf16[2,256,2048]{2,1,0:T(8,128)(2,1)S(1)} %bitcast.82) | data formatting | bytes 4194304 | tf_op jit(solution)/shard_map/reshape | solution.py:375
  146.8 13.9 %shard_map.146 = bf16[2,256,2048]{2,1,0:T(8,128)(2,1)} custom-call(bf16[2,2048,256]{2,1,0:T(8,128)(2,1)} %bitcast.84, bf16[2,704,2048]{2,1,0:T(8,128)(2,1)} %bitcast.86, bf16[2,704,2048]{2,1,0:T(8,128)(2,1)} %bitcast.87, bf16[2,704,2048]{2,1,0:T(8,128)(2,1)} %wd_ref.1), custom_call_target="tpu_custom_call" | custom-call | flops 4429185024 | bytes 21495808 | tf_op jit(solution)/shard_map/pallas_call | solution.py:199
  160.6 1.7 copy.67
  162.4 29.8 %all_to_all.30 = bf16[32,16,2048]{2,1,0:T(8,128)(2,1)S(1)} all-to-all(bf16[32,16,2048]{2,1,0:T(8,128)(2,1)S(1)} %bitcast.83), channel_id=1, replica_groups=mesh['req'=8,'exp'=16] {'exp'}, dimensions={0} | all-to-all | bytes 4194304 | tf_op jit(solution)/shard_map/all_to_all | solution.py:377
  192.1 1.2 fusion.10
  (33 shorter events, 0.2 us)
Async XLA Ops:
  6.5 17.1 %copy-start = (bf16[1024,128]{1,0:T(8,128)(2,1)S(1)}, bf16[1024,128]{1,0:T(8,128)(2,1)}, u32[]{:S(2)}) copy-start(bf16[1024,128]{1,0:T(8,128)(2,1)} %param.16) | copy-start | bytes 786436
  6.5 100.7 %all-gather.2.cloned.1.call-start = ((), (), s32[]{:S(2)}) async-start(), calls=%async_computation.3 | async-start | bytes 8912896 | tf_op jit(solution)/shard_map/all_gather | solution.py:351
  8.6 17.0 %copy-start.1 = (bf16[2,4,512,128]{3,2,1,0:T(8,128)(2,1)}, bf16[2,4,512,128]{3,2,1,0:T(8,128)(2,1)S(1)}, u32[]{:S(2)}) copy-start(bf16[2,4,512,128]{3,2,1,0:T(8,128)(2,1)S(1)} %pad_maximum_fusion.refs_0_.refs_1_) | copy-start | bytes 3145732
  8.6 26.1 %collective-permute-start = (bf16[2,4,512,128]{3,2,1,0:T(8,128)(2,1)S(1)}, bf16[2,4,512,128]{3,2,1,0:T(8,128)(2,1)S(1)}, u32[]{:S(2)}, u32[]{:S(2)}) collective-permute-start(bf16[2,4,512,128]{3,2,1,0:T(8,128)(2,1)S(1)} %pad_maximum_fusion.refs_0_.refs_1_), channel_id=1, source_target_pairs={{0,32},{16,48},{32,64},{48,80},{64,96},{80,112},{96,0},{112,16},{1... | collective-permute-start | bytes 3145736 | tf_op jit(solution)/shard_map/ppermute | solution.py:323
  10.2 48.1 %collective-permute-start.1 = (bf16[2,4,512,128]{3,2,1,0:T(8,128)(2,1)S(1)}, bf16[2,4,512,128]{3,2,1,0:T(8,128)(2,1)S(1)}, u32[]{:S(2)}, u32[]{:S(2)}) collective-permute-start(bf16[2,4,512,128]{3,2,1,0:T(8,128)(2,1)S(1)} %pad_maximum_fusion.refs_0_.refs_1_), channel_id=1, source_target_pairs={{0,64},{16,80},{32,96},{48,112},{64,0},{80,16},{96,32},{112,48},{1... | collective-permute-start | bytes 3145736 | tf_op jit(solution)/shard_map/ppermute | solution.py:323
  12.9 45.3 %collective-permute-start.2 = (bf16[2,4,512,128]{3,2,1,0:T(8,128)(2,1)S(1)}, bf16[2,4,512,128]{3,2,1,0:T(8,128)(2,1)}, u32[]{:S(2)}, u32[]{:S(2)}) collective-permute-start(bf16[2,4,512,128]{3,2,1,0:T(8,128)(2,1)S(1)} %pad_maximum_fusion.refs_0_.refs_1_), channel_id=1, source_target_pairs={{0,96},{16,112},{32,0},{48,16},{64,32},{80,48},{96,64},{112,80},{1... | collective-permute-start | bytes 3145736 | tf_op jit(solution)/shard_map/ppermute | solution.py:323
  14.4 49.2 %collective-permute-start.3 = (bf16[2,4,512,128]{3,2,1,0:T(8,128)(2,1)S(1)}, bf16[2,4,512,128]{3,2,1,0:T(8,128)(2,1)}, u32[]{:S(2)}, u32[]{:S(2)}) collective-permute-start(bf16[2,4,512,128]{3,2,1,0:T(8,128)(2,1)S(1)} %pad_maximum_fusion.refs_0_.refs_1_), channel_id=1, source_target_pairs={{0,16},{16,0},{32,48},{48,32},{64,80},{80,64},{96,112},{112,96},{1... | collective-permute-start | bytes 3145736 | tf_op jit(solution)/shard_map/ppermute | solution.py:321
  22.0 3.6 %copy-start.5 = (bf16[1792,128]{1,0:T(8,128)(2,1)}, bf16[1792,128]{1,0:T(8,128)(2,1)S(1)}, u32[]{:S(2)}) copy-start(bf16[1792,128]{1,0:T(8,128)(2,1)S(1)} %fusion.9.q_ref) | copy-start | bytes 1376260
  25.6 1.1 copy-start.6
  26.7 32.3 %copy-start.8 = (s32[64,4]{0,1:T(4,128)S(1)}, s32[64,4]{0,1:T(4,128)}, u32[]{:S(2)}) copy-start(s32[64,4]{0,1:T(4,128)} %param.25) | copy-start | bytes 3076
  26.7 33.7 %copy-start.10 = (bf16[64,4]{0,1:T(4,128)(2,1)S(1)}, bf16[64,4]{0,1:T(4,128)(2,1)}, u32[]{:S(2)}) copy-start(bf16[64,4]{0,1:T(4,128)(2,1)} %param.26) | copy-start | bytes 1540
  26.7 33.7 %copy-start.9 = (bf16[2048]{0:T(1024)(128)(2,1)S(1)}, bf16[2048]{0:T(1024)(128)(2,1)}, u32[]{:S(2)}) copy-start(bf16[2048]{0:T(1024)(128)(2,1)} %param.24) | copy-start | bytes 12292
  34.6 29.7 %copy-start.2 = (bf16[2,4,512,128]{3,2,1,0:T(8,128)(2,1)}, bf16[2,4,512,128]{3,2,1,0:T(8,128)(2,1)S(1)}, u32[]{:S(2)}) copy-start(bf16[2,4,512,128]{3,2,1,0:T(8,128)(2,1)S(1)} %collective-permute-done.refs_2_.refs_3_) | copy-start | bytes 3145732
  58.3 6.0 %copy-start.3 = (bf16[2,4,512,128]{3,2,1,0:T(8,128)(2,1)}, bf16[2,4,512,128]{3,2,1,0:T(8,128)(2,1)S(1)}, u32[]{:S(2)}) copy-start(bf16[2,4,512,128]{3,2,1,0:T(8,128)(2,1)S(1)} %collective-permute-done.1.refs_4_.refs_5_) | copy-start | bytes 3145732
  58.3 5.3 %collective-permute-start.4 = (bf16[2,4,512,128]{3,2,1,0:T(8,128)(2,1)S(1)}, bf16[2,4,512,128]{3,2,1,0:T(8,128)(2,1)}, u32[]{:S(2)}, u32[]{:S(2)}) collective-permute-start(bf16[2,4,512,128]{3,2,1,0:T(8,128)(2,1)S(1)} %collective-permute-done.refs_2_.refs_3_), channel_id=1, source_target_pairs={{0,16},{16,0},{32,48},{48,32},{64,80},{80,64},{96,112},{112,96},{1... | collective-permute-start | bytes 3145736 | tf_op jit(solution)/shard_map/ppermute | solution.py:340
  58.3 5.8 %collective-permute-start.5 = (bf16[2,4,512,128]{3,2,1,0:T(8,128)(2,1)S(1)}, bf16[2,4,512,128]{3,2,1,0:T(8,128)(2,1)}, u32[]{:S(2)}, u32[]{:S(2)}) collective-permute-start(bf16[2,4,512,128]{3,2,1,0:T(8,128)(2,1)S(1)} %collective-permute-done.1.refs_4_.refs_5_), channel_id=1, source_target_pairs={{0,16},{16,0},{32,48},{48,32},{64,80},{80,64},{96,112},{112,96},{1... | collective-permute-start | bytes 3145736 | tf_op jit(solution)/shard_map/ppermute | solution.py:340
  58.8 5.5 %collective-permute-start.6 = (bf16[2,4,512,128]{3,2,1,0:T(8,128)(2,1)}, bf16[2,4,512,128]{3,2,1,0:T(8,128)(2,1)}, u32[]{:S(2)}, u32[]{:S(2)}) collective-permute-start(bf16[2,4,512,128]{3,2,1,0:T(8,128)(2,1)} %collective-permute-done.2.refs_6_.refs_7_), channel_id=1, source_target_pairs={{0,16},{16,0},{32,48},{48,32},{64,80},{80,64},{96,112},{112,96},{1... | collective-permute-start | bytes 3145736 | tf_op jit(solution)/shard_map/ppermute | solution.py:340
  63.6 20.3 %copy-start.4 = (f32[1792,1]{1,0:T(8,128)S(1)}, f32[1792,1]{1,0:T(8,128)}, u32[]{:S(2)}) copy-start(f32[1792,1]{1,0:T(8,128)} %copy.57) | copy-start | bytes 21508
  83.8 23.4 %copy-start.7 = (bf16[64,2048]{1,0:T(8,128)(2,1)S(1)}, bf16[64,2048]{1,0:T(8,128)(2,1)}, u32[]{:S(2)}) copy-start(bf16[64,2048]{1,0:T(8,128)(2,1)} %param.22) | copy-start | bytes 786436
  90.3 16.9 %all-to-all-start = ((bf16[16,64,128]{2,1,0:T(8,128)(2,1)}), bf16[16,64,128]{2,1,0:T(8,128)(2,1)S(1)}, u32[]{:S(2)}, u32[]{:S(2)}) async-start(bf16[16,64,128]{2,1,0:T(8,128)(2,1)} %bitcast.9), calls=%async_computation | async-start | bytes 524288 | tf_op jit(solution)/shard_map/all_to_all | solution.py:352
Sparse Core Ops, SparseCore 0:
  9.5 73.3 all-gather.1
